TPU v7x, 32 devices: a whole 2x2x4 slice. The times are simulated.
32 devices in a mesh: dp: 16 (over z, x, core), tensor: 2 (over y).
Axes of the slice: x: 2, y: 2, z: 4, core: 2. Of those that a mesh axis runs over, the one named last changes fastest.
Arguments:
- layer_in: bfloat16 [8192, 1536], P(('dp', 'tensor')), may hold values from -6 to 6
- segment_ids: int32 [16, 512], P('dp'), may hold values from 0 to 1, never falling along the last dimension, each value on 1 to 384 neighbouring positions
- norm1_gain: bfloat16 [1536], P('dp'), may hold values from 0.5 to 1.5
- w_query: bfloat16 [1536, 1536], P('dp', 'tensor'), may hold values from -0.15625 to 0.15625
- w_key: bfloat16 [1536, 1536], P('dp', 'tensor'), may hold values from -0.15625 to 0.15625
- w_value: bfloat16 [1536, 1536], P('dp', 'tensor'), may hold values from -0.15625 to 0.15625
- w_forget: bfloat16 [1536, 24], P('dp', 'tensor'), may hold values from -0.15625 to 0.15625
- forget_bias: float32 [24], P('tensor'), may hold values from 2 to 7
- w_output: bfloat16 [1536, 1536], P('dp', 'tensor'), may hold values from -0.625 to 0.625
- norm2_gain: bfloat16 [1536], P('dp'), may hold values from 0.5 to 1.5
- w_gate: bfloat16 [1536, 4096], P('dp', 'tensor'), may hold values from -0.15625 to 0.15625
- w_up: bfloat16 [1536, 4096], P('dp', 'tensor'), may hold values from -0.15625 to 0.15625
- w_down: bfloat16 [1536, 4096], P('dp', 'tensor'), may hold values from -0.09375 to 0.09375
- clip_tau: float32 [24], P('tensor'), may hold values from 2 to 6
- out_grad: bfloat16 [8192, 1536], P(('dp', 'tensor')), may hold values from -6 to 6
Outputs:
- layer_out: bfloat16 [8192, 1536], P(('dp', 'tensor'))
- x_grad: bfloat16 [8192, 1536], P(('dp', 'tensor'))
- g_norm1: float32 [1536], P('tensor')
- g_query: float32 [1536, 1536], P('dp', 'tensor')
- g_key: float32 [1536, 1536], P('dp', 'tensor')
- g_value: float32 [1536, 1536], P('dp', 'tensor')
- g_forget: float32 [1536, 24], P('dp', 'tensor')
- g_bias: float32 [24], P('tensor')
- g_output: float32 [1536, 1536], P('dp', 'tensor')
- g_norm2: float32 [1536], P('tensor')
- g_gate: float32 [1536, 4096], P('dp', 'tensor')
- g_up: float32 [1536, 4096], P('dp', 'tensor')
- g_down: float32 [1536, 4096], P('dp', 'tensor')
- clip_factor: float32 [24], P('tensor')
- clipped_query: bfloat16 [1536, 1536], P('dp', 'tensor')
- clipped_key: bfloat16 [1536, 1536], P('dp', 'tensor')
Inputs may be any that keep to these rules, and one draw needn't show every extreme that they name: `segment_ids`: segment numbers never fall along a pack; each segment has 1 to 384 positions.
All inputs are finite; a program needn't handle non-finite values.
Results may differ from a plain program's by a relative error of at most 0.02.
Values may be sent and summed in bfloat16 or wider, within the bound.
No kernel may reach another device: no remote copies, remote signals or barrier semaphores. Data moves between devices by JAX's collectives and lax.ppermute only.
A program may use at most 192 MiB of HBM per device.

v0:
```python
import math

import jax
import jax.numpy as jnp
from jax import lax
from jax.sharding import PartitionSpec as P

HEAD_DIM = 64
BLOCK = 256


EPSILON = 1e-06
HIGHEST = lax.Precision.HIGHEST
NEGATIVE = -1e30


def combined_all(part, axis, combine):
    gathered = jax.tree.map(lambda a: lax.all_gather(a, axis), part)

    def take(source):
        return jax.tree.map(lambda a: lax.dynamic_index_in_dim(a, source, 0, False), gathered)

    return lax.fori_loop(
        1, lax.axis_size(axis), lambda source, state: combine(state, take(source)), take(0)
    )


def contract_last(left_op, right_op):
    return lax.dot_general(
        left_op, right_op, (((1,), (1,)), ((), ())), preferred_element_type=jnp.float32
    )


def contract_first(left_op, right_op):
    return lax.dot_general(
        left_op, right_op, (((0,), (0,)), ((), ())), preferred_element_type=jnp.float32
    )


def block_terms(q_blk, keys_all, cumul, seg_row, offset, rows_blk):
    positions = jnp.arange(keys_all.shape[0], dtype=jnp.int32)
    q_pos = offset + jnp.arange(rows_blk, dtype=jnp.int32)
    allowed = (seg_row[:, None] == seg_row[None, :]) & (
        q_pos[:, None] // BLOCK >= positions[None, :] // BLOCK
    )
    signs = jnp.where(positions[None, :] <= q_pos[:, None], 1.0, -1.0).astype(jnp.float32)
    raw_blk = jnp.einsum("qhe,khe->hqk", q_blk, keys_all, preferred_element_type=jnp.float32) * (
        1.0 / math.sqrt(HEAD_DIM)
    )
    differ = cumul.T[:, :, None] - cumul.T[:, None, :]
    scores = jnp.where(allowed[None], raw_blk + signs[None] * differ, NEGATIVE)
    return (raw_blk, scores, allowed, signs)


def combine(former, latter):
    return (
        jnp.maximum(former[0], latter[0]),
        former[1] + latter[1],
        former[2] + latter[2],
        former[3] + latter[3],
    )


def body(
    layer_in,
    segment_ids,
    norm1_gain,
    w_query,
    w_key,
    w_value,
    w_forget,
    forget_bias,
    w_output,
    norm2_gain,
    w_gate,
    w_up,
    w_down,
    clip_tau,
    out_grad,
):
    gain_one, wq_all, wk_all, wv_all, wf_all, wo_all, gain_two, wg_all, wu_all, wd_all = (
        lax.all_gather(norm1_gain, "dp", axis=0, tiled=True),
        lax.all_gather(w_query, "dp", axis=0, tiled=True),
        lax.all_gather(w_key, "dp", axis=0, tiled=True),
        lax.all_gather(w_value, "dp", axis=0, tiled=True),
        lax.all_gather(w_forget, "dp", axis=0, tiled=True),
        lax.all_gather(w_output, "dp", axis=0, tiled=True),
        lax.all_gather(norm2_gain, "dp", axis=0, tiled=True),
        lax.all_gather(w_gate, "dp", axis=0, tiled=True),
        lax.all_gather(w_up, "dp", axis=0, tiled=True),
        lax.all_gather(w_down, "dp", axis=0, tiled=True),
    )
    gain_one = gain_one.astype(jnp.float32)
    gain_two = gain_two.astype(jnp.float32)
    tok_local = layer_in.shape[0]
    tokens = tok_local * lax.axis_size("tensor")
    heads_loc = forget_bias.shape[0]
    row_start = lax.axis_index("tensor") * tok_local
    seg_row = segment_ids[0]
    factor = 1.0 / math.sqrt(HEAD_DIM)
    rows_full = lax.all_gather(layer_in, "tensor", axis=0, tiled=True).astype(jnp.float32)
    scale_one = lax.rsqrt(jnp.mean(rows_full * rows_full, axis=1, keepdims=True) + EPSILON)
    unit_one = rows_full * scale_one
    normed_one = (unit_one * gain_one).astype(jnp.bfloat16)
    queries = (
        jnp.dot(normed_one, wq_all, preferred_element_type=jnp.float32)
        .astype(jnp.bfloat16)
        .reshape(tokens, heads_loc, HEAD_DIM)
    )
    keys_all = (
        jnp.dot(normed_one, wk_all, preferred_element_type=jnp.float32)
        .astype(jnp.bfloat16)
        .reshape(tokens, heads_loc, HEAD_DIM)
    )
    values_all = (
        jnp.dot(normed_one, wv_all, preferred_element_type=jnp.float32)
        .astype(jnp.bfloat16)
        .reshape(tokens, heads_loc, HEAD_DIM)
    )
    logits = jnp.dot(normed_one, wf_all, preferred_element_type=jnp.float32) + forget_bias
    cumul = jnp.cumsum(jax.nn.log_sigmoid(logits), axis=0)
    rows_blk = min(512, tokens)
    blocks = tokens // rows_blk
    numbers = jnp.arange(blocks, dtype=jnp.int32)

    def forward_block(number):
        offset = number * rows_blk
        raw_blk, scores, allowed, signs = block_terms(
            queries, keys_all, cumul, seg_row, offset, rows_blk
        )
        top_blk = jnp.max(jnp.where(allowed[None], raw_blk, NEGATIVE), axis=(1, 2))
        row_peak = jnp.max(scores, axis=2, keepdims=True)
        expo_blk = jnp.exp(scores - row_peak)
        totals = jnp.sum(expo_blk, axis=2, keepdims=True)
        weights = (expo_blk / totals).astype(jnp.bfloat16)
        mixed_out = jnp.einsum(
            "hqk,khe->qhe", weights, values_all, preferred_element_type=jnp.float32
        ).astype(jnp.bfloat16)
        return (mixed_out, (row_peak + jnp.log(totals))[:, :, 0], top_blk)

    mixed_out, log_sums, top_blk = lax.map(forward_block, numbers)
    mixed_flat = mixed_out.reshape(tokens, heads_loc * HEAD_DIM)
    maxima = jnp.max(top_blk, axis=0)
    attn_part = contract_last(mixed_flat, wo_all)
    resid_full = rows_full + lax.psum(attn_part.astype(jnp.bfloat16), "tensor").astype(jnp.float32)
    scale_full = lax.rsqrt(jnp.mean(resid_full * resid_full, axis=1, keepdims=True) + EPSILON)
    normed_two = (resid_full * scale_full * gain_two).astype(jnp.bfloat16)
    resid_part = lax.dynamic_slice_in_dim(resid_full, row_start, tok_local, 0)
    scale_two = lax.dynamic_slice_in_dim(scale_full, row_start, tok_local, 0)
    gate_pre = jnp.dot(normed_two, wg_all, preferred_element_type=jnp.float32)
    up_pre = jnp.dot(normed_two, wu_all, preferred_element_type=jnp.float32)
    gate_sig = jax.nn.sigmoid(gate_pre)
    gate_act = gate_pre * gate_sig
    hidden = (gate_act * up_pre).astype(jnp.bfloat16)
    ffn_part = lax.psum_scatter(
        contract_last(hidden, wd_all).astype(jnp.bfloat16),
        "tensor",
        scatter_dimension=0,
        tiled=True,
    ).astype(jnp.float32)
    layer_out = (resid_part + ffn_part).astype(jnp.bfloat16)
    grad_full = lax.all_gather(out_grad, "tensor", axis=0, tiled=True)
    grad_hidden = jnp.dot(grad_full, wd_all, preferred_element_type=jnp.float32)
    grad_gate = (grad_hidden * up_pre * gate_sig * (1.0 + gate_pre * (1.0 - gate_sig))).astype(
        jnp.bfloat16
    )
    grad_up = (grad_hidden * gate_act).astype(jnp.bfloat16)
    g_down = contract_first(grad_full, hidden)
    g_gate = contract_first(normed_two, grad_gate)
    g_up = contract_first(normed_two, grad_up)
    grad_normed = contract_last(grad_gate, wg_all) + contract_last(grad_up, wu_all)
    grad_two = lax.psum_scatter(
        grad_normed.astype(jnp.bfloat16), "tensor", scatter_dimension=0, tiled=True
    ).astype(jnp.float32)
    unit_two = resid_part * scale_two
    inner_two = jnp.mean(unit_two * gain_two * grad_two, axis=1, keepdims=True)
    norm2_part = jnp.sum(grad_two * unit_two, axis=0)
    grad_resid = out_grad.astype(jnp.float32) + scale_two * (
        gain_two * grad_two - unit_two * inner_two
    )
    grad_attn = lax.all_gather(grad_resid.astype(jnp.bfloat16), "tensor", axis=0, tiled=True)
    g_output = contract_first(grad_attn, mixed_flat)
    grad_mixed = jnp.dot(grad_attn, wo_all, preferred_element_type=jnp.float32).astype(jnp.bfloat16)
    grad_mixed = grad_mixed.reshape(blocks, rows_blk, heads_loc, HEAD_DIM)

    def backward_block(carried, block_in):
        key_acc, value_acc, column_acc = carried
        number, log_blk, grad_blk = block_in
        offset = number * rows_blk
        raw_blk, scores, allowed, signs = block_terms(
            queries, keys_all, cumul, seg_row, offset, rows_blk
        )
        prob_blk = jnp.exp(scores - log_blk[:, :, None])
        weights = prob_blk.astype(jnp.bfloat16)
        grad_prob = jnp.einsum(
            "qhe,khe->hqk", grad_blk, values_all, preferred_element_type=jnp.float32
        )
        inner = jnp.sum(prob_blk * grad_prob, axis=2, keepdims=True)
        grad_scores = (prob_blk * (grad_prob - inner)).astype(jnp.bfloat16)
        value_acc = value_acc + jnp.einsum(
            "hqk,qhe->khe", weights, grad_blk, preferred_element_type=jnp.float32
        )
        key_acc = key_acc + jnp.einsum(
            "hqk,qhe->khe", grad_scores, queries, preferred_element_type=jnp.float32
        )
        grad_query = (
            jnp.einsum("hqk,khe->qhe", grad_scores, keys_all, preferred_element_type=jnp.float32)
            * factor
        ).astype(jnp.bfloat16)
        signed = grad_scores.astype(jnp.float32) * signs[None]
        column_acc = column_acc - jnp.sum(signed, axis=1).T
        return ((key_acc, value_acc, column_acc), (grad_query, jnp.sum(signed, axis=2).T))

    start_acc = (
        jnp.zeros((tokens, heads_loc, HEAD_DIM), jnp.float32),
        jnp.zeros((tokens, heads_loc, HEAD_DIM), jnp.float32),
        jnp.zeros((tokens, heads_loc), jnp.float32),
    )
    (key_acc, value_acc, column_acc), (grad_query, row_parts) = lax.scan(
        backward_block, start_acc, (numbers, log_sums, grad_mixed)
    )
    grad_q = grad_query.reshape(tokens, heads_loc * HEAD_DIM)
    grad_k = (key_acc * factor).astype(jnp.bfloat16).reshape(tokens, heads_loc * HEAD_DIM)
    grad_v = value_acc.astype(jnp.bfloat16).reshape(tokens, heads_loc * HEAD_DIM)
    grad_cum = row_parts.reshape(tokens, heads_loc) + column_acc
    grad_logs = jnp.cumsum(grad_cum[::-1], axis=0)[::-1]
    grad_logit = grad_logs * jax.nn.sigmoid(-logits)
    g_bias = jnp.sum(grad_logit, axis=0)
    g_forget = jnp.einsum(
        "td,th->dh", normed_one, grad_logit, precision=HIGHEST, preferred_element_type=jnp.float32
    )
    g_query = contract_first(normed_one, grad_q)
    g_key = contract_first(normed_one, grad_k)
    g_value = contract_first(normed_one, grad_v)
    grad_one = (
        contract_last(grad_q, wq_all)
        + contract_last(grad_k, wk_all)
        + contract_last(grad_v, wv_all)
    )
    grad_one = grad_one + jnp.einsum(
        "th,dh->td", grad_logit, wf_all, precision=HIGHEST, preferred_element_type=jnp.float32
    )
    weighted = gain_one * grad_one
    grad_rows_one = scale_one * (
        weighted - unit_one * jnp.mean(unit_one * weighted, axis=1, keepdims=True)
    )
    norm1_part = jnp.sum(grad_one * unit_one, axis=0)
    grad_input, g_norm1_part, g_norm2_part = (
        lax.psum_scatter(
            grad_rows_one.astype(jnp.bfloat16), "tensor", scatter_dimension=0, tiled=True
        ).astype(jnp.float32),
        lax.psum_scatter(
            norm1_part.astype(jnp.bfloat16), "tensor", scatter_dimension=0, tiled=True
        ).astype(jnp.float32),
        lax.psum_scatter(
            norm2_part.astype(jnp.bfloat16), "tensor", scatter_dimension=0, tiled=True
        ).astype(jnp.float32),
    )
    x_grad = (grad_resid + grad_input).astype(jnp.bfloat16)
    g_query, g_key, g_value, g_forget, g_output, g_gate, g_up, g_down = (
        lax.psum_scatter(
            g_query.astype(jnp.bfloat16), "dp", scatter_dimension=0, tiled=True
        ).astype(jnp.float32),
        lax.psum_scatter(g_key.astype(jnp.bfloat16), "dp", scatter_dimension=0, tiled=True).astype(
            jnp.float32
        ),
        lax.psum_scatter(
            g_value.astype(jnp.bfloat16), "dp", scatter_dimension=0, tiled=True
        ).astype(jnp.float32),
        lax.psum_scatter(
            g_forget.astype(jnp.bfloat16), "dp", scatter_dimension=0, tiled=True
        ).astype(jnp.float32),
        lax.psum_scatter(
            g_output.astype(jnp.bfloat16), "dp", scatter_dimension=0, tiled=True
        ).astype(jnp.float32),
        lax.psum_scatter(g_gate.astype(jnp.bfloat16), "dp", scatter_dimension=0, tiled=True).astype(
            jnp.float32
        ),
        lax.psum_scatter(g_up.astype(jnp.bfloat16), "dp", scatter_dimension=0, tiled=True).astype(
            jnp.float32
        ),
        lax.psum_scatter(g_down.astype(jnp.bfloat16), "dp", scatter_dimension=0, tiled=True).astype(
            jnp.float32
        ),
    )
    maxima, g_bias, g_norm1, g_norm2 = combined_all(
        (maxima, g_bias, g_norm1_part, g_norm2_part), "dp", combine
    )
    clip_factor = jnp.minimum(1.0, clip_tau / jnp.maximum(maxima, 1.0))
    columns = jnp.repeat(jnp.sqrt(clip_factor), HEAD_DIM)
    clipped_query = (w_query.astype(jnp.float32) * columns[None, :]).astype(jnp.bfloat16)
    clipped_key = (w_key.astype(jnp.float32) * columns[None, :]).astype(jnp.bfloat16)
    return (
        layer_out,
        x_grad,
        g_norm1,
        g_query,
        g_key,
        g_value,
        g_forget,
        g_bias,
        g_output,
        g_norm2,
        g_gate,
        g_up,
        g_down,
        clip_factor,
        clipped_query,
        clipped_key,
    )


def solution(mesh):
    return jax.shard_map(
        body,
        mesh=mesh,
        in_specs=(
            P(("dp", "tensor"), None),
            P("dp", None),
            P("dp"),
            P("dp", "tensor"),
            P("dp", "tensor"),
            P("dp", "tensor"),
            P("dp", "tensor"),
            P("tensor"),
            P("dp", "tensor"),
            P("dp"),
            P("dp", "tensor"),
            P("dp", "tensor"),
            P("dp", "tensor"),
            P("tensor"),
            P(("dp", "tensor"), None),
        ),
        out_specs=(
            P(("dp", "tensor"), None),
            P(("dp", "tensor"), None),
            P("tensor"),
            P("dp", "tensor"),
            P("dp", "tensor"),
            P("dp", "tensor"),
            P("dp", "tensor"),
            P("tensor"),
            P("dp", "tensor"),
            P("tensor"),
            P("dp", "tensor"),
            P("dp", "tensor"),
            P("dp", "tensor"),
            P("tensor"),
            P("dp", "tensor"),
            P("dp", "tensor"),
        ),
        check_vma=False,
    )
```

profile of v0, /device:TPU:0, one launch (start us, length us, event | category | flops | bytes accessed | tf_op | source)
XLA Modules:
  0.0 1251.9 jit_solution(14118993441883551326)
XLA Ops:
  14.4 35.4 %all-reduce.7 = (bf16[1536]{0:T(1024)(128)(2,1)S(1)}, bf16[1536]{0:T(1024)(128)(2,1)S(1)}) all-reduce(bf16[1536]{0:T(1024)(128)(2,1)S(1)} %dynamic-update-slice.1, bf16[1536]{0:T(1024)(128)(2,1)S(1)} %dynamic-update-slice), channel_id=1, replica_groups=mesh['dp'=16,'tensor'=2] {'dp'}, use_global_device_ids=true, to_apply=%add.1 | all-reduce | flops 3072 | bytes 12288
  49.8 17.8 %all-gather.4 = bf16[16,96,12]{1,2,0:T(8,128)(2,1)S(1)} all-gather(bf16[1,96,12]{1,2,0:T(8,128)(2,1)} %bitcast.153), channel_id=1, replica_groups=mesh['dp'=16,'tensor'=2] {'dp'}, dimensions={0}, use_global_device_ids=true | all-gather | bytes 39168 | tf_op jit(solution)/shard_map/all_gather | solution.py:86
  70.8 2.0 fusion.36
  74.3 9.9 all-gather.24.cloned.1.call-done
  84.2 4.0 convolution_convert_fusion.11
  88.2 39.4 %all-gather.22.cloned.1.call-done = bf16[1536,768]{1,0:T(8,128)(2,1)} async-done(((bf16[96,768]{1,0:T(8,128)(2,1)}), bf16[1536,768]{1,0:T(8,128)(2,1)}) %all-gather.22.cloned.1.call-update) | async-done | bytes 2359312 | tf_op jit(solution)/shard_map/all_gather | solution.py:83
  127.6 4.0 convolution_convert_fusion.12
  131.6 39.2 %all-gather.20.cloned.1.call-done = bf16[1536,768]{1,0:T(8,128)(2,1)} async-done(((bf16[96,768]{1,0:T(8,128)(2,1)}), bf16[1536,768]{1,0:T(8,128)(2,1)}) %all-gather.20.cloned.1.call-update) | async-done | bytes 2359312 | tf_op jit(solution)/shard_map/all_gather | solution.py:85
  170.8 4.0 convolution_convert_fusion.13
  174.8 2.3 copy.63
  177.1 2.3 copy.62
  179.4 2.3 copy.61
  181.7 5.8 fusion.54
  187.5 8.5 select_reduce_fusion
  196.0 6.4 fusion.34
  202.4 11.6 all-gather.26.cloned.1.call-done
  214.0 4.5 convolution_convert_fusion.8
  221.4 47.5 %all-reduce.11.cloned.1.call-done = bf16[512,1536]{1,0:T(8,128)(2,1)} async-done(((bf16[512,1536]{1,0:T(8,128)(2,1)}), bf16[512,1536]{1,0:T(8,128)(2,1)}) %all-reduce.11.cloned.1.call-update) | async-done | bytes 1572880 | tf_op jit(solution)/shard_map/psum | solution.py:145
  268.9 3.7 convert_add_fusion
  274.4 58.3 %all-gather.28.cloned.1.call-done = bf16[1536,2048]{1,0:T(8,128)(2,1)} async-done(((bf16[96,2048]{1,0:T(8,128)(2,1)}), bf16[1536,2048]{1,0:T(8,128)(2,1)}) %all-gather.28.cloned.1.call-update) | async-done | bytes 6291472 | tf_op jit(solution)/shard_map/all_gather | solution.py:89
  332.6 8.6 fusion.58
  341.3 53.8 %all-gather.30.cloned.1.call-done = bf16[1536,2048]{1,0:T(8,128)(2,1)} async-done(((bf16[96,2048]{1,0:T(8,128)(2,1)}), bf16[1536,2048]{1,0:T(8,128)(2,1)}) %all-gather.30.cloned.1.call-update) | async-done | bytes 6291472 | tf_op jit(solution)/shard_map/all_gather | solution.py:90
  395.1 8.7 fusion.59
  403.7 18.8 %all-gather.34.cloned.1.call-done = bf16[512,1536]{1,0:T(8,128)(2,1)} async-done(((bf16[256,1536]{1,0:T(8,128)(2,1)}), bf16[512,1536]{1,0:T(8,128)(2,1)}) %all-gather.34.cloned.1.call-update) | async-done | bytes 1572880 | tf_op jit(solution)/shard_map/all_gather | solution.py:162
  422.5 63.6 %all-gather.32.cloned.1.call-done = bf16[1536,2048]{1,0:T(8,128)(2,1)} async-done(((bf16[96,2048]{1,0:T(8,128)(2,1)}), bf16[1536,2048]{1,0:T(8,128)(2,1)}) %all-gather.32.cloned.1.call-update) | async-done | bytes 6291472 | tf_op jit(solution)/shard_map/all_gather | solution.py:91
  486.1 11.7 multiply_convert_fusion.1
  497.8 7.1 fusion.60
  505.0 4.7 fusion.25
  509.8 24.9 %reduce-scatter.18.cloned.1.call-done = bf16[256,1536]{1,0:T(8,128)(2,1)} async-done(((bf16[512,1536]{1,0:T(8,128)(2,1)}), bf16[256,1536]{1,0:T(8,128)(2,1)}) %reduce-scatter.18.cloned.1.call-update) | async-done | bytes 786448 | tf_op jit(solution)/shard_map/reduce_scatter | solution.py:172
  534.7 2.2 fusion.30
  537.0 3.2 fusion.45
  540.3 27.3 %all-gather.36.cloned.1.call-done = bf16[512,1536]{1,0:T(8,128)(2,1)} async-done(((bf16[256,1536]{1,0:T(8,128)(2,1)}), bf16[512,1536]{1,0:T(8,128)(2,1)}) %all-gather.36.cloned.1.call-update) | async-done | bytes 1572880 | tf_op jit(solution)/shard_map/all_gather | solution.py:181
  567.6 4.4 convolution_convert_fusion.10
  572.0 2.3 copy.68
  574.3 12.1 multiply_reduce_fusion
  586.5 11.1 fusion.4
  601.8 8.0 convolution_convert_fusion.7
  610.1 4.4 multiply_convert_fusion.6
  615.0 2.0 multiply_convert_fusion.5
  622.0 4.8 fusion.31
  629.2 2.4 fusion.23
  631.6 1.9 fusion.22
  633.9 3.0 convolution_convert_fusion.6
  637.0 3.0 convolution_convert_fusion.5
  640.1 3.0 convolution_convert_fusion.4
  643.3 4.3 convolution_convert_fusion.3
  647.7 7.0 fusion.8
  654.7 8.7 copy.81
  664.8 7.1 convolution_convert_fusion.2
  672.3 7.0 convolution_convert_fusion.1
  681.9 33.2 %all-reduce.6 = (f32[192]{0:T(256)S(1)}, f32[192]{0:T(256)S(1)}) all-reduce(f32[192]{0:T(256)S(1)} %dynamic-update-slice.2, f32[192]{0:T(256)S(1)} %dynamic-update-slice.3), channel_id=2, replica_groups=mesh['dp'=16,'tensor'=2] {'dp'}, use_global_device_ids=true, to_apply=%add.2 | all-reduce | flops 384 | bytes 3072
  717.4 5.0 all-reduce.8
  722.6 17.2 %all-gather.5 = f32[16,1,768]{2,1,0:T(1,128)S(1)} all-gather(f32[1,1,768]{2,1,0:T(1,128)S(1)} %reshape.344), channel_id=4, replica_groups=mesh['dp'=16,'tensor'=2] {'dp'}, dimensions={0}, use_global_device_ids=true | all-gather | bytes 52224 | tf_op jit(solution)/shard_map/all_gather | solution.py:18
  739.8 19.4 %all-gather.6 = f32[16,1,768]{2,1,0:T(1,128)S(1)} all-gather(f32[1,1,768]{2,1,0:T(1,128)S(1)} %reshape.346), channel_id=5, replica_groups=mesh['dp'=16,'tensor'=2] {'dp'}, dimensions={0}, use_global_device_ids=true | all-gather | bytes 52224 | tf_op jit(solution)/shard_map/all_gather | solution.py:18
  759.3 20.1 %while.6 = (s32[]{:T(128)}, f32[12]{0:T(128)}, f32[12]{0:T(128)}, f32[768]{0:T(1024)S(1)}, f32[768]{0:T(1024)S(1)}, /*index=5*/f32[16,12]{1,0:T(8,128)}, f32[16,...) while((s32[]{:T(128)}, f32[12]{0:T(128)}, f32[12]{0:T(128)}, ...), condition=%wide.region_24.25_spmd, body=%wide.region_23.24_spmd.sunk | while | flops 1565 | bytes 31175 | solution.py:23
  782.9 3.7 add_convert_fusion
  788.3 58.2 %reduce-scatter.24.cloned.1.call-done = bf16[96,768]{1,0:T(8,128)(2,1)} async-done(((bf16[1536,768]{1,0:T(8,128)(2,1)}), bf16[96,768]{1,0:T(8,128)(2,1)}) %reduce-scatter.24.cloned.1.call-update) | async-done | bytes 147472 | tf_op jit(solution)/shard_map/reduce_scatter | solution.py:264
  848.1 64.2 %reduce-scatter.26.cloned.1.call-done = bf16[96,768]{1,0:T(8,128)(2,1)} async-done(((bf16[1536,768]{1,0:T(8,128)(2,1)}), bf16[96,768]{1,0:T(8,128)(2,1)}) %reduce-scatter.26.cloned.1.call-update) | async-done | bytes 147472 | tf_op jit(solution)/shard_map/reduce_scatter | solution.py:267
  914.0 64.4 %reduce-scatter.28.cloned.1.call-done = bf16[96,768]{1,0:T(8,128)(2,1)} async-done(((bf16[1536,768]{1,0:T(8,128)(2,1)}), bf16[96,768]{1,0:T(8,128)(2,1)}) %reduce-scatter.28.cloned.1.call-update) | async-done | bytes 147472 | tf_op jit(solution)/shard_map/reduce_scatter | solution.py:273
  980.0 86.3 %reduce-scatter.36.cloned.1.call-done = bf16[96,2048]{1,0:T(8,128)(2,1)} async-done(((bf16[1536,2048]{1,0:T(8,128)(2,1)}), bf16[96,2048]{1,0:T(8,128)(2,1)}) %reduce-scatter.36.cloned.1.call-update) | async-done | bytes 393232
  1068.7 85.8 %reduce-scatter.30.cloned.1.call-done = bf16[96,2048]{1,0:T(8,128)(2,1)} async-done(((bf16[1536,2048]{1,0:T(8,128)(2,1)}), bf16[96,2048]{1,0:T(8,128)(2,1)}) %reduce-scatter.30.cloned.1.call-update) | async-done | bytes 393232 | tf_op jit(solution)/shard_map/reduce_scatter | solution.py:276
  1154.5 1.9 convert_element_type.234
  1156.4 86.2 %reduce-scatter.32.cloned.1.call-done = bf16[96,2048]{1,0:T(8,128)(2,1)} async-done(((bf16[1536,2048]{1,0:T(8,128)(2,1)}), bf16[96,2048]{1,0:T(8,128)(2,1)}) %reduce-scatter.32.cloned.1.call-update) | async-done | bytes 393232 | tf_op jit(solution)/shard_map/reduce_scatter | solution.py:279
  1242.6 1.9 convert_element_type.236
  (274 shorter events, 66.0 us)
Async XLA Ops:
  7.2 63.6 %copy-start.29 = (f32[12]{0:T(128)S(1)}, f32[12]{0:T(128)}, u32[]{:S(2)}) copy-start(f32[12]{0:T(128)} %param.24) | copy-start | bytes 148
  7.2 61.6 %all-gather.18.cloned.1.call-start = ((), (), s32[]{:S(2)}) async-start(), calls=%async_computation.11 | async-start | bytes 2359296 | tf_op jit(solution)/shard_map/all_gather | solution.py:101
  7.9 76.3 %all-gather.24.cloned.1.call-start = ((), (), s32[]{:S(2)}) async-start(), calls=%async_computation.14 | async-start | bytes 2506752 | tf_op jit(solution)/shard_map/all_gather | solution.py:84
  8.7 118.9 %all-gather.22.cloned.1.call-start = ((), (), s32[]{:S(2)}) async-start(), calls=%async_computation.13 | async-start | bytes 2506752 | tf_op jit(solution)/shard_map/all_gather | solution.py:83
  9.4 161.4 %all-gather.20.cloned.1.call-start = ((), (), s32[]{:S(2)}) async-start(), calls=%async_computation.12 | async-start | bytes 2506752 | tf_op jit(solution)/shard_map/all_gather | solution.py:85
  10.0 204.0 %all-gather.26.cloned.1.call-start = ((), (), s32[]{:S(2)}) async-start(), calls=%async_computation.15 | async-start | bytes 2506752 | tf_op jit(solution)/shard_map/all_gather | solution.py:87
  10.6 258.4 %all-reduce.11.cloned.1.call-start = ((), (), s32[]{:S(2)}) async-start(), calls=%async_computation.16 | async-start | bytes 3145728 | tf_op jit(solution)/shard_map/psum | solution.py:145
  68.8 15.4 %copy-start.1 = (bf16[512,1536]{1,0:T(8,128)(2,1)S(1)}, bf16[512,1536]{1,0:T(8,128)(2,1)}, u32[]{:S(2)}) copy-start(bf16[512,1536]{1,0:T(8,128)(2,1)} %all-gather.18.cloned.1.call-done) | copy-start | bytes 4718596
  187.5 8.5 copy-start
  187.5 8.5 copy-start.15
  218.5 114.1 %all-gather.28.cloned.1.call-start = ((), (), s32[]{:S(2)}) async-start(), calls=%async_computation.17 | async-start | bytes 6684672 | tf_op jit(solution)/shard_map/all_gather | solution.py:89
  219.3 175.8 %all-gather.30.cloned.1.call-start = ((), (), s32[]{:S(2)}) async-start(), calls=%async_computation.18 | async-start | bytes 6684672 | tf_op jit(solution)/shard_map/all_gather | solution.py:90
  220.0 202.5 %all-gather.34.cloned.1.call-start = ((), (), s32[]{:S(2)}) async-start(), calls=%async_computation.21 | async-start | bytes 2359296 | tf_op jit(solution)/shard_map/all_gather | solution.py:162
  220.8 265.3 %all-gather.32.cloned.1.call-start = ((), (), s32[]{:S(2)}) async-start(), calls=%async_computation.19 | async-start | bytes 6684672 | tf_op jit(solution)/shard_map/all_gather | solution.py:91
  221.3 313.4 %reduce-scatter.18.cloned.1.call-start = ((), (), s32[]{:S(2)}) async-start(), calls=%async_computation.22 | async-start | bytes 2359296 | tf_op jit(solution)/shard_map/reduce_scatter | solution.py:172
  268.9 3.7 copy-start.4
  497.8 7.2 copy-start.33
  497.8 7.2 copy-start.32
  497.8 7.2 copy-start.26
  509.7 57.8 %all-gather.36.cloned.1.call-start = ((), (), s32[]{:S(2)}) async-start(), calls=%async_computation.23 | async-start | bytes 2359296 | tf_op jit(solution)/shard_map/all_gather | solution.py:181
  509.8 30.3 %copy-start.23 = (f32[256]{0:T(256)}, f32[256]{0:T(256)S(1)}, u32[]{:S(2)}) copy-start(f32[256]{0:T(256)S(1)} %dynamic-slice.3) | copy-start | bytes 3076
  537.0 35.0 %copy-start.24 = (f32[256]{0:T(256)}, f32[256]{0:T(256)S(1)}, u32[]{:S(2)}) copy-start(f32[256]{0:T(256)S(1)} %broadcast_multiply_fusion.1) | copy-start | bytes 3076
  540.2 241.3 %reduce-scatter.34.cloned.1.call-start = ((), (), s32[]{:S(2)}) async-start(), calls=%async_computation.31 | async-start | bytes 417792
  540.3 46.1 %copy-start.21 = (f32[12,512]{1,0:T(8,128)}, f32[12,512]{1,0:T(8,128)S(1)}, u32[]{:S(2)}) copy-start(f32[12,512]{1,0:T(8,128)S(1)} %log_add_fusion) | copy-start | bytes 73732
  574.3 12.1 slice-start.2
  574.3 12.1 slice-start.3
  574.3 12.1 slice-start.4
  601.8 181.2 %reduce-scatter.16.cloned.1.call-start = ((), (), s32[]{:S(2)}) async-start(), calls=%async_computation.20 | async-start | bytes 2359296 | tf_op jit(solution)/shard_map/reduce_scatter | solution.py:155
  609.8 4.7 slice-start
  609.9 173.1 %reduce-scatter.20.cloned.1.call-start = ((), (), s32[]{:S(2)}) async-start(), calls=%async_computation.24 | async-start | bytes 2359296 | tf_op jit(solution)/shard_map/reduce_scatter | solution.py:249
  610.1 4.7 slice-start.1
  610.1 4.9 copy-start.7
  615.0 2.0 copy-start.8
  615.0 2.0 copy-start.27
  615.0 5.7 slice-start.5
  617.0 1.5 copy-start.5
  617.0 2.2 copy-start.10
  617.0 3.7 slice-start.6
  619.2 2.7 slice-start.7
  619.2 2.8 copy-start.16
  619.2 2.8 copy-start.22
  622.0 5.7 copy-start.11
  626.8 0.9 copy-start.13
  627.7 1.5 copy-start.2
  631.6 2.3 copy-start.9
  633.6 3.4 copy-start.6
  633.6 153.1 %reduce-scatter.22.cloned.1.call-start = ((), (), s32[]{:S(2)}) async-start(), calls=%async_computation.25 | async-start | bytes 2506752 | tf_op jit(solution)/shard_map/reduce_scatter | solution.py:261
  636.9 3.2 copy-start.14
  636.9 209.6 %reduce-scatter.24.cloned.1.call-start = ((), (), s32[]{:S(2)}) async-start(), calls=%async_computation.26 | async-start | bytes 2506752 | tf_op jit(solution)/shard_map/reduce_scatter | solution.py:264
  640.0 3.2 copy-start.30
  640.0 272.3 %reduce-scatter.26.cloned.1.call-start = ((), (), s32[]{:S(2)}) async-start(), calls=%async_computation.27 | async-start | bytes 2506752 | tf_op jit(solution)/shard_map/reduce_scatter | solution.py:267
  643.2 4.5 copy-start.28
  643.2 335.2 %reduce-scatter.28.cloned.1.call-start = ((), (), s32[]{:S(2)}) async-start(), calls=%async_computation.28 | async-start | bytes 2506752 | tf_op jit(solution)/shard_map/reduce_scatter | solution.py:273
  647.6 418.7 %reduce-scatter.36.cloned.1.call-start = ((), (), s32[]{:S(2)}) async-start(), calls=%async_computation.32 | async-start | bytes 6684672
  663.4 1.4 copy-start.12
  663.4 491.0 %reduce-scatter.30.cloned.1.call-start = ((), (), s32[]{:S(2)}) async-start(), calls=%async_computation.29 | async-start | bytes 6684672 | tf_op jit(solution)/shard_map/reduce_scatter | solution.py:276
  672.0 570.6 %reduce-scatter.32.cloned.1.call-start = ((), (), s32[]{:S(2)}) async-start(), calls=%async_computation.30 | async-start | bytes 6684672 | tf_op jit(solution)/shard_map/reduce_scatter | solution.py:279
  679.3 0.8 copy-start.31
  679.3 2.1 copy-start.25
  679.3 101.4 %copy-start.17 = (bf16[96,768]{1,0:T(8,128)(2,1)S(1)}, bf16[96,768]{1,0:T(8,128)(2,1)}, u32[]{:S(2)}) copy-start(bf16[96,768]{1,0:T(8,128)(2,1)} %param.21) | copy-start | bytes 442372
  679.3 101.4 %copy-start.18 = (bf16[96,768]{1,0:T(8,128)(2,1)S(1)}, bf16[96,768]{1,0:T(8,128)(2,1)}, u32[]{:S(2)}) copy-start(bf16[96,768]{1,0:T(8,128)(2,1)} %param.20) | copy-start | bytes 442372
  679.3 103.6 %copy-start.3 = (f32[512,1536]{1,0:T(8,128)S(1)}, f32[512,1536]{1,0:T(8,128)}, u32[]{:S(2)}) copy-start(f32[512,1536]{1,0:T(8,128)} %get-tuple-element.403) | copy-start | bytes 9437188
  779.4 7.3 copy-start.19
  779.4 7.3 copy-start.20
Sparse Core Ops, SparseCore 0:
  9.5 29.8 all-gather.17
  41.8 42.3 all-gather.23
  86.5 41.0 all-gather.21
  129.7 41.0 all-gather.19
  172.9 41.0 all-gather.25
  218.6 50.2 all-reduce.10
  271.2 61.3 all-gather.27
  334.9 60.0 all-gather.29
  396.6 25.8 all-gather.33
  424.7 61.3 all-gather.31
  509.8 24.8 reduce-scatter.17
  540.3 27.1 all-gather.35
  601.9 56.0 reduce-scatter.33
  660.1 25.1 reduce-scatter.15
  687.4 26.1 reduce-scatter.19
  717.2 63.3 reduce-scatter.21
  784.2 62.2 reduce-scatter.23
  850.1 62.2 reduce-scatter.25
  916.1 62.2 reduce-scatter.27
  982.2 84.0 reduce-scatter.35
  1070.3 84.1 reduce-scatter.29
  1158.4 84.1 reduce-scatter.31
where the time goes:
time: 1260 us; the launch traced here: 1250 us
  waiting for transfers between devices  845 us (67%)
  matrix products  150 us (12%)
  blocking collectives  128 us (10%)
  other arithmetic  74.1 us (6%)
  local copies, waits for them, and re-layouts  35.1 us (3%)
  between operations  17.7 us (1%)
    unnamed x24, waiting for transfers between devices  92.2 us
    reduce_scatter x1, waiting for transfers between devices, body(): lax.psum_scatter(g_up.astype(jnp.bfloat16), 'dp', scatter_dimension=0, ti...  86.2 us
    reduce_scatter x1, waiting for transfers between devices, body(): lax.psum_scatter(g_gate.astype(jnp.bfloat16), 'dp', scatter_dimension=0,...  85.8 us
    unnamed x3, blocking collectives  73.6 us
    reduce_scatter x1, waiting for transfers between devices, body(): lax.psum_scatter(g_output.astype(jnp.bfloat16), 'dp', scatter_dimension=0...  64.4 us
    reduce_scatter x1, waiting for transfers between devices, body(): lax.psum_scatter(g_value.astype(jnp.bfloat16), 'dp', scatter_dimension=0,...  64.2 us
    all_gather x1, waiting for transfers between devices, body(): lax.all_gather(w_down, 'dp', axis=0, tiled=True)  63.6 us
    all_gather x1, waiting for transfers between devices, body(): lax.all_gather(w_gate, 'dp', axis=0, tiled=True)  58.3 us
  transfers between devices with their start and end apart: 22, of which 17 were waited for; matrix products, arithmetic and copies ran while one was open for 15% of the time, Pallas kernels for 0%

commit v1 on v0

--- a/solution.py
+++ b/solution.py
@@ -1,19 +1,21 @@
 import math
+from functools import partial
 
 import jax
 import jax.numpy as jnp
 from jax import lax
+from jax.experimental import pallas as pl
+from jax.experimental.pallas import tpu as pltpu
 from jax.sharding import PartitionSpec as P
 
 HEAD_DIM = 64
 BLOCK = 256
-
-
+LANES = 128
 EPSILON = 1e-06
 HIGHEST = lax.Precision.HIGHEST
 NEGATIVE = -1e30
-
-
+F32 = jnp.float32
+BF16 = jnp.bfloat16
 def combined_all(part, axis, combine):
     gathered = jax.tree.map(lambda a: lax.all_gather(a, axis), part)
 
@@ -61,7 +63,7 @@
     )
 
 
-def body(
+def general_body(
     layer_in,
     segment_ids,
     norm1_gain,
@@ -310,9 +312,545 @@
     )
 
 
+def dot_nt(left, right):
+    return lax.dot_general(left, right, (((1,), (1,)), ((), ())), preferred_element_type=F32)
+
+
+def dot_nn(left, right):
+    return lax.dot_general(left, right, (((1,), (0,)), ((), ())), preferred_element_type=F32)
+
+
+def dot_tn(left, right):
+    return lax.dot_general(left, right, (((0,), (0,)), ((), ())), preferred_element_type=F32)
+
+
+def attend_kernel(y_ref, qkv_ref, aux_ref, o_ref, inv_ref, exp_ref, top_ref):
+    y = y_ref[0]
+    starts = (pl.multiple_of(y * BLOCK, BLOCK), pl.multiple_of((1 - y) * BLOCK, BLOCK))
+    lane = lax.broadcasted_iota(jnp.int32, (1, LANES), 1)
+    first = lane < HEAD_DIM
+    aux = [aux_ref[0, :, pl.ds(start, BLOCK)] for start in starts]
+    aux_col = [a.T for a in aux]
+    q_blk = [qkv_ref[pl.ds(s, BLOCK), 0:LANES] * 0.125 for s in starts]
+    k_blk = [qkv_ref[pl.ds(s, BLOCK), LANES : 2 * LANES] for s in starts]
+    v_blk = [qkv_ref[pl.ds(s, BLOCK), 2 * LANES : 3 * LANES] for s in starts]
+    same = {}
+    for i, j in ((0, 0), (1, 0), (1, 1)):
+        same[i, j] = aux_col[i][:, 2:3] == aux[j][2:3, :]
+    tops = []
+    results = [[], []]
+    for head in range(2):
+        mine = first if head == 0 else jnp.logical_not(first)
+        top = None
+        v_ext = [jnp.where(mine, v, jnp.ones_like(v)) for v in v_blk]
+        k_head = [jnp.where(mine, k, jnp.zeros_like(k)) for k in k_blk]
+        for i in range(2):
+            scores = []
+            for j in range(i + 1):
+                raw = dot_nt(q_blk[i], k_head[j])
+                seen = jnp.where(same[i, j], raw, NEGATIVE)
+                high = jnp.max(seen, axis=0, keepdims=True)
+                top = high if top is None else jnp.maximum(top, high)
+                differ = aux_col[i][:, head : head + 1] - aux[j][head : head + 1, :]
+                scores.append(seen - jnp.abs(differ))
+            peak = jnp.max(scores[0], axis=1, keepdims=True)
+            if i == 1:
+                peak = jnp.maximum(peak, jnp.max(scores[1], axis=1, keepdims=True))
+            acc = None
+            for j in range(i + 1):
+                weights = jnp.exp(scores[j] - peak).astype(BF16)
+                exp_ref[0, 0, head, :, (i + j) * BLOCK : (i + j + 1) * BLOCK] = weights
+                part = dot_nn(weights, v_ext[j])
+                acc = part if acc is None else acc + part
+            results[i].append(acc)
+        tops.append(jnp.maximum(top[:, :LANES], top[:, LANES:]))
+    for i in range(2):
+        one, two = results[i]
+        total = pltpu.roll(jnp.where(first, two, one), HEAD_DIM, 1)
+        inverse = 1.0 / total
+        inv_ref[pl.ds(starts[i], BLOCK), :] = inverse
+        o_ref[pl.ds(starts[i], BLOCK), :] = (jnp.where(first, one, two) * inverse).astype(BF16)
+    row = lax.broadcasted_iota(jnp.int32, (8, LANES), 0)
+    top_ref[0, 0] = jnp.where(row == 0, tops[0], tops[1])
+
+
+def attend(y_index, qkv, aux, packs, pairs):
+    rows = qkv.shape[0] // packs
+    wide = 3 * LANES
+    grid_spec = pltpu.PrefetchScalarGridSpec(
+        num_scalar_prefetch=1,
+        grid=(packs, pairs),
+        in_specs=[
+            pl.BlockSpec((rows, wide), lambda p, h, y: (p, h)),
+            pl.BlockSpec((1, 8, rows), lambda p, h, y: (h, 0, p)),
+        ],
+        out_specs=[
+            pl.BlockSpec((rows, LANES), lambda p, h, y: (p, h)),
+            pl.BlockSpec((rows, LANES), lambda p, h, y: (p, h)),
+            pl.BlockSpec((1, 1, 2, BLOCK, 3 * BLOCK), lambda p, h, y: (p, h, 0, 0, 0)),
+            pl.BlockSpec((1, 1, 8, LANES), lambda p, h, y: (p, h, 0, 0)),
+        ],
+    )
+    return pl.pallas_call(
+        attend_kernel,
+        grid_spec=grid_spec,
+        out_shape=(
+            jax.ShapeDtypeStruct((packs * rows, pairs * LANES), BF16),
+            jax.ShapeDtypeStruct((packs * rows, pairs * LANES), F32),
+            jax.ShapeDtypeStruct((packs, pairs, 2, BLOCK, 3 * BLOCK), BF16),
+            jax.ShapeDtypeStruct((packs, pairs, 8, LANES), F32),
+        ),
+        cost_estimate=pl.CostEstimate(
+            flops=packs * pairs * 2 * 6 * BLOCK * BLOCK * LANES * 2,
+            bytes_accessed=20_000_000,
+            transcendentals=packs * pairs * 2 * 3 * BLOCK * BLOCK,
+        ),
+        name="attend",
+    )(y_index, qkv, aux)
+
+
+def attend_back_kernel(y_ref, qkv_ref, do_ref, inv_ref, exp_ref, dqkv_ref, dc_ref):
+    y = y_ref[0]
+    starts = (pl.multiple_of(y * BLOCK, BLOCK), pl.multiple_of((1 - y) * BLOCK, BLOCK))
+    lane = lax.broadcasted_iota(jnp.int32, (1, LANES), 1)
+    first = lane < HEAD_DIM
+    ones = jnp.ones((8, BLOCK), BF16)
+    lower = lax.broadcasted_iota(jnp.int32, (BLOCK, BLOCK), 1) <= lax.broadcasted_iota(
+        jnp.int32, (BLOCK, BLOCK), 0
+    )
+    q_blk = [qkv_ref[pl.ds(s, BLOCK), 0:LANES] * 0.125 for s in starts]
+    k_blk = [qkv_ref[pl.ds(s, BLOCK), LANES : 2 * LANES] for s in starts]
+    v_blk = [qkv_ref[pl.ds(s, BLOCK), 2 * LANES : 3 * LANES] for s in starts]
+    inv_blk = [inv_ref[pl.ds(s, BLOCK), :] for s in starts]
+    do_blk = [
+        (do_ref[pl.ds(s, BLOCK), :].astype(F32) * inv).astype(BF16)
+        for s, inv in zip(starts, inv_blk)
+    ]
+    dq, dk, dv, dc = ([], []), ([], []), ([], []), ([], [])
+    for head in range(2):
+        mine = first if head == 0 else jnp.logical_not(first)
+        v_head = [jnp.where(mine, v, jnp.zeros_like(v)) for v in v_blk]
+        dk_acc, dv_acc, row_acc, col_acc = [None] * 2, [None] * 2, [None] * 2, [None] * 2
+        for i in range(2):
+            expos, probs, inner = [], [], None
+            inv_col = inv_blk[i][:, head * HEAD_DIM : head * HEAD_DIM + 1]
+            for j in range(i + 1):
+                expo = exp_ref[0, 0, head, :, (i + j) * BLOCK : (i + j + 1) * BLOCK]
+                grad_prob = dot_nt(do_blk[i], v_head[j])
+                wide = expo.astype(F32)
+                part = jnp.sum(wide * grad_prob, axis=1, keepdims=True)
+                inner = part if inner is None else inner + part
+                expos.append((expo, wide))
+                probs.append(grad_prob)
+            inner = inner * inv_col
+            dq_acc = None
+            for j in range(i + 1):
+                expo, wide = expos[j]
+                grad_score = wide * (probs[j] - inner)
+                low = grad_score.astype(BF16)
+                if i == j:
+                    signed = jnp.where(lower, low, -low)
+                else:
+                    signed = low
+                part = dot_nn(low, k_blk[j])
+                dq_acc = part if dq_acc is None else dq_acc + part
+                part = dot_tn(low, q_blk[i])
+                dk_acc[j] = part if dk_acc[j] is None else dk_acc[j] + part
+                part = dot_tn(expo, do_blk[i])
+                dv_acc[j] = part if dv_acc[j] is None else dv_acc[j] + part
+                part = dot_nt(ones, signed)
+                row_acc[i] = part if row_acc[i] is None else row_acc[i] + part
+                part = dot_nn(ones, signed)
+                col_acc[j] = part if col_acc[j] is None else col_acc[j] + part
+            dq[i].append(dq_acc)
+        for j in range(2):
+            dk[j].append(dk_acc[j])
+            dv[j].append(dv_acc[j])
+            dc[j].append(row_acc[j] - col_acc[j])
+    row = lax.broadcasted_iota(jnp.int32, (8, BLOCK), 0)
+    for i in range(2):
+        rows = pl.ds(starts[i], BLOCK)
+        dqkv_ref[rows, 0:LANES] = (jnp.where(first, *dq[i]) * 0.125).astype(BF16)
+        dqkv_ref[rows, LANES : 2 * LANES] = jnp.where(first, *dk[i]).astype(BF16)
+        dqkv_ref[rows, 2 * LANES : 3 * LANES] = jnp.where(first, *dv[i]).astype(BF16)
+        dc_ref[0, :, rows] = jnp.where(row == 0, *dc[i])
+
+
+def attend_back(y_index, qkv, d_out, inverse, expos, packs, pairs):
+    rows = qkv.shape[0] // packs
+    wide = 3 * LANES
+    grid_spec = pltpu.PrefetchScalarGridSpec(
+        num_scalar_prefetch=1,
+        grid=(packs, pairs),
+        in_specs=[
+            pl.BlockSpec((rows, wide), lambda p, h, y: (p, h)),
+            pl.BlockSpec((rows, LANES), lambda p, h, y: (p, h)),
+            pl.BlockSpec((rows, LANES), lambda p, h, y: (p, h)),
+            pl.BlockSpec((1, 1, 2, BLOCK, 3 * BLOCK), lambda p, h, y: (p, h, 0, 0, 0)),
+        ],
+        out_specs=[
+            pl.BlockSpec((rows, wide), lambda p, h, y: (p, h)),
+            pl.BlockSpec((1, 8, rows), lambda p, h, y: (h, 0, p)),
+        ],
+    )
+    return pl.pallas_call(
+        attend_back_kernel,
+        grid_spec=grid_spec,
+        out_shape=(
+            jax.ShapeDtypeStruct((packs * rows, pairs * wide), BF16),
+            jax.ShapeDtypeStruct((pairs, 8, packs * rows), F32),
+        ),
+        cost_estimate=pl.CostEstimate(
+            flops=packs * pairs * 2 * 18 * BLOCK * BLOCK * LANES * 2,
+            bytes_accessed=20_000_000,
+            transcendentals=0,
+        ),
+        name="attend_back",
+    )(y_index, qkv, d_out, inverse, expos)
+
+
+class Place:
+    def __init__(self):
+        self.dp = lax.axis_size("dp")
+        self.depth = self.dp // 4
+        index = lax.axis_index("dp")
+        self.core = index % 2
+        self.x = (index // 2) % 2
+        self.z = index // 4
+        self.y = lax.axis_index("tensor")
+
+    def swap_core(self, value):
+        return lax.ppermute(value, "dp", [(i, i ^ 1) for i in range(self.dp)])
+
+    def swap_x(self, value):
+        return lax.ppermute(value, "dp", [(i, i ^ 2) for i in range(self.dp)])
+
+    def swap_y(self, value):
+        return lax.ppermute(value, "tensor", [(0, 1), (1, 0)])
+
+    def swap_z(self, value, bit):
+        return lax.ppermute(value, "dp", [(i, i ^ (4 * bit)) for i in range(self.dp)])
+
+    def shift_z(self, value, step):
+        n = self.dp
+        return lax.ppermute(value, "dp", [(i, (i + 4 * step) % n) for i in range(n)])
+
+    def gather_rows(self, shard):
+        parts = [shard] + [self.shift_z(shard, s) for s in range(1, self.depth)]
+        others = [self.swap_x(part) for part in parts]
+        whole = jnp.zeros((self.depth, 2) + shard.shape, shard.dtype)
+        for step in range(self.depth):
+            spot = (self.z - step + self.depth) % self.depth
+            for side, source in ((self.x, parts), (1 - self.x, others)):
+                whole = lax.dynamic_update_slice(
+                    whole, source[step][None, None], (spot, side, 0, 0)
+                )
+        return whole.reshape(-1, shard.shape[1]), parts
+
+    def scatter_rows(self, grad):
+        rows = grad.shape[0] // (2 * self.depth)
+        blocks = grad.reshape(self.depth, 2, rows, grad.shape[1])
+        there = lax.dynamic_index_in_dim(blocks, 1 - self.x, 1, False)
+        here = lax.dynamic_index_in_dim(blocks, self.x, 1, False)
+        both = here.astype(F32) + self.swap_x(there).astype(F32)
+        low = both.astype(BF16)
+        own = lax.dynamic_index_in_dim(both, self.z, 0, False)
+        for step in range(1, self.depth):
+            spot = (self.z + step) % self.depth
+            sent = lax.dynamic_index_in_dim(low, spot, 0, False)
+            own = own + self.shift_z(sent, step).astype(F32)
+        return own
+
+    def by_core(self, mine, other, axis):
+        return jnp.where(
+            self.core == 0,
+            jnp.concatenate([mine, other], axis=axis),
+            jnp.concatenate([other, mine], axis=axis),
+        )
+
+    def core_columns(self, weights):
+        half = [w.shape[1] // 2 for w in weights]
+        keep = [
+            lax.dynamic_slice_in_dim(w, self.core * h, h, 1) for w, h in zip(weights, half)
+        ]
+        give = [
+            lax.dynamic_slice_in_dim(w, (1 - self.core) * h, h, 1) for w, h in zip(weights, half)
+        ]
+        return keep, give
+
+    def finish_grad(self, own):
+        rows = own.shape[0] // 2
+        keep = lax.dynamic_slice_in_dim(own, self.core * rows, rows, 0)
+        give = lax.dynamic_slice_in_dim(own, (1 - self.core) * rows, rows, 0)
+        return keep, self.swap_core(give.astype(BF16)).astype(F32)
+
+    def gather_tokens(self, rows):
+        near = self.swap_y(rows)
+        return jnp.concatenate(
+            [rows, near, self.swap_core(rows), self.swap_core(near)], axis=0
+        )
+
+    def scatter_tokens(self, partial_rows):
+        rows = partial_rows.shape[0] // 4
+        given = partial_rows[2 * rows :].astype(BF16)
+        pack = partial_rows[: 2 * rows].astype(F32) + self.swap_core(given).astype(F32)
+        return pack[:rows] + self.swap_y(pack[rows:].astype(BF16)).astype(F32)
+
+    def sum_plane(self, value, combine):
+        value = combine(value, self.swap_x(value))
+        bit = 1
+        while bit < self.depth:
+            value = combine(value, self.swap_z(value, bit))
+            bit *= 2
+        return value
+
+
+def after(value, *others):
+    return lax.optimization_barrier((value,) + others)[0]
+
+
+def interleave(parts):
+    rows = parts[0].shape[0]
+    stacked = jnp.stack([p.reshape(rows, -1, LANES) for p in parts], axis=2)
+    return stacked.reshape(rows, -1)
+
+
+def split_low(value):
+    high = value.astype(BF16)
+    return high, (value - high.astype(F32)).astype(BF16)
+
+
+def paired_body(
+    layer_in,
+    segment_ids,
+    norm1_gain,
+    w_query,
+    w_key,
+    w_value,
+    w_forget,
+    forget_bias,
+    w_output,
+    norm2_gain,
+    w_gate,
+    w_up,
+    w_down,
+    clip_tau,
+    out_grad,
+):
+    at = Place()
+    rows_loc = layer_in.shape[0]
+    pack = 2 * rows_loc
+    width = layer_in.shape[1]
+    heads = forget_bias.shape[0] // 2
+    pairs = heads // 2
+    y_index = at.y.astype(jnp.int32).reshape(1)
+    d_rows = norm1_gain.shape[0]
+
+    (wf_keep,), (wf_give,) = at.core_columns([w_forget])
+    gains = jnp.stack([norm1_gain, norm2_gain])
+    pad = jnp.zeros((16 - 2 - heads, d_rows), BF16)
+    mine = jnp.concatenate([gains, wf_keep.T, pad], axis=0)
+    theirs = at.swap_core(jnp.concatenate([gains, wf_give.T, pad], axis=0))
+    small = at.by_core(mine, theirs, 1)
+    small = jnp.where(
+        at.x == 0,
+        jnp.concatenate([small, at.swap_x(small)], axis=1),
+        jnp.concatenate([at.swap_x(small), small], axis=1),
+    )
+    whole = jnp.zeros((16, at.depth, 4 * d_rows), BF16)
+    for step in range(at.depth):
+        part = small if step == 0 else at.shift_z(small, step)
+        spot = (at.z - step + at.depth) % at.depth
+        whole = lax.dynamic_update_slice(whole, part[:, None], (0, spot, 0))
+    small = whole.reshape(16, width)
+    gain_one = small[0:1].astype(F32)
+    gain_two = small[1:2].astype(F32)
+    forget_t = small[2 : 2 + heads]
+
+    keep, give = at.core_columns([w_query, w_key, w_value, w_output, w_gate, w_up, w_down])
+
+    def shard_of(kept, given):
+        return at.by_core(kept, at.swap_core(given), 0)
+
+    attn_shard = shard_of(
+        jnp.concatenate([interleave(keep[:3]), keep[3]], axis=1),
+        jnp.concatenate([interleave(give[:3]), give[3]], axis=1),
+    )
+    ffn_shard = shard_of(
+        jnp.concatenate(keep[4:], axis=1),
+        jnp.concatenate(give[4:], axis=1),
+    )
+    attn_all, attn_parts = at.gather_rows(attn_shard)
+    units = keep[4].shape[1]
+    gu_shard = after(ffn_shard[:, : 2 * units], attn_parts[-1], attn_parts[-2])
+    gu_all, gu_parts = at.gather_rows(gu_shard)
+    down_shard = after(ffn_shard[:, 2 * units :], gu_parts[-1], gu_parts[-2])
+    down_all, _ = at.gather_rows(down_shard)
+    qkv_cols = 3 * heads * HEAD_DIM
+    w_qkv, wo_all = attn_all[:, :qkv_cols], attn_all[:, qkv_cols:]
+
+    x_own = layer_in.astype(F32)
+    scale_one = lax.rsqrt(jnp.mean(x_own * x_own, axis=1, keepdims=True) + EPSILON)
+    unit_one = x_own * scale_one
+    normed_one = at.gather_tokens((unit_one * gain_one).astype(BF16))
+    qkv = dot_nn(normed_one, w_qkv).astype(BF16)
+
+    bias = lax.dynamic_slice_in_dim(forget_bias, at.core * heads, heads, 0)
+    logits = dot_nt(forget_t, normed_one) + bias[:, None]
+    logs = jax.nn.log_sigmoid(logits).reshape(heads, 2, 2, rows_loc)
+    steps = jnp.arange(rows_loc, dtype=jnp.int32)
+    upper = (steps[:, None] <= steps[None, :]).astype(F32)
+    sums = jnp.einsum("hpbt,ts->hpbs", logs, upper, precision=HIGHEST)
+    total = sums[..., -1:]
+    later = at.y.astype(F32)
+    cumul = jnp.stack(
+        [sums[:, :, 0] + later * total[:, :, 1], sums[:, :, 1] + (1.0 - later) * total[:, :, 0]],
+        axis=2,
+    ).reshape(heads, 2 * pack)
+    seg_own = segment_ids[0].reshape(2, rows_loc)
+    seg_own = jnp.where(at.y == 0, seg_own, seg_own[::-1]).reshape(1, pack)
+    seg_both = jnp.concatenate([seg_own, at.swap_core(seg_own)], axis=1).astype(F32)
+    aux = jnp.concatenate(
+        [
+            cumul.reshape(pairs, 2, 2 * pack),
+            jnp.broadcast_to(seg_both[None], (pairs, 6, 2 * pack)),
+        ],
+        axis=1,
+    )
+    mixed, inverse, expos, tops = attend(y_index, qkv, aux, 2, pairs)
+
+    attn_part = dot_nt(mixed, wo_all)
+    resid = x_own + at.scatter_tokens(attn_part)
+    scale_two = lax.rsqrt(jnp.mean(resid * resid, axis=1, keepdims=True) + EPSILON)
+    unit_two = resid * scale_two
+    normed_two = at.gather_tokens((unit_two * gain_two).astype(BF16))
+    grad_rows = at.gather_tokens(out_grad)
+
+    maxima = jnp.max(tops[:, :, :2], axis=(0, 3)).reshape(1, heads)
+    maxima = jnp.pad(maxima, ((0, 7), (0, LANES - heads)))
+    maxima = at.sum_plane(maxima, jnp.maximum)
+    maxima = at.by_core(maxima[0, :heads], at.swap_core(maxima)[0, :heads], 0)
+    clip_factor = jnp.minimum(1.0, clip_tau / jnp.maximum(maxima, 1.0))
+    columns = jnp.repeat(jnp.sqrt(clip_factor), HEAD_DIM)
+    clipped_query = (w_query.astype(F32) * columns[None, :]).astype(BF16)
+    clipped_key = (w_key.astype(F32) * columns[None, :]).astype(BF16)
+
+    gate_up = dot_nn(normed_two, gu_all)
+    gate_pre, up_pre = gate_up[:, :units], gate_up[:, units:]
+    gate_sig = jax.nn.sigmoid(gate_pre)
+    gate_act = gate_pre * gate_sig
+    hidden = (gate_act * up_pre).astype(BF16)
+    g_down = at.scatter_rows(dot_tn(grad_rows, hidden).astype(BF16))
+    grad_hidden = dot_nn(grad_rows, down_all)
+    grad_gate = (grad_hidden * up_pre * gate_sig * (1.0 + gate_pre * (1.0 - gate_sig))).astype(BF16)
+    grad_up = (grad_hidden * gate_act).astype(BF16)
+    g_gate = at.scatter_rows(dot_tn(normed_two, grad_gate).astype(BF16))
+    g_up = at.scatter_rows(dot_tn(normed_two, grad_up).astype(BF16))
+    grad_gu = jnp.concatenate([grad_gate, grad_up], axis=1)
+    grad_two = at.scatter_tokens(dot_nt(grad_gu, gu_all))
+    layer_out = (resid + at.scatter_tokens(dot_nt(hidden, down_all))).astype(BF16)
+
+    weighted = gain_two * grad_two
+    inner_two = jnp.mean(unit_two * weighted, axis=1, keepdims=True)
+    norm2_part = jnp.sum(grad_two * unit_two, axis=0)
+    grad_resid = out_grad.astype(F32) + scale_two * (weighted - unit_two * inner_two)
+    grad_attn = at.gather_tokens(grad_resid.astype(BF16))
+
+    grad_mixed = dot_nn(grad_attn, wo_all).astype(BF16)
+    g_output = at.scatter_rows(dot_tn(grad_attn, mixed).astype(BF16))
+    d_qkv, d_cum = attend_back(y_index, qkv, grad_mixed, inverse, expos, 2, pairs)
+    g_qkv = at.scatter_rows(dot_tn(normed_one, d_qkv).astype(BF16))
+    d_cum = d_cum[:, :2].reshape(heads, 2, 2, rows_loc)
+    back = jnp.einsum("hpbt,st->hpbs", d_cum, upper, precision=HIGHEST)
+    total = back[..., :1]
+    d_log = jnp.stack(
+        [back[:, :, 0] + (1.0 - later) * total[:, :, 1], back[:, :, 1] + later * total[:, :, 0]],
+        axis=2,
+    ).reshape(heads, 2 * pack)
+    d_logit = d_log * jax.nn.sigmoid(-logits)
+    bias_part = jnp.sum(d_logit, axis=1)
+    d_split = jnp.concatenate(split_low(d_logit), axis=0)
+    forget_part = dot_nn(d_split, normed_one)
+    forget_part = forget_part[:heads] + forget_part[heads:]
+    grad_one = dot_nt(d_qkv, w_qkv) + dot_tn(d_split, jnp.concatenate([forget_t, forget_t], axis=0))
+    grad_one = at.scatter_tokens(grad_one)
+
+    weighted = gain_one * grad_one
+    inner_one = jnp.mean(unit_one * weighted, axis=1, keepdims=True)
+    norm1_part = jnp.sum(grad_one * unit_one, axis=0)
+    x_grad = (grad_resid + scale_one * (weighted - unit_one * inner_one)).astype(BF16)
+
+    small = jnp.concatenate(
+        [
+            norm1_part[None],
+            norm2_part[None],
+            forget_part,
+            jnp.pad(bias_part[None], ((0, 0), (0, width - heads))),
+            jnp.zeros((16 - 3 - heads, width), F32),
+        ],
+        axis=0,
+    )
+    small = at.sum_plane(small, jnp.add)
+    other = at.swap_core(small)
+    norms = small[:2] + other[:2]
+    norms = norms + at.swap_y(norms)
+    norms = lax.dynamic_slice_in_dim(norms, at.y * (width // 2), width // 2, 1)
+    forget = at.by_core(small[2 : 2 + heads], other[2 : 2 + heads], 0)
+    index = lax.axis_index("dp")
+    g_forget = lax.dynamic_slice_in_dim(forget, index * d_rows, d_rows, 1).T
+    g_bias = at.by_core(small[2 + heads, :heads], other[2 + heads, :heads], 0)
+
+    def place(own):
+        keep, got = at.finish_grad(own)
+        return at.by_core(keep, got, 1)
+
+    keep, got = at.finish_grad(g_qkv)
+
+    def third(which):
+        def cut(value):
+            return value.reshape(d_rows, pairs, 3, LANES)[:, :, which].reshape(d_rows, -1)
+
+        return at.by_core(cut(keep), cut(got), 1)
+
+    return (
+        layer_out,
+        x_grad,
+        norms[0],
+        third(0),
+        third(1),
+        third(2),
+        g_forget,
+        g_bias,
+        place(g_output),
+        norms[1],
+        place(g_gate),
+        place(g_up),
+        place(g_down),
+        clip_factor,
+        clipped_query,
+        clipped_key,
+    )
+
+
+def pick_body(mesh):
+    dp, tensor = mesh.shape["dp"], mesh.shape["tensor"]
+
+    def body(*args):
+        rows, heads = args[0].shape[0], args[7].shape[0]
+        depth = dp // 4
+        paired = (
+            tensor == 2
+            and dp % 4 == 0
+            and depth & (depth - 1) == 0
+            and rows == BLOCK
+            and heads % 4 == 0
+        )
+        return (paired_body if paired else general_body)(*args)
+
+    return body
 def solution(mesh):
     return jax.shard_map(
-        body,
+        pick_body(mesh),
         mesh=mesh,
         in_specs=(
             P(("dp", "tensor"), None),

time: 1260 us -> 730 us (0.58)
  waiting for transfers between devices: 845 us -> 395 us
  blocking collectives: 128 us -> 0 us
  starting transfers between devices: 1.64 us -> 114 us
  matrix products: 150 us -> 77.4 us
  Pallas kernels: 0 us -> 33.7 us
  other arithmetic: 74.1 us -> 44.8 us
  local copies, waits for them, and re-layouts: 35.1 us -> 55.4 us
  between operations: 17.7 us -> 2.77 us
    ppermute x0 -> x83, waiting for transfers between devices: none -> 395 us  [the longest x20 229 us: swap_x(): return lax.ppermute(value, 'dp', [(i, i ^ 2) for i in range(self.dp)])]
    reduce_scatter x9 -> x0, waiting for transfers between devices: 384 us -> none  [the longest x1 86.2 us: body(): lax.psum_scatter(g_up.astype(jnp.bfloat16), 'dp', scatter_dimension=0, ti...]
    all_gather x10 -> x0, waiting for transfers between devices: 322 us -> none  [the longest x1 63.6 us: body(): lax.all_gather(w_down, 'dp', axis=0, tiled=True)]
    ppermute x0 -> x83, starting transfers between devices: none -> 114 us  [the longest x27 73.9 us: shift_z(): lax.ppermute(value, 'dp', [(i, (i + 4 * step) % n) for i in range(n)])]
    unnamed x24 -> x0, waiting for transfers between devices: 92.2 us -> none
    unnamed x3 -> x0, blocking collectives: 73.6 us -> none
    dot_general x30 -> x18, matrix products: 150 us -> 77.4 us  [the longest x5 28.7 us: dot_nn(): lax.dot_general(left, right, (((1,), (0,)), ((), ())), preferred_element_...]
    all_gather x3 -> x0, blocking collectives: 54.4 us -> none  [the longest x2 36.6 us: combined_all(): gathered = jax.tree.map(lambda a: lax.all_gather(a, axis), part)]
  transfers between devices with their start and end apart: 22 -> 83, of which waited for: 17 -> 37; matrix products, arithmetic and copies ran while one was open for 15% -> 18% of each run, Pallas kernels for 0% -> 2%
where the time goes in v1:
time: 730 us; the launch traced here: 723 us
  waiting for transfers between devices  395 us (54%)
  starting transfers between devices  114 us (16%)
  matrix products  77.4 us (11%)
  local copies, waits for them, and re-layouts  55.4 us (8%)
  other arithmetic  44.8 us (6%)
  Pallas kernels  33.7 us (5%)
    ppermute x20, waiting for transfers between devices, swap_x(): return lax.ppermute(value, 'dp', [(i, i ^ 2) for i in range(self.dp)])  229 us
    ppermute x27, waiting for transfers between devices, shift_z(): lax.ppermute(value, 'dp', [(i, (i + 4 * step) % n) for i in range(n)])  122 us
    ppermute x27, starting transfers between devices, shift_z(): lax.ppermute(value, 'dp', [(i, (i + 4 * step) % n) for i in range(n)])  73.9 us
    ppermute x4, waiting for transfers between devices, swap_z(): return lax.ppermute(value, 'dp', [(i, i ^ 4 * bit) for i in range(self.dp)])  30 us
    dot_general x5, matrix products, dot_nn(): lax.dot_general(left, right, (((1,), (0,)), ((), ())), preferred_element_...  28.7 us
    dot_general x5, matrix products, dot_nt(): lax.dot_general(left, right, (((1,), (1,)), ((), ())), preferred_element_...  25.4 us
    dot_general x6, matrix products, dot_tn(): lax.dot_general(left, right, (((0,), (0,)), ((), ())), preferred_element_...  22.8 us
    ppermute x20, starting transfers between devices, swap_x(): return lax.ppermute(value, 'dp', [(i, i ^ 2) for i in range(self.dp)])  18.4 us
  transfers between devices with their start and end apart: 83, of which 37 were waited for; matrix products, arithmetic and copies ran while one was open for 18% of the time, Pallas kernels for 2%

profile of v1, /device:TPU:0, one launch (start us, length us, event | category | flops | bytes accessed | tf_op | source)
XLA Modules:
  0.0 722.9 jit_solution(8392513093798566959)
XLA Ops:
  0.7 3.1 collective-permute-start.39
  25.5 3.8 collective-permute-done.2
  30.1 3.8 collective-permute-done.3
  42.2 4.2 collective-permute-start.12
  49.1 2.1 constant_dynamic-update-slice_fusion.5
  51.2 4.2 collective-permute-done.5
  55.4 24.9 %collective-permute-done.12 = bf16[192,1536]{1,0:T(8,128)(2,1)S(1)} collective-permute-done((bf16[192,1536]{1,0:T(8,128)(2,1)S(1)}, bf16[192,1536]{1,0:T(8,128)(2,1)S(1)}, u32[]{:S(2)}, u32[]{:S(2)}) %collective-permute-start.12) | collective-permute-done | bytes 589856 | tf_op jit(solution)/shard_map/ppermute | solution.py:536
  83.0 30.0 %collective-permute-done.11 = bf16[192,1536]{1,0:T(8,128)(2,1)S(1)} collective-permute-done((bf16[192,1536]{1,0:T(8,128)(2,1)S(1)}, bf16[192,1536]{1,0:T(8,128)(2,1)S(1)}, u32[]{:S(2)}, u32[]{:S(2)}) %collective-permute-start.11) | collective-permute-done | bytes 589856 | tf_op jit(solution)/shard_map/ppermute | solution.py:526
  113.6 13.9 %collective-permute-done.13 = bf16[192,1536]{1,0:T(8,128)(2,1)S(1)} collective-permute-done((bf16[192,1536]{1,0:T(8,128)(2,1)S(1)}, bf16[192,1536]{1,0:T(8,128)(2,1)S(1)}, u32[]{:S(2)}, u32[]{:S(2)}) %collective-permute-start.13) | collective-permute-done | bytes 589856 | tf_op jit(solution)/shard_map/ppermute | solution.py:526
  128.1 13.0 %collective-permute-done.15 = bf16[192,1536]{1,0:T(8,128)(2,1)S(1)} collective-permute-done((bf16[192,1536]{1,0:T(8,128)(2,1)S(1)}, bf16[192,1536]{1,0:T(8,128)(2,1)S(1)}, u32[]{:S(2)}, u32[]{:S(2)}) %collective-permute-start.15) | collective-permute-done | bytes 589856 | tf_op jit(solution)/shard_map/ppermute | solution.py:526
  141.1 14.1 %collective-permute-start.24 = (bf16[192,2048]{1,0:T(8,128)(2,1)S(1)}, bf16[192,2048]{1,0:T(8,128)(2,1)}, u32[]{:S(2)}, u32[]{:S(2)}) collective-permute-start(bf16[192,2048]{1,0:T(8,128)(2,1)S(1)} %slice.245), channel_id=1, source_target_pairs={{0,8},{2,10},{4,12},{6,14},{8,16},{10,18},{12,20},{14,22},{16,24},... | collective-permute-start | bytes 2359304 | tf_op jit(solution)/shard_map/ppermute | solution.py:536
  155.3 3.7 fusion.44
  162.9 8.6 %convolution_convert_fusion.1.qkv_ref = bf16[1024,1152]{1,0:T(8,128)(2,1)} fusion(bf16[1536,1536]{1,0:T(8,128)(2,1)} %bitcast.230, bf16[256,1536]{1,0:T(8,128)(2,1)} %copy-done.38, bf16[256,1536]{1,0:T(8,128)(2,1)} %copy-done.35, bf16[256,1536]{1,0:T(8,128)(2,1)} %collective-permute-done.5, bf16[256,1536]{1,0:T(8,128)(2,1)} %fusion.11), kind=kOutput, calls=%fused_computation.11 | convolution fusion | flops 3637641216 | bytes 9043968 | tf_op jit(solution)/shard_map/dot_general | solution.py:320
  171.5 16.0 %attend.1 = (bf16[1024,384]{1,0:T(8,128)(2,1)}, f32[1024,384]{1,0:T(8,128)}, bf16[2,3,2,256,768]{4,3,2,1,0:T(8,128)(2,1)}, f32[2,3,8,128]{3,2,1,0:T(8,128)}) custom-call(s32[1]{0:T(128)} %bitcast.y_ref, bf16[1024,1152]{1,0:T(8,128)(2,1)} %convolution_convert_fusion.1.qkv_ref, f32[3,8,1024]{2,1,0:T(8,128)} %pad_maximum_fusion.9.aux_ref), custom_call_target="tpu_custom_call" | custom-call | flops 1207959552 | bytes 20000000 | tf_op jit(solution)/shard_map/attend/pallas_call | solution.py:394
  189.8 2.2 collective-permute-done.79
  196.2 23.3 %collective-permute-done.80 = f32[8,128]{1,0:T(8,128)S(1)} collective-permute-done((f32[8,128]{1,0:T(8,128)S(1)}, f32[8,128]{1,0:T(8,128)S(1)}, u32[]{:S(2)}, u32[]{:S(2)}) %collective-permute-start.80) | collective-permute-done | bytes 4128 | tf_op jit(solution)/shard_map/ppermute | solution.py:532
  219.5 3.1 fusion.22
  222.7 2.6 copy-done
  230.0 2.9 collective-permute-start.33
  234.4 2.2 bitcast_dynamic-update-slice_fusion.6
  236.6 2.2 bitcast_dynamic-update-slice_fusion.5
  239.2 2.3 collective-permute-done.30
  241.5 2.1 collective-permute-start.35
  245.4 12.9 %collective-permute-done.25 = bf16[192,2048]{1,0:T(8,128)(2,1)S(1)} collective-permute-done((bf16[192,2048]{1,0:T(8,128)(2,1)}, bf16[192,2048]{1,0:T(8,128)(2,1)S(1)}, u32[]{:S(2)}, u32[]{:S(2)}) %collective-permute-start.25) | collective-permute-done | bytes 786464 | tf_op jit(solution)/shard_map/ppermute | solution.py:526
  266.9 8.3 %collective-permute-done.27 = bf16[192,2048]{1,0:T(8,128)(2,1)S(1)} collective-permute-done((bf16[192,2048]{1,0:T(8,128)(2,1)}, bf16[192,2048]{1,0:T(8,128)(2,1)S(1)}, u32[]{:S(2)}, u32[]{:S(2)}) %collective-permute-start.27) | collective-permute-done | bytes 786464 | tf_op jit(solution)/shard_map/ppermute | solution.py:526
  275.8 4.3 collective-permute-done.18
  283.5 17.0 %collective-permute-done.32 = bf16[192,1024]{1,0:T(8,128)(2,1)S(1)} collective-permute-done((bf16[192,1024]{1,0:T(8,128)(2,1)S(1)}, bf16[192,1024]{1,0:T(8,128)(2,1)S(1)}, u32[]{:S(2)}, u32[]{:S(2)}) %collective-permute-start.32) | collective-permute-done | bytes 393248 | tf_op jit(solution)/shard_map/ppermute | solution.py:526
  300.5 8.3 %collective-permute-done.34 = bf16[192,1024]{1,0:T(8,128)(2,1)S(1)} collective-permute-done((bf16[192,1024]{1,0:T(8,128)(2,1)S(1)}, bf16[192,1024]{1,0:T(8,128)(2,1)S(1)}, u32[]{:S(2)}, u32[]{:S(2)}) %collective-permute-start.34) | collective-permute-done | bytes 393248 | tf_op jit(solution)/shard_map/ppermute | solution.py:526
  309.5 7.1 collective-permute-done.36
  316.8 6.7 fusion.70
  323.5 7.2 multiply_convert_fusion.1
  330.7 9.2 %fusion = f32[1024,1536]{1,0:T(8,128)S(1)} fusion(bf16[1536,2048]{1,0:T(8,128)(2,1)S(1)} %bitcast.237, bf16[1024,1024]{1,0:T(8,128)(2,1)} %get-tuple-element.69, bf16[1024,1024]{1,0:T(8,128)(2,1)} %get-tuple-element.68), kind=kOutput, calls=%fused_computation.2 | convolution fusion | flops 6450839552 | bytes 16777216 | tf_op jit(solution)/shard_map/dot_general | solution.py:316
  340.2 3.5 fusion.81
  345.3 3.7 convolution_convert_fusion.4
  350.6 3.7 convolution_convert_fusion.3
  356.2 5.5 convolution_convert_fusion.2
  368.6 18.0 %collective-permute-done.64 = bf16[4,192,1024]{2,1,0:T(8,128)(2,1)} collective-permute-done((bf16[4,192,1024]{2,1,0:T(8,128)(2,1)S(1)}, bf16[4,192,1024]{2,1,0:T(8,128)(2,1)}, u32[]{:S(2)}, u32[]{:S(2)}) %collective-permute-start.64) | collective-permute-done | bytes 1572896 | tf_op jit(solution)/shard_map/ppermute | solution.py:526
  386.6 2.2 fusion.75
  390.8 29.5 %collective-permute-done.69 = bf16[4,192,1024]{2,1,0:T(8,128)(2,1)} collective-permute-done((bf16[4,192,1024]{2,1,0:T(8,128)(2,1)S(1)}, bf16[4,192,1024]{2,1,0:T(8,128)(2,1)}, u32[]{:S(2)}, u32[]{:S(2)}) %collective-permute-start.69) | collective-permute-done | bytes 1572896 | tf_op jit(solution)/shard_map/ppermute | solution.py:526
  420.3 5.2 collective-permute-start.66
  425.5 2.2 fusion.74
  427.6 25.8 %collective-permute-done.74 = bf16[4,192,1024]{2,1,0:T(8,128)(2,1)S(1)} collective-permute-done((bf16[4,192,1024]{2,1,0:T(8,128)(2,1)S(1)}, bf16[4,192,1024]{2,1,0:T(8,128)(2,1)S(1)}, u32[]{:S(2)}, u32[]{:S(2)}) %collective-permute-start.74) | collective-permute-done | bytes 1572896 | tf_op jit(solution)/shard_map/ppermute | solution.py:526
  453.4 3.2 collective-permute-start.65
  458.3 3.4 collective-permute-start.71
  461.7 5.5 collective-permute-done.65
  467.2 18.3 %collective-permute-start.70 = (bf16[192,1024]{1,0:T(8,128)(2,1)S(1)}, bf16[192,1024]{1,0:T(8,128)(2,1)S(1)}, u32[]{:S(2)}, u32[]{:S(2)}) collective-permute-start(bf16[192,1024]{1,0:T(8,128)(2,1)S(1)} %get-tuple-element.77), channel_id=1, source_target_pairs={{0,8},{2,10},{4,12},{6,14},{8,16},{10,18},{12,20},{14,22},{16,24},... | collective-permute-start | bytes 1179656 | tf_op jit(solution)/shard_map/ppermute | solution.py:536
  486.5 4.0 collective-permute-start.76
  492.4 8.6 %collective-permute-done.71 = bf16[192,1024]{1,0:T(8,128)(2,1)S(1)} collective-permute-done((bf16[192,1024]{1,0:T(8,128)(2,1)S(1)}, bf16[192,1024]{1,0:T(8,128)(2,1)S(1)}, u32[]{:S(2)}, u32[]{:S(2)}) %collective-permute-start.71) | collective-permute-done | bytes 393248 | tf_op jit(solution)/shard_map/ppermute | solution.py:536
  503.8 29.5 %collective-permute-done.76 = bf16[192,1024]{1,0:T(8,128)(2,1)S(1)} collective-permute-done((bf16[192,1024]{1,0:T(8,128)(2,1)S(1)}, bf16[192,1024]{1,0:T(8,128)(2,1)S(1)}, u32[]{:S(2)}, u32[]{:S(2)}) %collective-permute-start.76) | collective-permute-done | bytes 393248 | tf_op jit(solution)/shard_map/ppermute | solution.py:536
  538.0 4.5 convolution_convert_fusion.6.do_ref
  542.6 17.7 %attend_back.1 = (bf16[1024,1152]{1,0:T(8,128)(2,1)}, f32[3,8,1024]{2,1,0:T(8,128)}) custom-call(s32[1]{0:T(128)} %bitcast.y_ref, bf16[1024,1152]{1,0:T(8,128)(2,1)} %convolution_convert_fusion.1.qkv_ref, bf16[1024,384]{1,0:T(8,128)(2,1)} %convolution_convert_fusion.6.do_ref, f32[1024,384]{1,0:T(8,128)} %get-tuple-element.27.inv_ref, ...), custom_call_target="tpu_custom_call" | custom-call | flops 3623878656 | bytes 20000000 | tf_op jit(solution)/shard_map/attend_back/pallas_call | solution.py:496
  561.8 6.8 convolution_convert_fusion
  574.3 6.0 convolution_add_fusion
  583.4 38.9 %collective-permute-done.59 = bf16[4,192,384]{2,1,0:T(8,128)(2,1)} collective-permute-done((bf16[4,192,384]{2,1,0:T(8,128)(2,1)S(1)}, bf16[4,192,384]{2,1,0:T(8,128)(2,1)}, u32[]{:S(2)}, u32[]{:S(2)}) %collective-permute-start.59) | collective-permute-done | bytes 589856 | tf_op jit(solution)/shard_map/ppermute | solution.py:526
  623.7 3.6 collective-permute-start.61
  627.3 2.2 collective-permute-start.60
  630.7 9.4 %collective-permute-done.61 = bf16[192,384]{1,0:T(8,128)(2,1)S(1)} collective-permute-done((bf16[192,384]{1,0:T(8,128)(2,1)S(1)}, bf16[192,384]{1,0:T(8,128)(2,1)S(1)}, u32[]{:S(2)}, u32[]{:S(2)}) %collective-permute-start.61) | collective-permute-done | bytes 147488 | tf_op jit(solution)/shard_map/ppermute | solution.py:536
  648.1 8.1 %collective-permute-done.57 = bf16[192,1152]{1,0:T(8,128)(2,1)S(1)} collective-permute-done((bf16[192,1152]{1,0:T(8,128)(2,1)S(1)}, bf16[192,1152]{1,0:T(8,128)(2,1)S(1)}, u32[]{:S(2)}, u32[]{:S(2)}) %collective-permute-start.57) | collective-permute-done | bytes 442400 | tf_op jit(solution)/shard_map/ppermute | solution.py:536
  656.1 25.6 %collective-permute-done.56 = bf16[192,1152]{1,0:T(8,128)(2,1)S(1)} collective-permute-done((bf16[192,1152]{1,0:T(8,128)(2,1)S(1)}, bf16[192,1152]{1,0:T(8,128)(2,1)S(1)}, u32[]{:S(2)}, u32[]{:S(2)}) %collective-permute-start.56) | collective-permute-done | bytes 442400 | tf_op jit(solution)/shard_map/ppermute | solution.py:536
  685.6 2.9 slice_reduce_fusion.1
  696.3 2.8 fusion.16
  706.2 3.0 collective-permute-done.50
  709.2 3.1 collective-permute-start.51
  713.1 3.7 collective-permute-done.51
  (425 shorter events, 141.1 us)
Async XLA Ops:
  0.7 41.5 %collective-permute-start.39 = (bf16[256,1536]{1,0:T(8,128)(2,1)}, bf16[256,1536]{1,0:T(8,128)(2,1)S(1)}, u32[]{:S(2)}, u32[]{:S(2)}) collective-permute-start(bf16[256,1536]{1,0:T(8,128)(2,1)} %param.29), channel_id=1, source_target_pairs={{0,1},{1,0},{2,3},{3,2},{4,5},{5,4},{6,7},{7,6},{8,9},{9,8},{10,11... | collective-permute-start | bytes 2359304 | tf_op jit(solution)/shard_map/ppermute | solution.py:529
  3.8 42.6 %collective-permute-start.40 = (bf16[256,1536]{1,0:T(8,128)(2,1)}, bf16[256,1536]{1,0:T(8,128)(2,1)}, u32[]{:S(2)}, u32[]{:S(2)}) collective-permute-start(bf16[256,1536]{1,0:T(8,128)(2,1)} %param.29), channel_id=1, source_target_pairs={{0,2},{2,0},{4,6},{6,4},{8,10},{10,8},{12,14},{14,12},{16,18},{18,... | collective-permute-start | bytes 2359304 | tf_op jit(solution)/shard_map/ppermute | solution.py:523
  8.0 31.7 %collective-permute-start.8 = (bf16[96,1536]{1,0:T(8,128)(2,1)}, bf16[96,1536]{1,0:T(8,128)(2,1)S(1)}, u32[]{:S(2)}, u32[]{:S(2)}) collective-permute-start(bf16[96,1536]{1,0:T(8,128)(2,1)} %pad_maximum_fusion.8), channel_id=1, source_target_pairs={{0,2},{2,0},{4,6},{6,4},{8,10},{10,8},{12,14},{14,12},{16,18},{18,... | collective-permute-start | bytes 884744 | tf_op jit(solution)/shard_map/ppermute | solution.py:523
  9.2 9.9 %collective-permute-start = (bf16[16,96]{1,0:T(8,128)(2,1)}, bf16[16,96]{1,0:T(8,128)(2,1)}, u32[]{:S(2)}, u32[]{:S(2)}) collective-permute-start(bf16[16,96]{1,0:T(8,128)(2,1)} %pad_maximum_fusion.15), channel_id=1, source_target_pairs={{0,2},{2,0},{4,6},{6,4},{8,10},{10,8},{12,14},{14,12},{16,18},{18,... | collective-permute-start | bytes 9224 | tf_op jit(solution)/shard_map/ppermute | solution.py:523
  11.1 8.9 %collective-permute-start.16 = (s32[1,512]{1,0:T(1,128)}, s32[1,512]{1,0:T(1,128)}, u32[]{:S(2)}, u32[]{:S(2)}) collective-permute-start(s32[1,512]{1,0:T(1,128)} %bitcast.95), channel_id=1, source_target_pairs={{0,2},{2,0},{4,6},{6,4},{8,10},{10,8},{12,14},{14,12},{16,18},{18,... | collective-permute-start | bytes 6152 | tf_op jit(solution)/shard_map/ppermute | solution.py:523
  19.1 23.0 %collective-permute-start.22 = (bf16[96,3072]{1,0:T(8,128)(2,1)}, bf16[96,3072]{1,0:T(8,128)(2,1)}, u32[]{:S(2)}, u32[]{:S(2)}) collective-permute-start(bf16[96,3072]{1,0:T(8,128)(2,1)} %pad_maximum_fusion.3), channel_id=1, source_target_pairs={{0,2},{2,0},{4,6},{6,4},{8,10},{10,8},{12,14},{14,12},{16,18},{18,... | collective-permute-start | bytes 1769480 | tf_op jit(solution)/shard_map/ppermute | solution.py:523
  39.4 16.0 %collective-permute-start.5 = (bf16[256,1536]{1,0:T(8,128)(2,1)}, bf16[256,1536]{1,0:T(8,128)(2,1)}, u32[]{:S(2)}, u32[]{:S(2)}) collective-permute-start(bf16[256,1536]{1,0:T(8,128)(2,1)} %fusion.11), channel_id=1, source_target_pairs={{0,1},{1,0},{2,3},{3,2},{4,5},{5,4},{6,7},{7,6},{8,9},{9,8},{10,11... | collective-permute-start | bytes 2359304 | tf_op jit(solution)/shard_map/ppermute | solution.py:529
  39.9 41.0 %collective-permute-start.9 = (bf16[192,1536]{1,0:T(8,128)(2,1)S(1)}, bf16[192,1536]{1,0:T(8,128)(2,1)S(1)}, u32[]{:S(2)}, u32[]{:S(2)}) collective-permute-start(bf16[192,1536]{1,0:T(8,128)(2,1)S(1)} %maximum_select_fusion.5), channel_id=1, source_target_pairs={{0,4},{2,6},{4,0},{6,2},{8,12},{10,14},{12,8},{14,10},{16,20},{18,... | collective-permute-start | bytes 1769480 | tf_op jit(solution)/shard_map/ppermute | solution.py:526
  42.2 39.2 %collective-permute-start.10 = (bf16[192,1536]{1,0:T(8,128)(2,1)S(1)}, bf16[192,1536]{1,0:T(8,128)(2,1)S(1)}, u32[]{:S(2)}, u32[]{:S(2)}) collective-permute-start(bf16[192,1536]{1,0:T(8,128)(2,1)S(1)} %maximum_select_fusion.5), channel_id=1, source_target_pairs={{0,8},{2,10},{4,12},{6,14},{8,16},{10,18},{12,20},{14,22},{16,24},... | collective-permute-start | bytes 1769480 | tf_op jit(solution)/shard_map/ppermute | solution.py:536
  42.2 38.1 %collective-permute-start.12 = (bf16[192,1536]{1,0:T(8,128)(2,1)S(1)}, bf16[192,1536]{1,0:T(8,128)(2,1)S(1)}, u32[]{:S(2)}, u32[]{:S(2)}) collective-permute-start(bf16[192,1536]{1,0:T(8,128)(2,1)S(1)} %maximum_select_fusion.5), channel_id=1, source_target_pairs={{0,16},{2,18},{4,20},{6,22},{8,24},{10,26},{12,28},{14,30},{16,0},... | collective-permute-start | bytes 1769480 | tf_op jit(solution)/shard_map/ppermute | solution.py:536
  46.4 34.0 %collective-permute-start.14 = (bf16[192,1536]{1,0:T(8,128)(2,1)S(1)}, bf16[192,1536]{1,0:T(8,128)(2,1)S(1)}, u32[]{:S(2)}, u32[]{:S(2)}) collective-permute-start(bf16[192,1536]{1,0:T(8,128)(2,1)S(1)} %maximum_select_fusion.5), channel_id=1, source_target_pairs={{0,24},{2,26},{4,28},{6,30},{8,0},{10,2},{12,4},{14,6},{16,8},{18,... | collective-permute-start | bytes 1769480 | tf_op jit(solution)/shard_map/ppermute | solution.py:536
  55.4 99.8 %collective-permute-start.6 = (bf16[256,1536]{1,0:T(8,128)(2,1)}, bf16[256,1536]{1,0:T(8,128)(2,1)S(1)}, u32[]{:S(2)}, u32[]{:S(2)}) collective-permute-start(bf16[256,1536]{1,0:T(8,128)(2,1)} %fusion.11), channel_id=1, source_target_pairs={{0,2},{2,0},{4,6},{6,4},{8,10},{10,8},{12,14},{14,12},{16,18},{18,... | collective-permute-start | bytes 2359304 | tf_op jit(solution)/shard_map/ppermute | solution.py:523
  80.4 113.4 %collective-permute-start.41 = (bf16[256,1536]{1,0:T(8,128)(2,1)S(1)}, bf16[256,1536]{1,0:T(8,128)(2,1)}, u32[]{:S(2)}, u32[]{:S(2)}) collective-permute-start(bf16[256,1536]{1,0:T(8,128)(2,1)S(1)} %collective-permute-done.39), channel_id=1, source_target_pairs={{0,2},{2,0},{4,6},{6,4},{8,10},{10,8},{12,14},{14,12},{16,18},{18,... | collective-permute-start | bytes 2359304 | tf_op jit(solution)/shard_map/ppermute | solution.py:523
  80.4 74.9 %collective-permute-start.7 = (bf16[256,1536]{1,0:T(8,128)(2,1)}, bf16[256,1536]{1,0:T(8,128)(2,1)S(1)}, u32[]{:S(2)}, u32[]{:S(2)}) collective-permute-start(bf16[256,1536]{1,0:T(8,128)(2,1)} %collective-permute-done.5), channel_id=1, source_target_pairs={{0,2},{2,0},{4,6},{6,4},{8,10},{10,8},{12,14},{14,12},{16,18},{18,... | collective-permute-start | bytes 2359304 | tf_op jit(solution)/shard_map/ppermute | solution.py:523
  80.9 149.2 %collective-permute-start.23 = (bf16[192,2048]{1,0:T(8,128)(2,1)S(1)}, bf16[192,2048]{1,0:T(8,128)(2,1)}, u32[]{:S(2)}, u32[]{:S(2)}) collective-permute-start(bf16[192,2048]{1,0:T(8,128)(2,1)S(1)} %slice.245), channel_id=1, source_target_pairs={{0,4},{2,6},{4,0},{6,2},{8,12},{10,14},{12,8},{14,10},{16,20},{18,... | collective-permute-start | bytes 2359304 | tf_op jit(solution)/shard_map/ppermute | solution.py:526
  81.4 31.7 %collective-permute-start.11 = (bf16[192,1536]{1,0:T(8,128)(2,1)S(1)}, bf16[192,1536]{1,0:T(8,128)(2,1)S(1)}, u32[]{:S(2)}, u32[]{:S(2)}) collective-permute-start(bf16[192,1536]{1,0:T(8,128)(2,1)S(1)} %collective-permute-done.10), channel_id=1, source_target_pairs={{0,4},{2,6},{4,0},{6,2},{8,12},{10,14},{12,8},{14,10},{16,20},{18,... | collective-permute-start | bytes 1769480 | tf_op jit(solution)/shard_map/ppermute | solution.py:526
  113.0 14.4 %collective-permute-start.13 = (bf16[192,1536]{1,0:T(8,128)(2,1)S(1)}, bf16[192,1536]{1,0:T(8,128)(2,1)S(1)}, u32[]{:S(2)}, u32[]{:S(2)}) collective-permute-start(bf16[192,1536]{1,0:T(8,128)(2,1)S(1)} %collective-permute-done.12), channel_id=1, source_target_pairs={{0,4},{2,6},{4,0},{6,2},{8,12},{10,14},{12,8},{14,10},{16,20},{18,... | collective-permute-start | bytes 1769480 | tf_op jit(solution)/shard_map/ppermute | solution.py:526
  127.5 13.6 %collective-permute-start.15 = (bf16[192,1536]{1,0:T(8,128)(2,1)S(1)}, bf16[192,1536]{1,0:T(8,128)(2,1)S(1)}, u32[]{:S(2)}, u32[]{:S(2)}) collective-permute-start(bf16[192,1536]{1,0:T(8,128)(2,1)S(1)} %collective-permute-done.14), channel_id=1, source_target_pairs={{0,4},{2,6},{4,0},{6,2},{8,12},{10,14},{12,8},{14,10},{16,20},{18,... | collective-permute-start | bytes 1769480 | tf_op jit(solution)/shard_map/ppermute | solution.py:526
  141.1 91.9 %collective-permute-start.24 = (bf16[192,2048]{1,0:T(8,128)(2,1)S(1)}, bf16[192,2048]{1,0:T(8,128)(2,1)}, u32[]{:S(2)}, u32[]{:S(2)}) collective-permute-start(bf16[192,2048]{1,0:T(8,128)(2,1)S(1)} %slice.245), channel_id=1, source_target_pairs={{0,8},{2,10},{4,12},{6,14},{8,16},{10,18},{12,20},{14,22},{16,24},... | collective-permute-start | bytes 2359304 | tf_op jit(solution)/shard_map/ppermute | solution.py:536
  155.2 74.2 %collective-permute-start.26 = (bf16[192,2048]{1,0:T(8,128)(2,1)S(1)}, bf16[192,2048]{1,0:T(8,128)(2,1)}, u32[]{:S(2)}, u32[]{:S(2)}) collective-permute-start(bf16[192,2048]{1,0:T(8,128)(2,1)S(1)} %slice.245), channel_id=1, source_target_pairs={{0,16},{2,18},{4,20},{6,22},{8,24},{10,26},{12,28},{14,30},{16,0},... | collective-permute-start | bytes 2359304 | tf_op jit(solution)/shard_map/ppermute | solution.py:536
  192.0 37.4 %collective-permute-start.28 = (bf16[192,2048]{1,0:T(8,128)(2,1)S(1)}, bf16[192,2048]{1,0:T(8,128)(2,1)}, u32[]{:S(2)}, u32[]{:S(2)}) collective-permute-start(bf16[192,2048]{1,0:T(8,128)(2,1)S(1)} %slice.245), channel_id=1, source_target_pairs={{0,24},{2,26},{4,28},{6,30},{8,0},{10,2},{12,4},{14,6},{16,8},{18,... | collective-permute-start | bytes 2359304 | tf_op jit(solution)/shard_map/ppermute | solution.py:536
  193.7 25.8 %collective-permute-start.80 = (f32[8,128]{1,0:T(8,128)S(1)}, f32[8,128]{1,0:T(8,128)S(1)}, u32[]{:S(2)}, u32[]{:S(2)}) collective-permute-start(f32[8,128]{1,0:T(8,128)S(1)} %pad_maximum_fusion.16), channel_id=1, source_target_pairs={{0,8},{2,10},{4,12},{6,14},{8,0},{10,2},{12,4},{14,6},{16,24},{18,... | collective-permute-start | bytes 12296 | tf_op jit(solution)/shard_map/ppermute | solution.py:532
  227.7 32.1 %collective-permute-start.17 = (bf16[512,1536]{1,0:T(8,128)(2,1)}, bf16[512,1536]{1,0:T(8,128)(2,1)}, u32[]{:S(2)}, u32[]{:S(2)}) collective-permute-start(bf16[512,1536]{1,0:T(8,128)(2,1)} %slice.373), channel_id=1, source_target_pairs={{0,2},{2,0},{4,6},{6,4},{8,10},{10,8},{12,14},{14,12},{16,18},{18,... | collective-permute-start | bytes 4718600 | tf_op jit(solution)/shard_map/ppermute | solution.py:523
  229.4 12.0 %collective-permute-start.30 = (bf16[192,1024]{1,0:T(8,128)(2,1)S(1)}, bf16[192,1024]{1,0:T(8,128)(2,1)S(1)}, u32[]{:S(2)}, u32[]{:S(2)}) collective-permute-start(bf16[192,1024]{1,0:T(8,128)(2,1)S(1)} %slice.248), channel_id=1, source_target_pairs={{0,4},{2,6},{4,0},{6,2},{8,12},{10,14},{12,8},{14,10},{16,20},{18,... | collective-permute-start | bytes 1179656 | tf_op jit(solution)/shard_map/ppermute | solution.py:526
  230.0 13.9 %collective-permute-start.31 = (bf16[192,1024]{1,0:T(8,128)(2,1)S(1)}, bf16[192,1024]{1,0:T(8,128)(2,1)S(1)}, u32[]{:S(2)}, u32[]{:S(2)}) collective-permute-start(bf16[192,1024]{1,0:T(8,128)(2,1)S(1)} %slice.248), channel_id=1, source_target_pairs={{0,8},{2,10},{4,12},{6,14},{8,16},{10,18},{12,20},{14,22},{16,24},... | collective-permute-start | bytes 1179656 | tf_op jit(solution)/shard_map/ppermute | solution.py:536
  230.0 34.7 %collective-permute-start.33 = (bf16[192,1024]{1,0:T(8,128)(2,1)S(1)}, bf16[192,1024]{1,0:T(8,128)(2,1)S(1)}, u32[]{:S(2)}, u32[]{:S(2)}) collective-permute-start(bf16[192,1024]{1,0:T(8,128)(2,1)S(1)} %slice.248), channel_id=1, source_target_pairs={{0,16},{2,18},{4,20},{6,22},{8,24},{10,26},{12,28},{14,30},{16,0},... | collective-permute-start | bytes 1179656 | tf_op jit(solution)/shard_map/ppermute | solution.py:536
  233.0 25.4 %collective-permute-start.25 = (bf16[192,2048]{1,0:T(8,128)(2,1)}, bf16[192,2048]{1,0:T(8,128)(2,1)S(1)}, u32[]{:S(2)}, u32[]{:S(2)}) collective-permute-start(bf16[192,2048]{1,0:T(8,128)(2,1)} %collective-permute-done.24), channel_id=1, source_target_pairs={{0,4},{2,6},{4,0},{6,2},{8,12},{10,14},{12,8},{14,10},{16,20},{18,... | collective-permute-start | bytes 2359304 | tf_op jit(solution)/shard_map/ppermute | solution.py:526
  241.5 24.9 %collective-permute-start.35 = (bf16[192,1024]{1,0:T(8,128)(2,1)S(1)}, bf16[192,1024]{1,0:T(8,128)(2,1)S(1)}, u32[]{:S(2)}, u32[]{:S(2)}) collective-permute-start(bf16[192,1024]{1,0:T(8,128)(2,1)S(1)} %slice.248), channel_id=1, source_target_pairs={{0,24},{2,26},{4,28},{6,30},{8,0},{10,2},{12,4},{14,6},{16,8},{18,... | collective-permute-start | bytes 1179656 | tf_op jit(solution)/shard_map/ppermute | solution.py:536
  243.9 31.2 %collective-permute-start.27 = (bf16[192,2048]{1,0:T(8,128)(2,1)}, bf16[192,2048]{1,0:T(8,128)(2,1)S(1)}, u32[]{:S(2)}, u32[]{:S(2)}) collective-permute-start(bf16[192,2048]{1,0:T(8,128)(2,1)} %collective-permute-done.26), channel_id=1, source_target_pairs={{0,4},{2,6},{4,0},{6,2},{8,12},{10,14},{12,8},{14,10},{16,20},{18,... | collective-permute-start | bytes 2359304 | tf_op jit(solution)/shard_map/ppermute | solution.py:526
  258.3 58.4 %collective-permute-start.29 = (bf16[192,2048]{1,0:T(8,128)(2,1)}, bf16[192,2048]{1,0:T(8,128)(2,1)S(1)}, u32[]{:S(2)}, u32[]{:S(2)}) collective-permute-start(bf16[192,2048]{1,0:T(8,128)(2,1)} %collective-permute-done.28), channel_id=1, source_target_pairs={{0,4},{2,6},{4,0},{6,2},{8,12},{10,14},{12,8},{14,10},{16,20},{18,... | collective-permute-start | bytes 2359304 | tf_op jit(solution)/shard_map/ppermute | solution.py:526
  262.0 18.1 %collective-permute-start.18 = (bf16[256,1536]{1,0:T(8,128)(2,1)S(1)}, bf16[256,1536]{1,0:T(8,128)(2,1)S(1)}, u32[]{:S(2)}, u32[]{:S(2)}) collective-permute-start(bf16[256,1536]{1,0:T(8,128)(2,1)S(1)} %slice.377), channel_id=1, source_target_pairs={{0,1},{1,0},{2,3},{3,2},{4,5},{5,4},{6,7},{7,6},{8,9},{9,8},{10,11... | collective-permute-start | bytes 2359304 | tf_op jit(solution)/shard_map/ppermute | solution.py:529
  264.8 35.7 %collective-permute-start.32 = (bf16[192,1024]{1,0:T(8,128)(2,1)S(1)}, bf16[192,1024]{1,0:T(8,128)(2,1)S(1)}, u32[]{:S(2)}, u32[]{:S(2)}) collective-permute-start(bf16[192,1024]{1,0:T(8,128)(2,1)S(1)} %collective-permute-done.31), channel_id=1, source_target_pairs={{0,4},{2,6},{4,0},{6,2},{8,12},{10,14},{12,8},{14,10},{16,20},{18,... | collective-permute-start | bytes 1179656 | tf_op jit(solution)/shard_map/ppermute | solution.py:526
  266.4 42.5 %collective-permute-start.34 = (bf16[192,1024]{1,0:T(8,128)(2,1)S(1)}, bf16[192,1024]{1,0:T(8,128)(2,1)S(1)}, u32[]{:S(2)}, u32[]{:S(2)}) collective-permute-start(bf16[192,1024]{1,0:T(8,128)(2,1)S(1)} %collective-permute-done.33), channel_id=1, source_target_pairs={{0,4},{2,6},{4,0},{6,2},{8,12},{10,14},{12,8},{14,10},{16,20},{18,... | collective-permute-start | bytes 1179656 | tf_op jit(solution)/shard_map/ppermute | solution.py:526
  275.2 41.5 %collective-permute-start.36 = (bf16[192,1024]{1,0:T(8,128)(2,1)S(1)}, bf16[192,1024]{1,0:T(8,128)(2,1)S(1)}, u32[]{:S(2)}, u32[]{:S(2)}) collective-permute-start(bf16[192,1024]{1,0:T(8,128)(2,1)S(1)} %collective-permute-done.35), channel_id=1, source_target_pairs={{0,4},{2,6},{4,0},{6,2},{8,12},{10,14},{12,8},{14,10},{16,20},{18,... | collective-permute-start | bytes 1179656 | tf_op jit(solution)/shard_map/ppermute | solution.py:526
  280.7 28.3 %collective-permute-start.19 = (bf16[256,1536]{1,0:T(8,128)(2,1)S(1)}, bf16[256,1536]{1,0:T(8,128)(2,1)S(1)}, u32[]{:S(2)}, u32[]{:S(2)}) collective-permute-start(bf16[256,1536]{1,0:T(8,128)(2,1)S(1)} %multiply_convert_fusion.3), channel_id=1, source_target_pairs={{0,1},{1,0},{2,3},{3,2},{4,5},{5,4},{6,7},{7,6},{8,9},{9,8},{10,11... | collective-permute-start | bytes 2359304 | tf_op jit(solution)/shard_map/ppermute | solution.py:529
  340.1 22.4 %collective-permute-start.42 = (bf16[512,1536]{1,0:T(8,128)(2,1)S(1)}, bf16[512,1536]{1,0:T(8,128)(2,1)}, u32[]{:S(2)}, u32[]{:S(2)}) collective-permute-start(bf16[512,1536]{1,0:T(8,128)(2,1)S(1)} %slice.371), channel_id=1, source_target_pairs={{0,2},{2,0},{4,6},{6,4},{8,10},{10,8},{12,14},{14,12},{16,18},{18,... | collective-permute-start | bytes 4718600 | tf_op jit(solution)/shard_map/ppermute | solution.py:523
  343.9 22.2 %collective-permute-start.37 = (bf16[512,1536]{1,0:T(8,128)(2,1)S(1)}, bf16[512,1536]{1,0:T(8,128)(2,1)}, u32[]{:S(2)}, u32[]{:S(2)}) collective-permute-start(bf16[512,1536]{1,0:T(8,128)(2,1)S(1)} %slice.372), channel_id=1, source_target_pairs={{0,2},{2,0},{4,6},{6,4},{8,10},{10,8},{12,14},{14,12},{16,18},{18,... | collective-permute-start | bytes 4718600 | tf_op jit(solution)/shard_map/ppermute | solution.py:523
  349.1 37.4 %collective-permute-start.64 = (bf16[4,192,1024]{2,1,0:T(8,128)(2,1)S(1)}, bf16[4,192,1024]{2,1,0:T(8,128)(2,1)}, u32[]{:S(2)}, u32[]{:S(2)}) collective-permute-start(bf16[4,192,1024]{2,1,0:T(8,128)(2,1)S(1)} %dynamic-slice_bitcast_fusion.3), channel_id=1, source_target_pairs={{0,4},{2,6},{4,0},{6,2},{8,12},{10,14},{12,8},{14,10},{16,20},{18,... | collective-permute-start | bytes 4718600 | tf_op jit(solution)/shard_map/ppermute | solution.py:526
  354.5 65.8 %collective-permute-start.69 = (bf16[4,192,1024]{2,1,0:T(8,128)(2,1)S(1)}, bf16[4,192,1024]{2,1,0:T(8,128)(2,1)}, u32[]{:S(2)}, u32[]{:S(2)}) collective-permute-start(bf16[4,192,1024]{2,1,0:T(8,128)(2,1)S(1)} %dynamic-slice_bitcast_fusion.2), channel_id=1, source_target_pairs={{0,4},{2,6},{4,0},{6,2},{8,12},{10,14},{12,8},{14,10},{16,20},{18,... | collective-permute-start | bytes 4718600 | tf_op jit(solution)/shard_map/ppermute | solution.py:526
  361.8 91.6 %collective-permute-start.74 = (bf16[4,192,1024]{2,1,0:T(8,128)(2,1)S(1)}, bf16[4,192,1024]{2,1,0:T(8,128)(2,1)S(1)}, u32[]{:S(2)}, u32[]{:S(2)}) collective-permute-start(bf16[4,192,1024]{2,1,0:T(8,128)(2,1)S(1)} %dynamic-slice_bitcast_fusion.1), channel_id=1, source_target_pairs={{0,4},{2,6},{4,0},{6,2},{8,12},{10,14},{12,8},{14,10},{16,20},{18,... | collective-permute-start | bytes 4718600 | tf_op jit(solution)/shard_map/ppermute | solution.py:526
  364.5 121.3 %collective-permute-start.43 = (bf16[256,1536]{1,0:T(8,128)(2,1)S(1)}, bf16[256,1536]{1,0:T(8,128)(2,1)S(1)}, u32[]{:S(2)}, u32[]{:S(2)}) collective-permute-start(bf16[256,1536]{1,0:T(8,128)(2,1)S(1)} %slice.375), channel_id=1, source_target_pairs={{0,1},{1,0},{2,3},{3,2},{4,5},{5,4},{6,7},{7,6},{8,9},{9,8},{10,11... | collective-permute-start | bytes 2359304 | tf_op jit(solution)/shard_map/ppermute | solution.py:529
  368.0 122.5 %collective-permute-start.38 = (bf16[256,1536]{1,0:T(8,128)(2,1)S(1)}, bf16[256,1536]{1,0:T(8,128)(2,1)S(1)}, u32[]{:S(2)}, u32[]{:S(2)}) collective-permute-start(bf16[256,1536]{1,0:T(8,128)(2,1)S(1)} %slice.376), channel_id=1, source_target_pairs={{0,1},{1,0},{2,3},{3,2},{4,5},{5,4},{6,7},{7,6},{8,9},{9,8},{10,11... | collective-permute-start | bytes 2359304 | tf_op jit(solution)/shard_map/ppermute | solution.py:529
  388.9 68.7 %collective-permute-start.67 = (bf16[192,1024]{1,0:T(8,128)(2,1)S(1)}, bf16[192,1024]{1,0:T(8,128)(2,1)S(1)}, u32[]{:S(2)}, u32[]{:S(2)}) collective-permute-start(bf16[192,1024]{1,0:T(8,128)(2,1)S(1)} %get-tuple-element.81), channel_id=1, source_target_pairs={{0,24},{2,26},{4,28},{6,30},{8,0},{10,2},{12,4},{14,6},{16,8},{18,... | collective-permute-start | bytes 1179656 | tf_op jit(solution)/shard_map/ppermute | solution.py:536
  420.3 38.0 %collective-permute-start.66 = (bf16[192,1024]{1,0:T(8,128)(2,1)S(1)}, bf16[192,1024]{1,0:T(8,128)(2,1)S(1)}, u32[]{:S(2)}, u32[]{:S(2)}) collective-permute-start(bf16[192,1024]{1,0:T(8,128)(2,1)S(1)} %get-tuple-element.82), channel_id=1, source_target_pairs={{0,16},{2,18},{4,20},{6,22},{8,24},{10,26},{12,28},{14,30},{16,0},... | collective-permute-start | bytes 1179656 | tf_op jit(solution)/shard_map/ppermute | solution.py:536
  453.4 13.8 %collective-permute-start.65 = (bf16[192,1024]{1,0:T(8,128)(2,1)S(1)}, bf16[192,1024]{1,0:T(8,128)(2,1)S(1)}, u32[]{:S(2)}, u32[]{:S(2)}) collective-permute-start(bf16[192,1024]{1,0:T(8,128)(2,1)S(1)} %get-tuple-element.80), channel_id=1, source_target_pairs={{0,8},{2,10},{4,12},{6,14},{8,16},{10,18},{12,20},{14,22},{16,24},... | collective-permute-start | bytes 1179656 | tf_op jit(solution)/shard_map/ppermute | solution.py:536
  457.6 29.0 %collective-permute-start.72 = (bf16[192,1024]{1,0:T(8,128)(2,1)S(1)}, bf16[192,1024]{1,0:T(8,128)(2,1)S(1)}, u32[]{:S(2)}, u32[]{:S(2)}) collective-permute-start(bf16[192,1024]{1,0:T(8,128)(2,1)S(1)} %get-tuple-element.78), channel_id=1, source_target_pairs={{0,24},{2,26},{4,28},{6,30},{8,0},{10,2},{12,4},{14,6},{16,8},{18,... | collective-permute-start | bytes 1179656 | tf_op jit(solution)/shard_map/ppermute | solution.py:536
  458.3 42.8 %collective-permute-start.71 = (bf16[192,1024]{1,0:T(8,128)(2,1)S(1)}, bf16[192,1024]{1,0:T(8,128)(2,1)S(1)}, u32[]{:S(2)}, u32[]{:S(2)}) collective-permute-start(bf16[192,1024]{1,0:T(8,128)(2,1)S(1)} %get-tuple-element.79), channel_id=1, source_target_pairs={{0,16},{2,18},{4,20},{6,22},{8,24},{10,26},{12,28},{14,30},{16,0},... | collective-permute-start | bytes 1179656 | tf_op jit(solution)/shard_map/ppermute | solution.py:536
  467.2 33.8 %collective-permute-start.70 = (bf16[192,1024]{1,0:T(8,128)(2,1)S(1)}, bf16[192,1024]{1,0:T(8,128)(2,1)S(1)}, u32[]{:S(2)}, u32[]{:S(2)}) collective-permute-start(bf16[192,1024]{1,0:T(8,128)(2,1)S(1)} %get-tuple-element.77), channel_id=1, source_target_pairs={{0,8},{2,10},{4,12},{6,14},{8,16},{10,18},{12,20},{14,22},{16,24},... | collective-permute-start | bytes 1179656 | tf_op jit(solution)/shard_map/ppermute | solution.py:536
  485.8 17.9 %collective-permute-start.77 = (bf16[192,1024]{1,0:T(8,128)(2,1)S(1)}, bf16[192,1024]{1,0:T(8,128)(2,1)S(1)}, u32[]{:S(2)}, u32[]{:S(2)}) collective-permute-start(bf16[192,1024]{1,0:T(8,128)(2,1)S(1)} %get-tuple-element.75), channel_id=1, source_target_pairs={{0,24},{2,26},{4,28},{6,30},{8,0},{10,2},{12,4},{14,6},{16,8},{18,... | collective-permute-start | bytes 1179656 | tf_op jit(solution)/shard_map/ppermute | solution.py:536
  486.5 46.8 %collective-permute-start.76 = (bf16[192,1024]{1,0:T(8,128)(2,1)S(1)}, bf16[192,1024]{1,0:T(8,128)(2,1)S(1)}, u32[]{:S(2)}, u32[]{:S(2)}) collective-permute-start(bf16[192,1024]{1,0:T(8,128)(2,1)S(1)} %get-tuple-element.76), channel_id=1, source_target_pairs={{0,16},{2,18},{4,20},{6,22},{8,24},{10,26},{12,28},{14,30},{16,0},... | collective-permute-start | bytes 1179656 | tf_op jit(solution)/shard_map/ppermute | solution.py:536
  490.5 42.8 %collective-permute-start.75 = (bf16[192,1024]{1,0:T(8,128)(2,1)S(1)}, bf16[192,1024]{1,0:T(8,128)(2,1)S(1)}, u32[]{:S(2)}, u32[]{:S(2)}) collective-permute-start(bf16[192,1024]{1,0:T(8,128)(2,1)S(1)} %get-tuple-element.74), channel_id=1, source_target_pairs={{0,8},{2,10},{4,12},{6,14},{8,16},{10,18},{12,20},{14,22},{16,24},... | collective-permute-start | bytes 1179656 | tf_op jit(solution)/shard_map/ppermute | solution.py:536
  501.0 33.4 %collective-permute-start.68 = (bf16[96,1024]{1,0:T(8,128)(2,1)S(1)}, bf16[96,1024]{1,0:T(8,128)(2,1)S(1)}, u32[]{:S(2)}, u32[]{:S(2)}) collective-permute-start(bf16[96,1024]{1,0:T(8,128)(2,1)S(1)} %dynamic-slice_convert_fusion.3), channel_id=1, source_target_pairs={{0,2},{2,0},{4,6},{6,4},{8,10},{10,8},{12,14},{14,12},{16,18},{18,... | collective-permute-start | bytes 589832 | tf_op jit(solution)/shard_map/ppermute | solution.py:523
  501.1 33.2 %collective-permute-start.44 = (bf16[256,1536]{1,0:T(8,128)(2,1)S(1)}, bf16[256,1536]{1,0:T(8,128)(2,1)S(1)}, u32[]{:S(2)}, u32[]{:S(2)}) collective-permute-start(bf16[256,1536]{1,0:T(8,128)(2,1)S(1)} %get-tuple-element.64), channel_id=1, source_target_pairs={{0,1},{1,0},{2,3},{3,2},{4,5},{5,4},{6,7},{7,6},{8,9},{9,8},{10,11... | collective-permute-start | bytes 2359304 | tf_op jit(solution)/shard_map/ppermute | solution.py:529
  503.8 30.7 %collective-permute-start.73 = (bf16[96,1024]{1,0:T(8,128)(2,1)S(1)}, bf16[96,1024]{1,0:T(8,128)(2,1)S(1)}, u32[]{:S(2)}, u32[]{:S(2)}) collective-permute-start(bf16[96,1024]{1,0:T(8,128)(2,1)S(1)} %dynamic-slice_convert_fusion.2), channel_id=1, source_target_pairs={{0,2},{2,0},{4,6},{6,4},{8,10},{10,8},{12,14},{14,12},{16,18},{18,... | collective-permute-start | bytes 589832 | tf_op jit(solution)/shard_map/ppermute | solution.py:523
  568.9 73.4 %collective-permute-start.54 = (bf16[4,192,1152]{2,1,0:T(8,128)(2,1)S(1)}, bf16[4,192,1152]{2,1,0:T(8,128)(2,1)S(1)}, u32[]{:S(2)}, u32[]{:S(2)}) collective-permute-start(bf16[4,192,1152]{2,1,0:T(8,128)(2,1)S(1)} %dynamic-slice_bitcast_fusion), channel_id=1, source_target_pairs={{0,4},{2,6},{4,0},{6,2},{8,12},{10,14},{12,8},{14,10},{16,20},{18,... | collective-permute-start | bytes 5308424 | tf_op jit(solution)/shard_map/ppermute | solution.py:526
  572.6 49.7 %collective-permute-start.59 = (bf16[4,192,384]{2,1,0:T(8,128)(2,1)S(1)}, bf16[4,192,384]{2,1,0:T(8,128)(2,1)}, u32[]{:S(2)}, u32[]{:S(2)}) collective-permute-start(bf16[4,192,384]{2,1,0:T(8,128)(2,1)S(1)} %dynamic-slice_bitcast_fusion.4), channel_id=1, source_target_pairs={{0,4},{2,6},{4,0},{6,2},{8,12},{10,14},{12,8},{14,10},{16,20},{18,... | collective-permute-start | bytes 1769480 | tf_op jit(solution)/shard_map/ppermute | solution.py:526
  580.5 64.4 %collective-permute-start.47 = (bf16[512,1536]{1,0:T(8,128)(2,1)S(1)}, bf16[512,1536]{1,0:T(8,128)(2,1)S(1)}, u32[]{:S(2)}, u32[]{:S(2)}) collective-permute-start(bf16[512,1536]{1,0:T(8,128)(2,1)S(1)} %slice.370), channel_id=1, source_target_pairs={{0,2},{2,0},{4,6},{6,4},{8,10},{10,8},{12,14},{14,12},{16,18},{18,... | collective-permute-start | bytes 4718600 | tf_op jit(solution)/shard_map/ppermute | solution.py:523
  623.7 16.4 %collective-permute-start.61 = (bf16[192,384]{1,0:T(8,128)(2,1)S(1)}, bf16[192,384]{1,0:T(8,128)(2,1)S(1)}, u32[]{:S(2)}, u32[]{:S(2)}) collective-permute-start(bf16[192,384]{1,0:T(8,128)(2,1)S(1)} %get-tuple-element.86), channel_id=1, source_target_pairs={{0,16},{2,18},{4,20},{6,22},{8,24},{10,26},{12,28},{14,30},{16,0},... | collective-permute-start | bytes 442376 | tf_op jit(solution)/shard_map/ppermute | solution.py:536
  627.3 12.8 %collective-permute-start.60 = (bf16[192,384]{1,0:T(8,128)(2,1)S(1)}, bf16[192,384]{1,0:T(8,128)(2,1)S(1)}, u32[]{:S(2)}, u32[]{:S(2)}) collective-permute-start(bf16[192,384]{1,0:T(8,128)(2,1)S(1)} %get-tuple-element.84), channel_id=1, source_target_pairs={{0,8},{2,10},{4,12},{6,14},{8,16},{10,18},{12,20},{14,22},{16,24},... | collective-permute-start | bytes 442376 | tf_op jit(solution)/shard_map/ppermute | solution.py:536
  642.9 13.2 %collective-permute-start.57 = (bf16[192,1152]{1,0:T(8,128)(2,1)S(1)}, bf16[192,1152]{1,0:T(8,128)(2,1)S(1)}, u32[]{:S(2)}, u32[]{:S(2)}) collective-permute-start(bf16[192,1152]{1,0:T(8,128)(2,1)S(1)} %get-tuple-element.72), channel_id=1, source_target_pairs={{0,24},{2,26},{4,28},{6,30},{8,0},{10,2},{12,4},{14,6},{16,8},{18,... | collective-permute-start | bytes 1327112 | tf_op jit(solution)/shard_map/ppermute | solution.py:536
  643.0 38.8 %collective-permute-start.56 = (bf16[192,1152]{1,0:T(8,128)(2,1)S(1)}, bf16[192,1152]{1,0:T(8,128)(2,1)S(1)}, u32[]{:S(2)}, u32[]{:S(2)}) collective-permute-start(bf16[192,1152]{1,0:T(8,128)(2,1)S(1)} %get-tuple-element.73), channel_id=1, source_target_pairs={{0,16},{2,18},{4,20},{6,22},{8,24},{10,26},{12,28},{14,30},{16,0},... | collective-permute-start | bytes 1327112 | tf_op jit(solution)/shard_map/ppermute | solution.py:536
  643.1 38.6 %collective-permute-start.55 = (bf16[192,1152]{1,0:T(8,128)(2,1)S(1)}, bf16[192,1152]{1,0:T(8,128)(2,1)S(1)}, u32[]{:S(2)}, u32[]{:S(2)}) collective-permute-start(bf16[192,1152]{1,0:T(8,128)(2,1)S(1)} %get-tuple-element.71), channel_id=1, source_target_pairs={{0,8},{2,10},{4,12},{6,14},{8,16},{10,18},{12,20},{14,22},{16,24},... | collective-permute-start | bytes 1327112 | tf_op jit(solution)/shard_map/ppermute | solution.py:536
  646.6 42.6 %collective-permute-start.48 = (bf16[256,1536]{1,0:T(8,128)(2,1)}, bf16[256,1536]{1,0:T(8,128)(2,1)S(1)}, u32[]{:S(2)}, u32[]{:S(2)}) collective-permute-start(bf16[256,1536]{1,0:T(8,128)(2,1)} %slice.374), channel_id=1, source_target_pairs={{0,1},{1,0},{2,3},{3,2},{4,5},{5,4},{6,7},{7,6},{8,9},{9,8},{10,11... | collective-permute-start | bytes 2359304 | tf_op jit(solution)/shard_map/ppermute | solution.py:529
  682.7 16.4 %collective-permute-start.58 = (bf16[96,1152]{1,0:T(8,128)(2,1)}, bf16[96,1152]{1,0:T(8,128)(2,1)}, u32[]{:S(2)}, u32[]{:S(2)}) collective-permute-start(bf16[96,1152]{1,0:T(8,128)(2,1)} %dynamic-slice_convert_fusion), channel_id=1, source_target_pairs={{0,2},{2,0},{4,6},{6,4},{8,10},{10,8},{12,14},{14,12},{16,18},{18,... | collective-permute-start | bytes 663560 | tf_op jit(solution)/shard_map/ppermute | solution.py:523
  (72 other events, 713.1 us)

commit v2 on v1

--- a/solution.py
+++ b/solution.py
@@ -522,44 +522,89 @@
     def swap_core(self, value):
         return lax.ppermute(value, "dp", [(i, i ^ 1) for i in range(self.dp)])
 
-    def swap_x(self, value):
-        return lax.ppermute(value, "dp", [(i, i ^ 2) for i in range(self.dp)])
-
     def swap_y(self, value):
         return lax.ppermute(value, "tensor", [(0, 1), (1, 0)])
 
-    def swap_z(self, value, bit):
-        return lax.ppermute(value, "dp", [(i, i ^ (4 * bit)) for i in range(self.dp)])
-
-    def shift_z(self, value, step):
+    def ring(self, value, step):
+        spots = [4 * z for z in range(self.depth)]
+        spots += [4 * z + 2 for z in reversed(range(self.depth))]
+        count = len(spots)
+        pairs = [
+            (spots[r] + core, spots[(r + step) % count] + core)
+            for r in range(count)
+            for core in (0, 1)
+        ]
+        return lax.ppermute(value, "dp", pairs)
+
+    def block_of(self, step):
+        count = 2 * self.depth
+        spot = (jnp.where(self.x == 0, self.z, count - 1 - self.z) + step + count) % count
+        return jnp.where(spot < self.depth, 2 * spot, 2 * (count - 1 - spot) + 1)
+
+    def gather_rings(self, shards):
+        count = 2 * self.depth
+        half = self.depth
+
+        def put(whole, part, step, side=0):
+            return lax.dynamic_update_slice(whole, part[None], (self.block_of(step), side, 0, 0))
+
+        wholes = [put(jnp.zeros((count,) + s.shape, s.dtype), s, 0) for s in shards]
+        up, down = list(shards), list(shards)
+        last = None
+        for step in range(1, half + 1):
+            for k in range(len(shards)):
+                if step < half:
+                    up[k], down[k] = self.ring(up[k], 1), self.ring(down[k], -1)
+                else:
+                    up[k], down[k] = self.ring(up[k][:1], 1), self.ring(down[k][1:], -1)
+            for k in range(len(shards)):
+                wholes[k] = put(wholes[k], up[k], -step)
+                wholes[k] = put(wholes[k], down[k], step, 0 if step < half else 1)
+            if step == half - 1:
+                last = up + down
+        wholes = [w.reshape(-1, w.shape[-1]) for w in wholes]
+        return wholes, last
+
+    def scatter_rings(self, grads):
+        count = 2 * self.depth
+        half = self.depth
+        blocks = [g.reshape(count, 2, g.shape[0] // (2 * count), g.shape[1]) for g in grads]
+
+        def own(k, step):
+            start = (self.block_of(step), 0, 0, 0)
+            return lax.dynamic_slice(blocks[k], start, (1,) + blocks[k].shape[1:])[0]
+
+        ups = [own(k, half)[:1] for k in range(len(grads))]
+        downs = [own(k, half)[1:] for k in range(len(grads))]
+        totals = []
+        for step in range(1, half + 1):
+            for k in range(len(grads)):
+                ups[k], downs[k] = self.ring(ups[k], 1), self.ring(downs[k], -1)
+                if step == half:
+                    total = own(k, 0).astype(F32) + ups[k].astype(F32) + downs[k].astype(F32)
+                    totals.append(total.reshape(-1, total.shape[-1]))
+                    continue
+                ahead, behind = own(k, half - step), own(k, step - half)
+                if step == 1:
+                    first = (ahead[:1].astype(F32) + ups[k].astype(F32)).astype(BF16)
+                    ups[k] = jnp.concatenate([first, ahead[1:]], axis=0)
+                    second = (behind[1:].astype(F32) + downs[k].astype(F32)).astype(BF16)
+                    downs[k] = jnp.concatenate([behind[:1], second], axis=0)
+                else:
+                    ups[k] = (ahead.astype(F32) + ups[k].astype(F32)).astype(BF16)
+                    downs[k] = (behind.astype(F32) + downs[k].astype(F32)).astype(BF16)
+        return totals
+
+    def share_plane(self, value):
+        count = 2 * self.depth
         n = self.dp
-        return lax.ppermute(value, "dp", [(i, (i + 4 * step) % n) for i in range(n)])
-
-    def gather_rows(self, shard):
-        parts = [shard] + [self.shift_z(shard, s) for s in range(1, self.depth)]
-        others = [self.swap_x(part) for part in parts]
-        whole = jnp.zeros((self.depth, 2) + shard.shape, shard.dtype)
-        for step in range(self.depth):
-            spot = (self.z - step + self.depth) % self.depth
-            for side, source in ((self.x, parts), (1 - self.x, others)):
-                whole = lax.dynamic_update_slice(
-                    whole, source[step][None, None], (spot, side, 0, 0)
-                )
-        return whole.reshape(-1, shard.shape[1]), parts
-
-    def scatter_rows(self, grad):
-        rows = grad.shape[0] // (2 * self.depth)
-        blocks = grad.reshape(self.depth, 2, rows, grad.shape[1])
-        there = lax.dynamic_index_in_dim(blocks, 1 - self.x, 1, False)
-        here = lax.dynamic_index_in_dim(blocks, self.x, 1, False)
-        both = here.astype(F32) + self.swap_x(there).astype(F32)
-        low = both.astype(BF16)
-        own = lax.dynamic_index_in_dim(both, self.z, 0, False)
-        for step in range(1, self.depth):
-            spot = (self.z + step) % self.depth
-            sent = lax.dynamic_index_in_dim(low, spot, 0, False)
-            own = own + self.shift_z(sent, step).astype(F32)
-        return own
+        parts = [value] + [
+            lax.ppermute(value, "dp", [(i, (i + 2 * k) % n) for i in range(n)])
+            for k in range(1, count)
+        ]
+        back = [parts[-m % count] for m in range(count)]
+        spot = 2 * self.z + self.x
+        return lax.dynamic_slice_in_dim(jnp.stack(back + back), (count - spot) % count, count, 0)
 
     def by_core(self, mine, other, axis):
         return jnp.where(
@@ -595,14 +640,6 @@
         given = partial_rows[2 * rows :].astype(BF16)
         pack = partial_rows[: 2 * rows].astype(F32) + self.swap_core(given).astype(F32)
         return pack[:rows] + self.swap_y(pack[rows:].astype(BF16)).astype(F32)
-
-    def sum_plane(self, value, combine):
-        value = combine(value, self.swap_x(value))
-        bit = 1
-        while bit < self.depth:
-            value = combine(value, self.swap_z(value, bit))
-            bit *= 2
-        return value
 
 
 def after(value, *others):
@@ -646,53 +683,44 @@
     y_index = at.y.astype(jnp.int32).reshape(1)
     d_rows = norm1_gain.shape[0]
 
-    (wf_keep,), (wf_give,) = at.core_columns([w_forget])
-    gains = jnp.stack([norm1_gain, norm2_gain])
-    pad = jnp.zeros((16 - 2 - heads, d_rows), BF16)
-    mine = jnp.concatenate([gains, wf_keep.T, pad], axis=0)
-    theirs = at.swap_core(jnp.concatenate([gains, wf_give.T, pad], axis=0))
-    small = at.by_core(mine, theirs, 1)
-    small = jnp.where(
-        at.x == 0,
-        jnp.concatenate([small, at.swap_x(small)], axis=1),
-        jnp.concatenate([at.swap_x(small), small], axis=1),
-    )
-    whole = jnp.zeros((16, at.depth, 4 * d_rows), BF16)
-    for step in range(at.depth):
-        part = small if step == 0 else at.shift_z(small, step)
-        spot = (at.z - step + at.depth) % at.depth
-        whole = lax.dynamic_update_slice(whole, part[:, None], (0, spot, 0))
-    small = whole.reshape(16, width)
-    gain_one = small[0:1].astype(F32)
-    gain_two = small[1:2].astype(F32)
-    forget_t = small[2 : 2 + heads]
-
-    keep, give = at.core_columns([w_query, w_key, w_value, w_output, w_gate, w_up, w_down])
+    keep, give = at.core_columns(
+        [w_query, w_key, w_value, w_output, w_gate, w_up, w_down, w_forget]
+    )
+    gains = jnp.stack([norm1_gain, norm2_gain], axis=1)
+    pad = jnp.zeros((d_rows, LANES - 2 * heads - 2), BF16)
 
     def shard_of(kept, given):
-        return at.by_core(kept, at.swap_core(given), 0)
-
-    attn_shard = shard_of(
-        jnp.concatenate([interleave(keep[:3]), keep[3]], axis=1),
-        jnp.concatenate([interleave(give[:3]), give[3]], axis=1),
-    )
+        return at.by_core(kept[None], at.swap_core(given)[None], 0)
+
+    def first_part(part):
+        return jnp.concatenate(
+            [interleave(part[:3]), part[7], part[7], gains, pad, part[3]], axis=1
+        )
+
+    attn_shard = shard_of(first_part(keep), first_part(give))
     ffn_shard = shard_of(
-        jnp.concatenate(keep[4:], axis=1),
-        jnp.concatenate(give[4:], axis=1),
-    )
-    attn_all, attn_parts = at.gather_rows(attn_shard)
+        jnp.concatenate(keep[4:7], axis=1),
+        jnp.concatenate(give[4:7], axis=1),
+    )
+    rows_all = at.gather_tokens(layer_in)
     units = keep[4].shape[1]
-    gu_shard = after(ffn_shard[:, : 2 * units], attn_parts[-1], attn_parts[-2])
-    gu_all, gu_parts = at.gather_rows(gu_shard)
-    down_shard = after(ffn_shard[:, 2 * units :], gu_parts[-1], gu_parts[-2])
-    down_all, _ = at.gather_rows(down_shard)
     qkv_cols = 3 * heads * HEAD_DIM
-    w_qkv, wo_all = attn_all[:, :qkv_cols], attn_all[:, qkv_cols:]
-
-    x_own = layer_in.astype(F32)
-    scale_one = lax.rsqrt(jnp.mean(x_own * x_own, axis=1, keepdims=True) + EPSILON)
-    unit_one = x_own * scale_one
-    normed_one = at.gather_tokens((unit_one * gain_one).astype(BF16))
+    in_cols = qkv_cols + LANES
+    (w_in, wo_all), last = at.gather_rings([attn_shard[..., :in_cols], attn_shard[..., in_cols:]])
+    gu_shard = after(ffn_shard[..., : 2 * units], *last)
+    (gu_all,), last = at.gather_rings([gu_shard])
+    (down_all,), _ = at.gather_rings([after(ffn_shard[..., 2 * units :], *last)])
+    w_qkv = w_in[:, :qkv_cols]
+    small = w_in[:, qkv_cols:].T
+    forget_t = small[:heads]
+    gain_one = small[2 * heads : 2 * heads + 1].astype(F32)
+    gain_two = small[2 * heads + 1 : 2 * heads + 2].astype(F32)
+
+    x_all = rows_all.astype(F32)
+    scale_one = lax.rsqrt(jnp.mean(x_all * x_all, axis=1, keepdims=True) + EPSILON)
+    unit_one = x_all * scale_one
+    normed_one = (unit_one * gain_one).astype(BF16)
+    x_own, scale_one, unit_one = x_all[:rows_loc], scale_one[:rows_loc], unit_one[:rows_loc]
     qkv = dot_nn(normed_one, w_qkv).astype(BF16)
 
     bias = lax.dynamic_slice_in_dim(forget_bias, at.core * heads, heads, 0)
@@ -726,26 +754,18 @@
     normed_two = at.gather_tokens((unit_two * gain_two).astype(BF16))
     grad_rows = at.gather_tokens(out_grad)
 
-    maxima = jnp.max(tops[:, :, :2], axis=(0, 3)).reshape(1, heads)
-    maxima = jnp.pad(maxima, ((0, 7), (0, LANES - heads)))
-    maxima = at.sum_plane(maxima, jnp.maximum)
-    maxima = at.by_core(maxima[0, :heads], at.swap_core(maxima)[0, :heads], 0)
-    clip_factor = jnp.minimum(1.0, clip_tau / jnp.maximum(maxima, 1.0))
-    columns = jnp.repeat(jnp.sqrt(clip_factor), HEAD_DIM)
-    clipped_query = (w_query.astype(F32) * columns[None, :]).astype(BF16)
-    clipped_key = (w_key.astype(F32) * columns[None, :]).astype(BF16)
-
     gate_up = dot_nn(normed_two, gu_all)
     gate_pre, up_pre = gate_up[:, :units], gate_up[:, units:]
     gate_sig = jax.nn.sigmoid(gate_pre)
     gate_act = gate_pre * gate_sig
     hidden = (gate_act * up_pre).astype(BF16)
-    g_down = at.scatter_rows(dot_tn(grad_rows, hidden).astype(BF16))
+    g_down = dot_tn(grad_rows, hidden).astype(BF16)
     grad_hidden = dot_nn(grad_rows, down_all)
     grad_gate = (grad_hidden * up_pre * gate_sig * (1.0 + gate_pre * (1.0 - gate_sig))).astype(BF16)
     grad_up = (grad_hidden * gate_act).astype(BF16)
-    g_gate = at.scatter_rows(dot_tn(normed_two, grad_gate).astype(BF16))
-    g_up = at.scatter_rows(dot_tn(normed_two, grad_up).astype(BF16))
+    g_gate = dot_tn(normed_two, grad_gate).astype(BF16)
+    g_up = dot_tn(normed_two, grad_up).astype(BF16)
+    g_down, g_gate, g_up = at.scatter_rings([g_down, g_gate, g_up])
     grad_gu = jnp.concatenate([grad_gate, grad_up], axis=1)
     grad_two = at.scatter_tokens(dot_nt(grad_gu, gu_all))
     layer_out = (resid + at.scatter_tokens(dot_nt(hidden, down_all))).astype(BF16)
@@ -757,9 +777,8 @@
     grad_attn = at.gather_tokens(grad_resid.astype(BF16))
 
     grad_mixed = dot_nn(grad_attn, wo_all).astype(BF16)
-    g_output = at.scatter_rows(dot_tn(grad_attn, mixed).astype(BF16))
+    g_output = dot_tn(grad_attn, mixed).astype(BF16)
     d_qkv, d_cum = attend_back(y_index, qkv, grad_mixed, inverse, expos, 2, pairs)
-    g_qkv = at.scatter_rows(dot_tn(normed_one, d_qkv).astype(BF16))
     d_cum = d_cum[:, :2].reshape(heads, 2, 2, rows_loc)
     back = jnp.einsum("hpbt,st->hpbs", d_cum, upper, precision=HIGHEST)
     total = back[..., :1]
@@ -769,10 +788,14 @@
     ).reshape(heads, 2 * pack)
     d_logit = d_log * jax.nn.sigmoid(-logits)
     bias_part = jnp.sum(d_logit, axis=1)
-    d_split = jnp.concatenate(split_low(d_logit), axis=0)
-    forget_part = dot_nn(d_split, normed_one)
-    forget_part = forget_part[:heads] + forget_part[heads:]
-    grad_one = dot_nt(d_qkv, w_qkv) + dot_tn(d_split, jnp.concatenate([forget_t, forget_t], axis=0))
+    d_split = jnp.concatenate(split_low(d_logit), axis=0).T
+    d_split = jnp.pad(d_split, ((0, 0), (0, LANES - 2 * heads)))
+    d_in = jnp.concatenate([d_qkv, d_split], axis=1)
+    g_in = dot_tn(normed_one, d_in).astype(BF16)
+    middle = in_cols // 2
+    g_output, g_low, g_high = at.scatter_rings([g_output, g_in[:, :middle], g_in[:, middle:]])
+    g_in = jnp.concatenate([g_low, g_high], axis=1)
+    grad_one = dot_nt(d_in, w_in)
     grad_one = at.scatter_tokens(grad_one)
 
     weighted = gain_one * grad_one
@@ -780,49 +803,51 @@
     norm1_part = jnp.sum(grad_one * unit_one, axis=0)
     x_grad = (grad_resid + scale_one * (weighted - unit_one * inner_one)).astype(BF16)
 
-    small = jnp.concatenate(
-        [
-            norm1_part[None],
-            norm2_part[None],
-            forget_part,
-            jnp.pad(bias_part[None], ((0, 0), (0, width - heads))),
-            jnp.zeros((16 - 3 - heads, width), F32),
-        ],
-        axis=0,
-    )
-    small = at.sum_plane(small, jnp.add)
-    other = at.swap_core(small)
-    norms = small[:2] + other[:2]
-    norms = norms + at.swap_y(norms)
-    norms = lax.dynamic_slice_in_dim(norms, at.y * (width // 2), width // 2, 1)
-    forget = at.by_core(small[2 : 2 + heads], other[2 : 2 + heads], 0)
-    index = lax.axis_index("dp")
-    g_forget = lax.dynamic_slice_in_dim(forget, index * d_rows, d_rows, 1).T
-    g_bias = at.by_core(small[2 + heads, :heads], other[2 + heads, :heads], 0)
+    norms = jnp.stack([norm1_part, norm2_part])
+    norms = norms + at.swap_core(norms)
+    cut = width // 2
+    norms = lax.dynamic_slice_in_dim(norms, at.y * cut, cut, 1) + at.swap_y(
+        lax.dynamic_slice_in_dim(norms, (1 - at.y) * cut, cut, 1)
+    )
+    maxima = jnp.max(tops[:, :, :2], axis=(0, 3)).reshape(heads)
+    lone = jnp.pad(jnp.stack([bias_part, maxima]), ((0, 4), (0, cut - heads)))
+    shared = at.share_plane(jnp.concatenate([norms, lone], axis=0))
+    sums = jnp.sum(shared[:, :3], axis=0)
+    lone = jnp.concatenate([sums[2:3], jnp.max(shared[:, 3:4], axis=0)], axis=0)[:, :LANES]
+    lone = at.by_core(lone[:, :heads], at.swap_core(lone)[:, :heads], 1)
+    g_bias = lone[0]
+    clip_factor = jnp.minimum(1.0, clip_tau / jnp.maximum(lone[1], 1.0))
+    columns = jnp.repeat(jnp.sqrt(clip_factor), HEAD_DIM)
+    clipped_query = (w_query.astype(F32) * columns[None, :]).astype(BF16)
+    clipped_key = (w_key.astype(F32) * columns[None, :]).astype(BF16)
 
     def place(own):
         keep, got = at.finish_grad(own)
         return at.by_core(keep, got, 1)
 
-    keep, got = at.finish_grad(g_qkv)
+    keep, got = at.finish_grad(g_in)
 
     def third(which):
-        def cut(value):
-            return value.reshape(d_rows, pairs, 3, LANES)[:, :, which].reshape(d_rows, -1)
-
-        return at.by_core(cut(keep), cut(got), 1)
+        def pick(value):
+            value = value[:, :qkv_cols].reshape(d_rows, pairs, 3, LANES)
+            return value[:, :, which].reshape(d_rows, -1)
+
+        return at.by_core(pick(keep), pick(got), 1)
+
+    def forget(value):
+        return value[:, qkv_cols : qkv_cols + heads] + value[:, qkv_cols + heads :][:, :heads]
 
     return (
         layer_out,
         x_grad,
-        norms[0],
+        sums[0],
         third(0),
         third(1),
         third(2),
-        g_forget,
+        at.by_core(forget(keep), forget(got), 1),
         g_bias,
         place(g_output),
-        norms[1],
+        sums[1],
         place(g_gate),
         place(g_up),
         place(g_down),

time: 730 us -> 592 us (0.81)
  waiting for transfers between devices: 395 us -> 243 us
  other arithmetic: 44.8 us -> 56.6 us
    ppermute x51 -> x87, waiting for transfers between devices: 381 us -> 206 us  [the longest x80 200 us: ring(): return lax.ppermute(value, 'dp', pairs)]
    ppermute x9, waiting for transfers between devices: 9.42 us -> 35.1 us  [swap_y(): return lax.ppermute(value, 'tensor', [(0, 1), (1, 0)])]
    another operation x0 -> x12, local copies, waits for them, and re-layouts: none -> 8.92 us  [the longest x6 7.48 us: pick(): return value[:, :, which].reshape(d_rows, -1)]
    dot_general x5 -> x4, matrix products: 28.7 us -> 32.5 us  [dot_nn(): lax.dot_general(left, right, (((1,), (0,)), ((), ())), preferred_element_...]
    dot_general x6 -> x5, matrix products: 22.8 us -> 20.1 us  [dot_tn(): lax.dot_general(left, right, (((0,), (0,)), ((), ())), preferred_element_...]
    ppermute x51 -> x87, starting transfers between devices: 97.1 us -> 95 us  [the longest x80 86 us: ring(): return lax.ppermute(value, 'dp', pairs)]
  transfers between devices with their start and end apart: 83 -> 118, of which waited for: 37 -> 56; matrix products, arithmetic and copies ran while one was open for 18% -> 24% of each run, Pallas kernels for 2% -> 6%
where the time goes in v2:
time: 592 us; the launch traced here: 583 us
  waiting for transfers between devices  243 us (41%)
  starting transfers between devices  113 us (19%)
  matrix products  78.1 us (13%)
  other arithmetic  56.6 us (10%)
  local copies, waits for them, and re-layouts  56.5 us (10%)
  Pallas kernels  33.4 us (6%)
    ppermute x80, waiting for transfers between devices, ring(): return lax.ppermute(value, 'dp', pairs)  200 us
    ppermute x80, starting transfers between devices, ring(): return lax.ppermute(value, 'dp', pairs)  86 us
    ppermute x9, waiting for transfers between devices, swap_y(): return lax.ppermute(value, 'tensor', [(0, 1), (1, 0)])  35.1 us
    dot_general x4, matrix products, dot_nn(): lax.dot_general(left, right, (((1,), (0,)), ((), ())), preferred_element_...  32.5 us
    dot_general x5, matrix products, dot_nt(): lax.dot_general(left, right, (((1,), (1,)), ((), ())), preferred_element_...  25 us
    dot_general x5, matrix products, dot_tn(): lax.dot_general(left, right, (((0,), (0,)), ((), ())), preferred_element_...  20.1 us
    pallas_call x1, Pallas kernels, attend_back(): pl.pallas_call(attend_back_kernel, grid_spec=grid_spec, out_shape=(jax.Sh...  17.5 us
    pallas_call x1, Pallas kernels, attend(): pl.pallas_call(attend_kernel, grid_spec=grid_spec, out_shape=(jax.ShapeDt...  16 us
  transfers between devices with their start and end apart: 118, of which 56 were waited for; matrix products, arithmetic and copies ran while one was open for 24% of the time, Pallas kernels for 6%

profile of v2, /device:TPU:0, one launch (start us, length us, event | category | flops | bytes accessed | tf_op | source)
XLA Modules:
  0.0 583.2 jit_solution(2606335926164840165)
XLA Ops:
  0.7 3.1 collective-permute-start.45
  19.2 3.4 collective-permute-done.13
  24.4 3.5 collective-permute-done.14
  35.2 3.0 collective-permute-done.17
  46.3 6.4 %collective-permute-done.4 = bf16[2,96,1280]{2,1,0:T(8,128)(2,1)S(1)} collective-permute-done((bf16[2,96,1280]{2,1,0:T(8,128)(2,1)S(1)}, bf16[2,96,1280]{2,1,0:T(8,128)(2,1)S(1)}, u32[]{:S(2)}, u32[]{:S(2)}) %collective-permute-start.4) | collective-permute-done | bytes 491552 | tf_op jit(solution)/shard_map/ppermute | solution.py:537
  56.6 9.4 %collective-permute-done.20 = bf16[1,96,384]{2,1,0:T(8,128)(2,1)S(1)} collective-permute-done((bf16[1,96,384]{2,1,0:T(8,128)(2,1)S(1)}, bf16[1,96,384]{2,1,0:T(8,128)(2,1)S(1)}, u32[]{:S(2)}, u32[]{:S(2)}) %collective-permute-start.20) | collective-permute-done | bytes 73760 | tf_op jit(solution)/shard_map/ppermute | solution.py:537
  69.0 6.7 %broadcast_multiply_fusion = f32[1024,1536]{1,0:T(8,128)} fusion(f32[1024]{0:T(1024)S(1)} %add_rsqrt_fusion, bf16[256,1536]{1,0:T(8,128)(2,1)S(1)} %collective-permute-done.2, bf16[256,1536]{1,0:T(8,128)(2,1)S(1)} %collective-permute-done.1, bf16[256,1536]{1,0:T(8,128)(2,1)S(1)} %collective-permute-done, bf16[256,1536]{1,0:T(8,128)(2,1)S(1)} %copy-done.2), kind=kLoop, calls=%fused_computation.30 | loop fusion | flops 14155776 | bytes 9441280 | tf_op jit(solution)/shard_map/mul | solution.py:721
  75.8 3.2 maximum_convert_fusion
  86.0 3.4 broadcast_in_dim.175
  89.5 2.1 bitcast_dynamic-update-slice_fusion.6
  91.7 14.6 %collective-permute-done.10 = bf16[1,96,1280]{2,1,0:T(8,128)(2,1)S(1)} collective-permute-done((bf16[1,96,1280]{2,1,0:T(8,128)(2,1)S(1)}, bf16[1,96,1280]{2,1,0:T(8,128)(2,1)S(1)}, u32[]{:S(2)}, u32[]{:S(2)}) %collective-permute-start.10) | collective-permute-done | bytes 245792 | tf_op jit(solution)/shard_map/ppermute | solution.py:537
  110.2 8.2 %convolution_convert_fusion.1.qkv_ref = bf16[1024,1152]{1,0:T(8,128)(2,1)} fusion(bf16[1536,1280]{1,0:T(8,128)(2,1)S(1)} %bitcast.395, f32[1536]{0:T(1024)S(1)} %get-tuple-element.69, f32[1024]{0:T(1024)S(1)} %add_rsqrt_fusion, bf16[256,1536]{1,0:T(8,128)(2,1)S(1)} %collective-permute-done.2, bf16[256,1536]{1,0:T(8,128)(2,1)S(1)} %collective-permute-done.1, ...), kind=kOutput, calls=%fused_computation.14 | convolution fusion | flops 3642359808 | bytes 9056256 | tf_op jit(solution)/shard_map/dot_general | solution.py:320
  121.8 16.0 %attend.1 = (bf16[1024,384]{1,0:T(8,128)(2,1)}, f32[1024,384]{1,0:T(8,128)}, bf16[2,3,2,256,768]{4,3,2,1,0:T(8,128)(2,1)}, f32[2,3,8,128]{3,2,1,0:T(8,128)}) custom-call(s32[1]{0:T(128)} %bitcast.y_ref, bf16[1024,1152]{1,0:T(8,128)(2,1)} %convolution_convert_fusion.1.qkv_ref, f32[3,8,1024]{2,1,0:T(8,128)} %pad_maximum_fusion.19.aux_ref), custom_call_target="tpu_custom_call" | custom-call | flops 1207959552 | bytes 20000000 | tf_op jit(solution)/shard_map/attend/pallas_call | solution.py:394
  137.8 3.3 fusion.95
  141.1 2.6 copy-done
  148.4 2.1 bitcast_dynamic-update-slice_fusion.5
  150.5 2.1 bitcast_dynamic-update-slice_fusion.4
  152.6 13.9 %collective-permute-done.29 = bf16[2,96,2048]{2,1,0:T(8,128)(2,1)S(1)} collective-permute-done((bf16[2,96,2048]{2,1,0:T(8,128)(2,1)}, bf16[2,96,2048]{2,1,0:T(8,128)(2,1)S(1)}, u32[]{:S(2)}, u32[]{:S(2)}) %collective-permute-start.29) | collective-permute-done | bytes 786464 | tf_op jit(solution)/shard_map/ppermute | solution.py:537
  174.2 11.5 %collective-permute-done.31 = bf16[2,96,2048]{2,1,0:T(8,128)(2,1)S(1)} collective-permute-done((bf16[2,96,2048]{2,1,0:T(8,128)(2,1)S(1)}, bf16[2,96,2048]{2,1,0:T(8,128)(2,1)S(1)}, u32[]{:S(2)}, u32[]{:S(2)}) %collective-permute-start.31) | collective-permute-done | bytes 786464 | tf_op jit(solution)/shard_map/ppermute | solution.py:537
  200.5 7.1 %collective-permute-done.33 = bf16[1,96,2048]{2,1,0:T(8,128)(2,1)S(1)} collective-permute-done((bf16[1,96,2048]{2,1,0:T(8,128)(2,1)S(1)}, bf16[1,96,2048]{2,1,0:T(8,128)(2,1)S(1)}, u32[]{:S(2)}, u32[]{:S(2)}) %collective-permute-start.33) | collective-permute-done | bytes 393248 | tf_op jit(solution)/shard_map/ppermute | solution.py:537
  209.5 4.0 collective-permute-done.37
  216.1 7.0 %collective-permute-done.39 = bf16[2,96,1024]{2,1,0:T(8,128)(2,1)S(1)} collective-permute-done((bf16[2,96,1024]{2,1,0:T(8,128)(2,1)S(1)}, bf16[2,96,1024]{2,1,0:T(8,128)(2,1)S(1)}, u32[]{:S(2)}, u32[]{:S(2)}) %collective-permute-start.39) | collective-permute-done | bytes 393248 | tf_op jit(solution)/shard_map/ppermute | solution.py:537
  225.3 3.5 collective-permute-done.41
  230.5 11.3 %fusion.86 = f32[1024,2048]{1,0:T(8,128)} fusion(bf16[1536,2048]{1,0:T(8,128)(2,1)} %bitcast.41, bf16[256,1536]{1,0:T(8,128)(2,1)S(1)} %collective-permute-done.25, bf16[256,1536]{1,0:T(8,128)(2,1)S(1)} %collective-permute-done.24, bf16[256,1536]{1,0:T(8,128)(2,1)S(1)} %collective-permute-done.23, bf16[256,1536]{1,0:T(8,128)(2,1)S(1)} %multiply_convert_fusion.4), kind=kOutput, calls=%fused_computation.359 | convolution fusion | flops 6455033856 | bytes 17825792 | tf_op jit(solution)/shard_map/dot_general | solution.py:320
  241.8 8.6 %multiply_convert_fusion.2 = (bf16[1024,1024]{1,0:T(8,128)(2,1)S(1)}, bf16[1024,1024]{1,0:T(8,128)(2,1)}, bf16[1024,1024]{1,0:T(8,128)(2,1)S(1)}) fusion(f32[1024,2048]{1,0:T(8,128)} %fusion.86, bf16[1024,1536]{1,0:T(8,128)(2,1)S(1)} %copy-done.30, bf16[1536,1024]{1,0:T(8,128)(2,1)S(1)} %bitcast.417), kind=kOutput, calls=%fused_computation.10 | convolution fusion | flops 3236954112 | bytes 20971520 | tf_op jit(solution)/shard_map/dot_general | solution.py:320
  250.3 3.7 convolution_convert_fusion.2
  254.1 3.5 fusion.96
  257.6 3.7 convolution_convert_fusion.3
  267.3 9.5 %fusion.1 = f32[1024,1536]{1,0:T(8,128)S(1)} fusion(bf16[1536,2048]{1,0:T(8,128)(2,1)} %bitcast.41, bf16[1024,1024]{1,0:T(8,128)(2,1)} %get-tuple-element.89, bf16[1024,1024]{1,0:T(8,128)(2,1)S(1)} %get-tuple-element.88), kind=kOutput, calls=%fused_computation.5 | convolution fusion | flops 6450839552 | bytes 16777216 | tf_op jit(solution)/shard_map/dot_general | solution.py:316
  276.8 6.0 %convolution_convert_fusion.4 = bf16[1536,1024]{1,0:T(8,128)(2,1)S(1)} fusion(bf16[1024,1024]{1,0:T(8,128)(2,1)} %copy-done.51, bf16[256,1536]{1,0:T(8,128)(2,1)} %copy-done.48, bf16[256,1536]{1,0:T(8,128)(2,1)} %copy-done.47, bf16[256,1536]{1,0:T(8,128)(2,1)} %copy-done.46, bf16[256,1536]{1,0:T(8,128)(2,1)} %copy-done.15), kind=kOutput, calls=%fused_computation.17 | convolution fusion | flops 3235381248 | bytes 8388608 | tf_op jit(solution)/shard_map/dot_general | solution.py:324
  292.4 6.9 %collective-permute-done.101 = bf16[2,96,1024]{2,1,0:T(8,128)(2,1)S(1)} collective-permute-done((bf16[2,96,1024]{2,1,0:T(8,128)(2,1)S(1)}, bf16[2,96,1024]{2,1,0:T(8,128)(2,1)S(1)}, u32[]{:S(2)}, u32[]{:S(2)}) %collective-permute-start.101) | collective-permute-done | bytes 393248 | tf_op jit(solution)/shard_map/ppermute | solution.py:537
  300.9 6.7 %collective-permute-done.110 = bf16[2,96,1024]{2,1,0:T(8,128)(2,1)S(1)} collective-permute-done((bf16[2,96,1024]{2,1,0:T(8,128)(2,1)S(1)}, bf16[2,96,1024]{2,1,0:T(8,128)(2,1)S(1)}, u32[]{:S(2)}, u32[]{:S(2)}) %collective-permute-start.110) | collective-permute-done | bytes 393248 | tf_op jit(solution)/shard_map/ppermute | solution.py:537
  309.3 6.7 %collective-permute-done.92 = bf16[2,96,1024]{2,1,0:T(8,128)(2,1)S(1)} collective-permute-done((bf16[2,96,1024]{2,1,0:T(8,128)(2,1)S(1)}, bf16[2,96,1024]{2,1,0:T(8,128)(2,1)S(1)}, u32[]{:S(2)}, u32[]{:S(2)}) %collective-permute-start.92) | collective-permute-done | bytes 393248 | tf_op jit(solution)/shard_map/ppermute | solution.py:537
  318.3 6.2 %collective-permute-done.102 = bf16[2,96,1024]{2,1,0:T(8,128)(2,1)S(1)} collective-permute-done((bf16[2,96,1024]{2,1,0:T(8,128)(2,1)S(1)}, bf16[2,96,1024]{2,1,0:T(8,128)(2,1)S(1)}, u32[]{:S(2)}, u32[]{:S(2)}) %collective-permute-start.102) | collective-permute-done | bytes 393248 | tf_op jit(solution)/shard_map/ppermute | solution.py:537
  326.4 6.5 %collective-permute-done.111 = bf16[2,96,1024]{2,1,0:T(8,128)(2,1)S(1)} collective-permute-done((bf16[2,96,1024]{2,1,0:T(8,128)(2,1)S(1)}, bf16[2,96,1024]{2,1,0:T(8,128)(2,1)S(1)}, u32[]{:S(2)}, u32[]{:S(2)}) %collective-permute-start.111) | collective-permute-done | bytes 393248 | tf_op jit(solution)/shard_map/ppermute | solution.py:537
  335.3 6.1 %collective-permute-done.93 = bf16[2,96,1024]{2,1,0:T(8,128)(2,1)S(1)} collective-permute-done((bf16[2,96,1024]{2,1,0:T(8,128)(2,1)S(1)}, bf16[2,96,1024]{2,1,0:T(8,128)(2,1)S(1)}, u32[]{:S(2)}, u32[]{:S(2)}) %collective-permute-start.93) | collective-permute-done | bytes 393248 | tf_op jit(solution)/shard_map/ppermute | solution.py:537
  343.4 10.0 %collective-permute-done.115 = bf16[2,96,1024]{2,1,0:T(8,128)(2,1)S(1)} collective-permute-done((bf16[2,96,1024]{2,1,0:T(8,128)(2,1)S(1)}, bf16[2,96,1024]{2,1,0:T(8,128)(2,1)S(1)}, u32[]{:S(2)}, u32[]{:S(2)}) %collective-permute-start.115) | collective-permute-done | bytes 393248 | tf_op jit(solution)/shard_map/ppermute | solution.py:537
  355.0 4.4 collective-permute-done.97
  365.4 6.0 %collective-permute-done.107 = bf16[2,96,1024]{2,1,0:T(8,128)(2,1)S(1)} collective-permute-done((bf16[2,96,1024]{2,1,0:T(8,128)(2,1)S(1)}, bf16[2,96,1024]{2,1,0:T(8,128)(2,1)S(1)}, u32[]{:S(2)}, u32[]{:S(2)}) %collective-permute-start.107) | collective-permute-done | bytes 393248 | tf_op jit(solution)/shard_map/ppermute | solution.py:537
  372.9 6.9 %collective-permute-done.116 = bf16[2,96,1024]{2,1,0:T(8,128)(2,1)S(1)} collective-permute-done((bf16[2,96,1024]{2,1,0:T(8,128)(2,1)S(1)}, bf16[2,96,1024]{2,1,0:T(8,128)(2,1)S(1)}, u32[]{:S(2)}, u32[]{:S(2)}) %collective-permute-start.116) | collective-permute-done | bytes 393248 | tf_op jit(solution)/shard_map/ppermute | solution.py:537
  382.2 12.5 %collective-permute-done.44 = bf16[256,1536]{1,0:T(8,128)(2,1)S(1)} collective-permute-done((bf16[256,1536]{1,0:T(8,128)(2,1)S(1)}, bf16[256,1536]{1,0:T(8,128)(2,1)S(1)}, u32[]{:S(2)}, u32[]{:S(2)}) %collective-permute-start.44) | collective-permute-done | bytes 786464 | tf_op jit(solution)/shard_map/ppermute | solution.py:526
  394.7 2.2 fusion.90
  400.1 12.6 %collective-permute-done.50 = bf16[256,1536]{1,0:T(8,128)(2,1)S(1)} collective-permute-done((bf16[256,1536]{1,0:T(8,128)(2,1)S(1)}, bf16[256,1536]{1,0:T(8,128)(2,1)S(1)}, u32[]{:S(2)}, u32[]{:S(2)}) %collective-permute-start.50) | collective-permute-done | bytes 786464 | tf_op jit(solution)/shard_map/ppermute | solution.py:526
  416.3 2.1 convolution_convert_fusion.5
  421.6 4.6 convolution_convert_fusion.6.do_ref
  426.2 17.5 %attend_back.1 = (bf16[1024,1152]{1,0:T(8,128)(2,1)}, f32[3,8,1024]{2,1,0:T(8,128)}) custom-call(s32[1]{0:T(128)} %bitcast.y_ref, bf16[1024,1152]{1,0:T(8,128)(2,1)} %convolution_convert_fusion.1.qkv_ref, bf16[1024,384]{1,0:T(8,128)(2,1)} %convolution_convert_fusion.6.do_ref, f32[1024,384]{1,0:T(8,128)} %get-tuple-element.27.inv_ref, ...), custom_call_target="tpu_custom_call" | custom-call | flops 3623878656 | bytes 20000000 | tf_op jit(solution)/shard_map/attend_back/pallas_call | solution.py:496
  447.3 7.1 %fusion.12 = f32[1024,1536]{1,0:T(8,128)S(1)} fusion(bf16[1536,1280]{1,0:T(8,128)(2,1)} %bitcast.396, bf16[1024,12]{1,0:T(8,128)(2,1)S(1)} %bitcast.444, bf16[1024,1152]{1,0:T(8,128)(2,1)} %get-tuple-element.29), kind=kOutput, calls=%fused_computation.59 | convolution fusion | flops 4034396160 | bytes 12607488 | tf_op jit(solution)/shard_map/dot_general | solution.py:316
  455.8 2.1 copy-done.7
  457.9 4.5 convolution_convert_fusion
  479.4 5.2 collective-permute-done.84
  487.0 4.7 collective-permute-done.73
  495.6 4.9 collective-permute-done.66
  502.9 3.3 collective-permute-done.74
  510.8 3.1 collective-permute-done.78
  517.5 4.9 collective-permute-done.71
  522.4 2.6 collective-permute-done.79
  529.5 2.8 slice_add_fusion
  547.0 6.8 %collective-permute-done.54 = bf16[256,1536]{1,0:T(8,128)(2,1)} collective-permute-done((bf16[256,1536]{1,0:T(8,128)(2,1)}, bf16[256,1536]{1,0:T(8,128)(2,1)}, u32[]{:S(2)}, u32[]{:S(2)}) %collective-permute-start.54) | collective-permute-done | bytes 786464 | tf_op jit(solution)/shard_map/ppermute | solution.py:526
  553.8 2.1 multiply_reduce_fusion.2
  560.9 2.1 collective-permute-start.57
  563.0 3.0 add_convert_fusion
  567.5 2.4 collective-permute-start.60
  573.0 2.9 collective-permute-done.61
  576.8 2.2 collective-permute-done.63
  (558 shorter events, 209.5 us)
Async XLA Ops:
  0.7 41.0 %collective-permute-start.45 = (bf16[256,1536]{1,0:T(8,128)(2,1)}, bf16[256,1536]{1,0:T(8,128)(2,1)}, u32[]{:S(2)}, u32[]{:S(2)}) collective-permute-start(bf16[256,1536]{1,0:T(8,128)(2,1)} %param.29), channel_id=1, source_target_pairs={{0,1},{1,0},{2,3},{3,2},{4,5},{5,4},{6,7},{7,6},{8,9},{9,8},{10,11... | collective-permute-start | bytes 2359304 | tf_op jit(solution)/shard_map/ppermute | solution.py:526
  3.8 39.7 %collective-permute-start.46 = (bf16[256,1536]{1,0:T(8,128)(2,1)}, bf16[256,1536]{1,0:T(8,128)(2,1)}, u32[]{:S(2)}, u32[]{:S(2)}) collective-permute-start(bf16[256,1536]{1,0:T(8,128)(2,1)} %param.29), channel_id=1, source_target_pairs={{0,2},{2,0},{4,6},{6,4},{8,10},{10,8},{12,14},{14,12},{16,18},{18,... | collective-permute-start | bytes 2359304 | tf_op jit(solution)/shard_map/ppermute | solution.py:523
  11.0 18.6 %collective-permute-start.26 = (bf16[96,3072]{1,0:T(8,128)(2,1)}, bf16[96,3072]{1,0:T(8,128)(2,1)}, u32[]{:S(2)}, u32[]{:S(2)}) collective-permute-start(bf16[96,3072]{1,0:T(8,128)(2,1)} %pad_maximum_fusion.2), channel_id=1, source_target_pairs={{0,2},{2,0},{4,6},{6,4},{8,10},{10,8},{12,14},{14,12},{16,18},{18,... | collective-permute-start | bytes 1769480 | tf_op jit(solution)/shard_map/ppermute | solution.py:523
  15.2 41.3 %collective-permute-start = (bf16[256,1536]{1,0:T(8,128)(2,1)S(1)}, bf16[256,1536]{1,0:T(8,128)(2,1)S(1)}, u32[]{:S(2)}, u32[]{:S(2)}) collective-permute-start(bf16[256,1536]{1,0:T(8,128)(2,1)S(1)} %copy-done.2), channel_id=1, source_target_pairs={{0,1},{1,0},{2,3},{3,2},{4,5},{5,4},{6,7},{7,6},{8,9},{9,8},{10,11... | collective-permute-start | bytes 2359304 | tf_op jit(solution)/shard_map/ppermute | solution.py:526
  38.1 30.0 %collective-permute-start.1 = (bf16[256,1536]{1,0:T(8,128)(2,1)S(1)}, bf16[256,1536]{1,0:T(8,128)(2,1)S(1)}, u32[]{:S(2)}, u32[]{:S(2)}) collective-permute-start(bf16[256,1536]{1,0:T(8,128)(2,1)S(1)} %copy-done.2), channel_id=1, source_target_pairs={{0,2},{2,0},{4,6},{6,4},{8,10},{10,8},{12,14},{14,12},{16,18},{18,... | collective-permute-start | bytes 2359304 | tf_op jit(solution)/shard_map/ppermute | solution.py:523
  40.1 12.6 %collective-permute-start.4 = (bf16[2,96,1280]{2,1,0:T(8,128)(2,1)S(1)}, bf16[2,96,1280]{2,1,0:T(8,128)(2,1)S(1)}, u32[]{:S(2)}, u32[]{:S(2)}) collective-permute-start(bf16[2,96,1280]{2,1,0:T(8,128)(2,1)S(1)} %slice.565), channel_id=1, source_target_pairs={{0,8},{2,10},{8,16},{10,18},{16,24},{18,26},{24,28},{26,30},{28,20... | collective-permute-start | bytes 1474568 | tf_op jit(solution)/shard_map/ppermute | solution.py:537
  41.8 12.9 %collective-permute-start.5 = (bf16[2,96,1280]{2,1,0:T(8,128)(2,1)S(1)}, bf16[2,96,1280]{2,1,0:T(8,128)(2,1)S(1)}, u32[]{:S(2)}, u32[]{:S(2)}) collective-permute-start(bf16[2,96,1280]{2,1,0:T(8,128)(2,1)S(1)} %slice.565), channel_id=1, source_target_pairs={{0,4},{2,6},{8,0},{10,2},{16,8},{18,10},{24,16},{26,18},{28,24},{3... | collective-permute-start | bytes 1474568 | tf_op jit(solution)/shard_map/ppermute | solution.py:537
  52.6 13.3 %collective-permute-start.6 = (bf16[2,96,1280]{2,1,0:T(8,128)(2,1)S(1)}, bf16[2,96,1280]{2,1,0:T(8,128)(2,1)S(1)}, u32[]{:S(2)}, u32[]{:S(2)}) collective-permute-start(bf16[2,96,1280]{2,1,0:T(8,128)(2,1)S(1)} %collective-permute-done.4), channel_id=1, source_target_pairs={{0,8},{2,10},{8,16},{10,18},{16,24},{18,26},{24,28},{26,30},{28,20... | collective-permute-start | bytes 1474568 | tf_op jit(solution)/shard_map/ppermute | solution.py:537
  54.6 13.0 %collective-permute-start.7 = (bf16[2,96,1280]{2,1,0:T(8,128)(2,1)S(1)}, bf16[2,96,1280]{2,1,0:T(8,128)(2,1)S(1)}, u32[]{:S(2)}, u32[]{:S(2)}) collective-permute-start(bf16[2,96,1280]{2,1,0:T(8,128)(2,1)S(1)} %collective-permute-done.5), channel_id=1, source_target_pairs={{0,4},{2,6},{8,0},{10,2},{16,8},{18,10},{24,16},{26,18},{28,24},{3... | collective-permute-start | bytes 1474568 | tf_op jit(solution)/shard_map/ppermute | solution.py:537
  56.5 19.3 %collective-permute-start.47 = (bf16[256,1536]{1,0:T(8,128)(2,1)}, bf16[256,1536]{1,0:T(8,128)(2,1)S(1)}, u32[]{:S(2)}, u32[]{:S(2)}) collective-permute-start(bf16[256,1536]{1,0:T(8,128)(2,1)} %collective-permute-done.45), channel_id=1, source_target_pairs={{0,2},{2,0},{4,6},{6,4},{8,10},{10,8},{12,14},{14,12},{16,18},{18,... | collective-permute-start | bytes 2359304 | tf_op jit(solution)/shard_map/ppermute | solution.py:523
  66.0 13.7 %collective-permute-start.8 = (bf16[2,96,1280]{2,1,0:T(8,128)(2,1)S(1)}, bf16[2,96,1280]{2,1,0:T(8,128)(2,1)S(1)}, u32[]{:S(2)}, u32[]{:S(2)}) collective-permute-start(bf16[2,96,1280]{2,1,0:T(8,128)(2,1)S(1)} %collective-permute-done.6), channel_id=1, source_target_pairs={{0,8},{2,10},{8,16},{10,18},{16,24},{18,26},{24,28},{26,30},{28,20... | collective-permute-start | bytes 1474568 | tf_op jit(solution)/shard_map/ppermute | solution.py:537
  67.6 14.1 %collective-permute-start.9 = (bf16[2,96,1280]{2,1,0:T(8,128)(2,1)S(1)}, bf16[2,96,1280]{2,1,0:T(8,128)(2,1)S(1)}, u32[]{:S(2)}, u32[]{:S(2)}) collective-permute-start(bf16[2,96,1280]{2,1,0:T(8,128)(2,1)S(1)} %collective-permute-done.7), channel_id=1, source_target_pairs={{0,4},{2,6},{8,0},{10,2},{16,8},{18,10},{24,16},{26,18},{28,24},{3... | collective-permute-start | bytes 1474568 | tf_op jit(solution)/shard_map/ppermute | solution.py:537
  81.7 64.7 %collective-permute-start.27 = (bf16[2,96,2048]{2,1,0:T(8,128)(2,1)}, bf16[2,96,2048]{2,1,0:T(8,128)(2,1)}, u32[]{:S(2)}, u32[]{:S(2)}) collective-permute-start(bf16[2,96,2048]{2,1,0:T(8,128)(2,1)} %slice.584), channel_id=1, source_target_pairs={{0,8},{2,10},{8,16},{10,18},{16,24},{18,26},{24,28},{26,30},{28,20... | collective-permute-start | bytes 2359304 | tf_op jit(solution)/shard_map/ppermute | solution.py:537
  83.4 64.7 %collective-permute-start.28 = (bf16[2,96,2048]{2,1,0:T(8,128)(2,1)}, bf16[2,96,2048]{2,1,0:T(8,128)(2,1)}, u32[]{:S(2)}, u32[]{:S(2)}) collective-permute-start(bf16[2,96,2048]{2,1,0:T(8,128)(2,1)} %slice.584), channel_id=1, source_target_pairs={{0,4},{2,6},{8,0},{10,2},{16,8},{18,10},{24,16},{26,18},{28,24},{3... | collective-permute-start | bytes 2359304 | tf_op jit(solution)/shard_map/ppermute | solution.py:537
  83.7 22.5 %collective-permute-start.10 = (bf16[1,96,1280]{2,1,0:T(8,128)(2,1)S(1)}, bf16[1,96,1280]{2,1,0:T(8,128)(2,1)S(1)}, u32[]{:S(2)}, u32[]{:S(2)}) collective-permute-start(bf16[1,96,1280]{2,1,0:T(8,128)(2,1)S(1)} %slice.566), channel_id=1, source_target_pairs={{0,8},{2,10},{8,16},{10,18},{16,24},{18,26},{24,28},{26,30},{28,20... | collective-permute-start | bytes 737288 | tf_op jit(solution)/shard_map/ppermute | solution.py:537
  85.5 21.9 %collective-permute-start.11 = (bf16[1,96,1280]{2,1,0:T(8,128)(2,1)S(1)}, bf16[1,96,1280]{2,1,0:T(8,128)(2,1)S(1)}, u32[]{:S(2)}, u32[]{:S(2)}) collective-permute-start(bf16[1,96,1280]{2,1,0:T(8,128)(2,1)S(1)} %slice.567), channel_id=1, source_target_pairs={{0,4},{2,6},{8,0},{10,2},{16,8},{18,10},{24,16},{26,18},{28,24},{3... | collective-permute-start | bytes 737288 | tf_op jit(solution)/shard_map/ppermute | solution.py:537
  145.0 25.6 %collective-permute-start.21 = (bf16[512,1536]{1,0:T(8,128)(2,1)}, bf16[512,1536]{1,0:T(8,128)(2,1)}, u32[]{:S(2)}, u32[]{:S(2)}) collective-permute-start(bf16[512,1536]{1,0:T(8,128)(2,1)} %slice.711), channel_id=1, source_target_pairs={{0,2},{2,0},{4,6},{6,4},{8,10},{10,8},{12,14},{14,12},{16,18},{18,... | collective-permute-start | bytes 4718600 | tf_op jit(solution)/shard_map/ppermute | solution.py:523
  146.4 20.2 %collective-permute-start.29 = (bf16[2,96,2048]{2,1,0:T(8,128)(2,1)}, bf16[2,96,2048]{2,1,0:T(8,128)(2,1)S(1)}, u32[]{:S(2)}, u32[]{:S(2)}) collective-permute-start(bf16[2,96,2048]{2,1,0:T(8,128)(2,1)} %collective-permute-done.27), channel_id=1, source_target_pairs={{0,8},{2,10},{8,16},{10,18},{16,24},{18,26},{24,28},{26,30},{28,20... | collective-permute-start | bytes 2359304 | tf_op jit(solution)/shard_map/ppermute | solution.py:537
  148.1 20.2 %collective-permute-start.30 = (bf16[2,96,2048]{2,1,0:T(8,128)(2,1)}, bf16[2,96,2048]{2,1,0:T(8,128)(2,1)S(1)}, u32[]{:S(2)}, u32[]{:S(2)}) collective-permute-start(bf16[2,96,2048]{2,1,0:T(8,128)(2,1)} %collective-permute-done.28), channel_id=1, source_target_pairs={{0,4},{2,6},{8,0},{10,2},{16,8},{18,10},{24,16},{26,18},{28,24},{3... | collective-permute-start | bytes 2359304 | tf_op jit(solution)/shard_map/ppermute | solution.py:537
  166.6 19.1 %collective-permute-start.31 = (bf16[2,96,2048]{2,1,0:T(8,128)(2,1)S(1)}, bf16[2,96,2048]{2,1,0:T(8,128)(2,1)S(1)}, u32[]{:S(2)}, u32[]{:S(2)}) collective-permute-start(bf16[2,96,2048]{2,1,0:T(8,128)(2,1)S(1)} %collective-permute-done.29), channel_id=1, source_target_pairs={{0,8},{2,10},{8,16},{10,18},{16,24},{18,26},{24,28},{26,30},{28,20... | collective-permute-start | bytes 2359304 | tf_op jit(solution)/shard_map/ppermute | solution.py:537
  168.3 18.8 %collective-permute-start.32 = (bf16[2,96,2048]{2,1,0:T(8,128)(2,1)S(1)}, bf16[2,96,2048]{2,1,0:T(8,128)(2,1)S(1)}, u32[]{:S(2)}, u32[]{:S(2)}) collective-permute-start(bf16[2,96,2048]{2,1,0:T(8,128)(2,1)S(1)} %collective-permute-done.30), channel_id=1, source_target_pairs={{0,4},{2,6},{8,0},{10,2},{16,8},{18,10},{24,16},{26,18},{28,24},{3... | collective-permute-start | bytes 2359304 | tf_op jit(solution)/shard_map/ppermute | solution.py:537
  172.6 21.1 %collective-permute-start.22 = (bf16[256,1536]{1,0:T(8,128)(2,1)S(1)}, bf16[256,1536]{1,0:T(8,128)(2,1)S(1)}, u32[]{:S(2)}, u32[]{:S(2)}) collective-permute-start(bf16[256,1536]{1,0:T(8,128)(2,1)S(1)} %slice.715), channel_id=1, source_target_pairs={{0,1},{1,0},{2,3},{3,2},{4,5},{5,4},{6,7},{7,6},{8,9},{9,8},{10,11... | collective-permute-start | bytes 2359304 | tf_op jit(solution)/shard_map/ppermute | solution.py:526
  187.1 12.0 %collective-permute-start.35 = (bf16[2,96,1024]{2,1,0:T(8,128)(2,1)S(1)}, bf16[2,96,1024]{2,1,0:T(8,128)(2,1)S(1)}, u32[]{:S(2)}, u32[]{:S(2)}) collective-permute-start(bf16[2,96,1024]{2,1,0:T(8,128)(2,1)S(1)} %slice.589), channel_id=1, source_target_pairs={{0,8},{2,10},{8,16},{10,18},{16,24},{18,26},{24,28},{26,30},{28,20... | collective-permute-start | bytes 1179656 | tf_op jit(solution)/shard_map/ppermute | solution.py:537
  189.2 18.4 %collective-permute-start.33 = (bf16[1,96,2048]{2,1,0:T(8,128)(2,1)S(1)}, bf16[1,96,2048]{2,1,0:T(8,128)(2,1)S(1)}, u32[]{:S(2)}, u32[]{:S(2)}) collective-permute-start(bf16[1,96,2048]{2,1,0:T(8,128)(2,1)S(1)} %slice.585), channel_id=1, source_target_pairs={{0,8},{2,10},{8,16},{10,18},{16,24},{18,26},{24,28},{26,30},{28,20... | collective-permute-start | bytes 1179656 | tf_op jit(solution)/shard_map/ppermute | solution.py:537
  190.2 18.4 %collective-permute-start.34 = (bf16[1,96,2048]{2,1,0:T(8,128)(2,1)S(1)}, bf16[1,96,2048]{2,1,0:T(8,128)(2,1)S(1)}, u32[]{:S(2)}, u32[]{:S(2)}) collective-permute-start(bf16[1,96,2048]{2,1,0:T(8,128)(2,1)S(1)} %slice.586), channel_id=1, source_target_pairs={{0,4},{2,6},{8,0},{10,2},{16,8},{18,10},{24,16},{26,18},{28,24},{3... | collective-permute-start | bytes 1179656 | tf_op jit(solution)/shard_map/ppermute | solution.py:537
  195.7 20.3 %collective-permute-start.23 = (bf16[256,1536]{1,0:T(8,128)(2,1)S(1)}, bf16[256,1536]{1,0:T(8,128)(2,1)S(1)}, u32[]{:S(2)}, u32[]{:S(2)}) collective-permute-start(bf16[256,1536]{1,0:T(8,128)(2,1)S(1)} %multiply_convert_fusion.4), channel_id=1, source_target_pairs={{0,1},{1,0},{2,3},{3,2},{4,5},{5,4},{6,7},{7,6},{8,9},{9,8},{10,11... | collective-permute-start | bytes 2359304 | tf_op jit(solution)/shard_map/ppermute | solution.py:526
  199.1 31.4 %collective-permute-start.24 = (bf16[256,1536]{1,0:T(8,128)(2,1)S(1)}, bf16[256,1536]{1,0:T(8,128)(2,1)S(1)}, u32[]{:S(2)}, u32[]{:S(2)}) collective-permute-start(bf16[256,1536]{1,0:T(8,128)(2,1)S(1)} %multiply_convert_fusion.4), channel_id=1, source_target_pairs={{0,2},{2,0},{4,6},{6,4},{8,10},{10,8},{12,14},{14,12},{16,18},{18,... | collective-permute-start | bytes 2359304 | tf_op jit(solution)/shard_map/ppermute | solution.py:523
  200.0 13.5 %collective-permute-start.37 = (bf16[2,96,1024]{2,1,0:T(8,128)(2,1)S(1)}, bf16[2,96,1024]{2,1,0:T(8,128)(2,1)S(1)}, u32[]{:S(2)}, u32[]{:S(2)}) collective-permute-start(bf16[2,96,1024]{2,1,0:T(8,128)(2,1)S(1)} %collective-permute-done.35), channel_id=1, source_target_pairs={{0,8},{2,10},{8,16},{10,18},{16,24},{18,26},{24,28},{26,30},{28,20... | collective-permute-start | bytes 1179656 | tf_op jit(solution)/shard_map/ppermute | solution.py:537
  216.0 14.5 %collective-permute-start.25 = (bf16[256,1536]{1,0:T(8,128)(2,1)S(1)}, bf16[256,1536]{1,0:T(8,128)(2,1)S(1)}, u32[]{:S(2)}, u32[]{:S(2)}) collective-permute-start(bf16[256,1536]{1,0:T(8,128)(2,1)S(1)} %collective-permute-done.23), channel_id=1, source_target_pairs={{0,2},{2,0},{4,6},{6,4},{8,10},{10,8},{12,14},{14,12},{16,18},{18,... | collective-permute-start | bytes 2359304 | tf_op jit(solution)/shard_map/ppermute | solution.py:523
  262.3 22.2 %collective-permute-start.100 = (bf16[1,96,1024]{2,1,0:T(8,128)(2,1)}, bf16[1,96,1024]{2,1,0:T(8,128)(2,1)}, u32[]{:S(2)}, u32[]{:S(2)}) collective-permute-start(bf16[1,96,1024]{2,1,0:T(8,128)(2,1)} %get-tuple-element.105), channel_id=1, source_target_pairs={{0,8},{2,10},{8,16},{10,18},{16,24},{18,26},{24,28},{26,30},{28,20... | collective-permute-start | bytes 589832 | tf_op jit(solution)/shard_map/ppermute | solution.py:537
  263.5 21.9 %collective-permute-start.104 = (bf16[1,96,1024]{2,1,0:T(8,128)(2,1)}, bf16[1,96,1024]{2,1,0:T(8,128)(2,1)}, u32[]{:S(2)}, u32[]{:S(2)}) collective-permute-start(bf16[1,96,1024]{2,1,0:T(8,128)(2,1)} %get-tuple-element.107), channel_id=1, source_target_pairs={{0,4},{2,6},{8,0},{10,2},{16,8},{18,10},{24,16},{26,18},{28,24},{3... | collective-permute-start | bytes 589832 | tf_op jit(solution)/shard_map/ppermute | solution.py:537
  265.1 21.6 %collective-permute-start.109 = (bf16[1,96,1024]{2,1,0:T(8,128)(2,1)}, bf16[1,96,1024]{2,1,0:T(8,128)(2,1)}, u32[]{:S(2)}, u32[]{:S(2)}) collective-permute-start(bf16[1,96,1024]{2,1,0:T(8,128)(2,1)} %get-tuple-element.97), channel_id=1, source_target_pairs={{0,8},{2,10},{8,16},{10,18},{16,24},{18,26},{24,28},{26,30},{28,20... | collective-permute-start | bytes 589832 | tf_op jit(solution)/shard_map/ppermute | solution.py:537
  266.3 20.9 %collective-permute-start.113 = (bf16[1,96,1024]{2,1,0:T(8,128)(2,1)}, bf16[1,96,1024]{2,1,0:T(8,128)(2,1)}, u32[]{:S(2)}, u32[]{:S(2)}) collective-permute-start(bf16[1,96,1024]{2,1,0:T(8,128)(2,1)} %get-tuple-element.99), channel_id=1, source_target_pairs={{0,4},{2,6},{8,0},{10,2},{16,8},{18,10},{24,16},{26,18},{28,24},{3... | collective-permute-start | bytes 589832 | tf_op jit(solution)/shard_map/ppermute | solution.py:537
  285.4 74.6 %collective-permute-start.48 = (bf16[512,1536]{1,0:T(8,128)(2,1)S(1)}, bf16[512,1536]{1,0:T(8,128)(2,1)S(1)}, u32[]{:S(2)}, u32[]{:S(2)}) collective-permute-start(bf16[512,1536]{1,0:T(8,128)(2,1)S(1)} %slice.709), channel_id=1, source_target_pairs={{0,2},{2,0},{4,6},{6,4},{8,10},{10,8},{12,14},{14,12},{16,18},{18,... | collective-permute-start | bytes 4718600 | tf_op jit(solution)/shard_map/ppermute | solution.py:523
  286.7 31.1 %collective-permute-start.105 = (bf16[2,96,1024]{2,1,0:T(8,128)(2,1)S(1)}, bf16[2,96,1024]{2,1,0:T(8,128)(2,1)S(1)}, u32[]{:S(2)}, u32[]{:S(2)}) collective-permute-start(bf16[2,96,1024]{2,1,0:T(8,128)(2,1)S(1)} %pad_maximum_fusion.8), channel_id=1, source_target_pairs={{0,4},{2,6},{8,0},{10,2},{16,8},{18,10},{24,16},{26,18},{28,24},{3... | collective-permute-start | bytes 1179656 | tf_op jit(solution)/shard_map/ppermute | solution.py:537
  287.2 12.0 %collective-permute-start.101 = (bf16[2,96,1024]{2,1,0:T(8,128)(2,1)S(1)}, bf16[2,96,1024]{2,1,0:T(8,128)(2,1)S(1)}, u32[]{:S(2)}, u32[]{:S(2)}) collective-permute-start(bf16[2,96,1024]{2,1,0:T(8,128)(2,1)S(1)} %pad_maximum_fusion.7), channel_id=1, source_target_pairs={{0,8},{2,10},{8,16},{10,18},{16,24},{18,26},{24,28},{26,30},{28,20... | collective-permute-start | bytes 1179656 | tf_op jit(solution)/shard_map/ppermute | solution.py:537
  290.1 36.3 %collective-permute-start.114 = (bf16[2,96,1024]{2,1,0:T(8,128)(2,1)S(1)}, bf16[2,96,1024]{2,1,0:T(8,128)(2,1)S(1)}, u32[]{:S(2)}, u32[]{:S(2)}) collective-permute-start(bf16[2,96,1024]{2,1,0:T(8,128)(2,1)S(1)} %pad_maximum_fusion.10), channel_id=1, source_target_pairs={{0,4},{2,6},{8,0},{10,2},{16,8},{18,10},{24,16},{26,18},{28,24},{3... | collective-permute-start | bytes 1179656 | tf_op jit(solution)/shard_map/ppermute | solution.py:537
  290.6 17.0 %collective-permute-start.110 = (bf16[2,96,1024]{2,1,0:T(8,128)(2,1)S(1)}, bf16[2,96,1024]{2,1,0:T(8,128)(2,1)S(1)}, u32[]{:S(2)}, u32[]{:S(2)}) collective-permute-start(bf16[2,96,1024]{2,1,0:T(8,128)(2,1)S(1)} %pad_maximum_fusion.9), channel_id=1, source_target_pairs={{0,8},{2,10},{8,16},{10,18},{16,24},{18,26},{24,28},{26,30},{28,20... | collective-permute-start | bytes 1179656 | tf_op jit(solution)/shard_map/ppermute | solution.py:537
  299.2 16.9 %collective-permute-start.92 = (bf16[2,96,1024]{2,1,0:T(8,128)(2,1)S(1)}, bf16[2,96,1024]{2,1,0:T(8,128)(2,1)S(1)}, u32[]{:S(2)}, u32[]{:S(2)}) collective-permute-start(bf16[2,96,1024]{2,1,0:T(8,128)(2,1)S(1)} %pad_maximum_fusion.5), channel_id=1, source_target_pairs={{0,8},{2,10},{8,16},{10,18},{16,24},{18,26},{24,28},{26,30},{28,20... | collective-permute-start | bytes 1179656 | tf_op jit(solution)/shard_map/ppermute | solution.py:537
  307.7 16.9 %collective-permute-start.102 = (bf16[2,96,1024]{2,1,0:T(8,128)(2,1)S(1)}, bf16[2,96,1024]{2,1,0:T(8,128)(2,1)S(1)}, u32[]{:S(2)}, u32[]{:S(2)}) collective-permute-start(bf16[2,96,1024]{2,1,0:T(8,128)(2,1)S(1)} %fusion.21), channel_id=1, source_target_pairs={{0,8},{2,10},{8,16},{10,18},{16,24},{18,26},{24,28},{26,30},{28,20... | collective-permute-start | bytes 1179656 | tf_op jit(solution)/shard_map/ppermute | solution.py:537
  316.1 16.9 %collective-permute-start.111 = (bf16[2,96,1024]{2,1,0:T(8,128)(2,1)S(1)}, bf16[2,96,1024]{2,1,0:T(8,128)(2,1)S(1)}, u32[]{:S(2)}, u32[]{:S(2)}) collective-permute-start(bf16[2,96,1024]{2,1,0:T(8,128)(2,1)S(1)} %fusion.16), channel_id=1, source_target_pairs={{0,8},{2,10},{8,16},{10,18},{16,24},{18,26},{24,28},{26,30},{28,20... | collective-permute-start | bytes 1179656 | tf_op jit(solution)/shard_map/ppermute | solution.py:537
  317.8 15.7 %collective-permute-start.96 = (bf16[2,96,1024]{2,1,0:T(8,128)(2,1)S(1)}, bf16[2,96,1024]{2,1,0:T(8,128)(2,1)S(1)}, u32[]{:S(2)}, u32[]{:S(2)}) collective-permute-start(bf16[2,96,1024]{2,1,0:T(8,128)(2,1)S(1)} %pad_maximum_fusion.6), channel_id=1, source_target_pairs={{0,4},{2,6},{8,0},{10,2},{16,8},{18,10},{24,16},{26,18},{28,24},{3... | collective-permute-start | bytes 1179656 | tf_op jit(solution)/shard_map/ppermute | solution.py:537
  324.5 16.9 %collective-permute-start.93 = (bf16[2,96,1024]{2,1,0:T(8,128)(2,1)S(1)}, bf16[2,96,1024]{2,1,0:T(8,128)(2,1)S(1)}, u32[]{:S(2)}, u32[]{:S(2)}) collective-permute-start(bf16[2,96,1024]{2,1,0:T(8,128)(2,1)S(1)} %fusion.26), channel_id=1, source_target_pairs={{0,8},{2,10},{8,16},{10,18},{16,24},{18,26},{24,28},{26,30},{28,20... | collective-permute-start | bytes 1179656 | tf_op jit(solution)/shard_map/ppermute | solution.py:537
  326.3 34.7 %collective-permute-start.43 = (bf16[512,1536]{1,0:T(8,128)(2,1)S(1)}, bf16[512,1536]{1,0:T(8,128)(2,1)S(1)}, u32[]{:S(2)}, u32[]{:S(2)}) collective-permute-start(bf16[512,1536]{1,0:T(8,128)(2,1)S(1)} %slice.710), channel_id=1, source_target_pairs={{0,2},{2,0},{4,6},{6,4},{8,10},{10,8},{12,14},{14,12},{16,18},{18,... | collective-permute-start | bytes 4718600 | tf_op jit(solution)/shard_map/ppermute | solution.py:523
  333.5 29.7 %collective-permute-start.103 = (bf16[2,96,1024]{2,1,0:T(8,128)(2,1)S(1)}, bf16[2,96,1024]{2,1,0:T(8,128)(2,1)S(1)}, u32[]{:S(2)}, u32[]{:S(2)}) collective-permute-start(bf16[2,96,1024]{2,1,0:T(8,128)(2,1)S(1)} %get-tuple-element.101), channel_id=1, source_target_pairs={{0,8},{2,10},{8,16},{10,18},{16,24},{18,26},{24,28},{26,30},{28,20... | collective-permute-start | bytes 1179656 | tf_op jit(solution)/shard_map/ppermute | solution.py:537
  342.7 16.7 %collective-permute-start.97 = (bf16[2,96,1024]{2,1,0:T(8,128)(2,1)S(1)}, bf16[2,96,1024]{2,1,0:T(8,128)(2,1)S(1)}, u32[]{:S(2)}, u32[]{:S(2)}) collective-permute-start(bf16[2,96,1024]{2,1,0:T(8,128)(2,1)S(1)} %get-tuple-element.110), channel_id=1, source_target_pairs={{0,4},{2,6},{8,0},{10,2},{16,8},{18,10},{24,16},{26,18},{28,24},{3... | collective-permute-start | bytes 1179656 | tf_op jit(solution)/shard_map/ppermute | solution.py:537
  360.0 19.9 %collective-permute-start.116 = (bf16[2,96,1024]{2,1,0:T(8,128)(2,1)S(1)}, bf16[2,96,1024]{2,1,0:T(8,128)(2,1)S(1)}, u32[]{:S(2)}, u32[]{:S(2)}) collective-permute-start(bf16[2,96,1024]{2,1,0:T(8,128)(2,1)S(1)} %fusion.15), channel_id=1, source_target_pairs={{0,4},{2,6},{8,0},{10,2},{16,8},{18,10},{24,16},{26,18},{28,24},{3... | collective-permute-start | bytes 1179656 | tf_op jit(solution)/shard_map/ppermute | solution.py:537
  361.1 20.5 %collective-permute-start.49 = (bf16[256,1536]{1,0:T(8,128)(2,1)S(1)}, bf16[256,1536]{1,0:T(8,128)(2,1)S(1)}, u32[]{:S(2)}, u32[]{:S(2)}) collective-permute-start(bf16[256,1536]{1,0:T(8,128)(2,1)S(1)} %slice.713), channel_id=1, source_target_pairs={{0,1},{1,0},{2,3},{3,2},{4,5},{5,4},{6,7},{7,6},{8,9},{9,8},{10,11... | collective-permute-start | bytes 2359304 | tf_op jit(solution)/shard_map/ppermute | solution.py:526
  363.3 35.8 %collective-permute-start.94 = (bf16[2,96,1024]{2,1,0:T(8,128)(2,1)}, bf16[2,96,1024]{2,1,0:T(8,128)(2,1)S(1)}, u32[]{:S(2)}, u32[]{:S(2)}) collective-permute-start(bf16[2,96,1024]{2,1,0:T(8,128)(2,1)} %get-tuple-element.109), channel_id=1, source_target_pairs={{0,8},{2,10},{8,16},{10,18},{16,24},{18,26},{24,28},{26,30},{28,20... | collective-permute-start | bytes 1179656 | tf_op jit(solution)/shard_map/ppermute | solution.py:537
  364.9 34.2 %collective-permute-start.98 = (bf16[2,96,1024]{2,1,0:T(8,128)(2,1)S(1)}, bf16[2,96,1024]{2,1,0:T(8,128)(2,1)S(1)}, u32[]{:S(2)}, u32[]{:S(2)}) collective-permute-start(bf16[2,96,1024]{2,1,0:T(8,128)(2,1)S(1)} %fusion.25), channel_id=1, source_target_pairs={{0,4},{2,6},{8,0},{10,2},{16,8},{18,10},{24,16},{26,18},{28,24},{3... | collective-permute-start | bytes 1179656 | tf_op jit(solution)/shard_map/ppermute | solution.py:537
  371.4 23.3 %collective-permute-start.44 = (bf16[256,1536]{1,0:T(8,128)(2,1)S(1)}, bf16[256,1536]{1,0:T(8,128)(2,1)S(1)}, u32[]{:S(2)}, u32[]{:S(2)}) collective-permute-start(bf16[256,1536]{1,0:T(8,128)(2,1)S(1)} %slice.714), channel_id=1, source_target_pairs={{0,1},{1,0},{2,3},{3,2},{4,5},{5,4},{6,7},{7,6},{8,9},{9,8},{10,11... | collective-permute-start | bytes 2359304 | tf_op jit(solution)/shard_map/ppermute | solution.py:526
  396.9 15.8 %collective-permute-start.50 = (bf16[256,1536]{1,0:T(8,128)(2,1)S(1)}, bf16[256,1536]{1,0:T(8,128)(2,1)S(1)}, u32[]{:S(2)}, u32[]{:S(2)}) collective-permute-start(bf16[256,1536]{1,0:T(8,128)(2,1)S(1)} %get-tuple-element.84), channel_id=1, source_target_pairs={{0,1},{1,0},{2,3},{3,2},{4,5},{5,4},{6,7},{7,6},{8,9},{9,8},{10,11... | collective-permute-start | bytes 2359304 | tf_op jit(solution)/shard_map/ppermute | solution.py:526
  398.4 14.3 %collective-permute-start.117 = (bf16[96,1024]{1,0:T(8,128)(2,1)S(1)}, bf16[96,1024]{1,0:T(8,128)(2,1)S(1)}, u32[]{:S(2)}, u32[]{:S(2)}) collective-permute-start(bf16[96,1024]{1,0:T(8,128)(2,1)S(1)} %dynamic-slice_convert_fusion), channel_id=1, source_target_pairs={{0,2},{2,0},{4,6},{6,4},{8,10},{10,8},{12,14},{14,12},{16,18},{18,... | collective-permute-start | bytes 589832 | tf_op jit(solution)/shard_map/ppermute | solution.py:523
  398.6 14.2 %collective-permute-start.108 = (bf16[96,1024]{1,0:T(8,128)(2,1)S(1)}, bf16[96,1024]{1,0:T(8,128)(2,1)S(1)}, u32[]{:S(2)}, u32[]{:S(2)}) collective-permute-start(bf16[96,1024]{1,0:T(8,128)(2,1)S(1)} %dynamic-slice_convert_fusion.1), channel_id=1, source_target_pairs={{0,2},{2,0},{4,6},{6,4},{8,10},{10,8},{12,14},{14,12},{16,18},{18,... | collective-permute-start | bytes 589832 | tf_op jit(solution)/shard_map/ppermute | solution.py:523
  399.4 13.5 %collective-permute-start.99 = (bf16[96,1024]{1,0:T(8,128)(2,1)S(1)}, bf16[96,1024]{1,0:T(8,128)(2,1)S(1)}, u32[]{:S(2)}, u32[]{:S(2)}) collective-permute-start(bf16[96,1024]{1,0:T(8,128)(2,1)S(1)} %dynamic-slice_convert_fusion.2), channel_id=1, source_target_pairs={{0,2},{2,0},{4,6},{6,4},{8,10},{10,8},{12,14},{14,12},{16,18},{18,... | collective-permute-start | bytes 589832 | tf_op jit(solution)/shard_map/ppermute | solution.py:523
  399.5 16.8 %collective-permute-start.51 = (bf16[256,1536]{1,0:T(8,128)(2,1)S(1)}, bf16[256,1536]{1,0:T(8,128)(2,1)S(1)}, u32[]{:S(2)}, u32[]{:S(2)}) collective-permute-start(bf16[256,1536]{1,0:T(8,128)(2,1)S(1)} %get-tuple-element.84), channel_id=1, source_target_pairs={{0,2},{2,0},{4,6},{6,4},{8,10},{10,8},{12,14},{14,12},{16,18},{18,... | collective-permute-start | bytes 2359304 | tf_op jit(solution)/shard_map/ppermute | solution.py:523
  419.2 46.0 %collective-permute-start.82 = (bf16[1,96,384]{2,1,0:T(8,128)(2,1)}, bf16[1,96,384]{2,1,0:T(8,128)(2,1)}, u32[]{:S(2)}, u32[]{:S(2)}) collective-permute-start(bf16[1,96,384]{2,1,0:T(8,128)(2,1)} %get-tuple-element.138), channel_id=1, source_target_pairs={{0,8},{2,10},{8,16},{10,18},{16,24},{18,26},{24,28},{26,30},{28,20... | collective-permute-start | bytes 221192 | tf_op jit(solution)/shard_map/ppermute | solution.py:537
  421.0 46.0 %collective-permute-start.86 = (bf16[1,96,384]{2,1,0:T(8,128)(2,1)}, bf16[1,96,384]{2,1,0:T(8,128)(2,1)}, u32[]{:S(2)}, u32[]{:S(2)}) collective-permute-start(bf16[1,96,384]{2,1,0:T(8,128)(2,1)} %get-tuple-element.140), channel_id=1, source_target_pairs={{0,4},{2,6},{8,0},{10,2},{16,8},{18,10},{24,16},{26,18},{28,24},{3... | collective-permute-start | bytes 221192 | tf_op jit(solution)/shard_map/ppermute | solution.py:537
  457.8 71.7 %collective-permute-start.53 = (bf16[512,1536]{1,0:T(8,128)(2,1)}, bf16[512,1536]{1,0:T(8,128)(2,1)}, u32[]{:S(2)}, u32[]{:S(2)}) collective-permute-start(bf16[512,1536]{1,0:T(8,128)(2,1)} %slice.708), channel_id=1, source_target_pairs={{0,2},{2,0},{4,6},{6,4},{8,10},{10,8},{12,14},{14,12},{16,18},{18,... | collective-permute-start | bytes 4718600 | tf_op jit(solution)/shard_map/ppermute | solution.py:523
  472.6 21.7 %collective-permute-start.69 = (bf16[2,96,640]{2,1,0:T(8,128)(2,1)S(1)}, bf16[2,96,640]{2,1,0:T(8,128)(2,1)S(1)}, u32[]{:S(2)}, u32[]{:S(2)}) collective-permute-start(bf16[2,96,640]{2,1,0:T(8,128)(2,1)S(1)} %pad_maximum_fusion.14), channel_id=1, source_target_pairs={{0,4},{2,6},{8,0},{10,2},{16,8},{18,10},{24,16},{26,18},{28,24},{3... | collective-permute-start | bytes 737288 | tf_op jit(solution)/shard_map/ppermute | solution.py:537
  473.7 12.4 %collective-permute-start.65 = (bf16[2,96,640]{2,1,0:T(8,128)(2,1)S(1)}, bf16[2,96,640]{2,1,0:T(8,128)(2,1)S(1)}, u32[]{:S(2)}, u32[]{:S(2)}) collective-permute-start(bf16[2,96,640]{2,1,0:T(8,128)(2,1)S(1)} %pad_maximum_fusion.13), channel_id=1, source_target_pairs={{0,8},{2,10},{8,16},{10,18},{16,24},{18,26},{24,28},{26,30},{28,20... | collective-permute-start | bytes 737288 | tf_op jit(solution)/shard_map/ppermute | solution.py:537
  479.1 23.2 %collective-permute-start.77 = (bf16[2,96,640]{2,1,0:T(8,128)(2,1)S(1)}, bf16[2,96,640]{2,1,0:T(8,128)(2,1)S(1)}, u32[]{:S(2)}, u32[]{:S(2)}) collective-permute-start(bf16[2,96,640]{2,1,0:T(8,128)(2,1)S(1)} %pad_maximum_fusion.16), channel_id=1, source_target_pairs={{0,4},{2,6},{8,0},{10,2},{16,8},{18,10},{24,16},{26,18},{28,24},{3... | collective-permute-start | bytes 737288 | tf_op jit(solution)/shard_map/ppermute | solution.py:537
  492.7 14.4 %collective-permute-start.85 = (bf16[2,96,384]{2,1,0:T(8,128)(2,1)S(1)}, bf16[2,96,384]{2,1,0:T(8,128)(2,1)S(1)}, u32[]{:S(2)}, u32[]{:S(2)}) collective-permute-start(bf16[2,96,384]{2,1,0:T(8,128)(2,1)S(1)} %get-tuple-element.134), channel_id=1, source_target_pairs={{0,8},{2,10},{8,16},{10,18},{16,24},{18,26},{24,28},{26,30},{28,20... | collective-permute-start | bytes 442376 | tf_op jit(solution)/shard_map/ppermute | solution.py:537
  533.3 20.5 %collective-permute-start.54 = (bf16[256,1536]{1,0:T(8,128)(2,1)}, bf16[256,1536]{1,0:T(8,128)(2,1)}, u32[]{:S(2)}, u32[]{:S(2)}) collective-permute-start(bf16[256,1536]{1,0:T(8,128)(2,1)} %slice.712), channel_id=1, source_target_pairs={{0,1},{1,0},{2,3},{3,2},{4,5},{5,4},{6,7},{7,6},{8,9},{9,8},{10,11... | collective-permute-start | bytes 2359304 | tf_op jit(solution)/shard_map/ppermute | solution.py:526
  (108 other events, 1057.4 us)

commit v3 on v2

--- a/solution.py
+++ b/solution.py
@@ -509,6 +509,77 @@
     )(y_index, qkv, d_out, inverse, expos)
 
 
+class Gathering:
+    def __init__(self, at, shard):
+        self.at, self.step, self.half = at, 1, at.depth
+        self.whole = jnp.zeros((2 * at.depth,) + shard.shape, shard.dtype)
+        self.put(shard, 0, 0)
+        self.send(shard, shard)
+
+    def put(self, part, step, side):
+        start = (self.at.block_of(step), side, 0, 0)
+        self.whole = lax.dynamic_update_slice(self.whole, part[None], start)
+
+    def send(self, up, down):
+        if self.step == self.half:
+            up, down = up[:1], down[1:]
+        self.came = (self.at.ring(up, 1), self.at.ring(down, -1))
+
+    def take(self, *others):
+        up, down = after_all(self.came, *others)
+        self.put(up, -self.step, 0)
+        self.put(down, self.step, 1 if self.step == self.half else 0)
+        return up, down
+
+    def advance(self, *others):
+        up, down = self.take(*others)
+        self.step += 1
+        self.send(up, down)
+        return up, down
+
+    def finish(self, *others):
+        self.take(*others)
+        return self.whole.reshape(-1, self.whole.shape[-1])
+
+
+class Reduction:
+    def __init__(self, at, grad, *others):
+        self.at, self.step, self.half = at, 1, at.depth
+        count = 2 * at.depth
+        self.blocks = grad.reshape(count, 2, grad.shape[0] // (2 * count), grad.shape[1])
+        far = self.own(self.half)
+        self.sent = after_all((far[:1], far[1:]), *others) if others else (far[:1], far[1:])
+        self.send()
+
+    def own(self, step):
+        start = (self.at.block_of(step), 0, 0, 0)
+        return lax.dynamic_slice(self.blocks, start, (1,) + self.blocks.shape[1:])[0]
+
+    def send(self):
+        self.came = (self.at.ring(self.sent[0], 1), self.at.ring(self.sent[1], -1))
+
+    def advance(self, *others):
+        up, down = after_all(self.came, *others)
+        ahead, behind = self.own(self.half - self.step), self.own(self.step - self.half)
+        if self.step == 1:
+            first = (ahead[:1].astype(F32) + up.astype(F32)).astype(BF16)
+            second = (behind[1:].astype(F32) + down.astype(F32)).astype(BF16)
+            up = jnp.concatenate([first, ahead[1:]], axis=0)
+            down = jnp.concatenate([behind[:1], second], axis=0)
+        else:
+            up = (ahead.astype(F32) + up.astype(F32)).astype(BF16)
+            down = (behind.astype(F32) + down.astype(F32)).astype(BF16)
+        self.sent = (up, down)
+        self.step += 1
+        self.send()
+        return up, down
+
+    def finish(self, *others):
+        up, down = after_all(self.came, *others)
+        total = self.own(0).astype(F32) + up.astype(F32) + down.astype(F32)
+        return total.reshape(-1, total.shape[-1])
+
+
 class Place:
     def __init__(self):
         self.dp = lax.axis_size("dp")
@@ -541,70 +612,14 @@
         spot = (jnp.where(self.x == 0, self.z, count - 1 - self.z) + step + count) % count
         return jnp.where(spot < self.depth, 2 * spot, 2 * (count - 1 - spot) + 1)
 
-    def gather_rings(self, shards):
-        count = 2 * self.depth
-        half = self.depth
-
-        def put(whole, part, step, side=0):
-            return lax.dynamic_update_slice(whole, part[None], (self.block_of(step), side, 0, 0))
-
-        wholes = [put(jnp.zeros((count,) + s.shape, s.dtype), s, 0) for s in shards]
-        up, down = list(shards), list(shards)
-        last = None
-        for step in range(1, half + 1):
-            for k in range(len(shards)):
-                if step < half:
-                    up[k], down[k] = self.ring(up[k], 1), self.ring(down[k], -1)
-                else:
-                    up[k], down[k] = self.ring(up[k][:1], 1), self.ring(down[k][1:], -1)
-            for k in range(len(shards)):
-                wholes[k] = put(wholes[k], up[k], -step)
-                wholes[k] = put(wholes[k], down[k], step, 0 if step < half else 1)
-            if step == half - 1:
-                last = up + down
-        wholes = [w.reshape(-1, w.shape[-1]) for w in wholes]
-        return wholes, last
-
-    def scatter_rings(self, grads):
-        count = 2 * self.depth
-        half = self.depth
-        blocks = [g.reshape(count, 2, g.shape[0] // (2 * count), g.shape[1]) for g in grads]
-
-        def own(k, step):
-            start = (self.block_of(step), 0, 0, 0)
-            return lax.dynamic_slice(blocks[k], start, (1,) + blocks[k].shape[1:])[0]
-
-        ups = [own(k, half)[:1] for k in range(len(grads))]
-        downs = [own(k, half)[1:] for k in range(len(grads))]
-        totals = []
-        for step in range(1, half + 1):
-            for k in range(len(grads)):
-                ups[k], downs[k] = self.ring(ups[k], 1), self.ring(downs[k], -1)
-                if step == half:
-                    total = own(k, 0).astype(F32) + ups[k].astype(F32) + downs[k].astype(F32)
-                    totals.append(total.reshape(-1, total.shape[-1]))
-                    continue
-                ahead, behind = own(k, half - step), own(k, step - half)
-                if step == 1:
-                    first = (ahead[:1].astype(F32) + ups[k].astype(F32)).astype(BF16)
-                    ups[k] = jnp.concatenate([first, ahead[1:]], axis=0)
-                    second = (behind[1:].astype(F32) + downs[k].astype(F32)).astype(BF16)
-                    downs[k] = jnp.concatenate([behind[:1], second], axis=0)
-                else:
-                    ups[k] = (ahead.astype(F32) + ups[k].astype(F32)).astype(BF16)
-                    downs[k] = (behind.astype(F32) + downs[k].astype(F32)).astype(BF16)
-        return totals
-
-    def share_plane(self, value):
-        count = 2 * self.depth
-        n = self.dp
-        parts = [value] + [
-            lax.ppermute(value, "dp", [(i, (i + 2 * k) % n) for i in range(n)])
-            for k in range(1, count)
-        ]
-        back = [parts[-m % count] for m in range(count)]
-        spot = 2 * self.z + self.x
-        return lax.dynamic_slice_in_dim(jnp.stack(back + back), (count - spot) % count, count, 0)
+    def sum_plane(self, value, combine):
+        step = 2
+        while step < self.dp:
+            value = combine(
+                value, lax.ppermute(value, "dp", [(i, i ^ step) for i in range(self.dp)])
+            )
+            step *= 2
+        return value
 
     def by_core(self, mine, other, axis):
         return jnp.where(
@@ -629,27 +644,29 @@
         give = lax.dynamic_slice_in_dim(own, (1 - self.core) * rows, rows, 0)
         return keep, self.swap_core(give.astype(BF16)).astype(F32)
 
-    def gather_tokens(self, rows):
-        near = self.swap_y(rows)
-        return jnp.concatenate(
-            [rows, near, self.swap_core(rows), self.swap_core(near)], axis=0
-        )
-
-    def scatter_tokens(self, partial_rows):
-        rows = partial_rows.shape[0] // 4
-        given = partial_rows[2 * rows :].astype(BF16)
-        pack = partial_rows[: 2 * rows].astype(F32) + self.swap_core(given).astype(F32)
-        return pack[:rows] + self.swap_y(pack[rows:].astype(BF16)).astype(F32)
+    def join(self, rows, near):
+        both = jnp.concatenate([rows, near], axis=0)
+        return jnp.concatenate([both, self.swap_core(both)], axis=0)
+
+    def meet_core(self, left, right, dot):
+        half = left.shape[0] // 2
+        given = dot(left[half:], right).astype(BF16)
+        got = self.swap_core(given)
+        part = dot(after(left, given)[:half], right)
+        return part, got
 
 
 def after(value, *others):
     return lax.optimization_barrier((value,) + others)[0]
 
 
+def after_all(values, *others):
+    return lax.optimization_barrier(tuple(values) + others)[: len(values)]
+
+
 def interleave(parts):
-    rows = parts[0].shape[0]
-    stacked = jnp.stack([p.reshape(rows, -1, LANES) for p in parts], axis=2)
-    return stacked.reshape(rows, -1)
+    starts = range(0, parts[0].shape[1], LANES)
+    return jnp.concatenate([p[:, s : s + LANES] for s in starts for p in parts], axis=1)
 
 
 def split_low(value):
@@ -683,44 +700,50 @@
     y_index = at.y.astype(jnp.int32).reshape(1)
     d_rows = norm1_gain.shape[0]
 
-    keep, give = at.core_columns(
-        [w_query, w_key, w_value, w_output, w_gate, w_up, w_down, w_forget]
-    )
+    units = w_gate.shape[1] // 2
+    keep, give = at.core_columns([w_query, w_key, w_value, w_output, w_forget])
     gains = jnp.stack([norm1_gain, norm2_gain], axis=1)
     pad = jnp.zeros((d_rows, LANES - 2 * heads - 2), BF16)
 
-    def shard_of(kept, given):
-        return at.by_core(kept[None], at.swap_core(given)[None], 0)
-
     def first_part(part):
         return jnp.concatenate(
-            [interleave(part[:3]), part[7], part[7], gains, pad, part[3]], axis=1
+            [interleave(part[:3]), part[4], part[4], gains, pad, part[3]], axis=1
         )
 
-    attn_shard = shard_of(first_part(keep), first_part(give))
-    ffn_shard = shard_of(
-        jnp.concatenate(keep[4:7], axis=1),
-        jnp.concatenate(give[4:7], axis=1),
-    )
-    rows_all = at.gather_tokens(layer_in)
-    units = keep[4].shape[1]
+    attn_shard = at.by_core(first_part(keep)[None], at.swap_core(first_part(give))[None], 0)
+    rows_near = at.swap_y(layer_in)
+    grad_near = at.swap_y(after(out_grad, rows_near))
     qkv_cols = 3 * heads * HEAD_DIM
     in_cols = qkv_cols + LANES
-    (w_in, wo_all), last = at.gather_rings([attn_shard[..., :in_cols], attn_shard[..., in_cols:]])
-    gu_shard = after(ffn_shard[..., : 2 * units], *last)
-    (gu_all,), last = at.gather_rings([gu_shard])
-    (down_all,), _ = at.gather_rings([after(ffn_shard[..., 2 * units :], *last)])
+    attn_ring = Gathering(at, attn_shard)
+    moved = attn_ring.advance()
+    keep, give = at.core_columns(after_all((w_gate, w_up, w_down), *moved))
+    ffn_shard = at.by_core(
+        jnp.concatenate(keep, axis=1)[None],
+        at.swap_core(jnp.concatenate(give, axis=1))[None],
+        0,
+    )
+    attn_ring.advance(rows_near)
+    attn_ring.advance(grad_near)
+    ffn_ring = Gathering(at, after(ffn_shard, *attn_ring.came))
+    attn_all = attn_ring.finish()
+    w_in, wo_all = attn_all[:, :in_cols], attn_all[:, in_cols:]
+    rows_all = at.join(layer_in, rows_near)
+    grad_rows = at.join(out_grad, grad_near)
     w_qkv = w_in[:, :qkv_cols]
     small = w_in[:, qkv_cols:].T
     forget_t = small[:heads]
     gain_one = small[2 * heads : 2 * heads + 1].astype(F32)
     gain_two = small[2 * heads + 1 : 2 * heads + 2].astype(F32)
 
-    x_all = rows_all.astype(F32)
-    scale_one = lax.rsqrt(jnp.mean(x_all * x_all, axis=1, keepdims=True) + EPSILON)
-    unit_one = x_all * scale_one
-    normed_one = (unit_one * gain_one).astype(BF16)
-    x_own, scale_one, unit_one = x_all[:rows_loc], scale_one[:rows_loc], unit_one[:rows_loc]
+    def first_norm(rows):
+        rows = rows.astype(F32)
+        return rows, lax.rsqrt(jnp.mean(rows * rows, axis=1, keepdims=True) + EPSILON)
+
+    x_all, scale_all = first_norm(rows_all)
+    normed_one = (x_all * scale_all * gain_one).astype(BF16)
+    x_own, scale_one = first_norm(layer_in)
+    unit_one = x_own * scale_one
     qkv = dot_nn(normed_one, w_qkv).astype(BF16)
 
     bias = lax.dynamic_slice_in_dim(forget_bias, at.core * heads, heads, 0)
@@ -747,43 +770,76 @@
     )
     mixed, inverse, expos, tops = attend(y_index, qkv, aux, 2, pairs)
 
-    attn_part = dot_nt(mixed, wo_all)
-    resid = x_own + at.scatter_tokens(attn_part)
+    moved = ffn_ring.advance(mixed)
+    part, got = at.meet_core(after(mixed, *moved), wo_all, dot_nt)
+    mine = part + got.astype(F32)
+    given = mine[rows_loc:].astype(BF16)
+    got = at.swap_y(given)
+    resid = x_own + (mine[:rows_loc] + got.astype(F32))
     scale_two = lax.rsqrt(jnp.mean(resid * resid, axis=1, keepdims=True) + EPSILON)
     unit_two = resid * scale_two
-    normed_two = at.gather_tokens((unit_two * gain_two).astype(BF16))
-    grad_rows = at.gather_tokens(out_grad)
+    normed_own = (unit_two * gain_two).astype(BF16)
+    near = at.swap_y(normed_own)
+    moved = ffn_ring.advance(normed_own)
+    (near,) = after_all((near,), *moved)
+    normed_two = at.join(normed_own, near)
+    ffn_ring.advance(normed_two)
+    ffn_all = ffn_ring.finish()
+    gu_all, down_all = ffn_all[:, : 2 * units], ffn_all[:, 2 * units :]
 
     gate_up = dot_nn(normed_two, gu_all)
     gate_pre, up_pre = gate_up[:, :units], gate_up[:, units:]
     gate_sig = jax.nn.sigmoid(gate_pre)
     gate_act = gate_pre * gate_sig
     hidden = (gate_act * up_pre).astype(BF16)
-    g_down = dot_tn(grad_rows, hidden).astype(BF16)
     grad_hidden = dot_nn(grad_rows, down_all)
     grad_gate = (grad_hidden * up_pre * gate_sig * (1.0 + gate_pre * (1.0 - gate_sig))).astype(BF16)
     grad_up = (grad_hidden * gate_act).astype(BF16)
-    g_gate = dot_tn(normed_two, grad_gate).astype(BF16)
-    g_up = dot_tn(normed_two, grad_up).astype(BF16)
-    g_down, g_gate, g_up = at.scatter_rings([g_down, g_gate, g_up])
     grad_gu = jnp.concatenate([grad_gate, grad_up], axis=1)
-    grad_two = at.scatter_tokens(dot_nt(grad_gu, gu_all))
-    layer_out = (resid + at.scatter_tokens(dot_nt(hidden, down_all))).astype(BF16)
-
+
+    part, got = at.meet_core(grad_gu, gu_all, dot_nt)
+    down_sum = Reduction(at, dot_tn(grad_rows, after(hidden, part)).astype(BF16))
+    mine = part + after(got, down_sum.blocks).astype(F32)
+    given = mine[rows_loc:].astype(BF16)
+    got = at.swap_y(given)
+    gu_sum = Reduction(at, dot_tn(normed_two, after(grad_gu, given)).astype(BF16))
+    moved = down_sum.advance(gu_sum.blocks)
+
+    (got,) = after_all((got,), *moved)
+    grad_two = mine[:rows_loc] + got.astype(F32)
     weighted = gain_two * grad_two
     inner_two = jnp.mean(unit_two * weighted, axis=1, keepdims=True)
     norm2_part = jnp.sum(grad_two * unit_two, axis=0)
     grad_resid = out_grad.astype(F32) + scale_two * (weighted - unit_two * inner_two)
-    grad_attn = at.gather_tokens(grad_resid.astype(BF16))
+    grad_own = grad_resid.astype(BF16)
+    near = at.swap_y(grad_own)
+    moved = gu_sum.advance(grad_own)
+    out_given = dot_nt(after(hidden, *moved)[pack:], down_all).astype(BF16)
+    moved = down_sum.advance(out_given)
+    out_part = dot_nt(after(hidden, *moved)[:pack], down_all)
+    (near,) = after_all((near,), out_part)
+    grad_attn = at.join(grad_own, near)
 
     grad_mixed = dot_nn(grad_attn, wo_all).astype(BF16)
-    g_output = dot_tn(grad_attn, mixed).astype(BF16)
-    d_qkv, d_cum = attend_back(y_index, qkv, grad_mixed, inverse, expos, 2, pairs)
+    out_got = at.swap_core(after(out_given, grad_attn))
+    moved = gu_sum.advance(grad_mixed)
+    d_qkv, d_cum = attend_back(
+        y_index, qkv, after(grad_mixed, *moved), inverse, expos, 2, pairs
+    )
+
+    def place(own):
+        keep, got = at.finish_grad(own)
+        return at.by_core(keep, got, 1)
+
+    moved = down_sum.advance(d_qkv)
+    moved = gu_sum.advance(*moved)
+    middle = 7 * LANES
+    low = dot_tn(normed_one, after(d_qkv, *moved)[:, :middle]).astype(BF16)
     d_cum = d_cum[:, :2].reshape(heads, 2, 2, rows_loc)
     back = jnp.einsum("hpbt,st->hpbs", d_cum, upper, precision=HIGHEST)
-    total = back[..., :1]
+    ends = back[..., :1]
     d_log = jnp.stack(
-        [back[:, :, 0] + (1.0 - later) * total[:, :, 1], back[:, :, 1] + later * total[:, :, 0]],
+        [back[:, :, 0] + (1.0 - later) * ends[:, :, 1], back[:, :, 1] + later * ends[:, :, 0]],
         axis=2,
     ).reshape(heads, 2 * pack)
     d_logit = d_log * jax.nn.sigmoid(-logits)
@@ -791,19 +847,40 @@
     d_split = jnp.concatenate(split_low(d_logit), axis=0).T
     d_split = jnp.pad(d_split, ((0, 0), (0, LANES - 2 * heads)))
     d_in = jnp.concatenate([d_qkv, d_split], axis=1)
-    g_in = dot_tn(normed_one, d_in).astype(BF16)
-    middle = in_cols // 2
-    g_output, g_low, g_high = at.scatter_rings([g_output, g_in[:, :middle], g_in[:, middle:]])
-    g_in = jnp.concatenate([g_low, g_high], axis=1)
-    grad_one = dot_nt(d_in, w_in)
-    grad_one = at.scatter_tokens(grad_one)
-
+    d_in_late, attn_late = after_all((d_in, grad_attn), low)
+    high = jnp.concatenate(
+        [dot_tn(normed_one, d_in_late[:, middle:]), dot_tn(attn_late, mixed)], axis=1
+    ).astype(BF16)
+    total = down_sum.finish(high)
+    low_sum = Reduction(at, low, total)
+    g_down = place(total)
+    part, got = at.meet_core(after(d_in, *low_sum.sent), w_in, dot_nt)
+    total = gu_sum.finish(part)
+    high_sum = Reduction(at, high, total)
+    mine = part + after(got, *high_sum.sent).astype(F32)
+    given = mine[rows_loc:].astype(BF16)
+    got = at.swap_y(given)
+    moved = low_sum.advance(given)
+    moved = high_sum.advance(*moved)
+    moved = low_sum.advance(*moved)
+    (got,) = after_all((got,), *moved)
+
+    grad_one = mine[:rows_loc] + got.astype(F32)
     weighted = gain_one * grad_one
     inner_one = jnp.mean(unit_one * weighted, axis=1, keepdims=True)
     norm1_part = jnp.sum(grad_one * unit_one, axis=0)
     x_grad = (grad_resid + scale_one * (weighted - unit_one * inner_one)).astype(BF16)
-
-    norms = jnp.stack([norm1_part, norm2_part])
+    out_own = out_part + after(out_got, norm1_part).astype(F32)
+    out_got = at.swap_y(out_own[rows_loc:].astype(BF16))
+    layer_out = (resid + (out_own[:rows_loc] + out_got.astype(F32))).astype(BF16)
+    moved = high_sum.advance(norm1_part)
+    keep, other = at.finish_grad(total)
+    g_gate = at.by_core(keep[:, :units], other[:, :units], 1)
+    g_up = at.by_core(keep[:, units:], other[:, units:], 1)
+    moved = low_sum.advance(*moved)
+    moved = high_sum.advance(*moved)
+
+    norms = after(jnp.stack([norm1_part, norm2_part]), *moved)
     norms = norms + at.swap_core(norms)
     cut = width // 2
     norms = lax.dynamic_slice_in_dim(norms, at.y * cut, cut, 1) + at.swap_y(
@@ -811,9 +888,13 @@
     )
     maxima = jnp.max(tops[:, :, :2], axis=(0, 3)).reshape(heads)
     lone = jnp.pad(jnp.stack([bias_part, maxima]), ((0, 4), (0, cut - heads)))
-    shared = at.share_plane(jnp.concatenate([norms, lone], axis=0))
-    sums = jnp.sum(shared[:, :3], axis=0)
-    lone = jnp.concatenate([sums[2:3], jnp.max(shared[:, 3:4], axis=0)], axis=0)[:, :LANES]
+    sums = at.sum_plane(
+        jnp.concatenate([norms, lone], axis=0),
+        lambda one, two: jnp.concatenate(
+            [one[:3] + two[:3], jnp.maximum(one[3:], two[3:])], axis=0
+        ),
+    )
+    lone = sums[2:4, :LANES]
     lone = at.by_core(lone[:, :heads], at.swap_core(lone)[:, :heads], 1)
     g_bias = lone[0]
     clip_factor = jnp.minimum(1.0, clip_tau / jnp.maximum(lone[1], 1.0))
@@ -821,10 +902,7 @@
     clipped_query = (w_query.astype(F32) * columns[None, :]).astype(BF16)
     clipped_key = (w_key.astype(F32) * columns[None, :]).astype(BF16)
 
-    def place(own):
-        keep, got = at.finish_grad(own)
-        return at.by_core(keep, got, 1)
-
+    g_in = jnp.concatenate([low_sum.finish(norms), high_sum.finish(norms)], axis=1)
     keep, got = at.finish_grad(g_in)
 
     def third(which):
@@ -846,11 +924,11 @@
         third(2),
         at.by_core(forget(keep), forget(got), 1),
         g_bias,
-        place(g_output),
+        at.by_core(keep[:, in_cols:], got[:, in_cols:], 1),
         sums[1],
-        place(g_gate),
-        place(g_up),
-        place(g_down),
+        g_gate,
+        g_up,
+        g_down,
         clip_factor,
         clipped_query,
         clipped_key,

time: 592 us -> 455 us (0.77)
  waiting for transfers between devices: 243 us -> 165 us
  starting transfers between devices: 113 us -> 69.4 us
  local copies, waits for them, and re-layouts: 56.5 us -> 35.2 us
    ppermute x80 -> x48, waiting for transfers between devices: 200 us -> 89.2 us  [ring(): return lax.ppermute(value, 'dp', pairs)]
    ppermute x80 -> x48, starting transfers between devices: 86 us -> 48.7 us  [ring(): return lax.ppermute(value, 'dp', pairs)]
    ppermute x9, waiting for transfers between devices: 35.1 us -> 64.9 us  [swap_y(): return lax.ppermute(value, 'tensor', [(0, 1), (1, 0)])]
    concatenate x15 -> x22, other arithmetic: 1.6 us -> 12.8 us  [the longest x1 3.54 us: join(): return jnp.concatenate([both, self.swap_core(both)], axis=0)]
    convert_element_type x27 -> x17, other arithmetic: 12.3 us -> 23 us  [the longest x8 13.1 us: advance(): down = (behind.astype(F32) + down.astype(F32)).astype(BF16)]
    another operation x17 -> x2, local copies, waits for them, and re-layouts: 8.84 us -> 0.01 us  [paired_body(): norms = after(jnp.stack([norm1_part, norm2_part]), *moved)]
    select_n x11, other arithmetic: 12.8 us -> 5.95 us  [by_core(): jnp.where(self.core == 0, jnp.concatenate([mine, other], axis=axis), jnp....]
    mul x3 -> x2, other arithmetic: 7.38 us -> 0.63 us  [the longest x1 0.53 us: paired_body(): normed_own = (unit_two * gain_two).astype(BF16)]
  transfers between devices with their start and end apart: 118 -> 76, of which waited for: 56 -> 35; matrix products, arithmetic and copies ran while one was open for 24% -> 31% of each run, Pallas kernels for 6% -> 7%
where the time goes in v3:
time: 455 us; the launch traced here: 449 us
  waiting for transfers between devices  165 us (36%)
  matrix products  80.9 us (18%)
  starting transfers between devices  69.4 us (15%)
  other arithmetic  62.3 us (14%)
  local copies, waits for them, and re-layouts  35.2 us (8%)
  Pallas kernels  33.3 us (7%)
    ppermute x48, waiting for transfers between devices, ring(): return lax.ppermute(value, 'dp', pairs)  89.2 us
    ppermute x9, waiting for transfers between devices, swap_y(): return lax.ppermute(value, 'tensor', [(0, 1), (1, 0)])  64.9 us
    ppermute x48, starting transfers between devices, ring(): return lax.ppermute(value, 'dp', pairs)  48.7 us
    dot_general x4, matrix products, dot_nn(): lax.dot_general(left, right, (((1,), (0,)), ((), ())), preferred_element_...  31.2 us
    dot_general x9, matrix products, dot_nt(): lax.dot_general(left, right, (((1,), (1,)), ((), ())), preferred_element_...  27.2 us
    dot_general x5, matrix products, dot_tn(): lax.dot_general(left, right, (((0,), (0,)), ((), ())), preferred_element_...  21.4 us
    pallas_call x1, Pallas kernels, attend_back(): pl.pallas_call(attend_back_kernel, grid_spec=grid_spec, out_shape=(jax.Sh...  17.4 us
    pallas_call x1, Pallas kernels, attend(): pl.pallas_call(attend_kernel, grid_spec=grid_spec, out_shape=(jax.ShapeDt...  16 us
  transfers between devices with their start and end apart: 76, of which 35 were waited for; matrix products, arithmetic and copies ran while one was open for 31% of the time, Pallas kernels for 7%

profile of v3, /device:TPU:0, one launch (start us, length us, event | category | flops | bytes accessed | tf_op | source)
XLA Modules:
  0.0 449.3 jit_solution(16120516990442489737)
XLA Ops:
  6.6 2.6 collective-permute-start
  15.5 12.0 %collective-permute-done = bf16[256,1536]{1,0:T(8,128)(2,1)S(1)} collective-permute-done((bf16[256,1536]{1,0:T(8,128)(2,1)}, bf16[256,1536]{1,0:T(8,128)(2,1)S(1)}, u32[]{:S(2)}, u32[]{:S(2)}) %collective-permute-start) | collective-permute-done | bytes 786464 | tf_op jit(solution)/shard_map/ppermute | solution.py:597
  27.5 1.7 collective-permute-start.9
  36.9 10.1 %collective-permute-done.9 = bf16[256,1536]{1,0:T(8,128)(2,1)S(1)} collective-permute-done((bf16[256,1536]{1,0:T(8,128)(2,1)S(1)}, bf16[256,1536]{1,0:T(8,128)(2,1)S(1)}, u32[]{:S(2)}, u32[]{:S(2)}) %collective-permute-start.9) | collective-permute-done | bytes 786464 | tf_op jit(solution)/shard_map/ppermute | solution.py:597
  50.6 14.6 %collective-permute-done.7 = bf16[2,96,1664]{2,1,0:T(8,128)(2,1)S(1)} collective-permute-done((bf16[2,96,1664]{2,1,0:T(8,128)(2,1)S(1)}, bf16[2,96,1664]{2,1,0:T(8,128)(2,1)S(1)}, u32[]{:S(2)}, u32[]{:S(2)}) %collective-permute-start.7) | collective-permute-done | bytes 639008 | tf_op jit(solution)/shard_map/ppermute | solution.py:608
  66.4 1.6 collective-permute-start.10
  69.5 5.7 %collective-permute-done.10 = bf16[1,96,1664]{2,1,0:T(8,128)(2,1)S(1)} collective-permute-done((bf16[1,96,1664]{2,1,0:T(8,128)(2,1)S(1)}, bf16[1,96,1664]{2,1,0:T(8,128)(2,1)S(1)}, u32[]{:S(2)}, u32[]{:S(2)}) %collective-permute-start.10) | collective-permute-done | bytes 319520 | tf_op jit(solution)/shard_map/ppermute | solution.py:608
  79.5 4.9 %fusion.2 = bf16[1024,1536]{1,0:T(8,128)(2,1)S(1)} fusion(f32[1536]{0:T(1024)S(1)} %get-tuple-element.271, f32[1024]{0:T(1024)S(1)} %add_rsqrt_fusion, bf16[512,1536]{1,0:T(8,128)(2,1)S(1)} %collective-permute-done.1, bf16[256,1536]{1,0:T(8,128)(2,1)S(1)} %collective-permute-done, bf16[256,1536]{1,0:T(8,128)(2,1)S(1)} %copy-done), kind=kLoop, calls=%fused_computation.5 | loop fusion | flops 14155776 | bytes 6301696 | tf_op jit(solution)/shard_map/convert_element_type | solution.py:744
  84.5 1.7 copy-done.2
  88.9 8.6 %convolution_convert_fusion.1.qkv_ref = bf16[1024,1152]{1,0:T(8,128)(2,1)} fusion(bf16[1024,1536]{1,0:T(8,128)(2,1)} %copy-done.2, bf16[1536,1664]{1,0:T(8,128)(2,1)} %bitcast.261), kind=kOutput, calls=%fused_computation.38 | convolution fusion | flops 3625058304 | bytes 9043968 | tf_op jit(solution)/shard_map/dot_general | solution.py:320
  97.5 16.0 %attend.1 = (bf16[1024,384]{1,0:T(8,128)(2,1)}, f32[1024,384]{1,0:T(8,128)}, bf16[2,3,2,256,768]{4,3,2,1,0:T(8,128)(2,1)}, f32[2,3,8,128]{3,2,1,0:T(8,128)}) custom-call(s32[1]{0:T(128)} %bitcast.y_ref, bf16[1024,1152]{1,0:T(8,128)(2,1)} %convolution_convert_fusion.1.qkv_ref, f32[3,8,1024]{2,1,0:T(8,128)} %pad_maximum_fusion.17.aux_ref), custom_call_target="tpu_custom_call" | custom-call | flops 1207959552 | bytes 20000000 | tf_op jit(solution)/shard_map/attend/pallas_call | solution.py:394
  113.5 3.6 convolution_convert_fusion.5
  121.5 1.6 collective-permute-start.19
  123.6 2.8 convert_add_fusion.3
  126.5 1.6 collective-permute-start.17
  130.9 15.2 %collective-permute-done.17 = bf16[256,1536]{1,0:T(8,128)(2,1)S(1)} collective-permute-done((bf16[256,1536]{1,0:T(8,128)(2,1)S(1)}, bf16[256,1536]{1,0:T(8,128)(2,1)S(1)}, u32[]{:S(2)}, u32[]{:S(2)}) %collective-permute-start.17) | collective-permute-done | bytes 786464 | tf_op jit(solution)/shard_map/ppermute | solution.py:597
  147.3 1.6 collective-permute-start.18
  153.7 12.3 %collective-permute-done.18 = bf16[256,1536]{1,0:T(8,128)(2,1)S(1)} collective-permute-done((bf16[256,1536]{1,0:T(8,128)(2,1)S(1)}, bf16[256,1536]{1,0:T(8,128)(2,1)S(1)}, u32[]{:S(2)}, u32[]{:S(2)}) %collective-permute-start.18) | collective-permute-done | bytes 786464 | tf_op jit(solution)/shard_map/ppermute | solution.py:597
  166.3 12.4 %collective-permute-done.22 = bf16[2,96,3072]{2,1,0:T(8,128)(2,1)S(1)} collective-permute-done((bf16[2,96,3072]{2,1,0:T(8,128)(2,1)S(1)}, bf16[2,96,3072]{2,1,0:T(8,128)(2,1)S(1)}, u32[]{:S(2)}, u32[]{:S(2)}) %collective-permute-start.22) | collective-permute-done | bytes 1179680 | tf_op jit(solution)/shard_map/ppermute | solution.py:608
  182.4 11.1 %collective-permute-done.24 = bf16[1,96,3072]{2,1,0:T(8,128)(2,1)S(1)} collective-permute-done((bf16[1,96,3072]{2,1,0:T(8,128)(2,1)S(1)}, bf16[1,96,3072]{2,1,0:T(8,128)(2,1)S(1)}, u32[]{:S(2)}, u32[]{:S(2)}) %collective-permute-start.24) | collective-permute-done | bytes 589856 | tf_op jit(solution)/shard_map/ppermute | solution.py:608
  195.1 9.5 %fusion.8 = f32[1024,2048]{1,0:T(8,128)} fusion(bf16[1536,3072]{1,0:T(8,128)(2,1)S(1)} %bitcast.254, bf16[512,1536]{1,0:T(8,128)(2,1)S(1)} %collective-permute-done.21, bf16[256,1536]{1,0:T(8,128)(2,1)S(1)} %collective-permute-done.18, bf16[256,1536]{1,0:T(8,128)(2,1)S(1)} %multiply_convert_fusion.3), kind=kOutput, calls=%fused_computation.12 | convolution fusion | flops 6451888128 | bytes 17825792 | tf_op jit(solution)/shard_map/dot_general | solution.py:320
  204.6 8.5 %multiply_convert_fusion.1 = (bf16[1024,1024]{1,0:T(8,128)(2,1)S(1)}, bf16[1024,1024]{1,0:T(8,128)(2,1)S(1)}, bf16[1024,1024]{1,0:T(8,128)(2,1)}) fusion(f32[1024,2048]{1,0:T(8,128)} %fusion.8, bf16[1024,1536]{1,0:T(8,128)(2,1)S(1)} %copy-done.27, bf16[1536,3072]{1,0:T(8,128)(2,1)S(1)} %bitcast.255), kind=kOutput, calls=%fused_computation.34 | convolution fusion | flops 3236954112 | bytes 20971520 | tf_op jit(solution)/shard_map/dot_general | solution.py:320
  213.1 4.7 %fusion.19 = bf16[512,1536]{1,0:T(8,128)(2,1)} fusion(bf16[1536,3072]{1,0:T(8,128)(2,1)S(1)} %bitcast.256, bf16[1024,1024]{1,0:T(8,128)(2,1)S(1)} %get-tuple-element.288, bf16[1024,1024]{1,0:T(8,128)(2,1)S(1)} %get-tuple-element.289), kind=kOutput, calls=%fused_computation.54 | convolution fusion | flops 3226206208 | bytes 12058624 | tf_op jit(solution)/shard_map/dot_general | solution.py:316
  218.3 3.5 fusion.4
  221.8 5.3 %convolution_convert_fusion.2 = bf16[1536,1024]{1,0:T(8,128)(2,1)S(1)} fusion(bf16[1024,1536]{1,0:T(8,128)(2,1)S(1)} %copy-done.28, bf16[1024,1024]{1,0:T(8,128)(2,1)} %get-tuple-element.138), kind=kOutput, calls=%fused_computation.39 | convolution fusion | flops 3222798336 | bytes 8388608 | tf_op jit(solution)/shard_map/dot_general | solution.py:324
  230.1 1.9 convert_add_fusion.2
  234.6 8.6 %convolution_convert_fusion = bf16[1536,2048]{1,0:T(8,128)(2,1)S(1)} fusion(bf16[1024,2048]{1,0:T(8,128)(2,1)S(1)} %pad_maximum_fusion, bf16[512,1536]{1,0:T(8,128)(2,1)} %copy-done.35, bf16[256,1536]{1,0:T(8,128)(2,1)} %copy-done.20, bf16[256,1536]{1,0:T(8,128)(2,1)S(1)} %multiply_convert_fusion.3), kind=kOutput, calls=%fused_computation.2 | convolution fusion | flops 6455033856 | bytes 13631488 | tf_op jit(solution)/shard_map/dot_general | solution.py:324
  247.8 4.8 %collective-permute-done.34 = bf16[256,1536]{1,0:T(8,128)(2,1)S(1)} collective-permute-done((bf16[256,1536]{1,0:T(8,128)(2,1)}, bf16[256,1536]{1,0:T(8,128)(2,1)S(1)}, u32[]{:S(2)}, u32[]{:S(2)}) %collective-permute-start.34) | collective-permute-done | bytes 786464 | tf_op jit(solution)/shard_map/ppermute | solution.py:597
  253.2 1.7 fusion.119
  258.7 3.0 convolution_convert_fusion.4
  262.9 2.2 fusion.65
  265.0 3.6 fusion.23
  268.6 4.9 %collective-permute-done.35 = bf16[256,1536]{1,0:T(8,128)(2,1)S(1)} collective-permute-done((bf16[256,1536]{1,0:T(8,128)(2,1)S(1)}, bf16[256,1536]{1,0:T(8,128)(2,1)S(1)}, u32[]{:S(2)}, u32[]{:S(2)}) %collective-permute-start.35) | collective-permute-done | bytes 786464 | tf_op jit(solution)/shard_map/ppermute | solution.py:597
  280.9 4.7 %convolution_convert_fusion.8.do_ref = bf16[1024,384]{1,0:T(8,128)(2,1)} fusion(bf16[1536,1664]{1,0:T(8,128)(2,1)} %bitcast.264, bf16[512,1536]{1,0:T(8,128)(2,1)} %collective-permute-done.36, bf16[256,1536]{1,0:T(8,128)(2,1)S(1)} %collective-permute-done.35, bf16[256,1536]{1,0:T(8,128)(2,1)} %copy-done.9), kind=kOutput, calls=%fused_computation.114 | convolution fusion | flops 1217789952 | bytes 5111808 | tf_op jit(solution)/shard_map/dot_general | solution.py:320
  285.5 10.0 %collective-permute-done.39 = bf16[2,96,2048]{2,1,0:T(8,128)(2,1)} collective-permute-done((bf16[2,96,2048]{2,1,0:T(8,128)(2,1)}, bf16[2,96,2048]{2,1,0:T(8,128)(2,1)}, u32[]{:S(2)}, u32[]{:S(2)}) %collective-permute-start.39) | collective-permute-done | bytes 786464 | tf_op jit(solution)/shard_map/ppermute | solution.py:608
  297.0 3.7 fusion.47
  301.2 1.6 collective-permute-start.41
  302.9 17.4 %attend_back.1 = (bf16[1024,1152]{1,0:T(8,128)(2,1)}, f32[3,8,1024]{2,1,0:T(8,128)}) custom-call(s32[1]{0:T(128)} %bitcast.y_ref, bf16[1024,1152]{1,0:T(8,128)(2,1)} %convolution_convert_fusion.1.qkv_ref, bf16[1024,384]{1,0:T(8,128)(2,1)} %convolution_convert_fusion.8.do_ref, f32[1024,384]{1,0:T(8,128)} %get-tuple-element.144.inv_ref, ...), custom_call_target="tpu_custom_call" | custom-call | flops 3623878656 | bytes 20000000 | tf_op jit(solution)/shard_map/attend_back/pallas_call | solution.py:496
  320.3 2.6 fusion.63
  329.9 3.5 pad_maximum_fusion.3
  333.7 1.9 fusion.22
  339.6 3.2 fusion.45
  344.9 3.7 convolution_convert_fusion.3
  348.8 2.2 fusion.16
  352.0 1.8 convolution_convert_fusion.6
  353.8 1.8 convolution_convert_fusion.7
  355.8 2.2 fusion.12
  358.0 5.3 %collective-permute-done.47 = bf16[2,96,2048]{2,1,0:T(8,128)(2,1)S(1)} collective-permute-done((bf16[2,96,2048]{2,1,0:T(8,128)(2,1)S(1)}, bf16[2,96,2048]{2,1,0:T(8,128)(2,1)S(1)}, u32[]{:S(2)}, u32[]{:S(2)}) %collective-permute-start.47) | collective-permute-done | bytes 786464 | tf_op jit(solution)/shard_map/ppermute | solution.py:608
  365.6 1.6 collective-permute-done.74
  370.8 1.6 collective-permute-start.49
  376.8 6.7 %collective-permute-done.53 = bf16[2,96,896]{2,1,0:T(8,128)(2,1)S(1)} collective-permute-done((bf16[2,96,896]{2,1,0:T(8,128)(2,1)S(1)}, bf16[2,96,896]{2,1,0:T(8,128)(2,1)S(1)}, u32[]{:S(2)}, u32[]{:S(2)}) %collective-permute-start.53) | collective-permute-done | bytes 344096 | tf_op jit(solution)/shard_map/ppermute | solution.py:608
  385.9 4.0 collective-permute-done.49
  391.1 2.3 collective-permute-done.57
  395.7 5.1 %collective-permute-done.61 = bf16[2,96,896]{2,1,0:T(8,128)(2,1)S(1)} collective-permute-done((bf16[2,96,896]{2,1,0:T(8,128)(2,1)S(1)}, bf16[2,96,896]{2,1,0:T(8,128)(2,1)S(1)}, u32[]{:S(2)}, u32[]{:S(2)}) %collective-permute-start.61) | collective-permute-done | bytes 344096 | tf_op jit(solution)/shard_map/ppermute | solution.py:608
  401.0 3.5 collective-permute-done.59
  410.9 1.6 collective-permute-done.64
  415.7 2.0 collective-permute-done.65
  419.5 1.8 collective-permute-start.70
  421.9 2.3 collective-permute-start.67
  425.6 5.5 %collective-permute-done.67 = f32[8,768]{1,0:T(8,128)S(1)} collective-permute-done((f32[8,768]{1,0:T(8,128)S(1)}, f32[8,768]{1,0:T(8,128)S(1)}, u32[]{:S(2)}, u32[]{:S(2)}) %collective-permute-start.67) | collective-permute-done | bytes 24608 | tf_op jit(solution)/shard_map/ppermute | solution.py:619
  434.2 1.7 multiply_convert_fusion.4
  435.9 2.1 fusion.76
  439.4 1.7 fusion.61
  441.9 2.4 fusion.43
  (381 shorter events, 130.9 us)
Async XLA Ops:
  6.6 20.9 %collective-permute-start = (bf16[256,1536]{1,0:T(8,128)(2,1)}, bf16[256,1536]{1,0:T(8,128)(2,1)S(1)}, u32[]{:S(2)}, u32[]{:S(2)}) collective-permute-start(bf16[256,1536]{1,0:T(8,128)(2,1)} %param.15), channel_id=1, source_target_pairs={{0,1},{1,0},{2,3},{3,2},{4,5},{5,4},{6,7},{7,6},{8,9},{9,8},{10,11... | collective-permute-start | bytes 2359304 | tf_op jit(solution)/shard_map/ppermute | solution.py:597
  12.7 16.9 %collective-permute-start.3 = (bf16[2,96,1664]{2,1,0:T(8,128)(2,1)}, bf16[2,96,1664]{2,1,0:T(8,128)(2,1)}, u32[]{:S(2)}, u32[]{:S(2)}) collective-permute-start(bf16[2,96,1664]{2,1,0:T(8,128)(2,1)} %maximum_select_fusion.5), channel_id=1, source_target_pairs={{0,8},{2,10},{8,16},{10,18},{16,24},{18,26},{24,28},{26,30},{28,20... | collective-permute-start | bytes 1916936 | tf_op jit(solution)/shard_map/ppermute | solution.py:608
  14.2 16.6 %collective-permute-start.4 = (bf16[2,96,1664]{2,1,0:T(8,128)(2,1)}, bf16[2,96,1664]{2,1,0:T(8,128)(2,1)}, u32[]{:S(2)}, u32[]{:S(2)}) collective-permute-start(bf16[2,96,1664]{2,1,0:T(8,128)(2,1)} %maximum_select_fusion.5), channel_id=1, source_target_pairs={{0,4},{2,6},{8,0},{10,2},{16,8},{18,10},{24,16},{26,18},{28,24},{3... | collective-permute-start | bytes 1916936 | tf_op jit(solution)/shard_map/ppermute | solution.py:608
  27.5 19.4 %collective-permute-start.9 = (bf16[256,1536]{1,0:T(8,128)(2,1)S(1)}, bf16[256,1536]{1,0:T(8,128)(2,1)S(1)}, u32[]{:S(2)}, u32[]{:S(2)}) collective-permute-start(bf16[256,1536]{1,0:T(8,128)(2,1)S(1)} %copy-done.8), channel_id=1, source_target_pairs={{0,1},{1,0},{2,3},{3,2},{4,5},{5,4},{6,7},{7,6},{8,9},{9,8},{10,11... | collective-permute-start | bytes 2359304 | tf_op jit(solution)/shard_map/ppermute | solution.py:597
  29.4 39.3 %collective-permute-start.1 = (bf16[512,1536]{1,0:T(8,128)(2,1)S(1)}, bf16[512,1536]{1,0:T(8,128)(2,1)S(1)}, u32[]{:S(2)}, u32[]{:S(2)}) collective-permute-start(bf16[512,1536]{1,0:T(8,128)(2,1)S(1)} %pad_maximum_fusion.4), channel_id=1, source_target_pairs={{0,2},{2,0},{4,6},{6,4},{8,10},{10,8},{12,14},{14,12},{16,18},{18,... | collective-permute-start | bytes 4718600 | tf_op jit(solution)/shard_map/ppermute | solution.py:594
  30.9 17.4 %collective-permute-start.5 = (bf16[2,96,1664]{2,1,0:T(8,128)(2,1)}, bf16[2,96,1664]{2,1,0:T(8,128)(2,1)S(1)}, u32[]{:S(2)}, u32[]{:S(2)}) collective-permute-start(bf16[2,96,1664]{2,1,0:T(8,128)(2,1)} %collective-permute-done.3), channel_id=1, source_target_pairs={{0,8},{2,10},{8,16},{10,18},{16,24},{18,26},{24,28},{26,30},{28,20... | collective-permute-start | bytes 1916936 | tf_op jit(solution)/shard_map/ppermute | solution.py:608
  32.5 15.9 %collective-permute-start.6 = (bf16[2,96,1664]{2,1,0:T(8,128)(2,1)}, bf16[2,96,1664]{2,1,0:T(8,128)(2,1)S(1)}, u32[]{:S(2)}, u32[]{:S(2)}) collective-permute-start(bf16[2,96,1664]{2,1,0:T(8,128)(2,1)} %collective-permute-done.4), channel_id=1, source_target_pairs={{0,4},{2,6},{8,0},{10,2},{16,8},{18,10},{24,16},{26,18},{28,24},{3... | collective-permute-start | bytes 1916936 | tf_op jit(solution)/shard_map/ppermute | solution.py:608
  48.3 71.6 %collective-permute-start.26 = (bf16[512,1536]{1,0:T(8,128)(2,1)}, bf16[512,1536]{1,0:T(8,128)(2,1)}, u32[]{:S(2)}, u32[]{:S(2)}) collective-permute-start(bf16[512,1536]{1,0:T(8,128)(2,1)} %pad_maximum_fusion.6), channel_id=1, source_target_pairs={{0,2},{2,0},{4,6},{6,4},{8,10},{10,8},{12,14},{14,12},{16,18},{18,... | collective-permute-start | bytes 4718600 | tf_op jit(solution)/shard_map/ppermute | solution.py:594
  48.3 16.8 %collective-permute-start.7 = (bf16[2,96,1664]{2,1,0:T(8,128)(2,1)S(1)}, bf16[2,96,1664]{2,1,0:T(8,128)(2,1)S(1)}, u32[]{:S(2)}, u32[]{:S(2)}) collective-permute-start(bf16[2,96,1664]{2,1,0:T(8,128)(2,1)S(1)} %collective-permute-done.5), channel_id=1, source_target_pairs={{0,8},{2,10},{8,16},{10,18},{16,24},{18,26},{24,28},{26,30},{28,20... | collective-permute-start | bytes 1916936 | tf_op jit(solution)/shard_map/ppermute | solution.py:608
  49.9 16.5 %collective-permute-start.8 = (bf16[2,96,1664]{2,1,0:T(8,128)(2,1)S(1)}, bf16[2,96,1664]{2,1,0:T(8,128)(2,1)S(1)}, u32[]{:S(2)}, u32[]{:S(2)}) collective-permute-start(bf16[2,96,1664]{2,1,0:T(8,128)(2,1)S(1)} %collective-permute-done.6), channel_id=1, source_target_pairs={{0,4},{2,6},{8,0},{10,2},{16,8},{18,10},{24,16},{26,18},{28,24},{3... | collective-permute-start | bytes 1916936 | tf_op jit(solution)/shard_map/ppermute | solution.py:608
  66.4 8.8 %collective-permute-start.10 = (bf16[1,96,1664]{2,1,0:T(8,128)(2,1)S(1)}, bf16[1,96,1664]{2,1,0:T(8,128)(2,1)S(1)}, u32[]{:S(2)}, u32[]{:S(2)}) collective-permute-start(bf16[1,96,1664]{2,1,0:T(8,128)(2,1)S(1)} %slice.449), channel_id=1, source_target_pairs={{0,8},{2,10},{8,16},{10,18},{16,24},{18,26},{24,28},{26,30},{28,20... | collective-permute-start | bytes 958472 | tf_op jit(solution)/shard_map/ppermute | solution.py:608
  68.1 8.5 %collective-permute-start.11 = (bf16[1,96,1664]{2,1,0:T(8,128)(2,1)S(1)}, bf16[1,96,1664]{2,1,0:T(8,128)(2,1)S(1)}, u32[]{:S(2)}, u32[]{:S(2)}) collective-permute-start(bf16[1,96,1664]{2,1,0:T(8,128)(2,1)S(1)} %slice.450), channel_id=1, source_target_pairs={{0,4},{2,6},{8,0},{10,2},{16,8},{18,10},{24,16},{26,18},{28,24},{3... | collective-permute-start | bytes 958472 | tf_op jit(solution)/shard_map/ppermute | solution.py:608
  76.6 36.9 %collective-permute-start.14 = (bf16[2,96,3072]{2,1,0:T(8,128)(2,1)}, bf16[2,96,3072]{2,1,0:T(8,128)(2,1)}, u32[]{:S(2)}, u32[]{:S(2)}) collective-permute-start(bf16[2,96,3072]{2,1,0:T(8,128)(2,1)} %maximum_select_fusion), channel_id=1, source_target_pairs={{0,8},{2,10},{8,16},{10,18},{16,24},{18,26},{24,28},{26,30},{28,20... | collective-permute-start | bytes 3538952 | tf_op jit(solution)/shard_map/ppermute | solution.py:608
  78.2 35.3 %collective-permute-start.15 = (bf16[2,96,3072]{2,1,0:T(8,128)(2,1)}, bf16[2,96,3072]{2,1,0:T(8,128)(2,1)}, u32[]{:S(2)}, u32[]{:S(2)}) collective-permute-start(bf16[2,96,3072]{2,1,0:T(8,128)(2,1)} %maximum_select_fusion), channel_id=1, source_target_pairs={{0,4},{2,6},{8,0},{10,2},{16,8},{18,10},{24,16},{26,18},{28,24},{3... | collective-permute-start | bytes 3538952 | tf_op jit(solution)/shard_map/ppermute | solution.py:608
  117.1 6.4 %collective-permute-start.16 = (bf16[512,1536]{1,0:T(8,128)(2,1)}, bf16[512,1536]{1,0:T(8,128)(2,1)}, u32[]{:S(2)}, u32[]{:S(2)}) collective-permute-start(bf16[512,1536]{1,0:T(8,128)(2,1)} %convolution_convert_fusion.5), channel_id=1, source_target_pairs={{0,2},{2,0},{4,6},{6,4},{8,10},{10,8},{12,14},{14,12},{16,18},{18,... | collective-permute-start | bytes 4718600 | tf_op jit(solution)/shard_map/ppermute | solution.py:594
  121.5 28.6 %collective-permute-start.19 = (bf16[2,96,3072]{2,1,0:T(8,128)(2,1)}, bf16[2,96,3072]{2,1,0:T(8,128)(2,1)S(1)}, u32[]{:S(2)}, u32[]{:S(2)}) collective-permute-start(bf16[2,96,3072]{2,1,0:T(8,128)(2,1)} %collective-permute-done.14), channel_id=1, source_target_pairs={{0,8},{2,10},{8,16},{10,18},{16,24},{18,26},{24,28},{26,30},{28,20... | collective-permute-start | bytes 3538952 | tf_op jit(solution)/shard_map/ppermute | solution.py:608
  123.1 28.3 %collective-permute-start.20 = (bf16[2,96,3072]{2,1,0:T(8,128)(2,1)}, bf16[2,96,3072]{2,1,0:T(8,128)(2,1)S(1)}, u32[]{:S(2)}, u32[]{:S(2)}) collective-permute-start(bf16[2,96,3072]{2,1,0:T(8,128)(2,1)} %collective-permute-done.15), channel_id=1, source_target_pairs={{0,4},{2,6},{8,0},{10,2},{16,8},{18,10},{24,16},{26,18},{28,24},{3... | collective-permute-start | bytes 3538952 | tf_op jit(solution)/shard_map/ppermute | solution.py:608
  126.5 19.6 %collective-permute-start.17 = (bf16[256,1536]{1,0:T(8,128)(2,1)S(1)}, bf16[256,1536]{1,0:T(8,128)(2,1)S(1)}, u32[]{:S(2)}, u32[]{:S(2)}) collective-permute-start(bf16[256,1536]{1,0:T(8,128)(2,1)S(1)} %slice.777), channel_id=1, source_target_pairs={{0,1},{1,0},{2,3},{3,2},{4,5},{5,4},{6,7},{7,6},{8,9},{9,8},{10,11... | collective-permute-start | bytes 2359304 | tf_op jit(solution)/shard_map/ppermute | solution.py:597
  147.3 18.7 %collective-permute-start.18 = (bf16[256,1536]{1,0:T(8,128)(2,1)S(1)}, bf16[256,1536]{1,0:T(8,128)(2,1)S(1)}, u32[]{:S(2)}, u32[]{:S(2)}) collective-permute-start(bf16[256,1536]{1,0:T(8,128)(2,1)S(1)} %multiply_convert_fusion.3), channel_id=1, source_target_pairs={{0,1},{1,0},{2,3},{3,2},{4,5},{5,4},{6,7},{7,6},{8,9},{9,8},{10,11... | collective-permute-start | bytes 2359304 | tf_op jit(solution)/shard_map/ppermute | solution.py:597
  151.4 27.2 %collective-permute-start.22 = (bf16[2,96,3072]{2,1,0:T(8,128)(2,1)S(1)}, bf16[2,96,3072]{2,1,0:T(8,128)(2,1)S(1)}, u32[]{:S(2)}, u32[]{:S(2)}) collective-permute-start(bf16[2,96,3072]{2,1,0:T(8,128)(2,1)S(1)} %collective-permute-done.19), channel_id=1, source_target_pairs={{0,8},{2,10},{8,16},{10,18},{16,24},{18,26},{24,28},{26,30},{28,20... | collective-permute-start | bytes 3538952 | tf_op jit(solution)/shard_map/ppermute | solution.py:608
  152.9 27.0 %collective-permute-start.23 = (bf16[2,96,3072]{2,1,0:T(8,128)(2,1)S(1)}, bf16[2,96,3072]{2,1,0:T(8,128)(2,1)S(1)}, u32[]{:S(2)}, u32[]{:S(2)}) collective-permute-start(bf16[2,96,3072]{2,1,0:T(8,128)(2,1)S(1)} %collective-permute-done.20), channel_id=1, source_target_pairs={{0,4},{2,6},{8,0},{10,2},{16,8},{18,10},{24,16},{26,18},{28,24},{3... | collective-permute-start | bytes 3538952 | tf_op jit(solution)/shard_map/ppermute | solution.py:608
  166.2 27.8 %collective-permute-start.21 = (bf16[512,1536]{1,0:T(8,128)(2,1)S(1)}, bf16[512,1536]{1,0:T(8,128)(2,1)S(1)}, u32[]{:S(2)}, u32[]{:S(2)}) collective-permute-start(bf16[512,1536]{1,0:T(8,128)(2,1)S(1)} %pad_maximum_fusion.5), channel_id=1, source_target_pairs={{0,2},{2,0},{4,6},{6,4},{8,10},{10,8},{12,14},{14,12},{16,18},{18,... | collective-permute-start | bytes 4718600 | tf_op jit(solution)/shard_map/ppermute | solution.py:594
  179.9 13.5 %collective-permute-start.24 = (bf16[1,96,3072]{2,1,0:T(8,128)(2,1)S(1)}, bf16[1,96,3072]{2,1,0:T(8,128)(2,1)S(1)}, u32[]{:S(2)}, u32[]{:S(2)}) collective-permute-start(bf16[1,96,3072]{2,1,0:T(8,128)(2,1)S(1)} %slice.465), channel_id=1, source_target_pairs={{0,8},{2,10},{8,16},{10,18},{16,24},{18,26},{24,28},{26,30},{28,20... | collective-permute-start | bytes 1769480 | tf_op jit(solution)/shard_map/ppermute | solution.py:608
  180.6 13.2 %collective-permute-start.25 = (bf16[1,96,3072]{2,1,0:T(8,128)(2,1)S(1)}, bf16[1,96,3072]{2,1,0:T(8,128)(2,1)S(1)}, u32[]{:S(2)}, u32[]{:S(2)}) collective-permute-start(bf16[1,96,3072]{2,1,0:T(8,128)(2,1)S(1)} %slice.466), channel_id=1, source_target_pairs={{0,4},{2,6},{8,0},{10,2},{16,8},{18,10},{24,16},{26,18},{28,24},{3... | collective-permute-start | bytes 1769480 | tf_op jit(solution)/shard_map/ppermute | solution.py:608
  218.2 11.9 %collective-permute-start.29 = (bf16[512,1536]{1,0:T(8,128)(2,1)}, bf16[512,1536]{1,0:T(8,128)(2,1)}, u32[]{:S(2)}, u32[]{:S(2)}) collective-permute-start(bf16[512,1536]{1,0:T(8,128)(2,1)} %fusion.19), channel_id=1, source_target_pairs={{0,2},{2,0},{4,6},{6,4},{8,10},{10,8},{12,14},{14,12},{16,18},{18,... | collective-permute-start | bytes 4718600 | tf_op jit(solution)/shard_map/ppermute | solution.py:594
  228.0 15.3 %collective-permute-start.27 = (bf16[1,96,1024]{2,1,0:T(8,128)(2,1)}, bf16[1,96,1024]{2,1,0:T(8,128)(2,1)S(1)}, u32[]{:S(2)}, u32[]{:S(2)}) collective-permute-start(bf16[1,96,1024]{2,1,0:T(8,128)(2,1)} %get-tuple-element.306), channel_id=1, source_target_pairs={{0,8},{2,10},{8,16},{10,18},{16,24},{18,26},{24,28},{26,30},{28,20... | collective-permute-start | bytes 589832 | tf_op jit(solution)/shard_map/ppermute | solution.py:608
  228.6 14.6 %collective-permute-start.28 = (bf16[1,96,1024]{2,1,0:T(8,128)(2,1)S(1)}, bf16[1,96,1024]{2,1,0:T(8,128)(2,1)S(1)}, u32[]{:S(2)}, u32[]{:S(2)}) collective-permute-start(bf16[1,96,1024]{2,1,0:T(8,128)(2,1)S(1)} %get-tuple-element.307), channel_id=1, source_target_pairs={{0,4},{2,6},{8,0},{10,2},{16,8},{18,10},{24,16},{26,18},{28,24},{3... | collective-permute-start | bytes 589832 | tf_op jit(solution)/shard_map/ppermute | solution.py:608
  233.0 19.6 %collective-permute-start.34 = (bf16[256,1536]{1,0:T(8,128)(2,1)}, bf16[256,1536]{1,0:T(8,128)(2,1)S(1)}, u32[]{:S(2)}, u32[]{:S(2)}) collective-permute-start(bf16[256,1536]{1,0:T(8,128)(2,1)} %slice.776), channel_id=1, source_target_pairs={{0,1},{1,0},{2,3},{3,2},{4,5},{5,4},{6,7},{7,6},{8,9},{9,8},{10,11... | collective-permute-start | bytes 2359304 | tf_op jit(solution)/shard_map/ppermute | solution.py:597
  243.4 13.1 %collective-permute-start.32 = (bf16[1,96,2048]{2,1,0:T(8,128)(2,1)S(1)}, bf16[1,96,2048]{2,1,0:T(8,128)(2,1)S(1)}, u32[]{:S(2)}, u32[]{:S(2)}) collective-permute-start(bf16[1,96,2048]{2,1,0:T(8,128)(2,1)S(1)} %get-tuple-element.296), channel_id=1, source_target_pairs={{0,8},{2,10},{8,16},{10,18},{16,24},{18,26},{24,28},{26,30},{28,20... | collective-permute-start | bytes 1179656 | tf_op jit(solution)/shard_map/ppermute | solution.py:608
  244.0 12.5 %collective-permute-start.33 = (bf16[1,96,2048]{2,1,0:T(8,128)(2,1)S(1)}, bf16[1,96,2048]{2,1,0:T(8,128)(2,1)S(1)}, u32[]{:S(2)}, u32[]{:S(2)}) collective-permute-start(bf16[1,96,2048]{2,1,0:T(8,128)(2,1)S(1)} %get-tuple-element.297), channel_id=1, source_target_pairs={{0,4},{2,6},{8,0},{10,2},{16,8},{18,10},{24,16},{26,18},{28,24},{3... | collective-permute-start | bytes 1179656 | tf_op jit(solution)/shard_map/ppermute | solution.py:608
  245.7 17.2 %collective-permute-start.31 = (bf16[2,96,1024]{2,1,0:T(8,128)(2,1)S(1)}, bf16[2,96,1024]{2,1,0:T(8,128)(2,1)S(1)}, u32[]{:S(2)}, u32[]{:S(2)}) collective-permute-start(bf16[2,96,1024]{2,1,0:T(8,128)(2,1)S(1)} %pad_maximum_fusion.12), channel_id=1, source_target_pairs={{0,4},{2,6},{8,0},{10,2},{16,8},{18,10},{24,16},{26,18},{28,24},{3... | collective-permute-start | bytes 1179656 | tf_op jit(solution)/shard_map/ppermute | solution.py:608
  247.2 15.7 %collective-permute-start.30 = (bf16[2,96,1024]{2,1,0:T(8,128)(2,1)S(1)}, bf16[2,96,1024]{2,1,0:T(8,128)(2,1)S(1)}, u32[]{:S(2)}, u32[]{:S(2)}) collective-permute-start(bf16[2,96,1024]{2,1,0:T(8,128)(2,1)S(1)} %pad_maximum_fusion.11), channel_id=1, source_target_pairs={{0,8},{2,10},{8,16},{10,18},{16,24},{18,26},{24,28},{26,30},{28,20... | collective-permute-start | bytes 1179656 | tf_op jit(solution)/shard_map/ppermute | solution.py:608
  255.0 18.5 %collective-permute-start.35 = (bf16[256,1536]{1,0:T(8,128)(2,1)S(1)}, bf16[256,1536]{1,0:T(8,128)(2,1)S(1)}, u32[]{:S(2)}, u32[]{:S(2)}) collective-permute-start(bf16[256,1536]{1,0:T(8,128)(2,1)S(1)} %get-tuple-element.284), channel_id=1, source_target_pairs={{0,1},{1,0},{2,3},{3,2},{4,5},{5,4},{6,7},{7,6},{8,9},{9,8},{10,11... | collective-permute-start | bytes 2359304 | tf_op jit(solution)/shard_map/ppermute | solution.py:597
  274.8 20.7 %collective-permute-start.39 = (bf16[2,96,2048]{2,1,0:T(8,128)(2,1)}, bf16[2,96,2048]{2,1,0:T(8,128)(2,1)}, u32[]{:S(2)}, u32[]{:S(2)}) collective-permute-start(bf16[2,96,2048]{2,1,0:T(8,128)(2,1)} %pad_maximum_fusion.9), channel_id=1, source_target_pairs={{0,4},{2,6},{8,0},{10,2},{16,8},{18,10},{24,16},{26,18},{28,24},{3... | collective-permute-start | bytes 2359304 | tf_op jit(solution)/shard_map/ppermute | solution.py:608
  276.3 20.7 %collective-permute-start.38 = (bf16[2,96,2048]{2,1,0:T(8,128)(2,1)}, bf16[2,96,2048]{2,1,0:T(8,128)(2,1)}, u32[]{:S(2)}, u32[]{:S(2)}) collective-permute-start(bf16[2,96,2048]{2,1,0:T(8,128)(2,1)} %pad_maximum_fusion.8), channel_id=1, source_target_pairs={{0,8},{2,10},{8,16},{10,18},{16,24},{18,26},{24,28},{26,30},{28,20... | collective-permute-start | bytes 2359304 | tf_op jit(solution)/shard_map/ppermute | solution.py:608
  278.8 41.4 %collective-permute-start.42 = (bf16[2,96,1024]{2,1,0:T(8,128)(2,1)}, bf16[2,96,1024]{2,1,0:T(8,128)(2,1)}, u32[]{:S(2)}, u32[]{:S(2)}) collective-permute-start(bf16[2,96,1024]{2,1,0:T(8,128)(2,1)} %get-tuple-element.304), channel_id=1, source_target_pairs={{0,8},{2,10},{8,16},{10,18},{16,24},{18,26},{24,28},{26,30},{28,20... | collective-permute-start | bytes 1179656 | tf_op jit(solution)/shard_map/ppermute | solution.py:608
  279.5 40.8 %collective-permute-start.43 = (bf16[2,96,1024]{2,1,0:T(8,128)(2,1)S(1)}, bf16[2,96,1024]{2,1,0:T(8,128)(2,1)}, u32[]{:S(2)}, u32[]{:S(2)}) collective-permute-start(bf16[2,96,1024]{2,1,0:T(8,128)(2,1)S(1)} %get-tuple-element.303), channel_id=1, source_target_pairs={{0,4},{2,6},{8,0},{10,2},{16,8},{18,10},{24,16},{26,18},{28,24},{3... | collective-permute-start | bytes 1179656 | tf_op jit(solution)/shard_map/ppermute | solution.py:608
  300.6 39.0 %collective-permute-start.40 = (bf16[2,96,2048]{2,1,0:T(8,128)(2,1)}, bf16[2,96,2048]{2,1,0:T(8,128)(2,1)}, u32[]{:S(2)}, u32[]{:S(2)}) collective-permute-start(bf16[2,96,2048]{2,1,0:T(8,128)(2,1)} %get-tuple-element.294), channel_id=1, source_target_pairs={{0,8},{2,10},{8,16},{10,18},{16,24},{18,26},{24,28},{26,30},{28,20... | collective-permute-start | bytes 2359304 | tf_op jit(solution)/shard_map/ppermute | solution.py:608
  301.2 38.4 %collective-permute-start.41 = (bf16[2,96,2048]{2,1,0:T(8,128)(2,1)}, bf16[2,96,2048]{2,1,0:T(8,128)(2,1)}, u32[]{:S(2)}, u32[]{:S(2)}) collective-permute-start(bf16[2,96,2048]{2,1,0:T(8,128)(2,1)} %get-tuple-element.293), channel_id=1, source_target_pairs={{0,4},{2,6},{8,0},{10,2},{16,8},{18,10},{24,16},{26,18},{28,24},{3... | collective-permute-start | bytes 2359304 | tf_op jit(solution)/shard_map/ppermute | solution.py:608
  322.9 12.7 %collective-permute-start.44 = (bf16[2,96,1024]{2,1,0:T(8,128)(2,1)}, bf16[2,96,1024]{2,1,0:T(8,128)(2,1)S(1)}, u32[]{:S(2)}, u32[]{:S(2)}) collective-permute-start(bf16[2,96,1024]{2,1,0:T(8,128)(2,1)} %get-tuple-element.302), channel_id=1, source_target_pairs={{0,8},{2,10},{8,16},{10,18},{16,24},{18,26},{24,28},{26,30},{28,20... | collective-permute-start | bytes 1179656 | tf_op jit(solution)/shard_map/ppermute | solution.py:608
  323.5 12.2 %collective-permute-start.45 = (bf16[2,96,1024]{2,1,0:T(8,128)(2,1)}, bf16[2,96,1024]{2,1,0:T(8,128)(2,1)}, u32[]{:S(2)}, u32[]{:S(2)}) collective-permute-start(bf16[2,96,1024]{2,1,0:T(8,128)(2,1)} %get-tuple-element.301), channel_id=1, source_target_pairs={{0,4},{2,6},{8,0},{10,2},{16,8},{18,10},{24,16},{26,18},{28,24},{3... | collective-permute-start | bytes 1179656 | tf_op jit(solution)/shard_map/ppermute | solution.py:608
  333.6 75.2 %collective-permute-start.37 = (bf16[512,1536]{1,0:T(8,128)(2,1)}, bf16[512,1536]{1,0:T(8,128)(2,1)S(1)}, u32[]{:S(2)}, u32[]{:S(2)}) collective-permute-start(bf16[512,1536]{1,0:T(8,128)(2,1)} %convolution_convert_fusion.4), channel_id=1, source_target_pairs={{0,2},{2,0},{4,6},{6,4},{8,10},{10,8},{12,14},{14,12},{16,18},{18,... | collective-permute-start | bytes 4718600 | tf_op jit(solution)/shard_map/ppermute | solution.py:594
  342.8 20.5 %collective-permute-start.47 = (bf16[2,96,2048]{2,1,0:T(8,128)(2,1)S(1)}, bf16[2,96,2048]{2,1,0:T(8,128)(2,1)S(1)}, u32[]{:S(2)}, u32[]{:S(2)}) collective-permute-start(bf16[2,96,2048]{2,1,0:T(8,128)(2,1)S(1)} %get-tuple-element.292), channel_id=1, source_target_pairs={{0,8},{2,10},{8,16},{10,18},{16,24},{18,26},{24,28},{26,30},{28,20... | collective-permute-start | bytes 2359304 | tf_op jit(solution)/shard_map/ppermute | solution.py:608
  343.4 20.4 %collective-permute-start.48 = (bf16[2,96,2048]{2,1,0:T(8,128)(2,1)S(1)}, bf16[2,96,2048]{2,1,0:T(8,128)(2,1)S(1)}, u32[]{:S(2)}, u32[]{:S(2)}) collective-permute-start(bf16[2,96,2048]{2,1,0:T(8,128)(2,1)S(1)} %get-tuple-element.291), channel_id=1, source_target_pairs={{0,4},{2,6},{8,0},{10,2},{16,8},{18,10},{24,16},{26,18},{28,24},{3... | collective-permute-start | bytes 2359304 | tf_op jit(solution)/shard_map/ppermute | solution.py:608
  351.0 18.7 %collective-permute-start.46 = (bf16[512,1536]{1,0:T(8,128)(2,1)S(1)}, bf16[512,1536]{1,0:T(8,128)(2,1)S(1)}, u32[]{:S(2)}, u32[]{:S(2)}) collective-permute-start(bf16[512,1536]{1,0:T(8,128)(2,1)S(1)} %fusion.16), channel_id=1, source_target_pairs={{0,2},{2,0},{4,6},{6,4},{8,10},{10,8},{12,14},{14,12},{16,18},{18,... | collective-permute-start | bytes 4718600 | tf_op jit(solution)/shard_map/ppermute | solution.py:594
  351.1 19.7 %collective-permute-start.50 = (bf16[1,96,896]{2,1,0:T(8,128)(2,1)S(1)}, bf16[1,96,896]{2,1,0:T(8,128)(2,1)S(1)}, u32[]{:S(2)}, u32[]{:S(2)}) collective-permute-start(bf16[1,96,896]{2,1,0:T(8,128)(2,1)S(1)} %get-tuple-element.155), channel_id=1, source_target_pairs={{0,8},{2,10},{8,16},{10,18},{16,24},{18,26},{24,28},{26,30},{28,20... | collective-permute-start | bytes 516104 | tf_op jit(solution)/shard_map/ppermute | solution.py:608
  363.3 9.1 %collective-permute-start.51 = (bf16[1,96,896]{2,1,0:T(8,128)(2,1)S(1)}, bf16[1,96,896]{2,1,0:T(8,128)(2,1)S(1)}, u32[]{:S(2)}, u32[]{:S(2)}) collective-permute-start(bf16[1,96,896]{2,1,0:T(8,128)(2,1)S(1)} %get-tuple-element.156), channel_id=1, source_target_pairs={{0,4},{2,6},{8,0},{10,2},{16,8},{18,10},{24,16},{26,18},{28,24},{3... | collective-permute-start | bytes 516104 | tf_op jit(solution)/shard_map/ppermute | solution.py:608
  367.2 6.1 %collective-permute-start.54 = (bf16[1,96,768]{2,1,0:T(8,128)(2,1)S(1)}, bf16[1,96,768]{2,1,0:T(8,128)(2,1)S(1)}, u32[]{:S(2)}, u32[]{:S(2)}) collective-permute-start(bf16[1,96,768]{2,1,0:T(8,128)(2,1)S(1)} %get-tuple-element.163), channel_id=1, source_target_pairs={{0,8},{2,10},{8,16},{10,18},{16,24},{18,26},{24,28},{26,30},{28,20... | collective-permute-start | bytes 442376 | tf_op jit(solution)/shard_map/ppermute | solution.py:608
  369.7 6.4 %collective-permute-start.55 = (bf16[1,96,768]{2,1,0:T(8,128)(2,1)S(1)}, bf16[1,96,768]{2,1,0:T(8,128)(2,1)S(1)}, u32[]{:S(2)}, u32[]{:S(2)}) collective-permute-start(bf16[1,96,768]{2,1,0:T(8,128)(2,1)S(1)} %get-tuple-element.164), channel_id=1, source_target_pairs={{0,4},{2,6},{8,0},{10,2},{16,8},{18,10},{24,16},{26,18},{28,24},{3... | collective-permute-start | bytes 442376 | tf_op jit(solution)/shard_map/ppermute | solution.py:608
  370.8 19.1 %collective-permute-start.49 = (bf16[256,1536]{1,0:T(8,128)(2,1)S(1)}, bf16[256,1536]{1,0:T(8,128)(2,1)S(1)}, u32[]{:S(2)}, u32[]{:S(2)}) collective-permute-start(bf16[256,1536]{1,0:T(8,128)(2,1)S(1)} %slice.775), channel_id=1, source_target_pairs={{0,1},{1,0},{2,3},{3,2},{4,5},{5,4},{6,7},{7,6},{8,9},{9,8},{10,11... | collective-permute-start | bytes 2359304 | tf_op jit(solution)/shard_map/ppermute | solution.py:597
  372.5 11.0 %collective-permute-start.53 = (bf16[2,96,896]{2,1,0:T(8,128)(2,1)S(1)}, bf16[2,96,896]{2,1,0:T(8,128)(2,1)S(1)}, u32[]{:S(2)}, u32[]{:S(2)}) collective-permute-start(bf16[2,96,896]{2,1,0:T(8,128)(2,1)S(1)} %pad_maximum_fusion.14), channel_id=1, source_target_pairs={{0,4},{2,6},{8,0},{10,2},{16,8},{18,10},{24,16},{26,18},{28,24},{3... | collective-permute-start | bytes 1032200 | tf_op jit(solution)/shard_map/ppermute | solution.py:608
  373.3 11.8 %collective-permute-start.52 = (bf16[2,96,896]{2,1,0:T(8,128)(2,1)S(1)}, bf16[2,96,896]{2,1,0:T(8,128)(2,1)S(1)}, u32[]{:S(2)}, u32[]{:S(2)}) collective-permute-start(bf16[2,96,896]{2,1,0:T(8,128)(2,1)S(1)} %pad_maximum_fusion.13), channel_id=1, source_target_pairs={{0,8},{2,10},{8,16},{10,18},{16,24},{18,26},{24,28},{26,30},{28,20... | collective-permute-start | bytes 1032200 | tf_op jit(solution)/shard_map/ppermute | solution.py:608
  376.2 14.9 %collective-permute-start.58 = (bf16[2,96,768]{2,1,0:T(8,128)(2,1)S(1)}, bf16[2,96,768]{2,1,0:T(8,128)(2,1)S(1)}, u32[]{:S(2)}, u32[]{:S(2)}) collective-permute-start(bf16[2,96,768]{2,1,0:T(8,128)(2,1)S(1)} %pad_maximum_fusion.16), channel_id=1, source_target_pairs={{0,4},{2,6},{8,0},{10,2},{16,8},{18,10},{24,16},{26,18},{28,24},{3... | collective-permute-start | bytes 884744 | tf_op jit(solution)/shard_map/ppermute | solution.py:608
  383.5 9.9 %collective-permute-start.57 = (bf16[2,96,768]{2,1,0:T(8,128)(2,1)S(1)}, bf16[2,96,768]{2,1,0:T(8,128)(2,1)S(1)}, u32[]{:S(2)}, u32[]{:S(2)}) collective-permute-start(bf16[2,96,768]{2,1,0:T(8,128)(2,1)S(1)} %pad_maximum_fusion.15), channel_id=1, source_target_pairs={{0,8},{2,10},{8,16},{10,18},{16,24},{18,26},{24,28},{26,30},{28,20... | collective-permute-start | bytes 884744 | tf_op jit(solution)/shard_map/ppermute | solution.py:608
  385.2 15.6 %collective-permute-start.61 = (bf16[2,96,896]{2,1,0:T(8,128)(2,1)S(1)}, bf16[2,96,896]{2,1,0:T(8,128)(2,1)S(1)}, u32[]{:S(2)}, u32[]{:S(2)}) collective-permute-start(bf16[2,96,896]{2,1,0:T(8,128)(2,1)S(1)} %get-tuple-element.314), channel_id=1, source_target_pairs={{0,8},{2,10},{8,16},{10,18},{16,24},{18,26},{24,28},{26,30},{28,20... | collective-permute-start | bytes 1032200 | tf_op jit(solution)/shard_map/ppermute | solution.py:608
  389.9 10.9 %collective-permute-start.62 = (bf16[2,96,896]{2,1,0:T(8,128)(2,1)S(1)}, bf16[2,96,896]{2,1,0:T(8,128)(2,1)S(1)}, u32[]{:S(2)}, u32[]{:S(2)}) collective-permute-start(bf16[2,96,896]{2,1,0:T(8,128)(2,1)S(1)} %get-tuple-element.313), channel_id=1, source_target_pairs={{0,4},{2,6},{8,0},{10,2},{16,8},{18,10},{24,16},{26,18},{28,24},{3... | collective-permute-start | bytes 1032200 | tf_op jit(solution)/shard_map/ppermute | solution.py:608
  393.6 11.0 %collective-permute-start.59 = (bf16[2,96,768]{2,1,0:T(8,128)(2,1)S(1)}, bf16[2,96,768]{2,1,0:T(8,128)(2,1)S(1)}, u32[]{:S(2)}, u32[]{:S(2)}) collective-permute-start(bf16[2,96,768]{2,1,0:T(8,128)(2,1)S(1)} %get-tuple-element.324), channel_id=1, source_target_pairs={{0,8},{2,10},{8,16},{10,18},{16,24},{18,26},{24,28},{26,30},{28,20... | collective-permute-start | bytes 884744 | tf_op jit(solution)/shard_map/ppermute | solution.py:608
  395.1 9.8 %collective-permute-start.60 = (bf16[2,96,768]{2,1,0:T(8,128)(2,1)S(1)}, bf16[2,96,768]{2,1,0:T(8,128)(2,1)S(1)}, u32[]{:S(2)}, u32[]{:S(2)}) collective-permute-start(bf16[2,96,768]{2,1,0:T(8,128)(2,1)S(1)} %get-tuple-element.323), channel_id=1, source_target_pairs={{0,4},{2,6},{8,0},{10,2},{16,8},{18,10},{24,16},{26,18},{28,24},{3... | collective-permute-start | bytes 884744 | tf_op jit(solution)/shard_map/ppermute | solution.py:608
  406.8 14.6 %collective-permute-start.68 = (bf16[2,96,896]{2,1,0:T(8,128)(2,1)S(1)}, bf16[2,96,896]{2,1,0:T(8,128)(2,1)S(1)}, u32[]{:S(2)}, u32[]{:S(2)}) collective-permute-start(bf16[2,96,896]{2,1,0:T(8,128)(2,1)S(1)} %get-tuple-element.312), channel_id=1, source_target_pairs={{0,8},{2,10},{8,16},{10,18},{16,24},{18,26},{24,28},{26,30},{28,20... | collective-permute-start | bytes 1032200 | tf_op jit(solution)/shard_map/ppermute | solution.py:608
  408.3 13.5 %collective-permute-start.69 = (bf16[2,96,896]{2,1,0:T(8,128)(2,1)S(1)}, bf16[2,96,896]{2,1,0:T(8,128)(2,1)S(1)}, u32[]{:S(2)}, u32[]{:S(2)}) collective-permute-start(bf16[2,96,896]{2,1,0:T(8,128)(2,1)S(1)} %get-tuple-element.311), channel_id=1, source_target_pairs={{0,4},{2,6},{8,0},{10,2},{16,8},{18,10},{24,16},{26,18},{28,24},{3... | collective-permute-start | bytes 1032200 | tf_op jit(solution)/shard_map/ppermute | solution.py:608
  414.2 27.7 %collective-permute-start.56 = (bf16[256,1536]{1,0:T(8,128)(2,1)}, bf16[256,1536]{1,0:T(8,128)(2,1)}, u32[]{:S(2)}, u32[]{:S(2)}) collective-permute-start(bf16[256,1536]{1,0:T(8,128)(2,1)} %slice.774), channel_id=1, source_target_pairs={{0,1},{1,0},{2,3},{3,2},{4,5},{5,4},{6,7},{7,6},{8,9},{9,8},{10,11... | collective-permute-start | bytes 2359304 | tf_op jit(solution)/shard_map/ppermute | solution.py:597
  419.5 16.4 %collective-permute-start.70 = (bf16[2,96,768]{2,1,0:T(8,128)(2,1)}, bf16[2,96,768]{2,1,0:T(8,128)(2,1)}, u32[]{:S(2)}, u32[]{:S(2)}) collective-permute-start(bf16[2,96,768]{2,1,0:T(8,128)(2,1)} %get-tuple-element.322), channel_id=1, source_target_pairs={{0,8},{2,10},{8,16},{10,18},{16,24},{18,26},{24,28},{26,30},{28,20... | collective-permute-start | bytes 884744 | tf_op jit(solution)/shard_map/ppermute | solution.py:608
  421.4 14.6 %collective-permute-start.71 = (bf16[2,96,768]{2,1,0:T(8,128)(2,1)}, bf16[2,96,768]{2,1,0:T(8,128)(2,1)}, u32[]{:S(2)}, u32[]{:S(2)}) collective-permute-start(bf16[2,96,768]{2,1,0:T(8,128)(2,1)} %get-tuple-element.321), channel_id=1, source_target_pairs={{0,4},{2,6},{8,0},{10,2},{16,8},{18,10},{24,16},{26,18},{28,24},{3... | collective-permute-start | bytes 884744 | tf_op jit(solution)/shard_map/ppermute | solution.py:608
  421.9 9.2 %collective-permute-start.67 = (f32[8,768]{1,0:T(8,128)S(1)}, f32[8,768]{1,0:T(8,128)S(1)}, u32[]{:S(2)}, u32[]{:S(2)}) collective-permute-start(f32[8,768]{1,0:T(8,128)S(1)} %pad_maximum_fusion.23), channel_id=1, source_target_pairs={{0,16},{2,18},{4,20},{6,22},{8,24},{10,26},{12,28},{14,30},{16,0},... | collective-permute-start | bytes 73736 | tf_op jit(solution)/shard_map/ppermute | solution.py:619
  (52 other events, 479.0 us)

commit v4 on v3

--- a/solution.py
+++ b/solution.py
@@ -324,7 +324,8 @@
     return lax.dot_general(left, right, (((0,), (0,)), ((), ())), preferred_element_type=F32)
 
 
-def attend_kernel(y_ref, qkv_ref, aux_ref, o_ref, inv_ref, exp_ref, top_ref):
+def attend_kernel(y_ref, qkv_ref, aux_ref, *refs):
+    o_ref, inv_ref, exp_ref, top_ref = refs[-4:]
     y = y_ref[0]
     starts = (pl.multiple_of(y * BLOCK, BLOCK), pl.multiple_of((1 - y) * BLOCK, BLOCK))
     lane = lax.broadcasted_iota(jnp.int32, (1, LANES), 1)
@@ -374,42 +375,46 @@
     top_ref[0, 0] = jnp.where(row == 0, tops[0], tops[1])
 
 
-def attend(y_index, qkv, aux, packs, pairs):
+def attend(y_index, qkv, aux, packs, pairs, pack, kept=()):
     rows = qkv.shape[0] // packs
     wide = 3 * LANES
     grid_spec = pltpu.PrefetchScalarGridSpec(
         num_scalar_prefetch=1,
-        grid=(packs, pairs),
+        grid=(pairs,),
         in_specs=[
-            pl.BlockSpec((rows, wide), lambda p, h, y: (p, h)),
-            pl.BlockSpec((1, 8, rows), lambda p, h, y: (h, 0, p)),
-        ],
+            pl.BlockSpec((rows, wide), lambda h, y: (pack, h)),
+            pl.BlockSpec((1, 8, rows), lambda h, y: (h, 0, pack)),
+        ]
+        + [pl.BlockSpec(memory_space=pl.ANY) for _ in kept],
         out_specs=[
-            pl.BlockSpec((rows, LANES), lambda p, h, y: (p, h)),
-            pl.BlockSpec((rows, LANES), lambda p, h, y: (p, h)),
-            pl.BlockSpec((1, 1, 2, BLOCK, 3 * BLOCK), lambda p, h, y: (p, h, 0, 0, 0)),
-            pl.BlockSpec((1, 1, 8, LANES), lambda p, h, y: (p, h, 0, 0)),
+            pl.BlockSpec((rows, LANES), lambda h, y: (0, h)),
+            pl.BlockSpec((rows, LANES), lambda h, y: (pack, h)),
+            pl.BlockSpec((1, 1, 2, BLOCK, 3 * BLOCK), lambda h, y: (pack, h, 0, 0, 0)),
+            pl.BlockSpec((1, 1, 8, LANES), lambda h, y: (0, h, 0, 0)),
         ],
     )
     return pl.pallas_call(
         attend_kernel,
         grid_spec=grid_spec,
         out_shape=(
-            jax.ShapeDtypeStruct((packs * rows, pairs * LANES), BF16),
+            jax.ShapeDtypeStruct((rows, pairs * LANES), BF16),
             jax.ShapeDtypeStruct((packs * rows, pairs * LANES), F32),
             jax.ShapeDtypeStruct((packs, pairs, 2, BLOCK, 3 * BLOCK), BF16),
-            jax.ShapeDtypeStruct((packs, pairs, 8, LANES), F32),
+            jax.ShapeDtypeStruct((1, pairs, 8, LANES), F32),
         ),
+        input_output_aliases={3: 1, 4: 2} if kept else {},
         cost_estimate=pl.CostEstimate(
-            flops=packs * pairs * 2 * 6 * BLOCK * BLOCK * LANES * 2,
-            bytes_accessed=20_000_000,
-            transcendentals=packs * pairs * 2 * 3 * BLOCK * BLOCK,
+            flops=pairs * 2 * 6 * BLOCK * BLOCK * LANES * 2,
+            bytes_accessed=10_000_000,
+            transcendentals=pairs * 2 * 3 * BLOCK * BLOCK,
         ),
         name="attend",
-    )(y_index, qkv, aux)
-
-
-def attend_back_kernel(y_ref, qkv_ref, do_ref, inv_ref, exp_ref, dqkv_ref, dc_ref):
+    )(y_index, qkv, aux, *kept)
+
+
+def attend_back_kernel(
+    pairs, y_ref, qkv_ref, do_ref, inv_ref, exp_ref, aux_ref, dqkv_ref, split_ref
+):
     y = y_ref[0]
     starts = (pl.multiple_of(y * BLOCK, BLOCK), pl.multiple_of((1 - y) * BLOCK, BLOCK))
     lane = lax.broadcasted_iota(jnp.int32, (1, LANES), 1)
@@ -467,16 +472,48 @@
             dk[j].append(dk_acc[j])
             dv[j].append(dv_acc[j])
             dc[j].append(row_acc[j] - col_acc[j])
-    row = lax.broadcasted_iota(jnp.int32, (8, BLOCK), 0)
     for i in range(2):
         rows = pl.ds(starts[i], BLOCK)
         dqkv_ref[rows, 0:LANES] = (jnp.where(first, *dq[i]) * 0.125).astype(BF16)
         dqkv_ref[rows, LANES : 2 * LANES] = jnp.where(first, *dk[i]).astype(BF16)
         dqkv_ref[rows, 2 * LANES : 3 * LANES] = jnp.where(first, *dv[i]).astype(BF16)
-        dc_ref[0, :, rows] = jnp.where(row == 0, *dc[i])
-
-
-def attend_back(y_index, qkv, d_out, inverse, expos, packs, pairs):
+
+    row = lax.broadcasted_iota(jnp.int32, (8, BLOCK), 0)
+    until = jnp.where(lower, 1.0, 0.0).astype(BF16)
+    d_cum = [jnp.where(row == 0, *dc[i]) for i in range(2)]
+    ends = jnp.sum(d_cum[1], axis=1, keepdims=True)
+    pair = pl.program_id(1)
+    spot = lax.broadcasted_iota(jnp.int32, (8, LANES), 0)
+    place = jnp.where(spot < 2, 2 * pair + spot, 2 * pairs + 2 * pair + spot - 2)
+    hit = (lax.broadcasted_iota(jnp.int32, (8, LANES), 1) == place) & (spot < 4)
+    hit = jnp.where(hit, 1.0, 0.0).astype(F32)
+
+    @pl.when(pair == 0)
+    def _():
+        split_ref[...] = jnp.zeros_like(split_ref)
+
+    for i in range(2):
+        rows = pl.ds(starts[i], BLOCK)
+        high = d_cum[i].astype(BF16).astype(F32)
+        rest = d_cum[i] - high
+        middle = rest.astype(BF16).astype(F32)
+        low = pltpu.roll(rest - middle, 4, 0)
+        parts = jnp.where(row < 4, pltpu.roll(middle, 2, 0), jnp.where(row < 6, low, 0.0))
+        parts = jnp.where(row < 2, high, parts).astype(BF16)
+        sums = dot_nn(parts, until)
+        back = sums + pltpu.roll(sums, 6, 0) + pltpu.roll(sums, 4, 0)
+        if i == 0:
+            back = back + ends
+        logit = pltpu.roll(aux_ref[0, :, rows], 4, 0)
+        grad = back * jax.nn.sigmoid(-logit)
+        high = grad.astype(BF16).astype(F32)
+        rest = pltpu.roll((grad - high).astype(BF16).astype(F32), 2, 0)
+        both = jnp.where(row < 2, high, jnp.where(row < 4, rest, 0.0))
+        old = split_ref[rows, :].astype(F32)
+        split_ref[rows, :] = (old + dot_tn(both, hit)).astype(BF16)
+
+
+def attend_back(y_index, qkv, d_out, inverse, expos, aux, packs, pairs):
     rows = qkv.shape[0] // packs
     wide = 3 * LANES
     grid_spec = pltpu.PrefetchScalarGridSpec(
@@ -487,18 +524,19 @@
             pl.BlockSpec((rows, LANES), lambda p, h, y: (p, h)),
             pl.BlockSpec((rows, LANES), lambda p, h, y: (p, h)),
             pl.BlockSpec((1, 1, 2, BLOCK, 3 * BLOCK), lambda p, h, y: (p, h, 0, 0, 0)),
+            pl.BlockSpec((1, 8, rows), lambda p, h, y: (h, 0, p)),
         ],
         out_specs=[
             pl.BlockSpec((rows, wide), lambda p, h, y: (p, h)),
-            pl.BlockSpec((1, 8, rows), lambda p, h, y: (h, 0, p)),
+            pl.BlockSpec((rows, LANES), lambda p, h, y: (p, 0)),
         ],
     )
     return pl.pallas_call(
-        attend_back_kernel,
+        partial(attend_back_kernel, pairs),
         grid_spec=grid_spec,
         out_shape=(
             jax.ShapeDtypeStruct((packs * rows, pairs * wide), BF16),
-            jax.ShapeDtypeStruct((pairs, 8, packs * rows), F32),
+            jax.ShapeDtypeStruct((packs * rows, LANES), BF16),
         ),
         cost_estimate=pl.CostEstimate(
             flops=packs * pairs * 2 * 18 * BLOCK * BLOCK * LANES * 2,
@@ -506,19 +544,62 @@
             transcendentals=0,
         ),
         name="attend_back",
-    )(y_index, qkv, d_out, inverse, expos)
+    )(y_index, qkv, d_out, inverse, expos, aux)
+
+
+def assemble_kernel(core_ref, low_ref, got_low_ref, high_ref, got_high_ref, *outs):
+    core = core_ref[0]
+    rows = outs[0].shape[0]
+    own = pl.ds(pl.multiple_of(core * rows, 8), rows)
+    count = outs[0].shape[1] // (2 * LANES)
+    middle = low_ref.shape[1]
+    spots = [[3 * p + which for p in range(count)] for which in range(3)]
+    spots.append([3 * count + 1 + p for p in range(count)])
+    for out, chosen in zip(outs, spots):
+        for p, spot in enumerate(chosen):
+            start = spot * LANES
+            mine_ref, got_ref = low_ref, got_low_ref
+            if start >= middle:
+                start -= middle
+                mine_ref, got_ref = high_ref, got_high_ref
+            lanes = slice(start, start + LANES)
+            mine, got = mine_ref[own, lanes], got_ref[:, lanes].astype(F32)
+            left = slice(p * LANES, (p + 1) * LANES)
+            right = slice((count + p) * LANES, (count + p + 1) * LANES)
+            out[:, left] = jnp.where(core == 0, mine, got)
+            out[:, right] = jnp.where(core == 0, got, mine)
+
+
+def assemble(core, low, got_low, high, got_high, pairs):
+    shape = jax.ShapeDtypeStruct((got_low.shape[0], 2 * pairs * LANES), F32)
+    spec = pl.BlockSpec(memory_space=pltpu.VMEM)
+    return pl.pallas_call(
+        assemble_kernel,
+        in_specs=[pl.BlockSpec(memory_space=pltpu.SMEM)] + [spec] * 4,
+        out_specs=[spec] * 4,
+        out_shape=[shape] * 4,
+        name="assemble",
+    )(core.astype(jnp.int32).reshape(1), low, got_low, high, got_high)
 
 
 class Gathering:
     def __init__(self, at, shard):
         self.at, self.step, self.half = at, 1, at.depth
-        self.whole = jnp.zeros((2 * at.depth,) + shard.shape, shard.dtype)
-        self.put(shard, 0, 0)
+        self.whole = None
+        self.waiting = [(shard, 0, 0)]
         self.send(shard, shard)
 
-    def put(self, part, step, side):
-        start = (self.at.block_of(step), side, 0, 0)
-        self.whole = lax.dynamic_update_slice(self.whole, part[None], start)
+    def store(self, *others):
+        for part, step, side in self.waiting:
+            if others:
+                part = after(part, *others)
+            if self.whole is None:
+                self.whole = jnp.zeros((2 * self.half,) + part.shape, part.dtype)
+                if others:
+                    self.whole = after(self.whole, *others)
+            start = (self.at.block_of(step), side, 0, 0)
+            self.whole = lax.dynamic_update_slice(self.whole, part[None], start)
+        self.waiting = []
 
     def send(self, up, down):
         if self.step == self.half:
@@ -527,8 +608,8 @@
 
     def take(self, *others):
         up, down = after_all(self.came, *others)
-        self.put(up, -self.step, 0)
-        self.put(down, self.step, 1 if self.step == self.half else 0)
+        side = 1 if self.step == self.half else 0
+        self.waiting += [(up, -self.step, 0), (down, self.step, side)]
         return up, down
 
     def advance(self, *others):
@@ -539,6 +620,7 @@
 
     def finish(self, *others):
         self.take(*others)
+        self.store()
         return self.whole.reshape(-1, self.whole.shape[-1])
 
 
@@ -612,12 +694,15 @@
         spot = (jnp.where(self.x == 0, self.z, count - 1 - self.z) + step + count) % count
         return jnp.where(spot < self.depth, 2 * spot, 2 * (count - 1 - spot) + 1)
 
-    def sum_plane(self, value, combine):
+    def sum_plane(self, value, rings, combine):
         step = 2
+        rings = list(rings)
         while step < self.dp:
             value = combine(
                 value, lax.ppermute(value, "dp", [(i, i ^ step) for i in range(self.dp)])
             )
+            if rings:
+                value = after(value, *rings.pop(0).advance(value))
             step *= 2
         return value
 
@@ -641,8 +726,11 @@
     def finish_grad(self, own):
         rows = own.shape[0] // 2
         keep = lax.dynamic_slice_in_dim(own, self.core * rows, rows, 0)
-        give = lax.dynamic_slice_in_dim(own, (1 - self.core) * rows, rows, 0)
-        return keep, self.swap_core(give.astype(BF16)).astype(F32)
+        return keep, self.swap_core(self.theirs(own)).astype(F32)
+
+    def theirs(self, own):
+        rows = own.shape[0] // 2
+        return lax.dynamic_slice_in_dim(own, (1 - self.core) * rows, rows, 0).astype(BF16)
 
     def join(self, rows, near):
         both = jnp.concatenate([rows, near], axis=0)
@@ -716,15 +804,18 @@
     qkv_cols = 3 * heads * HEAD_DIM
     in_cols = qkv_cols + LANES
     attn_ring = Gathering(at, attn_shard)
-    moved = attn_ring.advance()
-    keep, give = at.core_columns(after_all((w_gate, w_up, w_down), *moved))
+    early = attn_ring.advance()
+    attn_ring.store()
+    keep, give = at.core_columns(after_all((w_gate, w_up, w_down), *early))
     ffn_shard = at.by_core(
         jnp.concatenate(keep, axis=1)[None],
         at.swap_core(jnp.concatenate(give, axis=1))[None],
         0,
     )
     attn_ring.advance(rows_near)
+    attn_ring.store()
     attn_ring.advance(grad_near)
+    attn_ring.store()
     ffn_ring = Gathering(at, after(ffn_shard, *attn_ring.came))
     attn_all = attn_ring.finish()
     w_in, wo_all = attn_all[:, :in_cols], attn_all[:, in_cols:]
@@ -758,32 +849,44 @@
         [sums[:, :, 0] + later * total[:, :, 1], sums[:, :, 1] + (1.0 - later) * total[:, :, 0]],
         axis=2,
     ).reshape(heads, 2 * pack)
-    seg_own = segment_ids[0].reshape(2, rows_loc)
+    seg_own = after(segment_ids, *early)[0].reshape(2, rows_loc)
     seg_own = jnp.where(at.y == 0, seg_own, seg_own[::-1]).reshape(1, pack)
     seg_both = jnp.concatenate([seg_own, at.swap_core(seg_own)], axis=1).astype(F32)
     aux = jnp.concatenate(
         [
             cumul.reshape(pairs, 2, 2 * pack),
-            jnp.broadcast_to(seg_both[None], (pairs, 6, 2 * pack)),
+            jnp.broadcast_to(seg_both[None], (pairs, 2, 2 * pack)),
+            logits.reshape(pairs, 2, 2 * pack),
+            jnp.zeros((pairs, 2, 2 * pack), F32),
         ],
         axis=1,
     )
-    mixed, inverse, expos, tops = attend(y_index, qkv, aux, 2, pairs)
-
-    moved = ffn_ring.advance(mixed)
-    part, got = at.meet_core(after(mixed, *moved), wo_all, dot_nt)
-    mine = part + got.astype(F32)
+    mixed_other, inverse, expos, tops_other = attend(y_index, qkv, aux, 2, pairs, 1)
+    moved = ffn_ring.advance(mixed_other)
+
+    given = dot_nt(after(mixed_other, *moved), wo_all).astype(BF16)
+    got = at.swap_core(given)
+    mixed_own, inverse, expos, tops = attend(
+        y_index, after(qkv, given), aux, 2, pairs, 0, (inverse, expos)
+    )
+    tops = jnp.concatenate([tops, tops_other], axis=0)
+    mixed = jnp.concatenate([mixed_own, mixed_other], axis=0)
+    mine = dot_nt(mixed_own, wo_all) + after(got, mixed_own).astype(F32)
     given = mine[rows_loc:].astype(BF16)
     got = at.swap_y(given)
+    ffn_ring.store(given)
+    moved = ffn_ring.advance(given)
+    (got,) = after_all((got,), *moved)
     resid = x_own + (mine[:rows_loc] + got.astype(F32))
     scale_two = lax.rsqrt(jnp.mean(resid * resid, axis=1, keepdims=True) + EPSILON)
     unit_two = resid * scale_two
     normed_own = (unit_two * gain_two).astype(BF16)
     near = at.swap_y(normed_own)
+    ffn_ring.store(normed_own)
     moved = ffn_ring.advance(normed_own)
     (near,) = after_all((near,), *moved)
     normed_two = at.join(normed_own, near)
-    ffn_ring.advance(normed_two)
+    ffn_ring.store(near)
     ffn_all = ffn_ring.finish()
     gu_all, down_all = ffn_all[:, : 2 * units], ffn_all[:, 2 * units :]
 
@@ -817,52 +920,43 @@
     out_given = dot_nt(after(hidden, *moved)[pack:], down_all).astype(BF16)
     moved = down_sum.advance(out_given)
     out_part = dot_nt(after(hidden, *moved)[:pack], down_all)
-    (near,) = after_all((near,), out_part)
+    moved = gu_sum.advance(out_part)
+    (near,) = after_all((near,), *moved)
     grad_attn = at.join(grad_own, near)
 
+    out_got = at.swap_core(after(out_given, grad_attn))
     grad_mixed = dot_nn(grad_attn, wo_all).astype(BF16)
-    out_got = at.swap_core(after(out_given, grad_attn))
-    moved = gu_sum.advance(grad_mixed)
-    d_qkv, d_cum = attend_back(
-        y_index, qkv, after(grad_mixed, *moved), inverse, expos, 2, pairs
-    )
-
-    def place(own):
-        keep, got = at.finish_grad(own)
-        return at.by_core(keep, got, 1)
-
-    moved = down_sum.advance(d_qkv)
-    moved = gu_sum.advance(*moved)
+    out_own = out_part + after(out_got, grad_mixed).astype(F32)
+    out_given = out_own[rows_loc:].astype(BF16)
+    out_got = at.swap_y(out_given)
+    moved = down_sum.advance(out_given)
+    d_qkv, d_split = attend_back(
+        y_index, qkv, after(grad_mixed, *moved), inverse, expos, aux, 2, pairs
+    )
+    moved = gu_sum.advance(d_qkv)
     middle = 7 * LANES
     low = dot_tn(normed_one, after(d_qkv, *moved)[:, :middle]).astype(BF16)
-    d_cum = d_cum[:, :2].reshape(heads, 2, 2, rows_loc)
-    back = jnp.einsum("hpbt,st->hpbs", d_cum, upper, precision=HIGHEST)
-    ends = back[..., :1]
-    d_log = jnp.stack(
-        [back[:, :, 0] + (1.0 - later) * ends[:, :, 1], back[:, :, 1] + later * ends[:, :, 0]],
-        axis=2,
-    ).reshape(heads, 2 * pack)
-    d_logit = d_log * jax.nn.sigmoid(-logits)
-    bias_part = jnp.sum(d_logit, axis=1)
-    d_split = jnp.concatenate(split_low(d_logit), axis=0).T
-    d_split = jnp.pad(d_split, ((0, 0), (0, LANES - 2 * heads)))
-    d_in = jnp.concatenate([d_qkv, d_split], axis=1)
-    d_in_late, attn_late = after_all((d_in, grad_attn), low)
+    total_down = down_sum.finish(low)
+    low_sum = Reduction(at, low, total_down)
+    d_in = jnp.concatenate([d_qkv, after(d_split, *low_sum.sent)], axis=1)
+    bias_part = jnp.sum(d_split.astype(F32), axis=0)
+    bias_part = bias_part[:heads] + bias_part[heads : 2 * heads]
+    given = dot_nt(d_in[pack:], w_in).astype(BF16)
+    got = at.swap_core(given)
+    d_in_late, attn_late = after_all((d_in, grad_attn), given)
     high = jnp.concatenate(
         [dot_tn(normed_one, d_in_late[:, middle:]), dot_tn(attn_late, mixed)], axis=1
     ).astype(BF16)
-    total = down_sum.finish(high)
-    low_sum = Reduction(at, low, total)
-    g_down = place(total)
-    part, got = at.meet_core(after(d_in, *low_sum.sent), w_in, dot_nt)
-    total = gu_sum.finish(part)
-    high_sum = Reduction(at, high, total)
-    mine = part + after(got, *high_sum.sent).astype(F32)
+    part = dot_nt(after(d_in, high)[:pack], w_in)
+    mine = part + after(got, part).astype(F32)
     given = mine[rows_loc:].astype(BF16)
     got = at.swap_y(given)
-    moved = low_sum.advance(given)
+    total_gu = gu_sum.finish(given)
+    high_sum = Reduction(at, high, total_gu)
+    layer_out = resid + (out_own[:rows_loc] + after(out_got, low).astype(F32))
+    layer_out = layer_out.astype(BF16)
+    moved = low_sum.advance(layer_out, *high_sum.sent)
     moved = high_sum.advance(*moved)
-    moved = low_sum.advance(*moved)
     (got,) = after_all((got,), *moved)
 
     grad_one = mine[:rows_loc] + got.astype(F32)
@@ -870,62 +964,59 @@
     inner_one = jnp.mean(unit_one * weighted, axis=1, keepdims=True)
     norm1_part = jnp.sum(grad_one * unit_one, axis=0)
     x_grad = (grad_resid + scale_one * (weighted - unit_one * inner_one)).astype(BF16)
-    out_own = out_part + after(out_got, norm1_part).astype(F32)
-    out_got = at.swap_y(out_own[rows_loc:].astype(BF16))
-    layer_out = (resid + (out_own[:rows_loc] + out_got.astype(F32))).astype(BF16)
-    moved = high_sum.advance(norm1_part)
-    keep, other = at.finish_grad(total)
-    g_gate = at.by_core(keep[:, :units], other[:, :units], 1)
-    g_up = at.by_core(keep[:, units:], other[:, units:], 1)
-    moved = low_sum.advance(*moved)
+    moved = low_sum.advance(norm1_part)
     moved = high_sum.advance(*moved)
 
-    norms = after(jnp.stack([norm1_part, norm2_part]), *moved)
-    norms = norms + at.swap_core(norms)
-    cut = width // 2
-    norms = lax.dynamic_slice_in_dim(norms, at.y * cut, cut, 1) + at.swap_y(
-        lax.dynamic_slice_in_dim(norms, (1 - at.y) * cut, cut, 1)
-    )
     maxima = jnp.max(tops[:, :, :2], axis=(0, 3)).reshape(heads)
-    lone = jnp.pad(jnp.stack([bias_part, maxima]), ((0, 4), (0, cut - heads)))
+    lone = jnp.pad(jnp.stack([bias_part, maxima]), ((0, 4), (0, width - heads)))
     sums = at.sum_plane(
-        jnp.concatenate([norms, lone], axis=0),
+        jnp.concatenate([jnp.stack([norm1_part, norm2_part]), lone], axis=0),
+        (low_sum, high_sum),
         lambda one, two: jnp.concatenate(
             [one[:3] + two[:3], jnp.maximum(one[3:], two[3:])], axis=0
         ),
     )
-    lone = sums[2:4, :LANES]
-    lone = at.by_core(lone[:, :heads], at.swap_core(lone)[:, :heads], 1)
+    other = at.swap_core(sums)
+    cut = width // 2
+    norms = sums[:2] + other[:2]
+    norms = lax.dynamic_slice_in_dim(norms, at.y * cut, cut, 1) + at.swap_y(
+        lax.dynamic_slice_in_dim(norms, (1 - at.y) * cut, cut, 1)
+    )
+    lone = at.by_core(sums[2:4, :heads], other[2:4, :heads], 1)
     g_bias = lone[0]
     clip_factor = jnp.minimum(1.0, clip_tau / jnp.maximum(lone[1], 1.0))
     columns = jnp.repeat(jnp.sqrt(clip_factor), HEAD_DIM)
     clipped_query = (w_query.astype(F32) * columns[None, :]).astype(BF16)
     clipped_key = (w_key.astype(F32) * columns[None, :]).astype(BF16)
 
-    g_in = jnp.concatenate([low_sum.finish(norms), high_sum.finish(norms)], axis=1)
-    keep, got = at.finish_grad(g_in)
-
-    def third(which):
-        def pick(value):
-            value = value[:, :qkv_cols].reshape(d_rows, pairs, 3, LANES)
-            return value[:, :, which].reshape(d_rows, -1)
-
-        return at.by_core(pick(keep), pick(got), 1)
-
-    def forget(value):
-        return value[:, qkv_cols : qkv_cols + heads] + value[:, qkv_cols + heads :][:, :heads]
+    def place(own):
+        keep, got = at.finish_grad(own)
+        return at.by_core(keep, got, 1)
+
+    g_down = place(total_down)
+    keep, got = at.finish_grad(total_gu)
+    g_gate = at.by_core(keep[:, :units], got[:, :units], 1)
+    g_up = at.by_core(keep[:, units:], got[:, units:], 1)
+    low, high = low_sum.finish(), high_sum.finish()
+    got_low, got_high = at.swap_core(at.theirs(low)), at.swap_core(at.theirs(high))
+    g_query, g_key, g_value, g_output = assemble(at.core, low, got_low, high, got_high, pairs)
+    start = qkv_cols - middle
+    mine = lax.dynamic_slice(high, (at.core * d_rows, start), (d_rows, 2 * heads))
+    both = at.by_core(mine[None], got_high[None, :, start : start + 2 * heads].astype(F32), 0)
+    g_forget = both[..., :heads] + both[..., heads:]
+    g_forget = jnp.concatenate([g_forget[0], g_forget[1]], axis=1)
 
     return (
         layer_out,
         x_grad,
-        sums[0],
-        third(0),
-        third(1),
-        third(2),
-        at.by_core(forget(keep), forget(got), 1),
+        norms[0],
+        g_query,
+        g_key,
+        g_value,
+        g_forget,
         g_bias,
-        at.by_core(keep[:, in_cols:], got[:, in_cols:], 1),
-        sums[1],
+        g_output,
+        norms[1],
         g_gate,
         g_up,
         g_down,

time: 455 us -> 424 us (0.932)
  waiting for transfers between devices: 165 us -> 131 us
  Pallas kernels: 33.3 us -> 42.2 us
    ppermute x9, waiting for transfers between devices: 64.9 us -> 28.5 us  [swap_y(): return lax.ppermute(value, 'tensor', [(0, 1), (1, 0)])]
    pallas_call x1 -> x2, Pallas kernels: 17.4 us -> 24.2 us  [the longest x1 21.8 us: attend_back(): pl.pallas_call(partial(attend_back_kernel, pairs), grid_spec=grid_spec, o...]
    dynamic_update_slice x17, local copies, waits for them, and re-layouts: 7.56 us -> 12.7 us  [store(): self.whole = lax.dynamic_update_slice(self.whole, part[None], start)]
    pallas_call x1 -> x2, Pallas kernels: 16 us -> 18 us  [attend(): pl.pallas_call(attend_kernel, grid_spec=grid_spec, out_shape=(jax.ShapeDt...]
  transfers between devices with their start and end apart: 76 -> 76, of which waited for: 35 -> 33; matrix products, arithmetic and copies ran while one was open for 31% -> 33% of each run, Pallas kernels for 7% -> 10%
where the time goes in v4:
time: 424 us; the launch traced here: 419 us
  waiting for transfers between devices  131 us (31%)
  matrix products  80.8 us (19%)
  starting transfers between devices  68.3 us (16%)
  other arithmetic  58.1 us (14%)
  Pallas kernels  42.2 us (10%)
  local copies, waits for them, and re-layouts  36 us (8%)
    ppermute x48, waiting for transfers between devices, ring(): return lax.ppermute(value, 'dp', pairs)  88.8 us
    ppermute x48, starting transfers between devices, ring(): return lax.ppermute(value, 'dp', pairs)  51.7 us
    dot_general x4, matrix products, dot_nn(): lax.dot_general(left, right, (((1,), (0,)), ((), ())), preferred_element_...  28.8 us
    ppermute x9, waiting for transfers between devices, swap_y(): return lax.ppermute(value, 'tensor', [(0, 1), (1, 0)])  28.5 us
    dot_general x9, matrix products, dot_nt(): lax.dot_general(left, right, (((1,), (1,)), ((), ())), preferred_element_...  28.1 us
    dot_general x5, matrix products, dot_tn(): lax.dot_general(left, right, (((0,), (0,)), ((), ())), preferred_element_...  23.7 us
    pallas_call x1, Pallas kernels, attend_back(): pl.pallas_call(partial(attend_back_kernel, pairs), grid_spec=grid_spec, o...  21.8 us
    pallas_call x2, Pallas kernels, attend(): pl.pallas_call(attend_kernel, grid_spec=grid_spec, out_shape=(jax.ShapeDt...  18 us
  transfers between devices with their start and end apart: 76, of which 33 were waited for; matrix products, arithmetic and copies ran while one was open for 33% of the time, Pallas kernels for 10%

profile of v4, /device:TPU:0, one launch (start us, length us, event | category | flops | bytes accessed | tf_op | source)
XLA Modules:
  0.0 418.8 jit_solution(9762456865098236608)
XLA Ops:
  6.6 2.6 collective-permute-start
  13.4 14.2 %collective-permute-done = bf16[256,1536]{1,0:T(8,128)(2,1)S(1)} collective-permute-done((bf16[256,1536]{1,0:T(8,128)(2,1)}, bf16[256,1536]{1,0:T(8,128)(2,1)S(1)}, u32[]{:S(2)}, u32[]{:S(2)}) %collective-permute-start) | collective-permute-done | bytes 786464 | tf_op jit(solution)/shard_map/ppermute | solution.py:679
  27.5 1.7 collective-permute-start.9
  30.6 1.6 collective-permute-start.5
  35.8 2.0 bitcast_dynamic-update-slice_fusion.12
  37.8 2.0 bitcast_dynamic-update-slice_fusion.11
  41.4 2.4 maximum_select_fusion
  43.8 3.1 collective-permute-done.9
  48.3 9.3 %collective-permute-done.6 = bf16[2,96,1664]{2,1,0:T(8,128)(2,1)S(1)} collective-permute-done((bf16[2,96,1664]{2,1,0:T(8,128)(2,1)}, bf16[2,96,1664]{2,1,0:T(8,128)(2,1)S(1)}, u32[]{:S(2)}, u32[]{:S(2)}) %collective-permute-start.6) | collective-permute-done | bytes 639008 | tf_op jit(solution)/shard_map/ppermute | solution.py:690
  60.9 12.5 %collective-permute-done.7 = bf16[2,96,1664]{2,1,0:T(8,128)(2,1)S(1)} collective-permute-done((bf16[2,96,1664]{2,1,0:T(8,128)(2,1)}, bf16[2,96,1664]{2,1,0:T(8,128)(2,1)S(1)}, u32[]{:S(2)}, u32[]{:S(2)}) %collective-permute-start.7) | collective-permute-done | bytes 639008 | tf_op jit(solution)/shard_map/ppermute | solution.py:690
  74.6 1.6 collective-permute-start.10
  76.9 1.9 fusion
  78.8 3.4 collective-permute-done.10
  86.5 4.8 %fusion.2 = bf16[1024,1536]{1,0:T(8,128)(2,1)S(1)} fusion(f32[1536]{0:T(1024)S(1)} %get-tuple-element.279, f32[1024]{0:T(1024)S(1)} %add_rsqrt_fusion, bf16[512,1536]{1,0:T(8,128)(2,1)} %collective-permute-done.1, bf16[256,1536]{1,0:T(8,128)(2,1)S(1)} %collective-permute-done, bf16[256,1536]{1,0:T(8,128)(2,1)S(1)} %copy-done), kind=kLoop, calls=%fused_computation.5 | loop fusion | flops 14155776 | bytes 6301696 | tf_op jit(solution)/shard_map/convert_element_type | solution.py:835
  92.7 5.4 %convolution_convert_fusion.1.qkv_ref = bf16[1024,1152]{1,0:T(8,128)(2,1)} fusion(bf16[1024,1536]{1,0:T(8,128)(2,1)S(1)} %fusion.2, bf16[1536,1664]{1,0:T(8,128)(2,1)S(1)} %bitcast.252), kind=kOutput, calls=%fused_computation.36 | convolution fusion | flops 3625058304 | bytes 9043968 | tf_op jit(solution)/shard_map/dot_general | solution.py:320
  98.9 9.1 %attend.2 = (bf16[512,384]{1,0:T(8,128)(2,1)}, f32[1024,384]{1,0:T(8,128)}, bf16[2,3,2,256,768]{4,3,2,1,0:T(8,128)(2,1)}, f32[1,3,8,128]{3,2,1,0:T(8,128)}) custom-call(s32[1]{0:T(128)} %bitcast.y_ref, bf16[1024,1152]{1,0:T(8,128)(2,1)} %convolution_convert_fusion.1.qkv_ref, f32[3,8,1024]{2,1,0:T(8,128)} %maximum_maximum_fusion.aux_ref), custom_call_target="tpu_custom_call" | custom-call | flops 603979776 | bytes 10000000 | tf_op jit(solution)/shard_map/attend/pallas_call | solution.py:396
  110.2 3.6 convolution_convert_fusion.5
  117.7 2.7 constant_dynamic-update-slice_fusion
  120.5 9.0 %attend.3 = (bf16[512,384]{1,0:T(8,128)(2,1)}, f32[1024,384]{1,0:T(8,128)}, bf16[2,3,2,256,768]{4,3,2,1,0:T(8,128)(2,1)}, f32[1,3,8,128]{3,2,1,0:T(8,128)}) custom-call(s32[1]{0:T(128)} %bitcast.y_ref, bf16[1024,1152]{1,0:T(8,128)(2,1)} %convolution_convert_fusion.1.qkv_ref, ...), custom_call_target="tpu_custom_call", output_to_operand_aliasing={{1}: (3, {}), {2}: (4, {})} | custom-call | flops 603979776 | bytes 10000000 | tf_op jit(solution)/shard_map/attend/pallas_call | solution.py:396
  129.4 2.4 fusion.52
  131.9 1.9 convert_add_fusion.3
  134.4 10.0 %collective-permute-done.18 = bf16[2,96,3072]{2,1,0:T(8,128)(2,1)} collective-permute-done((bf16[2,96,3072]{2,1,0:T(8,128)(2,1)}, bf16[2,96,3072]{2,1,0:T(8,128)(2,1)}, u32[]{:S(2)}, u32[]{:S(2)}) %collective-permute-start.18) | collective-permute-done | bytes 1179680 | tf_op jit(solution)/shard_map/ppermute | solution.py:690
  145.7 1.8 collective-permute-start.22
  153.4 2.2 multiply_reduce_fusion.2
  159.2 13.4 %collective-permute-done.21 = bf16[2,96,3072]{2,1,0:T(8,128)(2,1)S(1)} collective-permute-done((bf16[2,96,3072]{2,1,0:T(8,128)(2,1)}, bf16[2,96,3072]{2,1,0:T(8,128)(2,1)S(1)}, u32[]{:S(2)}, u32[]{:S(2)}) %collective-permute-start.21) | collective-permute-done | bytes 1179680 | tf_op jit(solution)/shard_map/ppermute | solution.py:690
  175.8 11.0 %collective-permute-done.24 = bf16[1,96,3072]{2,1,0:T(8,128)(2,1)S(1)} collective-permute-done((bf16[1,96,3072]{2,1,0:T(8,128)(2,1)S(1)}, bf16[1,96,3072]{2,1,0:T(8,128)(2,1)S(1)}, u32[]{:S(2)}, u32[]{:S(2)}) %collective-permute-start.24) | collective-permute-done | bytes 589856 | tf_op jit(solution)/shard_map/ppermute | solution.py:690
  188.4 8.8 %fusion.7 = f32[1024,2048]{1,0:T(8,128)} fusion(bf16[1536,3072]{1,0:T(8,128)(2,1)S(1)} %bitcast.245, bf16[512,1536]{1,0:T(8,128)(2,1)S(1)} %collective-permute-done.23, bf16[256,1536]{1,0:T(8,128)(2,1)S(1)} %collective-permute-done.20, bf16[256,1536]{1,0:T(8,128)(2,1)S(1)} %multiply_convert_fusion.3), kind=kOutput, calls=%fused_computation.10 | convolution fusion | flops 6451888128 | bytes 17825792 | tf_op jit(solution)/shard_map/dot_general | solution.py:320
  197.2 9.9 %multiply_convert_fusion.1 = (bf16[1024,1024]{1,0:T(8,128)(2,1)S(1)}, bf16[1024,1024]{1,0:T(8,128)(2,1)S(1)}, bf16[1024,1024]{1,0:T(8,128)(2,1)}) fusion(f32[1024,2048]{1,0:T(8,128)} %fusion.7, bf16[1024,1536]{1,0:T(8,128)(2,1)} %constant_dynamic-update-slice_fusion, bf16[1536,3072]{1,0:T(8,128)(2,1)S(1)} %bitcast.246), kind=kOutput, calls=%fused_computation.32 | convolution fusion | flops 3236954112 | bytes 20971520 | tf_op jit(solution)/shard_map/dot_general | solution.py:320
  207.1 4.7 %fusion.18 = bf16[512,1536]{1,0:T(8,128)(2,1)} fusion(bf16[1536,3072]{1,0:T(8,128)(2,1)S(1)} %bitcast.247, bf16[1024,1024]{1,0:T(8,128)(2,1)S(1)} %get-tuple-element.290, bf16[1024,1024]{1,0:T(8,128)(2,1)S(1)} %get-tuple-element.291), kind=kOutput, calls=%fused_computation.52 | convolution fusion | flops 3226206208 | bytes 12058624 | tf_op jit(solution)/shard_map/dot_general | solution.py:316
  212.3 3.5 fusion.3
  215.8 6.0 %convolution_convert_fusion.2 = bf16[1536,1024]{1,0:T(8,128)(2,1)S(1)} fusion(bf16[1024,1536]{1,0:T(8,128)(2,1)} %constant_dynamic-update-slice_fusion, bf16[1024,1024]{1,0:T(8,128)(2,1)} %get-tuple-element.172), kind=kOutput, calls=%fused_computation.37 | convolution fusion | flops 3222798336 | bytes 8388608 | tf_op jit(solution)/shard_map/dot_general | solution.py:324
  225.8 8.6 %convolution_convert_fusion = bf16[1536,2048]{1,0:T(8,128)(2,1)S(1)} fusion(bf16[1024,2048]{1,0:T(8,128)(2,1)S(1)} %pad_maximum_fusion, bf16[512,1536]{1,0:T(8,128)(2,1)} %copy-done.41, bf16[256,1536]{1,0:T(8,128)(2,1)S(1)} %collective-permute-done.20, bf16[256,1536]{1,0:T(8,128)(2,1)S(1)} %multiply_convert_fusion.3), kind=kOutput, calls=%fused_computation.2 | convolution fusion | flops 6455033856 | bytes 13631488 | tf_op jit(solution)/shard_map/dot_general | solution.py:324
  240.1 4.6 %collective-permute-done.34 = bf16[256,1536]{1,0:T(8,128)(2,1)S(1)} collective-permute-done((bf16[256,1536]{1,0:T(8,128)(2,1)S(1)}, bf16[256,1536]{1,0:T(8,128)(2,1)S(1)}, u32[]{:S(2)}, u32[]{:S(2)}) %collective-permute-start.34) | collective-permute-done | bytes 786464 | tf_op jit(solution)/shard_map/ppermute | solution.py:679
  245.3 1.8 fusion.111
  251.2 3.0 convolution_convert_fusion.4
  255.5 2.2 fusion.61
  257.8 3.5 fusion.21
  261.2 9.6 %collective-permute-done.37 = bf16[2,96,2048]{2,1,0:T(8,128)(2,1)S(1)} collective-permute-done((bf16[2,96,2048]{2,1,0:T(8,128)(2,1)S(1)}, bf16[2,96,2048]{2,1,0:T(8,128)(2,1)S(1)}, u32[]{:S(2)}, u32[]{:S(2)}) %collective-permute-start.37) | collective-permute-done | bytes 786464 | tf_op jit(solution)/shard_map/ppermute | solution.py:690
  270.8 1.8 fusion.45
  272.8 3.4 collective-permute-done.38
  276.2 2.0 pad_maximum_fusion.3
  284.6 4.6 %convolution_convert_fusion.8.do_ref = bf16[1024,384]{1,0:T(8,128)(2,1)} fusion(bf16[1536,1664]{1,0:T(8,128)(2,1)} %bitcast.255, bf16[512,1536]{1,0:T(8,128)(2,1)} %copy-done.23, bf16[256,1536]{1,0:T(8,128)(2,1)S(1)} %collective-permute-done.35, bf16[256,1536]{1,0:T(8,128)(2,1)} %copy-done.11), kind=kOutput, calls=%fused_computation.107 | convolution fusion | flops 1217789952 | bytes 5111808 | tf_op jit(solution)/shard_map/dot_general | solution.py:320
  289.2 1.9 convert_add_fusion.1
  291.2 1.6 copy-done.5
  293.7 2.2 fusion.59
  297.9 21.8 %attend_back.1 = (bf16[1024,1152]{1,0:T(8,128)(2,1)}, bf16[1024,128]{1,0:T(8,128)(2,1)}) custom-call(s32[1]{0:T(128)} %bitcast.y_ref, bf16[1024,1152]{1,0:T(8,128)(2,1)} %convolution_convert_fusion.1.qkv_ref, bf16[1024,384]{1,0:T(8,128)(2,1)} %convolution_convert_fusion.8.do_ref, f32[1024,384]{1,0:T(8,128)} %get-tuple-element.181.inv_ref, ...), custom_call_target="tpu_custom_call" | custom-call | flops 3623878656 | bytes 20000000 | tf_op jit(solution)/shard_map/attend_back/pallas_call | solution.py:534
  319.8 2.6 fusion.43
  326.2 5.4 %convolution_convert_fusion.3 = bf16[1536,896]{1,0:T(8,128)(2,1)S(1)} fusion(bf16[1024,1536]{1,0:T(8,128)(2,1)S(1)} %copy-done.4, bf16[1024,1152]{1,0:T(8,128)(2,1)} %get-tuple-element.186), kind=kOutput, calls=%fused_computation.38 | convolution fusion | flops 2819948544 | bytes 7733248 | tf_op jit(solution)/shard_map/dot_general | solution.py:324
  332.1 1.9 fusion.58
  334.2 4.4 %fusion.15 = bf16[512,1536]{1,0:T(8,128)(2,1)S(1)} fusion(bf16[1536,1664]{1,0:T(8,128)(2,1)} %bitcast.256, bf16[1024,1280]{1,0:T(8,128)(2,1)S(1)} %constant_dynamic-update-slice_fusion.3), kind=kOutput, calls=%fused_computation.51 | convolution fusion | flops 2014052352 | bytes 6815744 | tf_op jit(solution)/shard_map/dot_general | solution.py:316
  339.3 2.2 fusion.13
  341.5 1.9 convolution_convert_fusion.6
  343.4 1.8 convolution_convert_fusion.7
  356.6 2.3 collective-permute-done.51
  364.9 4.4 %collective-permute-done.48 = bf16[256,1536]{1,0:T(8,128)(2,1)S(1)} collective-permute-done((bf16[256,1536]{1,0:T(8,128)(2,1)S(1)}, bf16[256,1536]{1,0:T(8,128)(2,1)S(1)}, u32[]{:S(2)}, u32[]{:S(2)}) %collective-permute-start.48) | collective-permute-done | bytes 786464 | tf_op jit(solution)/shard_map/ppermute | solution.py:679
  372.3 1.8 collective-permute-done.62
  374.1 2.0 collective-permute-done.61
  376.1 1.6 collective-permute-start.55
  380.0 4.5 %collective-permute-done.55 = f32[8,1536]{1,0:T(8,128)S(1)} collective-permute-done((f32[8,1536]{1,0:T(8,128)S(1)}, f32[8,1536]{1,0:T(8,128)S(1)}, u32[]{:S(2)}, u32[]{:S(2)}) %collective-permute-start.55) | collective-permute-done | bytes 49184 | tf_op jit(solution)/shard_map/ppermute | solution.py:702
  385.6 4.1 collective-permute-done.60
  393.1 2.4 collective-permute-start.68
  395.8 1.7 collective-permute-start.71
  405.1 4.0 collective-permute-done.71
  416.0 2.4 assemble.1
  (385 shorter events, 123.9 us)
Async XLA Ops:
  6.6 20.9 %collective-permute-start = (bf16[256,1536]{1,0:T(8,128)(2,1)}, bf16[256,1536]{1,0:T(8,128)(2,1)S(1)}, u32[]{:S(2)}, u32[]{:S(2)}) collective-permute-start(bf16[256,1536]{1,0:T(8,128)(2,1)} %param.15), channel_id=1, source_target_pairs={{0,1},{1,0},{2,3},{3,2},{4,5},{5,4},{6,7},{7,6},{8,9},{9,8},{10,11... | collective-permute-start | bytes 2359304 | tf_op jit(solution)/shard_map/ppermute | solution.py:679
  10.4 20.2 %collective-permute-start.3 = (bf16[2,96,1664]{2,1,0:T(8,128)(2,1)}, bf16[2,96,1664]{2,1,0:T(8,128)(2,1)}, u32[]{:S(2)}, u32[]{:S(2)}) collective-permute-start(bf16[2,96,1664]{2,1,0:T(8,128)(2,1)} %maximum_select_fusion.5), channel_id=1, source_target_pairs={{0,8},{2,10},{8,16},{10,18},{16,24},{18,26},{24,28},{26,30},{28,20... | collective-permute-start | bytes 1916936 | tf_op jit(solution)/shard_map/ppermute | solution.py:690
  12.0 18.6 %collective-permute-start.4 = (bf16[2,96,1664]{2,1,0:T(8,128)(2,1)}, bf16[2,96,1664]{2,1,0:T(8,128)(2,1)}, u32[]{:S(2)}, u32[]{:S(2)}) collective-permute-start(bf16[2,96,1664]{2,1,0:T(8,128)(2,1)} %maximum_select_fusion.5), channel_id=1, source_target_pairs={{0,4},{2,6},{8,0},{10,2},{16,8},{18,10},{24,16},{26,18},{28,24},{3... | collective-permute-start | bytes 1916936 | tf_op jit(solution)/shard_map/ppermute | solution.py:690
  27.5 19.4 %collective-permute-start.9 = (bf16[256,1536]{1,0:T(8,128)(2,1)S(1)}, bf16[256,1536]{1,0:T(8,128)(2,1)S(1)}, u32[]{:S(2)}, u32[]{:S(2)}) collective-permute-start(bf16[256,1536]{1,0:T(8,128)(2,1)S(1)} %copy-done.10), channel_id=1, source_target_pairs={{0,1},{1,0},{2,3},{3,2},{4,5},{5,4},{6,7},{7,6},{8,9},{9,8},{10,11... | collective-permute-start | bytes 2359304 | tf_op jit(solution)/shard_map/ppermute | solution.py:679
  30.6 46.3 %collective-permute-start.1 = (bf16[512,1536]{1,0:T(8,128)(2,1)}, bf16[512,1536]{1,0:T(8,128)(2,1)}, u32[]{:S(2)}, u32[]{:S(2)}) collective-permute-start(bf16[512,1536]{1,0:T(8,128)(2,1)} %pad_maximum_fusion.4), channel_id=1, source_target_pairs={{0,2},{2,0},{4,6},{6,4},{8,10},{10,8},{12,14},{14,12},{16,18},{18,... | collective-permute-start | bytes 4718600 | tf_op jit(solution)/shard_map/ppermute | solution.py:676
  30.6 17.7 %collective-permute-start.5 = (bf16[2,96,1664]{2,1,0:T(8,128)(2,1)}, bf16[2,96,1664]{2,1,0:T(8,128)(2,1)}, u32[]{:S(2)}, u32[]{:S(2)}) collective-permute-start(bf16[2,96,1664]{2,1,0:T(8,128)(2,1)} %collective-permute-done.3), channel_id=1, source_target_pairs={{0,8},{2,10},{8,16},{10,18},{16,24},{18,26},{24,28},{26,30},{28,20... | collective-permute-start | bytes 1916936 | tf_op jit(solution)/shard_map/ppermute | solution.py:690
  33.9 7.4 %collective-permute-start.13 = (bf16[96,3072]{1,0:T(8,128)(2,1)}, bf16[96,3072]{1,0:T(8,128)(2,1)}, u32[]{:S(2)}, u32[]{:S(2)}) collective-permute-start(bf16[96,3072]{1,0:T(8,128)(2,1)} %pad_maximum_fusion.12), channel_id=1, source_target_pairs={{0,2},{2,0},{4,6},{6,4},{8,10},{10,8},{12,14},{14,12},{16,18},{18,... | collective-permute-start | bytes 1769480 | tf_op jit(solution)/shard_map/ppermute | solution.py:676
  40.9 16.7 %collective-permute-start.6 = (bf16[2,96,1664]{2,1,0:T(8,128)(2,1)}, bf16[2,96,1664]{2,1,0:T(8,128)(2,1)S(1)}, u32[]{:S(2)}, u32[]{:S(2)}) collective-permute-start(bf16[2,96,1664]{2,1,0:T(8,128)(2,1)} %collective-permute-done.4), channel_id=1, source_target_pairs={{0,4},{2,6},{8,0},{10,2},{16,8},{18,10},{24,16},{26,18},{28,24},{3... | collective-permute-start | bytes 1916936 | tf_op jit(solution)/shard_map/ppermute | solution.py:690
  48.3 69.4 %collective-permute-start.26 = (bf16[512,1536]{1,0:T(8,128)(2,1)}, bf16[512,1536]{1,0:T(8,128)(2,1)}, u32[]{:S(2)}, u32[]{:S(2)}) collective-permute-start(bf16[512,1536]{1,0:T(8,128)(2,1)} %pad_maximum_fusion.6), channel_id=1, source_target_pairs={{0,2},{2,0},{4,6},{6,4},{8,10},{10,8},{12,14},{14,12},{16,18},{18,... | collective-permute-start | bytes 4718600 | tf_op jit(solution)/shard_map/ppermute | solution.py:676
  57.6 15.8 %collective-permute-start.7 = (bf16[2,96,1664]{2,1,0:T(8,128)(2,1)}, bf16[2,96,1664]{2,1,0:T(8,128)(2,1)S(1)}, u32[]{:S(2)}, u32[]{:S(2)}) collective-permute-start(bf16[2,96,1664]{2,1,0:T(8,128)(2,1)} %collective-permute-done.5), channel_id=1, source_target_pairs={{0,8},{2,10},{8,16},{10,18},{16,24},{18,26},{24,28},{26,30},{28,20... | collective-permute-start | bytes 1916936 | tf_op jit(solution)/shard_map/ppermute | solution.py:690
  59.2 15.3 %collective-permute-start.8 = (bf16[2,96,1664]{2,1,0:T(8,128)(2,1)S(1)}, bf16[2,96,1664]{2,1,0:T(8,128)(2,1)S(1)}, u32[]{:S(2)}, u32[]{:S(2)}) collective-permute-start(bf16[2,96,1664]{2,1,0:T(8,128)(2,1)S(1)} %collective-permute-done.6), channel_id=1, source_target_pairs={{0,4},{2,6},{8,0},{10,2},{16,8},{18,10},{24,16},{26,18},{28,24},{3... | collective-permute-start | bytes 1916936 | tf_op jit(solution)/shard_map/ppermute | solution.py:690
  74.6 7.7 %collective-permute-start.10 = (bf16[1,96,1664]{2,1,0:T(8,128)(2,1)S(1)}, bf16[1,96,1664]{2,1,0:T(8,128)(2,1)S(1)}, u32[]{:S(2)}, u32[]{:S(2)}) collective-permute-start(bf16[1,96,1664]{2,1,0:T(8,128)(2,1)S(1)} %slice.410), channel_id=1, source_target_pairs={{0,8},{2,10},{8,16},{10,18},{16,24},{18,26},{24,28},{26,30},{28,20... | collective-permute-start | bytes 958472 | tf_op jit(solution)/shard_map/ppermute | solution.py:690
  76.2 7.4 %collective-permute-start.11 = (bf16[1,96,1664]{2,1,0:T(8,128)(2,1)S(1)}, bf16[1,96,1664]{2,1,0:T(8,128)(2,1)S(1)}, u32[]{:S(2)}, u32[]{:S(2)}) collective-permute-start(bf16[1,96,1664]{2,1,0:T(8,128)(2,1)S(1)} %slice.411), channel_id=1, source_target_pairs={{0,4},{2,6},{8,0},{10,2},{16,8},{18,10},{24,16},{26,18},{28,24},{3... | collective-permute-start | bytes 958472 | tf_op jit(solution)/shard_map/ppermute | solution.py:690
  83.6 25.2 %collective-permute-start.14 = (bf16[2,96,3072]{2,1,0:T(8,128)(2,1)}, bf16[2,96,3072]{2,1,0:T(8,128)(2,1)}, u32[]{:S(2)}, u32[]{:S(2)}) collective-permute-start(bf16[2,96,3072]{2,1,0:T(8,128)(2,1)} %maximum_select_fusion), channel_id=1, source_target_pairs={{0,8},{2,10},{8,16},{10,18},{16,24},{18,26},{24,28},{26,30},{28,20... | collective-permute-start | bytes 3538952 | tf_op jit(solution)/shard_map/ppermute | solution.py:690
  85.1 25.1 %collective-permute-start.15 = (bf16[2,96,3072]{2,1,0:T(8,128)(2,1)}, bf16[2,96,3072]{2,1,0:T(8,128)(2,1)}, u32[]{:S(2)}, u32[]{:S(2)}) collective-permute-start(bf16[2,96,3072]{2,1,0:T(8,128)(2,1)} %maximum_select_fusion), channel_id=1, source_target_pairs={{0,4},{2,6},{8,0},{10,2},{16,8},{18,10},{24,16},{26,18},{28,24},{3... | collective-permute-start | bytes 3538952 | tf_op jit(solution)/shard_map/ppermute | solution.py:690
  113.8 18.0 %collective-permute-start.16 = (bf16[512,1536]{1,0:T(8,128)(2,1)}, bf16[512,1536]{1,0:T(8,128)(2,1)}, u32[]{:S(2)}, u32[]{:S(2)}) collective-permute-start(bf16[512,1536]{1,0:T(8,128)(2,1)} %convolution_convert_fusion.5), channel_id=1, source_target_pairs={{0,2},{2,0},{4,6},{6,4},{8,10},{10,8},{12,14},{14,12},{16,18},{18,... | collective-permute-start | bytes 4718600 | tf_op jit(solution)/shard_map/ppermute | solution.py:676
  115.7 28.7 %collective-permute-start.18 = (bf16[2,96,3072]{2,1,0:T(8,128)(2,1)}, bf16[2,96,3072]{2,1,0:T(8,128)(2,1)}, u32[]{:S(2)}, u32[]{:S(2)}) collective-permute-start(bf16[2,96,3072]{2,1,0:T(8,128)(2,1)} %collective-permute-done.14), channel_id=1, source_target_pairs={{0,8},{2,10},{8,16},{10,18},{16,24},{18,26},{24,28},{26,30},{28,20... | collective-permute-start | bytes 3538952 | tf_op jit(solution)/shard_map/ppermute | solution.py:690
  116.8 28.4 %collective-permute-start.19 = (bf16[2,96,3072]{2,1,0:T(8,128)(2,1)}, bf16[2,96,3072]{2,1,0:T(8,128)(2,1)}, u32[]{:S(2)}, u32[]{:S(2)}) collective-permute-start(bf16[2,96,3072]{2,1,0:T(8,128)(2,1)} %collective-permute-done.15), channel_id=1, source_target_pairs={{0,4},{2,6},{8,0},{10,2},{16,8},{18,10},{24,16},{26,18},{28,24},{3... | collective-permute-start | bytes 3538952 | tf_op jit(solution)/shard_map/ppermute | solution.py:690
  133.8 19.6 %collective-permute-start.17 = (bf16[256,1536]{1,0:T(8,128)(2,1)S(1)}, bf16[256,1536]{1,0:T(8,128)(2,1)}, u32[]{:S(2)}, u32[]{:S(2)}) collective-permute-start(bf16[256,1536]{1,0:T(8,128)(2,1)S(1)} %slice.715), channel_id=1, source_target_pairs={{0,1},{1,0},{2,3},{3,2},{4,5},{5,4},{6,7},{7,6},{8,9},{9,8},{10,11... | collective-permute-start | bytes 2359304 | tf_op jit(solution)/shard_map/ppermute | solution.py:679
  145.2 27.5 %collective-permute-start.21 = (bf16[2,96,3072]{2,1,0:T(8,128)(2,1)}, bf16[2,96,3072]{2,1,0:T(8,128)(2,1)S(1)}, u32[]{:S(2)}, u32[]{:S(2)}) collective-permute-start(bf16[2,96,3072]{2,1,0:T(8,128)(2,1)} %collective-permute-done.18), channel_id=1, source_target_pairs={{0,8},{2,10},{8,16},{10,18},{16,24},{18,26},{24,28},{26,30},{28,20... | collective-permute-start | bytes 3538952 | tf_op jit(solution)/shard_map/ppermute | solution.py:690
  145.7 27.5 %collective-permute-start.22 = (bf16[2,96,3072]{2,1,0:T(8,128)(2,1)}, bf16[2,96,3072]{2,1,0:T(8,128)(2,1)S(1)}, u32[]{:S(2)}, u32[]{:S(2)}) collective-permute-start(bf16[2,96,3072]{2,1,0:T(8,128)(2,1)} %collective-permute-done.19), channel_id=1, source_target_pairs={{0,4},{2,6},{8,0},{10,2},{16,8},{18,10},{24,16},{26,18},{28,24},{3... | collective-permute-start | bytes 3538952 | tf_op jit(solution)/shard_map/ppermute | solution.py:690
  155.8 19.6 %collective-permute-start.20 = (bf16[256,1536]{1,0:T(8,128)(2,1)S(1)}, bf16[256,1536]{1,0:T(8,128)(2,1)S(1)}, u32[]{:S(2)}, u32[]{:S(2)}) collective-permute-start(bf16[256,1536]{1,0:T(8,128)(2,1)S(1)} %multiply_convert_fusion.3), channel_id=1, source_target_pairs={{0,1},{1,0},{2,3},{3,2},{4,5},{5,4},{6,7},{7,6},{8,9},{9,8},{10,11... | collective-permute-start | bytes 2359304 | tf_op jit(solution)/shard_map/ppermute | solution.py:679
  173.2 13.6 %collective-permute-start.24 = (bf16[1,96,3072]{2,1,0:T(8,128)(2,1)S(1)}, bf16[1,96,3072]{2,1,0:T(8,128)(2,1)S(1)}, u32[]{:S(2)}, u32[]{:S(2)}) collective-permute-start(bf16[1,96,3072]{2,1,0:T(8,128)(2,1)S(1)} %slice.424), channel_id=1, source_target_pairs={{0,8},{2,10},{8,16},{10,18},{16,24},{18,26},{24,28},{26,30},{28,20... | collective-permute-start | bytes 1769480 | tf_op jit(solution)/shard_map/ppermute | solution.py:690
  173.8 13.3 %collective-permute-start.25 = (bf16[1,96,3072]{2,1,0:T(8,128)(2,1)S(1)}, bf16[1,96,3072]{2,1,0:T(8,128)(2,1)S(1)}, u32[]{:S(2)}, u32[]{:S(2)}) collective-permute-start(bf16[1,96,3072]{2,1,0:T(8,128)(2,1)S(1)} %slice.425), channel_id=1, source_target_pairs={{0,4},{2,6},{8,0},{10,2},{16,8},{18,10},{24,16},{26,18},{28,24},{3... | collective-permute-start | bytes 1769480 | tf_op jit(solution)/shard_map/ppermute | solution.py:690
  175.5 11.8 %collective-permute-start.23 = (bf16[512,1536]{1,0:T(8,128)(2,1)S(1)}, bf16[512,1536]{1,0:T(8,128)(2,1)S(1)}, u32[]{:S(2)}, u32[]{:S(2)}) collective-permute-start(bf16[512,1536]{1,0:T(8,128)(2,1)S(1)} %pad_maximum_fusion.5), channel_id=1, source_target_pairs={{0,2},{2,0},{4,6},{6,4},{8,10},{10,8},{12,14},{14,12},{16,18},{18,... | collective-permute-start | bytes 4718600 | tf_op jit(solution)/shard_map/ppermute | solution.py:676
  212.2 12.4 %collective-permute-start.29 = (bf16[512,1536]{1,0:T(8,128)(2,1)}, bf16[512,1536]{1,0:T(8,128)(2,1)S(1)}, u32[]{:S(2)}, u32[]{:S(2)}) collective-permute-start(bf16[512,1536]{1,0:T(8,128)(2,1)} %fusion.18), channel_id=1, source_target_pairs={{0,2},{2,0},{4,6},{6,4},{8,10},{10,8},{12,14},{14,12},{16,18},{18,... | collective-permute-start | bytes 4718600 | tf_op jit(solution)/shard_map/ppermute | solution.py:676
  222.6 11.8 %collective-permute-start.27 = (bf16[1,96,1024]{2,1,0:T(8,128)(2,1)}, bf16[1,96,1024]{2,1,0:T(8,128)(2,1)S(1)}, u32[]{:S(2)}, u32[]{:S(2)}) collective-permute-start(bf16[1,96,1024]{2,1,0:T(8,128)(2,1)} %get-tuple-element.308), channel_id=1, source_target_pairs={{0,8},{2,10},{8,16},{10,18},{16,24},{18,26},{24,28},{26,30},{28,20... | collective-permute-start | bytes 589832 | tf_op jit(solution)/shard_map/ppermute | solution.py:690
  223.1 11.3 %collective-permute-start.28 = (bf16[1,96,1024]{2,1,0:T(8,128)(2,1)S(1)}, bf16[1,96,1024]{2,1,0:T(8,128)(2,1)S(1)}, u32[]{:S(2)}, u32[]{:S(2)}) collective-permute-start(bf16[1,96,1024]{2,1,0:T(8,128)(2,1)S(1)} %get-tuple-element.309), channel_id=1, source_target_pairs={{0,4},{2,6},{8,0},{10,2},{16,8},{18,10},{24,16},{26,18},{28,24},{3... | collective-permute-start | bytes 589832 | tf_op jit(solution)/shard_map/ppermute | solution.py:690
  225.2 19.4 %collective-permute-start.34 = (bf16[256,1536]{1,0:T(8,128)(2,1)S(1)}, bf16[256,1536]{1,0:T(8,128)(2,1)S(1)}, u32[]{:S(2)}, u32[]{:S(2)}) collective-permute-start(bf16[256,1536]{1,0:T(8,128)(2,1)S(1)} %slice.714), channel_id=1, source_target_pairs={{0,1},{1,0},{2,3},{3,2},{4,5},{5,4},{6,7},{7,6},{8,9},{9,8},{10,11... | collective-permute-start | bytes 2359304 | tf_op jit(solution)/shard_map/ppermute | solution.py:679
  234.6 12.4 %collective-permute-start.32 = (bf16[1,96,2048]{2,1,0:T(8,128)(2,1)S(1)}, bf16[1,96,2048]{2,1,0:T(8,128)(2,1)S(1)}, u32[]{:S(2)}, u32[]{:S(2)}) collective-permute-start(bf16[1,96,2048]{2,1,0:T(8,128)(2,1)S(1)} %get-tuple-element.298), channel_id=1, source_target_pairs={{0,8},{2,10},{8,16},{10,18},{16,24},{18,26},{24,28},{26,30},{28,20... | collective-permute-start | bytes 1179656 | tf_op jit(solution)/shard_map/ppermute | solution.py:690
  235.1 12.0 %collective-permute-start.33 = (bf16[1,96,2048]{2,1,0:T(8,128)(2,1)S(1)}, bf16[1,96,2048]{2,1,0:T(8,128)(2,1)S(1)}, u32[]{:S(2)}, u32[]{:S(2)}) collective-permute-start(bf16[1,96,2048]{2,1,0:T(8,128)(2,1)S(1)} %get-tuple-element.299), channel_id=1, source_target_pairs={{0,4},{2,6},{8,0},{10,2},{16,8},{18,10},{24,16},{26,18},{28,24},{3... | collective-permute-start | bytes 1179656 | tf_op jit(solution)/shard_map/ppermute | solution.py:690
  237.9 17.7 %collective-permute-start.31 = (bf16[2,96,1024]{2,1,0:T(8,128)(2,1)S(1)}, bf16[2,96,1024]{2,1,0:T(8,128)(2,1)S(1)}, u32[]{:S(2)}, u32[]{:S(2)}) collective-permute-start(bf16[2,96,1024]{2,1,0:T(8,128)(2,1)S(1)} %pad_maximum_fusion.14), channel_id=1, source_target_pairs={{0,4},{2,6},{8,0},{10,2},{16,8},{18,10},{24,16},{26,18},{28,24},{3... | collective-permute-start | bytes 1179656 | tf_op jit(solution)/shard_map/ppermute | solution.py:690
  239.5 16.1 %collective-permute-start.30 = (bf16[2,96,1024]{2,1,0:T(8,128)(2,1)S(1)}, bf16[2,96,1024]{2,1,0:T(8,128)(2,1)S(1)}, u32[]{:S(2)}, u32[]{:S(2)}) collective-permute-start(bf16[2,96,1024]{2,1,0:T(8,128)(2,1)S(1)} %pad_maximum_fusion.13), channel_id=1, source_target_pairs={{0,8},{2,10},{8,16},{10,18},{16,24},{18,26},{24,28},{26,30},{28,20... | collective-permute-start | bytes 1179656 | tf_op jit(solution)/shard_map/ppermute | solution.py:690
  247.5 23.3 %collective-permute-start.37 = (bf16[2,96,2048]{2,1,0:T(8,128)(2,1)S(1)}, bf16[2,96,2048]{2,1,0:T(8,128)(2,1)S(1)}, u32[]{:S(2)}, u32[]{:S(2)}) collective-permute-start(bf16[2,96,2048]{2,1,0:T(8,128)(2,1)S(1)} %pad_maximum_fusion.11), channel_id=1, source_target_pairs={{0,4},{2,6},{8,0},{10,2},{16,8},{18,10},{24,16},{26,18},{28,24},{3... | collective-permute-start | bytes 2359304 | tf_op jit(solution)/shard_map/ppermute | solution.py:690
  249.2 21.6 %collective-permute-start.36 = (bf16[2,96,2048]{2,1,0:T(8,128)(2,1)S(1)}, bf16[2,96,2048]{2,1,0:T(8,128)(2,1)S(1)}, u32[]{:S(2)}, u32[]{:S(2)}) collective-permute-start(bf16[2,96,2048]{2,1,0:T(8,128)(2,1)S(1)} %pad_maximum_fusion.10), channel_id=1, source_target_pairs={{0,8},{2,10},{8,16},{10,18},{16,24},{18,26},{24,28},{26,30},{28,20... | collective-permute-start | bytes 2359304 | tf_op jit(solution)/shard_map/ppermute | solution.py:690
  249.7 22.9 %collective-permute-start.35 = (bf16[256,1536]{1,0:T(8,128)(2,1)S(1)}, bf16[256,1536]{1,0:T(8,128)(2,1)S(1)}, u32[]{:S(2)}, u32[]{:S(2)}) collective-permute-start(bf16[256,1536]{1,0:T(8,128)(2,1)S(1)} %get-tuple-element.286), channel_id=1, source_target_pairs={{0,1},{1,0},{2,3},{3,2},{4,5},{5,4},{6,7},{7,6},{8,9},{9,8},{10,11... | collective-permute-start | bytes 2359304 | tf_op jit(solution)/shard_map/ppermute | solution.py:679
  278.3 10.9 %collective-permute-start.39 = (bf16[512,1536]{1,0:T(8,128)(2,1)}, bf16[512,1536]{1,0:T(8,128)(2,1)}, u32[]{:S(2)}, u32[]{:S(2)}) collective-permute-start(bf16[512,1536]{1,0:T(8,128)(2,1)} %convolution_convert_fusion.4), channel_id=1, source_target_pairs={{0,2},{2,0},{4,6},{6,4},{8,10},{10,8},{12,14},{14,12},{16,18},{18,... | collective-permute-start | bytes 4718600 | tf_op jit(solution)/shard_map/ppermute | solution.py:676
  280.5 13.3 %collective-permute-start.41 = (bf16[2,96,1024]{2,1,0:T(8,128)(2,1)}, bf16[2,96,1024]{2,1,0:T(8,128)(2,1)S(1)}, u32[]{:S(2)}, u32[]{:S(2)}) collective-permute-start(bf16[2,96,1024]{2,1,0:T(8,128)(2,1)} %get-tuple-element.306), channel_id=1, source_target_pairs={{0,8},{2,10},{8,16},{10,18},{16,24},{18,26},{24,28},{26,30},{28,20... | collective-permute-start | bytes 1179656 | tf_op jit(solution)/shard_map/ppermute | solution.py:690
  281.2 12.5 %collective-permute-start.42 = (bf16[2,96,1024]{2,1,0:T(8,128)(2,1)S(1)}, bf16[2,96,1024]{2,1,0:T(8,128)(2,1)S(1)}, u32[]{:S(2)}, u32[]{:S(2)}) collective-permute-start(bf16[2,96,1024]{2,1,0:T(8,128)(2,1)S(1)} %get-tuple-element.305), channel_id=1, source_target_pairs={{0,4},{2,6},{8,0},{10,2},{16,8},{18,10},{24,16},{26,18},{28,24},{3... | collective-permute-start | bytes 1179656 | tf_op jit(solution)/shard_map/ppermute | solution.py:690
  282.5 37.2 %collective-permute-start.43 = (bf16[2,96,2048]{2,1,0:T(8,128)(2,1)}, bf16[2,96,2048]{2,1,0:T(8,128)(2,1)}, u32[]{:S(2)}, u32[]{:S(2)}) collective-permute-start(bf16[2,96,2048]{2,1,0:T(8,128)(2,1)} %get-tuple-element.296), channel_id=1, source_target_pairs={{0,8},{2,10},{8,16},{10,18},{16,24},{18,26},{24,28},{26,30},{28,20... | collective-permute-start | bytes 2359304 | tf_op jit(solution)/shard_map/ppermute | solution.py:690
  283.3 36.4 %collective-permute-start.44 = (bf16[2,96,2048]{2,1,0:T(8,128)(2,1)}, bf16[2,96,2048]{2,1,0:T(8,128)(2,1)}, u32[]{:S(2)}, u32[]{:S(2)}) collective-permute-start(bf16[2,96,2048]{2,1,0:T(8,128)(2,1)} %get-tuple-element.295), channel_id=1, source_target_pairs={{0,4},{2,6},{8,0},{10,2},{16,8},{18,10},{24,16},{26,18},{28,24},{3... | collective-permute-start | bytes 2359304 | tf_op jit(solution)/shard_map/ppermute | solution.py:690
  295.9 36.2 %collective-permute-start.45 = (bf16[2,96,1024]{2,1,0:T(8,128)(2,1)}, bf16[2,96,1024]{2,1,0:T(8,128)(2,1)S(1)}, u32[]{:S(2)}, u32[]{:S(2)}) collective-permute-start(bf16[2,96,1024]{2,1,0:T(8,128)(2,1)} %get-tuple-element.304), channel_id=1, source_target_pairs={{0,8},{2,10},{8,16},{10,18},{16,24},{18,26},{24,28},{26,30},{28,20... | collective-permute-start | bytes 1179656 | tf_op jit(solution)/shard_map/ppermute | solution.py:690
  297.0 35.2 %collective-permute-start.46 = (bf16[2,96,1024]{2,1,0:T(8,128)(2,1)S(1)}, bf16[2,96,1024]{2,1,0:T(8,128)(2,1)S(1)}, u32[]{:S(2)}, u32[]{:S(2)}) collective-permute-start(bf16[2,96,1024]{2,1,0:T(8,128)(2,1)S(1)} %get-tuple-element.303), channel_id=1, source_target_pairs={{0,4},{2,6},{8,0},{10,2},{16,8},{18,10},{24,16},{26,18},{28,24},{3... | collective-permute-start | bytes 1179656 | tf_op jit(solution)/shard_map/ppermute | solution.py:690
  322.4 28.6 %collective-permute-start.49 = (bf16[2,96,2048]{2,1,0:T(8,128)(2,1)S(1)}, bf16[2,96,2048]{2,1,0:T(8,128)(2,1)S(1)}, u32[]{:S(2)}, u32[]{:S(2)}) collective-permute-start(bf16[2,96,2048]{2,1,0:T(8,128)(2,1)S(1)} %get-tuple-element.294), channel_id=1, source_target_pairs={{0,8},{2,10},{8,16},{10,18},{16,24},{18,26},{24,28},{26,30},{28,20... | collective-permute-start | bytes 2359304 | tf_op jit(solution)/shard_map/ppermute | solution.py:690
  323.5 27.5 %collective-permute-start.50 = (bf16[2,96,2048]{2,1,0:T(8,128)(2,1)S(1)}, bf16[2,96,2048]{2,1,0:T(8,128)(2,1)S(1)}, u32[]{:S(2)}, u32[]{:S(2)}) collective-permute-start(bf16[2,96,2048]{2,1,0:T(8,128)(2,1)S(1)} %get-tuple-element.293), channel_id=1, source_target_pairs={{0,4},{2,6},{8,0},{10,2},{16,8},{18,10},{24,16},{26,18},{28,24},{3... | collective-permute-start | bytes 2359304 | tf_op jit(solution)/shard_map/ppermute | solution.py:690
  324.6 22.9 %collective-permute-start.40 = (bf16[256,1536]{1,0:T(8,128)(2,1)}, bf16[256,1536]{1,0:T(8,128)(2,1)S(1)}, u32[]{:S(2)}, u32[]{:S(2)}) collective-permute-start(bf16[256,1536]{1,0:T(8,128)(2,1)} %slice.713), channel_id=1, source_target_pairs={{0,1},{1,0},{2,3},{3,2},{4,5},{5,4},{6,7},{7,6},{8,9},{9,8},{10,11... | collective-permute-start | bytes 2359304 | tf_op jit(solution)/shard_map/ppermute | solution.py:679
  338.6 11.3 %collective-permute-start.47 = (bf16[512,1536]{1,0:T(8,128)(2,1)S(1)}, bf16[512,1536]{1,0:T(8,128)(2,1)S(1)}, u32[]{:S(2)}, u32[]{:S(2)}) collective-permute-start(bf16[512,1536]{1,0:T(8,128)(2,1)S(1)} %fusion.15), channel_id=1, source_target_pairs={{0,2},{2,0},{4,6},{6,4},{8,10},{10,8},{12,14},{14,12},{16,18},{18,... | collective-permute-start | bytes 4718600 | tf_op jit(solution)/shard_map/ppermute | solution.py:676
  345.5 8.2 %collective-permute-start.53 = (bf16[1,96,896]{2,1,0:T(8,128)(2,1)S(1)}, bf16[1,96,896]{2,1,0:T(8,128)(2,1)S(1)}, u32[]{:S(2)}, u32[]{:S(2)}) collective-permute-start(bf16[1,96,896]{2,1,0:T(8,128)(2,1)S(1)} %get-tuple-element.191), channel_id=1, source_target_pairs={{0,8},{2,10},{8,16},{10,18},{16,24},{18,26},{24,28},{26,30},{28,20... | collective-permute-start | bytes 516104 | tf_op jit(solution)/shard_map/ppermute | solution.py:690
  350.4 19.0 %collective-permute-start.48 = (bf16[256,1536]{1,0:T(8,128)(2,1)S(1)}, bf16[256,1536]{1,0:T(8,128)(2,1)S(1)}, u32[]{:S(2)}, u32[]{:S(2)}) collective-permute-start(bf16[256,1536]{1,0:T(8,128)(2,1)S(1)} %slice.712), channel_id=1, source_target_pairs={{0,1},{1,0},{2,3},{3,2},{4,5},{5,4},{6,7},{7,6},{8,9},{9,8},{10,11... | collective-permute-start | bytes 2359304 | tf_op jit(solution)/shard_map/ppermute | solution.py:679
  352.5 9.1 %collective-permute-start.74 = (bf16[96,2048]{1,0:T(8,128)(2,1)S(1)}, bf16[96,2048]{1,0:T(8,128)(2,1)S(1)}, u32[]{:S(2)}, u32[]{:S(2)}) collective-permute-start(bf16[96,2048]{1,0:T(8,128)(2,1)S(1)} %dynamic-slice_convert_fusion), channel_id=1, source_target_pairs={{0,2},{2,0},{4,6},{6,4},{8,10},{10,8},{12,14},{14,12},{16,18},{18,... | collective-permute-start | bytes 1179656 | tf_op jit(solution)/shard_map/ppermute | solution.py:676
  354.8 15.2 %collective-permute-start.57 = (bf16[2,96,896]{2,1,0:T(8,128)(2,1)S(1)}, bf16[2,96,896]{2,1,0:T(8,128)(2,1)S(1)}, u32[]{:S(2)}, u32[]{:S(2)}) collective-permute-start(bf16[2,96,896]{2,1,0:T(8,128)(2,1)S(1)} %pad_maximum_fusion.16), channel_id=1, source_target_pairs={{0,4},{2,6},{8,0},{10,2},{16,8},{18,10},{24,16},{26,18},{28,24},{3... | collective-permute-start | bytes 1032200 | tf_op jit(solution)/shard_map/ppermute | solution.py:690
  358.8 11.2 %collective-permute-start.56 = (bf16[2,96,896]{2,1,0:T(8,128)(2,1)S(1)}, bf16[2,96,896]{2,1,0:T(8,128)(2,1)S(1)}, u32[]{:S(2)}, u32[]{:S(2)}) collective-permute-start(bf16[2,96,896]{2,1,0:T(8,128)(2,1)S(1)} %pad_maximum_fusion.15), channel_id=1, source_target_pairs={{0,8},{2,10},{8,16},{10,18},{16,24},{18,26},{24,28},{26,30},{28,20... | collective-permute-start | bytes 1032200 | tf_op jit(solution)/shard_map/ppermute | solution.py:690
  360.5 13.6 %collective-permute-start.62 = (bf16[2,96,768]{2,1,0:T(8,128)(2,1)S(1)}, bf16[2,96,768]{2,1,0:T(8,128)(2,1)S(1)}, u32[]{:S(2)}, u32[]{:S(2)}) collective-permute-start(bf16[2,96,768]{2,1,0:T(8,128)(2,1)S(1)} %pad_maximum_fusion.18), channel_id=1, source_target_pairs={{0,4},{2,6},{8,0},{10,2},{16,8},{18,10},{24,16},{26,18},{28,24},{3... | collective-permute-start | bytes 884744 | tf_op jit(solution)/shard_map/ppermute | solution.py:690
  361.6 14.5 %collective-permute-start.61 = (bf16[2,96,768]{2,1,0:T(8,128)(2,1)S(1)}, bf16[2,96,768]{2,1,0:T(8,128)(2,1)S(1)}, u32[]{:S(2)}, u32[]{:S(2)}) collective-permute-start(bf16[2,96,768]{2,1,0:T(8,128)(2,1)S(1)} %pad_maximum_fusion.17), channel_id=1, source_target_pairs={{0,8},{2,10},{8,16},{10,18},{16,24},{18,26},{24,28},{26,30},{28,20... | collective-permute-start | bytes 884744 | tf_op jit(solution)/shard_map/ppermute | solution.py:690
  370.2 14.3 %collective-permute-start.58 = (bf16[2,96,896]{2,1,0:T(8,128)(2,1)S(1)}, bf16[2,96,896]{2,1,0:T(8,128)(2,1)S(1)}, u32[]{:S(2)}, u32[]{:S(2)}) collective-permute-start(bf16[2,96,896]{2,1,0:T(8,128)(2,1)S(1)} %get-tuple-element.316), channel_id=1, source_target_pairs={{0,8},{2,10},{8,16},{10,18},{16,24},{18,26},{24,28},{26,30},{28,20... | collective-permute-start | bytes 1032200 | tf_op jit(solution)/shard_map/ppermute | solution.py:690
  371.3 13.2 %collective-permute-start.59 = (bf16[2,96,896]{2,1,0:T(8,128)(2,1)S(1)}, bf16[2,96,896]{2,1,0:T(8,128)(2,1)S(1)}, u32[]{:S(2)}, u32[]{:S(2)}) collective-permute-start(bf16[2,96,896]{2,1,0:T(8,128)(2,1)S(1)} %get-tuple-element.315), channel_id=1, source_target_pairs={{0,4},{2,6},{8,0},{10,2},{16,8},{18,10},{24,16},{26,18},{28,24},{3... | collective-permute-start | bytes 1032200 | tf_op jit(solution)/shard_map/ppermute | solution.py:690
  376.1 8.4 %collective-permute-start.55 = (f32[8,1536]{1,0:T(8,128)S(1)}, f32[8,1536]{1,0:T(8,128)S(1)}, u32[]{:S(2)}, u32[]{:S(2)}) collective-permute-start(f32[8,1536]{1,0:T(8,128)S(1)} %pad_maximum_fusion.20), channel_id=1, source_target_pairs={{0,4},{2,6},{4,0},{6,2},{8,12},{10,14},{12,8},{14,10},{16,20},{18,... | collective-permute-start | bytes 147464 | tf_op jit(solution)/shard_map/ppermute | solution.py:702
  377.9 11.9 %collective-permute-start.63 = (bf16[2,96,768]{2,1,0:T(8,128)(2,1)S(1)}, bf16[2,96,768]{2,1,0:T(8,128)(2,1)S(1)}, u32[]{:S(2)}, u32[]{:S(2)}) collective-permute-start(bf16[2,96,768]{2,1,0:T(8,128)(2,1)S(1)} %get-tuple-element.326), channel_id=1, source_target_pairs={{0,8},{2,10},{8,16},{10,18},{16,24},{18,26},{24,28},{26,30},{28,20... | collective-permute-start | bytes 884744 | tf_op jit(solution)/shard_map/ppermute | solution.py:690
  379.4 10.3 %collective-permute-start.64 = (bf16[2,96,768]{2,1,0:T(8,128)(2,1)S(1)}, bf16[2,96,768]{2,1,0:T(8,128)(2,1)S(1)}, u32[]{:S(2)}, u32[]{:S(2)}) collective-permute-start(bf16[2,96,768]{2,1,0:T(8,128)(2,1)S(1)} %get-tuple-element.325), channel_id=1, source_target_pairs={{0,4},{2,6},{8,0},{10,2},{16,8},{18,10},{24,16},{26,18},{28,24},{3... | collective-permute-start | bytes 884744 | tf_op jit(solution)/shard_map/ppermute | solution.py:690
  390.8 7.1 %collective-permute-start.65 = (f32[8,1536]{1,0:T(8,128)S(1)}, f32[8,1536]{1,0:T(8,128)S(1)}, u32[]{:S(2)}, u32[]{:S(2)}) collective-permute-start(f32[8,1536]{1,0:T(8,128)S(1)} %pad_maximum_fusion.22), channel_id=1, source_target_pairs={{0,16},{2,18},{4,20},{6,22},{8,24},{10,26},{12,28},{14,30},{16,0},... | collective-permute-start | bytes 147464 | tf_op jit(solution)/shard_map/ppermute | solution.py:702
  393.1 18.3 %collective-permute-start.68 = (bf16[2,96,896]{2,1,0:T(8,128)(2,1)}, bf16[2,96,896]{2,1,0:T(8,128)(2,1)S(1)}, u32[]{:S(2)}, u32[]{:S(2)}) collective-permute-start(bf16[2,96,896]{2,1,0:T(8,128)(2,1)} %get-tuple-element.314), channel_id=1, source_target_pairs={{0,8},{2,10},{8,16},{10,18},{16,24},{18,26},{24,28},{26,30},{28,20... | collective-permute-start | bytes 1032200 | tf_op jit(solution)/shard_map/ppermute | solution.py:690
  395.5 16.8 %collective-permute-start.69 = (bf16[2,96,896]{2,1,0:T(8,128)(2,1)}, bf16[2,96,896]{2,1,0:T(8,128)(2,1)}, u32[]{:S(2)}, u32[]{:S(2)}) collective-permute-start(bf16[2,96,896]{2,1,0:T(8,128)(2,1)} %get-tuple-element.313), channel_id=1, source_target_pairs={{0,4},{2,6},{8,0},{10,2},{16,8},{18,10},{24,16},{26,18},{28,24},{3... | collective-permute-start | bytes 1032200 | tf_op jit(solution)/shard_map/ppermute | solution.py:690
  395.8 13.2 %collective-permute-start.71 = (bf16[2,96,768]{2,1,0:T(8,128)(2,1)}, bf16[2,96,768]{2,1,0:T(8,128)(2,1)S(1)}, u32[]{:S(2)}, u32[]{:S(2)}) collective-permute-start(bf16[2,96,768]{2,1,0:T(8,128)(2,1)} %get-tuple-element.324), channel_id=1, source_target_pairs={{0,8},{2,10},{8,16},{10,18},{16,24},{18,26},{24,28},{26,30},{28,20... | collective-permute-start | bytes 884744 | tf_op jit(solution)/shard_map/ppermute | solution.py:690
  397.5 12.7 %collective-permute-start.72 = (bf16[2,96,768]{2,1,0:T(8,128)(2,1)}, bf16[2,96,768]{2,1,0:T(8,128)(2,1)}, u32[]{:S(2)}, u32[]{:S(2)}) collective-permute-start(bf16[2,96,768]{2,1,0:T(8,128)(2,1)} %get-tuple-element.323), channel_id=1, source_target_pairs={{0,4},{2,6},{8,0},{10,2},{16,8},{18,10},{24,16},{26,18},{28,24},{3... | collective-permute-start | bytes 884744 | tf_op jit(solution)/shard_map/ppermute | solution.py:690
  (59 other events, 601.1 us)

commit v5 on v4

--- a/solution.py
+++ b/solution.py
@@ -800,21 +800,17 @@
 
     attn_shard = at.by_core(first_part(keep)[None], at.swap_core(first_part(give))[None], 0)
     rows_near = at.swap_y(layer_in)
-    grad_near = at.swap_y(after(out_grad, rows_near))
     qkv_cols = 3 * heads * HEAD_DIM
     in_cols = qkv_cols + LANES
     attn_ring = Gathering(at, attn_shard)
-    early = attn_ring.advance()
+    keep, give = at.core_columns(after_all((w_gate, w_up, w_down), attn_shard))
+    keep, give = jnp.concatenate(keep, axis=1), jnp.concatenate(give, axis=1)
+    early = attn_ring.advance(keep, give)
+    ffn_shard = at.by_core(after(keep, *early)[None], at.swap_core(after(give, *early))[None], 0)
+    moved = attn_ring.advance(rows_near)
     attn_ring.store()
-    keep, give = at.core_columns(after_all((w_gate, w_up, w_down), *early))
-    ffn_shard = at.by_core(
-        jnp.concatenate(keep, axis=1)[None],
-        at.swap_core(jnp.concatenate(give, axis=1))[None],
-        0,
-    )
-    attn_ring.advance(rows_near)
-    attn_ring.store()
-    attn_ring.advance(grad_near)
+    grad_near = at.swap_y(after(out_grad, *moved))
+    attn_ring.advance(ffn_shard)
     attn_ring.store()
     ffn_ring = Gathering(at, after(ffn_shard, *attn_ring.came))
     attn_all = attn_ring.finish()
@@ -861,6 +857,7 @@
         ],
         axis=1,
     )
+    aux = after(aux, grad_near)
     mixed_other, inverse, expos, tops_other = attend(y_index, qkv, aux, 2, pairs, 1)
     moved = ffn_ring.advance(mixed_other)
 
@@ -870,6 +867,7 @@
         y_index, after(qkv, given), aux, 2, pairs, 0, (inverse, expos)
     )
     tops = jnp.concatenate([tops, tops_other], axis=0)
+    maxima = jnp.max(tops[:, :, :2], axis=(0, 3)).reshape(heads)
     mixed = jnp.concatenate([mixed_own, mixed_other], axis=0)
     mine = dot_nt(mixed_own, wo_all) + after(got, mixed_own).astype(F32)
     given = mine[rows_loc:].astype(BF16)
@@ -884,7 +882,7 @@
     near = at.swap_y(normed_own)
     ffn_ring.store(normed_own)
     moved = ffn_ring.advance(normed_own)
-    (near,) = after_all((near,), *moved)
+    (near,) = after_all((near,), maxima, *moved)
     normed_two = at.join(normed_own, near)
     ffn_ring.store(near)
     ffn_all = ffn_ring.finish()
@@ -900,9 +898,9 @@
     grad_up = (grad_hidden * gate_act).astype(BF16)
     grad_gu = jnp.concatenate([grad_gate, grad_up], axis=1)
 
-    part, got = at.meet_core(grad_gu, gu_all, dot_nt)
-    down_sum = Reduction(at, dot_tn(grad_rows, after(hidden, part)).astype(BF16))
-    mine = part + after(got, down_sum.blocks).astype(F32)
+    down_sum = Reduction(at, dot_tn(grad_rows, hidden).astype(BF16))
+    part, got = at.meet_core(after(grad_gu, *down_sum.sent), gu_all, dot_nt)
+    mine = part + after(got, part).astype(F32)
     given = mine[rows_loc:].astype(BF16)
     got = at.swap_y(given)
     gu_sum = Reduction(at, dot_tn(normed_two, after(grad_gu, given)).astype(BF16))
@@ -941,18 +939,17 @@
     d_in = jnp.concatenate([d_qkv, after(d_split, *low_sum.sent)], axis=1)
     bias_part = jnp.sum(d_split.astype(F32), axis=0)
     bias_part = bias_part[:heads] + bias_part[heads : 2 * heads]
-    given = dot_nt(d_in[pack:], w_in).astype(BF16)
+    high = jnp.concatenate(
+        [dot_tn(normed_one, d_in[:, middle:]), dot_tn(grad_attn, mixed)], axis=1
+    ).astype(BF16)
+    given = dot_nt(after(d_in, high)[pack:], w_in).astype(BF16)
     got = at.swap_core(given)
-    d_in_late, attn_late = after_all((d_in, grad_attn), given)
-    high = jnp.concatenate(
-        [dot_tn(normed_one, d_in_late[:, middle:]), dot_tn(attn_late, mixed)], axis=1
-    ).astype(BF16)
-    part = dot_nt(after(d_in, high)[:pack], w_in)
+    total_gu = gu_sum.finish(given)
+    high_sum = Reduction(at, high, total_gu)
+    part = dot_nt(after(d_in, *high_sum.sent)[:pack], w_in)
     mine = part + after(got, part).astype(F32)
     given = mine[rows_loc:].astype(BF16)
     got = at.swap_y(given)
-    total_gu = gu_sum.finish(given)
-    high_sum = Reduction(at, high, total_gu)
     layer_out = resid + (out_own[:rows_loc] + after(out_got, low).astype(F32))
     layer_out = layer_out.astype(BF16)
     moved = low_sum.advance(layer_out, *high_sum.sent)
@@ -967,7 +964,6 @@
     moved = low_sum.advance(norm1_part)
     moved = high_sum.advance(*moved)
 
-    maxima = jnp.max(tops[:, :, :2], axis=(0, 3)).reshape(heads)
     lone = jnp.pad(jnp.stack([bias_part, maxima]), ((0, 4), (0, width - heads)))
     sums = at.sum_plane(
         jnp.concatenate([jnp.stack([norm1_part, norm2_part]), lone], axis=0),

time: 424 us -> 416 us (0.981)
  waiting for transfers between devices: 131 us -> 112 us
  local copies, waits for them, and re-layouts: 36 us -> 49.8 us
  other arithmetic: 58.1 us -> 53.1 us
    ppermute x48, waiting for transfers between devices: 88.8 us -> 68.6 us  [ring(): return lax.ppermute(value, 'dp', pairs)]
    dynamic_update_slice x17, local copies, waits for them, and re-layouts: 12.7 us -> 18.5 us  [store(): self.whole = lax.dynamic_update_slice(self.whole, part[None], start)]
    unnamed x103 -> x111, local copies, waits for them, and re-layouts: 6.92 us -> 11.8 us
  transfers between devices with their start and end apart: 76 -> 76, of which waited for: 33 -> 26; matrix products, arithmetic and copies ran while one was open for 33% -> 34% of each run, Pallas kernels for 10% -> 10%
where the time goes in v5:
time: 416 us; the launch traced here: 411 us
  waiting for transfers between devices  112 us (27%)
  matrix products  80.8 us (19%)
  starting transfers between devices  70.7 us (17%)
  other arithmetic  53.1 us (13%)
  local copies, waits for them, and re-layouts  49.8 us (12%)
  Pallas kernels  42.2 us (10%)
    ppermute x48, waiting for transfers between devices, ring(): return lax.ppermute(value, 'dp', pairs)  68.6 us
    ppermute x48, starting transfers between devices, ring(): return lax.ppermute(value, 'dp', pairs)  51.8 us
    ppermute x9, waiting for transfers between devices, swap_y(): return lax.ppermute(value, 'tensor', [(0, 1), (1, 0)])  31.5 us
    dot_general x4, matrix products, dot_nn(): lax.dot_general(left, right, (((1,), (0,)), ((), ())), preferred_element_...  29.8 us
    dot_general x9, matrix products, dot_nt(): lax.dot_general(left, right, (((1,), (1,)), ((), ())), preferred_element_...  29.2 us
    pallas_call x1, Pallas kernels, attend_back(): pl.pallas_call(partial(attend_back_kernel, pairs), grid_spec=grid_spec, o...  21.8 us
    dot_general x5, matrix products, dot_tn(): lax.dot_general(left, right, (((0,), (0,)), ((), ())), preferred_element_...  21.7 us
    dynamic_update_slice x17, local copies, waits for them, and re-layouts, store(): self.whole = lax.dynamic_update_slice(self.whole, part[None], start)  18.5 us
  transfers between devices with their start and end apart: 76, of which 26 were waited for; matrix products, arithmetic and copies ran while one was open for 34% of the time, Pallas kernels for 10%

profile of v5, /device:TPU:0, one launch (start us, length us, event | category | flops | bytes accessed | tf_op | source)
XLA Modules:
  0.0 411.2 jit_solution(8487566307448819229)
XLA Ops:
  6.7 2.6 collective-permute-start
  10.5 1.6 collective-permute-start.3
  13.6 2.8 broadcast_in_dim.97
  17.4 10.2 %collective-permute-done = bf16[256,1536]{1,0:T(8,128)(2,1)S(1)} collective-permute-done((bf16[256,1536]{1,0:T(8,128)(2,1)}, bf16[256,1536]{1,0:T(8,128)(2,1)S(1)}, u32[]{:S(2)}, u32[]{:S(2)}) %collective-permute-start) | collective-permute-done | bytes 786464 | tf_op jit(solution)/shard_map/ppermute | solution.py:679
  29.0 1.9 collective-permute-start.5
  33.0 2.0 bitcast_dynamic-update-slice_fusion.12
  34.9 2.0 bitcast_dynamic-update-slice_fusion.11
  36.9 2.4 maximum_select_fusion
  39.3 6.8 %collective-permute-done.5 = bf16[2,96,1664]{2,1,0:T(8,128)(2,1)} collective-permute-done((bf16[2,96,1664]{2,1,0:T(8,128)(2,1)}, bf16[2,96,1664]{2,1,0:T(8,128)(2,1)}, u32[]{:S(2)}, u32[]{:S(2)}) %collective-permute-start.5) | collective-permute-done | bytes 639008 | tf_op jit(solution)/shard_map/ppermute | solution.py:690
  51.2 2.0 bitcast_dynamic-update-slice_fusion.10
  53.1 2.0 bitcast_dynamic-update-slice_fusion.9
  55.1 8.3 %collective-permute-done.7 = bf16[2,96,1664]{2,1,0:T(8,128)(2,1)S(1)} collective-permute-done((bf16[2,96,1664]{2,1,0:T(8,128)(2,1)}, bf16[2,96,1664]{2,1,0:T(8,128)(2,1)S(1)}, u32[]{:S(2)}, u32[]{:S(2)}) %collective-permute-start.7) | collective-permute-done | bytes 639008 | tf_op jit(solution)/shard_map/ppermute | solution.py:690
  64.7 1.6 collective-permute-start.10
  68.7 1.9 fusion
  79.1 4.4 %fusion.2 = bf16[1024,1536]{1,0:T(8,128)(2,1)S(1)} fusion(f32[1536]{0:T(1024)S(1)} %get-tuple-element.283, f32[1024]{0:T(1024)S(1)} %add_rsqrt_fusion, bf16[512,1536]{1,0:T(8,128)(2,1)} %collective-permute-done.1, bf16[256,1536]{1,0:T(8,128)(2,1)S(1)} %collective-permute-done, bf16[256,1536]{1,0:T(8,128)(2,1)S(1)} %copy-done), kind=kLoop, calls=%fused_computation.5 | loop fusion | flops 14155776 | bytes 6301696 | tf_op jit(solution)/shard_map/convert_element_type | solution.py:831
  83.5 1.7 copy-done.3
  87.4 8.6 %convolution_convert_fusion.1.qkv_ref = bf16[1024,1152]{1,0:T(8,128)(2,1)} fusion(bf16[1024,1536]{1,0:T(8,128)(2,1)} %copy-done.3, bf16[1536,1664]{1,0:T(8,128)(2,1)} %bitcast.17), kind=kOutput, calls=%fused_computation.34 | convolution fusion | flops 3625058304 | bytes 9043968 | tf_op jit(solution)/shard_map/dot_general | solution.py:320
  96.0 9.1 %attend.2 = (bf16[512,384]{1,0:T(8,128)(2,1)}, f32[1024,384]{1,0:T(8,128)}, bf16[2,3,2,256,768]{4,3,2,1,0:T(8,128)(2,1)}, f32[1,3,8,128]{3,2,1,0:T(8,128)}) custom-call(s32[1]{0:T(128)} %bitcast.y_ref, bf16[1024,1152]{1,0:T(8,128)(2,1)} %convolution_convert_fusion.1.qkv_ref, f32[3,8,1024]{2,1,0:T(8,128)} %maximum_maximum_fusion.aux_ref), custom_call_target="tpu_custom_call" | custom-call | flops 603979776 | bytes 10000000 | tf_op jit(solution)/shard_map/attend/pallas_call | solution.py:396
  105.1 3.6 convolution_convert_fusion.5
  108.9 1.6 copy-done.35
  112.7 9.0 %attend.3 = (bf16[512,384]{1,0:T(8,128)(2,1)}, f32[1024,384]{1,0:T(8,128)}, bf16[2,3,2,256,768]{4,3,2,1,0:T(8,128)(2,1)}, f32[1,3,8,128]{3,2,1,0:T(8,128)}) custom-call(s32[1]{0:T(128)} %bitcast.y_ref, bf16[1024,1152]{1,0:T(8,128)(2,1)} %convolution_convert_fusion.1.qkv_ref, ...), custom_call_target="tpu_custom_call", output_to_operand_aliasing={{1}: (3, {}), {2}: (4, {})} | custom-call | flops 603979776 | bytes 10000000 | tf_op jit(solution)/shard_map/attend/pallas_call | solution.py:396
  121.7 2.5 fusion.51
  125.8 1.7 copy-done.37
  127.5 1.9 convert_add_fusion.3
  131.0 8.1 %collective-permute-done.18 = bf16[2,96,3072]{2,1,0:T(8,128)(2,1)} collective-permute-done((bf16[2,96,3072]{2,1,0:T(8,128)(2,1)}, bf16[2,96,3072]{2,1,0:T(8,128)(2,1)}, u32[]{:S(2)}, u32[]{:S(2)}) %collective-permute-start.18) | collective-permute-done | bytes 1179680 | tf_op jit(solution)/shard_map/ppermute | solution.py:690
  149.0 2.2 multiply_reduce_fusion.2
  155.8 12.3 %collective-permute-done.21 = bf16[2,96,3072]{2,1,0:T(8,128)(2,1)S(1)} collective-permute-done((bf16[2,96,3072]{2,1,0:T(8,128)(2,1)}, bf16[2,96,3072]{2,1,0:T(8,128)(2,1)S(1)}, u32[]{:S(2)}, u32[]{:S(2)}) %collective-permute-start.21) | collective-permute-done | bytes 1179680 | tf_op jit(solution)/shard_map/ppermute | solution.py:690
  169.2 2.0 collective-permute-start.25
  171.6 10.4 %collective-permute-done.24 = bf16[1,96,3072]{2,1,0:T(8,128)(2,1)S(1)} collective-permute-done((bf16[1,96,3072]{2,1,0:T(8,128)(2,1)S(1)}, bf16[1,96,3072]{2,1,0:T(8,128)(2,1)S(1)}, u32[]{:S(2)}, u32[]{:S(2)}) %collective-permute-start.24) | collective-permute-done | bytes 589856 | tf_op jit(solution)/shard_map/ppermute | solution.py:690
  184.2 8.8 %fusion.7 = f32[1024,2048]{1,0:T(8,128)} fusion(bf16[1536,3072]{1,0:T(8,128)(2,1)S(1)} %bitcast.243, bf16[512,1536]{1,0:T(8,128)(2,1)S(1)} %collective-permute-done.23, bf16[256,1536]{1,0:T(8,128)(2,1)S(1)} %collective-permute-done.20, bf16[256,1536]{1,0:T(8,128)(2,1)S(1)} %multiply_convert_fusion.3), kind=kOutput, calls=%fused_computation.10 | convolution fusion | flops 6451888128 | bytes 17825792 | tf_op jit(solution)/shard_map/dot_general | solution.py:320
  193.0 7.5 %multiply_convert_fusion.1 = (bf16[1024,1024]{1,0:T(8,128)(2,1)S(1)}, bf16[1024,1024]{1,0:T(8,128)(2,1)S(1)}, bf16[1024,1024]{1,0:T(8,128)(2,1)S(1)}) fusion(f32[1024,2048]{1,0:T(8,128)} %fusion.7, bf16[1024,1536]{1,0:T(8,128)(2,1)S(1)} %copy-done.38, bf16[1536,3072]{1,0:T(8,128)(2,1)S(1)} %bitcast.244), kind=kOutput, calls=%fused_computation.30 | convolution fusion | flops 3236954112 | bytes 20971520 | tf_op jit(solution)/shard_map/dot_general | solution.py:320
  200.5 3.7 convolution_convert_fusion.2
  205.7 3.5 fusion.18
  209.8 1.6 collective-permute-start.28
  211.5 3.5 fusion.3
  217.9 8.6 %convolution_convert_fusion = bf16[1536,2048]{1,0:T(8,128)(2,1)S(1)} fusion(bf16[1024,2048]{1,0:T(8,128)(2,1)S(1)} %pad_maximum_fusion, bf16[512,1536]{1,0:T(8,128)(2,1)} %copy-done.47, bf16[256,1536]{1,0:T(8,128)(2,1)} %copy-done.26, bf16[256,1536]{1,0:T(8,128)(2,1)S(1)} %copy-done.19), kind=kOutput, calls=%fused_computation.2 | convolution fusion | flops 6455033856 | bytes 13631488 | tf_op jit(solution)/shard_map/dot_general | solution.py:324
  231.1 4.8 %collective-permute-done.34 = bf16[256,1536]{1,0:T(8,128)(2,1)S(1)} collective-permute-done((bf16[256,1536]{1,0:T(8,128)(2,1)}, bf16[256,1536]{1,0:T(8,128)(2,1)S(1)}, u32[]{:S(2)}, u32[]{:S(2)}) %collective-permute-start.34) | collective-permute-done | bytes 786464 | tf_op jit(solution)/shard_map/ppermute | solution.py:679
  236.5 1.7 fusion.109
  242.6 3.0 convolution_convert_fusion.4
  245.5 2.1 collective-permute-done.31
  248.7 3.5 fusion.21
  252.2 10.7 %collective-permute-done.37 = bf16[2,96,2048]{2,1,0:T(8,128)(2,1)S(1)} collective-permute-done((bf16[2,96,2048]{2,1,0:T(8,128)(2,1)S(1)}, bf16[2,96,2048]{2,1,0:T(8,128)(2,1)S(1)}, u32[]{:S(2)}, u32[]{:S(2)}) %collective-permute-start.37) | collective-permute-done | bytes 786464 | tf_op jit(solution)/shard_map/ppermute | solution.py:690
  272.4 4.9 %convolution_convert_fusion.8.do_ref = bf16[1024,384]{1,0:T(8,128)(2,1)} fusion(bf16[1536,1664]{1,0:T(8,128)(2,1)} %bitcast.17, bf16[512,1536]{1,0:T(8,128)(2,1)} %collective-permute-done.38, bf16[256,1536]{1,0:T(8,128)(2,1)} %copy-done.24, bf16[256,1536]{1,0:T(8,128)(2,1)} %copy-done.12), kind=kOutput, calls=%fused_computation.105 | convolution fusion | flops 1217789952 | bytes 5111808 | tf_op jit(solution)/shard_map/dot_general | solution.py:320
  277.3 1.9 convert_add_fusion.1
  279.2 1.6 copy-done.5
  281.8 2.3 fusion.59
  286.2 21.8 %attend_back.1 = (bf16[1024,1152]{1,0:T(8,128)(2,1)}, bf16[1024,128]{1,0:T(8,128)(2,1)}) custom-call(s32[1]{0:T(128)} %bitcast.y_ref, bf16[1024,1152]{1,0:T(8,128)(2,1)} %convolution_convert_fusion.1.qkv_ref, bf16[1024,384]{1,0:T(8,128)(2,1)} %convolution_convert_fusion.8.do_ref, f32[1024,384]{1,0:T(8,128)} %get-tuple-element.186.inv_ref, ...), custom_call_target="tpu_custom_call" | custom-call | flops 3623878656 | bytes 20000000 | tf_op jit(solution)/shard_map/attend_back/pallas_call | solution.py:534
  308.0 2.0 constant_dynamic-update-slice_fusion.4
  310.0 2.6 fusion.42
  313.1 1.9 collective-permute-start.48
  315.6 3.7 convolution_convert_fusion.3
  319.7 3.8 convolution_convert_fusion.6
  325.0 1.8 convolution_convert_fusion.7
  327.5 4.3 %fusion.15 = bf16[512,1536]{1,0:T(8,128)(2,1)S(1)} fusion(bf16[1536,1664]{1,0:T(8,128)(2,1)} %bitcast.17, bf16[1024,1280]{1,0:T(8,128)(2,1)S(1)} %constant_dynamic-update-slice_fusion.3), kind=kOutput, calls=%fused_computation.49 | convolution fusion | flops 2014052352 | bytes 6815744 | tf_op jit(solution)/shard_map/dot_general | solution.py:316
  332.0 1.7 collective-permute-start.54
  338.5 1.6 collective-permute-start.52
  341.8 4.3 %fusion.11 = f32[512,1536]{1,0:T(8,128)S(1)} fusion(bf16[1536,1664]{1,0:T(8,128)(2,1)} %bitcast.17, bf16[1024,1280]{1,0:T(8,128)(2,1)S(1)} %constant_dynamic-update-slice_fusion.3), kind=kOutput, calls=%fused_computation.38 | convolution fusion | flops 2013265920 | bytes 8388608 | tf_op jit(solution)/shard_map/dot_general | solution.py:316
  353.6 13.9 %collective-permute-done.50 = bf16[256,1536]{1,0:T(8,128)(2,1)S(1)} collective-permute-done((bf16[256,1536]{1,0:T(8,128)(2,1)S(1)}, bf16[256,1536]{1,0:T(8,128)(2,1)S(1)}, u32[]{:S(2)}, u32[]{:S(2)}) %collective-permute-start.50) | collective-permute-done | bytes 786464 | tf_op jit(solution)/shard_map/ppermute | solution.py:679
  374.2 6.2 %collective-permute-done.55 = f32[8,1536]{1,0:T(8,128)S(1)} collective-permute-done((f32[8,1536]{1,0:T(8,128)S(1)}, f32[8,1536]{1,0:T(8,128)S(1)}, u32[]{:S(2)}, u32[]{:S(2)}) %collective-permute-start.55) | collective-permute-done | bytes 49184 | tf_op jit(solution)/shard_map/ppermute | solution.py:702
  381.5 4.1 collective-permute-done.60
  389.6 2.2 collective-permute-start.68
  391.8 2.0 collective-permute-start.71
  398.8 1.6 collective-permute-done.67
  408.3 2.4 assemble.1
  (391 shorter events, 125.6 us)
Async XLA Ops:
  6.7 20.9 %collective-permute-start = (bf16[256,1536]{1,0:T(8,128)(2,1)}, bf16[256,1536]{1,0:T(8,128)(2,1)S(1)}, u32[]{:S(2)}, u32[]{:S(2)}) collective-permute-start(bf16[256,1536]{1,0:T(8,128)(2,1)} %param.15), channel_id=1, source_target_pairs={{0,1},{1,0},{2,3},{3,2},{4,5},{5,4},{6,7},{7,6},{8,9},{9,8},{10,11... | collective-permute-start | bytes 2359304 | tf_op jit(solution)/shard_map/ppermute | solution.py:679
  10.5 18.5 %collective-permute-start.3 = (bf16[2,96,1664]{2,1,0:T(8,128)(2,1)S(1)}, bf16[2,96,1664]{2,1,0:T(8,128)(2,1)}, u32[]{:S(2)}, u32[]{:S(2)}) collective-permute-start(bf16[2,96,1664]{2,1,0:T(8,128)(2,1)S(1)} %maximum_select_fusion.5), channel_id=1, source_target_pairs={{0,8},{2,10},{8,16},{10,18},{16,24},{18,26},{24,28},{26,30},{28,20... | collective-permute-start | bytes 1916936 | tf_op jit(solution)/shard_map/ppermute | solution.py:690
  12.1 16.8 %collective-permute-start.4 = (bf16[2,96,1664]{2,1,0:T(8,128)(2,1)S(1)}, bf16[2,96,1664]{2,1,0:T(8,128)(2,1)}, u32[]{:S(2)}, u32[]{:S(2)}) collective-permute-start(bf16[2,96,1664]{2,1,0:T(8,128)(2,1)S(1)} %maximum_select_fusion.5), channel_id=1, source_target_pairs={{0,4},{2,6},{8,0},{10,2},{16,8},{18,10},{24,16},{26,18},{28,24},{3... | collective-permute-start | bytes 1916936 | tf_op jit(solution)/shard_map/ppermute | solution.py:690
  29.0 39.7 %collective-permute-start.1 = (bf16[512,1536]{1,0:T(8,128)(2,1)}, bf16[512,1536]{1,0:T(8,128)(2,1)}, u32[]{:S(2)}, u32[]{:S(2)}) collective-permute-start(bf16[512,1536]{1,0:T(8,128)(2,1)} %pad_maximum_fusion.4), channel_id=1, source_target_pairs={{0,2},{2,0},{4,6},{6,4},{8,10},{10,8},{12,14},{14,12},{16,18},{18,... | collective-permute-start | bytes 4718600 | tf_op jit(solution)/shard_map/ppermute | solution.py:676
  29.0 17.1 %collective-permute-start.5 = (bf16[2,96,1664]{2,1,0:T(8,128)(2,1)}, bf16[2,96,1664]{2,1,0:T(8,128)(2,1)}, u32[]{:S(2)}, u32[]{:S(2)}) collective-permute-start(bf16[2,96,1664]{2,1,0:T(8,128)(2,1)} %collective-permute-done.3), channel_id=1, source_target_pairs={{0,8},{2,10},{8,16},{10,18},{16,24},{18,26},{24,28},{26,30},{28,20... | collective-permute-start | bytes 1916936 | tf_op jit(solution)/shard_map/ppermute | solution.py:690
  30.8 16.8 %collective-permute-start.6 = (bf16[2,96,1664]{2,1,0:T(8,128)(2,1)}, bf16[2,96,1664]{2,1,0:T(8,128)(2,1)}, u32[]{:S(2)}, u32[]{:S(2)}) collective-permute-start(bf16[2,96,1664]{2,1,0:T(8,128)(2,1)} %collective-permute-done.4), channel_id=1, source_target_pairs={{0,4},{2,6},{8,0},{10,2},{16,8},{18,10},{24,16},{26,18},{28,24},{3... | collective-permute-start | bytes 1916936 | tf_op jit(solution)/shard_map/ppermute | solution.py:690
  47.6 15.8 %collective-permute-start.7 = (bf16[2,96,1664]{2,1,0:T(8,128)(2,1)}, bf16[2,96,1664]{2,1,0:T(8,128)(2,1)S(1)}, u32[]{:S(2)}, u32[]{:S(2)}) collective-permute-start(bf16[2,96,1664]{2,1,0:T(8,128)(2,1)} %collective-permute-done.5), channel_id=1, source_target_pairs={{0,8},{2,10},{8,16},{10,18},{16,24},{18,26},{24,28},{26,30},{28,20... | collective-permute-start | bytes 1916936 | tf_op jit(solution)/shard_map/ppermute | solution.py:690
  49.2 15.5 %collective-permute-start.8 = (bf16[2,96,1664]{2,1,0:T(8,128)(2,1)}, bf16[2,96,1664]{2,1,0:T(8,128)(2,1)S(1)}, u32[]{:S(2)}, u32[]{:S(2)}) collective-permute-start(bf16[2,96,1664]{2,1,0:T(8,128)(2,1)} %collective-permute-done.6), channel_id=1, source_target_pairs={{0,4},{2,6},{8,0},{10,2},{16,8},{18,10},{24,16},{26,18},{28,24},{3... | collective-permute-start | bytes 1916936 | tf_op jit(solution)/shard_map/ppermute | solution.py:690
  49.6 20.9 %collective-permute-start.13 = (bf16[256,1536]{1,0:T(8,128)(2,1)S(1)}, bf16[256,1536]{1,0:T(8,128)(2,1)S(1)}, u32[]{:S(2)}, u32[]{:S(2)}) collective-permute-start(bf16[256,1536]{1,0:T(8,128)(2,1)S(1)} %copy-done.7), channel_id=1, source_target_pairs={{0,1},{1,0},{2,3},{3,2},{4,5},{5,4},{6,7},{7,6},{8,9},{9,8},{10,11... | collective-permute-start | bytes 2359304 | tf_op jit(solution)/shard_map/ppermute | solution.py:679
  64.7 7.7 %collective-permute-start.10 = (bf16[1,96,1664]{2,1,0:T(8,128)(2,1)S(1)}, bf16[1,96,1664]{2,1,0:T(8,128)(2,1)S(1)}, u32[]{:S(2)}, u32[]{:S(2)}) collective-permute-start(bf16[1,96,1664]{2,1,0:T(8,128)(2,1)S(1)} %slice.410), channel_id=1, source_target_pairs={{0,8},{2,10},{8,16},{10,18},{16,24},{18,26},{24,28},{26,30},{28,20... | collective-permute-start | bytes 958472 | tf_op jit(solution)/shard_map/ppermute | solution.py:690
  66.4 7.4 %collective-permute-start.11 = (bf16[1,96,1664]{2,1,0:T(8,128)(2,1)S(1)}, bf16[1,96,1664]{2,1,0:T(8,128)(2,1)S(1)}, u32[]{:S(2)}, u32[]{:S(2)}) collective-permute-start(bf16[1,96,1664]{2,1,0:T(8,128)(2,1)S(1)} %slice.411), channel_id=1, source_target_pairs={{0,4},{2,6},{8,0},{10,2},{16,8},{18,10},{24,16},{26,18},{28,24},{3... | collective-permute-start | bytes 958472 | tf_op jit(solution)/shard_map/ppermute | solution.py:690
  72.0 52.2 %collective-permute-start.26 = (bf16[512,1536]{1,0:T(8,128)(2,1)}, bf16[512,1536]{1,0:T(8,128)(2,1)}, u32[]{:S(2)}, u32[]{:S(2)}) collective-permute-start(bf16[512,1536]{1,0:T(8,128)(2,1)} %pad_maximum_fusion.6), channel_id=1, source_target_pairs={{0,2},{2,0},{4,6},{6,4},{8,10},{10,8},{12,14},{14,12},{16,18},{18,... | collective-permute-start | bytes 4718600 | tf_op jit(solution)/shard_map/ppermute | solution.py:676
  73.8 31.3 %collective-permute-start.14 = (bf16[2,96,3072]{2,1,0:T(8,128)(2,1)}, bf16[2,96,3072]{2,1,0:T(8,128)(2,1)}, u32[]{:S(2)}, u32[]{:S(2)}) collective-permute-start(bf16[2,96,3072]{2,1,0:T(8,128)(2,1)} %maximum_select_fusion), channel_id=1, source_target_pairs={{0,8},{2,10},{8,16},{10,18},{16,24},{18,26},{24,28},{26,30},{28,20... | collective-permute-start | bytes 3538952 | tf_op jit(solution)/shard_map/ppermute | solution.py:690
  75.3 29.8 %collective-permute-start.15 = (bf16[2,96,3072]{2,1,0:T(8,128)(2,1)}, bf16[2,96,3072]{2,1,0:T(8,128)(2,1)}, u32[]{:S(2)}, u32[]{:S(2)}) collective-permute-start(bf16[2,96,3072]{2,1,0:T(8,128)(2,1)} %maximum_select_fusion), channel_id=1, source_target_pairs={{0,4},{2,6},{8,0},{10,2},{16,8},{18,10},{24,16},{26,18},{28,24},{3... | collective-permute-start | bytes 3538952 | tf_op jit(solution)/shard_map/ppermute | solution.py:690
  108.7 18.8 %collective-permute-start.16 = (bf16[512,1536]{1,0:T(8,128)(2,1)}, bf16[512,1536]{1,0:T(8,128)(2,1)}, u32[]{:S(2)}, u32[]{:S(2)}) collective-permute-start(bf16[512,1536]{1,0:T(8,128)(2,1)} %convolution_convert_fusion.5), channel_id=1, source_target_pairs={{0,2},{2,0},{4,6},{6,4},{8,10},{10,8},{12,14},{14,12},{16,18},{18,... | collective-permute-start | bytes 4718600 | tf_op jit(solution)/shard_map/ppermute | solution.py:676
  110.5 28.7 %collective-permute-start.18 = (bf16[2,96,3072]{2,1,0:T(8,128)(2,1)}, bf16[2,96,3072]{2,1,0:T(8,128)(2,1)}, u32[]{:S(2)}, u32[]{:S(2)}) collective-permute-start(bf16[2,96,3072]{2,1,0:T(8,128)(2,1)} %collective-permute-done.14), channel_id=1, source_target_pairs={{0,8},{2,10},{8,16},{10,18},{16,24},{18,26},{24,28},{26,30},{28,20... | collective-permute-start | bytes 3538952 | tf_op jit(solution)/shard_map/ppermute | solution.py:690
  112.0 28.6 %collective-permute-start.19 = (bf16[2,96,3072]{2,1,0:T(8,128)(2,1)}, bf16[2,96,3072]{2,1,0:T(8,128)(2,1)}, u32[]{:S(2)}, u32[]{:S(2)}) collective-permute-start(bf16[2,96,3072]{2,1,0:T(8,128)(2,1)} %collective-permute-done.15), channel_id=1, source_target_pairs={{0,4},{2,6},{8,0},{10,2},{16,8},{18,10},{24,16},{26,18},{28,24},{3... | collective-permute-start | bytes 3538952 | tf_op jit(solution)/shard_map/ppermute | solution.py:690
  129.5 19.6 %collective-permute-start.17 = (bf16[256,1536]{1,0:T(8,128)(2,1)S(1)}, bf16[256,1536]{1,0:T(8,128)(2,1)}, u32[]{:S(2)}, u32[]{:S(2)}) collective-permute-start(bf16[256,1536]{1,0:T(8,128)(2,1)S(1)} %slice.707), channel_id=1, source_target_pairs={{0,1},{1,0},{2,3},{3,2},{4,5},{5,4},{6,7},{7,6},{8,9},{9,8},{10,11... | collective-permute-start | bytes 2359304 | tf_op jit(solution)/shard_map/ppermute | solution.py:679
  140.6 27.5 %collective-permute-start.21 = (bf16[2,96,3072]{2,1,0:T(8,128)(2,1)}, bf16[2,96,3072]{2,1,0:T(8,128)(2,1)S(1)}, u32[]{:S(2)}, u32[]{:S(2)}) collective-permute-start(bf16[2,96,3072]{2,1,0:T(8,128)(2,1)} %collective-permute-done.18), channel_id=1, source_target_pairs={{0,8},{2,10},{8,16},{10,18},{16,24},{18,26},{24,28},{26,30},{28,20... | collective-permute-start | bytes 3538952 | tf_op jit(solution)/shard_map/ppermute | solution.py:690
  141.3 27.2 %collective-permute-start.22 = (bf16[2,96,3072]{2,1,0:T(8,128)(2,1)}, bf16[2,96,3072]{2,1,0:T(8,128)(2,1)S(1)}, u32[]{:S(2)}, u32[]{:S(2)}) collective-permute-start(bf16[2,96,3072]{2,1,0:T(8,128)(2,1)} %collective-permute-done.19), channel_id=1, source_target_pairs={{0,4},{2,6},{8,0},{10,2},{16,8},{18,10},{24,16},{26,18},{28,24},{3... | collective-permute-start | bytes 3538952 | tf_op jit(solution)/shard_map/ppermute | solution.py:690
  151.5 19.7 %collective-permute-start.20 = (bf16[256,1536]{1,0:T(8,128)(2,1)S(1)}, bf16[256,1536]{1,0:T(8,128)(2,1)S(1)}, u32[]{:S(2)}, u32[]{:S(2)}) collective-permute-start(bf16[256,1536]{1,0:T(8,128)(2,1)S(1)} %multiply_convert_fusion.3), channel_id=1, source_target_pairs={{0,1},{1,0},{2,3},{3,2},{4,5},{5,4},{6,7},{7,6},{8,9},{9,8},{10,11... | collective-permute-start | bytes 2359304 | tf_op jit(solution)/shard_map/ppermute | solution.py:679
  168.5 13.5 %collective-permute-start.24 = (bf16[1,96,3072]{2,1,0:T(8,128)(2,1)S(1)}, bf16[1,96,3072]{2,1,0:T(8,128)(2,1)S(1)}, u32[]{:S(2)}, u32[]{:S(2)}) collective-permute-start(bf16[1,96,3072]{2,1,0:T(8,128)(2,1)S(1)} %slice.424), channel_id=1, source_target_pairs={{0,8},{2,10},{8,16},{10,18},{16,24},{18,26},{24,28},{26,30},{28,20... | collective-permute-start | bytes 1769480 | tf_op jit(solution)/shard_map/ppermute | solution.py:690
  169.2 13.7 %collective-permute-start.25 = (bf16[1,96,3072]{2,1,0:T(8,128)(2,1)S(1)}, bf16[1,96,3072]{2,1,0:T(8,128)(2,1)S(1)}, u32[]{:S(2)}, u32[]{:S(2)}) collective-permute-start(bf16[1,96,3072]{2,1,0:T(8,128)(2,1)S(1)} %slice.425), channel_id=1, source_target_pairs={{0,4},{2,6},{8,0},{10,2},{16,8},{18,10},{24,16},{26,18},{28,24},{3... | collective-permute-start | bytes 1769480 | tf_op jit(solution)/shard_map/ppermute | solution.py:690
  171.2 11.7 %collective-permute-start.23 = (bf16[512,1536]{1,0:T(8,128)(2,1)S(1)}, bf16[512,1536]{1,0:T(8,128)(2,1)S(1)}, u32[]{:S(2)}, u32[]{:S(2)}) collective-permute-start(bf16[512,1536]{1,0:T(8,128)(2,1)S(1)} %pad_maximum_fusion.5), channel_id=1, source_target_pairs={{0,2},{2,0},{4,6},{6,4},{8,10},{10,8},{12,14},{14,12},{16,18},{18,... | collective-permute-start | bytes 4718600 | tf_op jit(solution)/shard_map/ppermute | solution.py:676
  209.2 17.2 %collective-permute-start.27 = (bf16[1,96,1024]{2,1,0:T(8,128)(2,1)}, bf16[1,96,1024]{2,1,0:T(8,128)(2,1)S(1)}, u32[]{:S(2)}, u32[]{:S(2)}) collective-permute-start(bf16[1,96,1024]{2,1,0:T(8,128)(2,1)} %get-tuple-element.312), channel_id=1, source_target_pairs={{0,8},{2,10},{8,16},{10,18},{16,24},{18,26},{24,28},{26,30},{28,20... | collective-permute-start | bytes 589832 | tf_op jit(solution)/shard_map/ppermute | solution.py:690
  209.8 16.6 %collective-permute-start.28 = (bf16[1,96,1024]{2,1,0:T(8,128)(2,1)S(1)}, bf16[1,96,1024]{2,1,0:T(8,128)(2,1)S(1)}, u32[]{:S(2)}, u32[]{:S(2)}) collective-permute-start(bf16[1,96,1024]{2,1,0:T(8,128)(2,1)S(1)} %get-tuple-element.313), channel_id=1, source_target_pairs={{0,4},{2,6},{8,0},{10,2},{16,8},{18,10},{24,16},{26,18},{28,24},{3... | collective-permute-start | bytes 589832 | tf_op jit(solution)/shard_map/ppermute | solution.py:690
  216.4 19.5 %collective-permute-start.34 = (bf16[256,1536]{1,0:T(8,128)(2,1)}, bf16[256,1536]{1,0:T(8,128)(2,1)S(1)}, u32[]{:S(2)}, u32[]{:S(2)}) collective-permute-start(bf16[256,1536]{1,0:T(8,128)(2,1)} %slice.706), channel_id=1, source_target_pairs={{0,1},{1,0},{2,3},{3,2},{4,5},{5,4},{6,7},{7,6},{8,9},{9,8},{10,11... | collective-permute-start | bytes 2359304 | tf_op jit(solution)/shard_map/ppermute | solution.py:679
  226.6 12.0 %collective-permute-start.32 = (bf16[1,96,2048]{2,1,0:T(8,128)(2,1)S(1)}, bf16[1,96,2048]{2,1,0:T(8,128)(2,1)S(1)}, u32[]{:S(2)}, u32[]{:S(2)}) collective-permute-start(bf16[1,96,2048]{2,1,0:T(8,128)(2,1)S(1)} %get-tuple-element.302), channel_id=1, source_target_pairs={{0,8},{2,10},{8,16},{10,18},{16,24},{18,26},{24,28},{26,30},{28,20... | collective-permute-start | bytes 1179656 | tf_op jit(solution)/shard_map/ppermute | solution.py:690
  227.2 12.0 %collective-permute-start.33 = (bf16[1,96,2048]{2,1,0:T(8,128)(2,1)S(1)}, bf16[1,96,2048]{2,1,0:T(8,128)(2,1)S(1)}, u32[]{:S(2)}, u32[]{:S(2)}) collective-permute-start(bf16[1,96,2048]{2,1,0:T(8,128)(2,1)S(1)} %get-tuple-element.303), channel_id=1, source_target_pairs={{0,4},{2,6},{8,0},{10,2},{16,8},{18,10},{24,16},{26,18},{28,24},{3... | collective-permute-start | bytes 1179656 | tf_op jit(solution)/shard_map/ppermute | solution.py:690
  228.9 18.8 %collective-permute-start.31 = (bf16[2,96,1024]{2,1,0:T(8,128)(2,1)S(1)}, bf16[2,96,1024]{2,1,0:T(8,128)(2,1)S(1)}, u32[]{:S(2)}, u32[]{:S(2)}) collective-permute-start(bf16[2,96,1024]{2,1,0:T(8,128)(2,1)S(1)} %pad_maximum_fusion.15), channel_id=1, source_target_pairs={{0,4},{2,6},{8,0},{10,2},{16,8},{18,10},{24,16},{26,18},{28,24},{3... | collective-permute-start | bytes 1179656 | tf_op jit(solution)/shard_map/ppermute | solution.py:690
  230.4 17.3 %collective-permute-start.30 = (bf16[2,96,1024]{2,1,0:T(8,128)(2,1)S(1)}, bf16[2,96,1024]{2,1,0:T(8,128)(2,1)S(1)}, u32[]{:S(2)}, u32[]{:S(2)}) collective-permute-start(bf16[2,96,1024]{2,1,0:T(8,128)(2,1)S(1)} %pad_maximum_fusion.14), channel_id=1, source_target_pairs={{0,8},{2,10},{8,16},{10,18},{16,24},{18,26},{24,28},{26,30},{28,20... | collective-permute-start | bytes 1179656 | tf_op jit(solution)/shard_map/ppermute | solution.py:690
  239.6 23.3 %collective-permute-start.37 = (bf16[2,96,2048]{2,1,0:T(8,128)(2,1)S(1)}, bf16[2,96,2048]{2,1,0:T(8,128)(2,1)S(1)}, u32[]{:S(2)}, u32[]{:S(2)}) collective-permute-start(bf16[2,96,2048]{2,1,0:T(8,128)(2,1)S(1)} %pad_maximum_fusion.11), channel_id=1, source_target_pairs={{0,4},{2,6},{8,0},{10,2},{16,8},{18,10},{24,16},{26,18},{28,24},{3... | collective-permute-start | bytes 2359304 | tf_op jit(solution)/shard_map/ppermute | solution.py:690
  241.2 21.7 %collective-permute-start.36 = (bf16[2,96,2048]{2,1,0:T(8,128)(2,1)S(1)}, bf16[2,96,2048]{2,1,0:T(8,128)(2,1)S(1)}, u32[]{:S(2)}, u32[]{:S(2)}) collective-permute-start(bf16[2,96,2048]{2,1,0:T(8,128)(2,1)S(1)} %pad_maximum_fusion.10), channel_id=1, source_target_pairs={{0,8},{2,10},{8,16},{10,18},{16,24},{18,26},{24,28},{26,30},{28,20... | collective-permute-start | bytes 2359304 | tf_op jit(solution)/shard_map/ppermute | solution.py:690
  242.0 22.3 %collective-permute-start.35 = (bf16[256,1536]{1,0:T(8,128)(2,1)S(1)}, bf16[256,1536]{1,0:T(8,128)(2,1)S(1)}, u32[]{:S(2)}, u32[]{:S(2)}) collective-permute-start(bf16[256,1536]{1,0:T(8,128)(2,1)S(1)} %get-tuple-element.290), channel_id=1, source_target_pairs={{0,1},{1,0},{2,3},{3,2},{4,5},{5,4},{6,7},{7,6},{8,9},{9,8},{10,11... | collective-permute-start | bytes 2359304 | tf_op jit(solution)/shard_map/ppermute | solution.py:679
  265.8 11.5 %collective-permute-start.39 = (bf16[512,1536]{1,0:T(8,128)(2,1)}, bf16[512,1536]{1,0:T(8,128)(2,1)}, u32[]{:S(2)}, u32[]{:S(2)}) collective-permute-start(bf16[512,1536]{1,0:T(8,128)(2,1)} %convolution_convert_fusion.4), channel_id=1, source_target_pairs={{0,2},{2,0},{4,6},{6,4},{8,10},{10,8},{12,14},{14,12},{16,18},{18,... | collective-permute-start | bytes 4718600 | tf_op jit(solution)/shard_map/ppermute | solution.py:676
  268.3 13.5 %collective-permute-start.41 = (bf16[2,96,1024]{2,1,0:T(8,128)(2,1)}, bf16[2,96,1024]{2,1,0:T(8,128)(2,1)S(1)}, u32[]{:S(2)}, u32[]{:S(2)}) collective-permute-start(bf16[2,96,1024]{2,1,0:T(8,128)(2,1)} %get-tuple-element.310), channel_id=1, source_target_pairs={{0,8},{2,10},{8,16},{10,18},{16,24},{18,26},{24,28},{26,30},{28,20... | collective-permute-start | bytes 1179656 | tf_op jit(solution)/shard_map/ppermute | solution.py:690
  268.7 13.1 %collective-permute-start.42 = (bf16[2,96,1024]{2,1,0:T(8,128)(2,1)S(1)}, bf16[2,96,1024]{2,1,0:T(8,128)(2,1)S(1)}, u32[]{:S(2)}, u32[]{:S(2)}) collective-permute-start(bf16[2,96,1024]{2,1,0:T(8,128)(2,1)S(1)} %get-tuple-element.309), channel_id=1, source_target_pairs={{0,4},{2,6},{8,0},{10,2},{16,8},{18,10},{24,16},{26,18},{28,24},{3... | collective-permute-start | bytes 1179656 | tf_op jit(solution)/shard_map/ppermute | solution.py:690
  270.3 39.7 %collective-permute-start.43 = (bf16[2,96,2048]{2,1,0:T(8,128)(2,1)}, bf16[2,96,2048]{2,1,0:T(8,128)(2,1)}, u32[]{:S(2)}, u32[]{:S(2)}) collective-permute-start(bf16[2,96,2048]{2,1,0:T(8,128)(2,1)} %get-tuple-element.300), channel_id=1, source_target_pairs={{0,8},{2,10},{8,16},{10,18},{16,24},{18,26},{24,28},{26,30},{28,20... | collective-permute-start | bytes 2359304 | tf_op jit(solution)/shard_map/ppermute | solution.py:690
  270.8 39.2 %collective-permute-start.44 = (bf16[2,96,2048]{2,1,0:T(8,128)(2,1)S(1)}, bf16[2,96,2048]{2,1,0:T(8,128)(2,1)}, u32[]{:S(2)}, u32[]{:S(2)}) collective-permute-start(bf16[2,96,2048]{2,1,0:T(8,128)(2,1)S(1)} %get-tuple-element.299), channel_id=1, source_target_pairs={{0,4},{2,6},{8,0},{10,2},{16,8},{18,10},{24,16},{26,18},{28,24},{3... | collective-permute-start | bytes 2359304 | tf_op jit(solution)/shard_map/ppermute | solution.py:690
  284.1 39.4 %collective-permute-start.45 = (bf16[2,96,1024]{2,1,0:T(8,128)(2,1)}, bf16[2,96,1024]{2,1,0:T(8,128)(2,1)}, u32[]{:S(2)}, u32[]{:S(2)}) collective-permute-start(bf16[2,96,1024]{2,1,0:T(8,128)(2,1)} %get-tuple-element.308), channel_id=1, source_target_pairs={{0,8},{2,10},{8,16},{10,18},{16,24},{18,26},{24,28},{26,30},{28,20... | collective-permute-start | bytes 1179656 | tf_op jit(solution)/shard_map/ppermute | solution.py:690
  284.6 39.0 %collective-permute-start.46 = (bf16[2,96,1024]{2,1,0:T(8,128)(2,1)}, bf16[2,96,1024]{2,1,0:T(8,128)(2,1)}, u32[]{:S(2)}, u32[]{:S(2)}) collective-permute-start(bf16[2,96,1024]{2,1,0:T(8,128)(2,1)} %get-tuple-element.307), channel_id=1, source_target_pairs={{0,4},{2,6},{8,0},{10,2},{16,8},{18,10},{24,16},{26,18},{28,24},{3... | collective-permute-start | bytes 1179656 | tf_op jit(solution)/shard_map/ppermute | solution.py:690
  312.6 22.1 %collective-permute-start.47 = (bf16[2,96,2048]{2,1,0:T(8,128)(2,1)S(1)}, bf16[2,96,2048]{2,1,0:T(8,128)(2,1)S(1)}, u32[]{:S(2)}, u32[]{:S(2)}) collective-permute-start(bf16[2,96,2048]{2,1,0:T(8,128)(2,1)S(1)} %get-tuple-element.298), channel_id=1, source_target_pairs={{0,8},{2,10},{8,16},{10,18},{16,24},{18,26},{24,28},{26,30},{28,20... | collective-permute-start | bytes 2359304 | tf_op jit(solution)/shard_map/ppermute | solution.py:690
  313.1 21.8 %collective-permute-start.48 = (bf16[2,96,2048]{2,1,0:T(8,128)(2,1)S(1)}, bf16[2,96,2048]{2,1,0:T(8,128)(2,1)S(1)}, u32[]{:S(2)}, u32[]{:S(2)}) collective-permute-start(bf16[2,96,2048]{2,1,0:T(8,128)(2,1)S(1)} %get-tuple-element.297), channel_id=1, source_target_pairs={{0,4},{2,6},{8,0},{10,2},{16,8},{18,10},{24,16},{26,18},{28,24},{3... | collective-permute-start | bytes 2359304 | tf_op jit(solution)/shard_map/ppermute | solution.py:690
  315.0 21.8 %collective-permute-start.40 = (bf16[256,1536]{1,0:T(8,128)(2,1)S(1)}, bf16[256,1536]{1,0:T(8,128)(2,1)S(1)}, u32[]{:S(2)}, u32[]{:S(2)}) collective-permute-start(bf16[256,1536]{1,0:T(8,128)(2,1)S(1)} %copy-done.23), channel_id=1, source_target_pairs={{0,1},{1,0},{2,3},{3,2},{4,5},{5,4},{6,7},{7,6},{8,9},{9,8},{10,11... | collective-permute-start | bytes 2359304 | tf_op jit(solution)/shard_map/ppermute | solution.py:679
  326.9 11.6 %collective-permute-start.53 = (bf16[1,96,896]{2,1,0:T(8,128)(2,1)S(1)}, bf16[1,96,896]{2,1,0:T(8,128)(2,1)S(1)}, u32[]{:S(2)}, u32[]{:S(2)}) collective-permute-start(bf16[1,96,896]{2,1,0:T(8,128)(2,1)S(1)} %get-tuple-element.196), channel_id=1, source_target_pairs={{0,8},{2,10},{8,16},{10,18},{16,24},{18,26},{24,28},{26,30},{28,20... | collective-permute-start | bytes 516104 | tf_op jit(solution)/shard_map/ppermute | solution.py:690
  332.0 8.1 %collective-permute-start.54 = (bf16[1,96,896]{2,1,0:T(8,128)(2,1)S(1)}, bf16[1,96,896]{2,1,0:T(8,128)(2,1)S(1)}, u32[]{:S(2)}, u32[]{:S(2)}) collective-permute-start(bf16[1,96,896]{2,1,0:T(8,128)(2,1)S(1)} %get-tuple-element.197), channel_id=1, source_target_pairs={{0,4},{2,6},{8,0},{10,2},{16,8},{18,10},{24,16},{26,18},{28,24},{3... | collective-permute-start | bytes 516104 | tf_op jit(solution)/shard_map/ppermute | solution.py:690
  334.7 13.9 %collective-permute-start.49 = (bf16[512,1536]{1,0:T(8,128)(2,1)S(1)}, bf16[512,1536]{1,0:T(8,128)(2,1)S(1)}, u32[]{:S(2)}, u32[]{:S(2)}) collective-permute-start(bf16[512,1536]{1,0:T(8,128)(2,1)S(1)} %fusion.15), channel_id=1, source_target_pairs={{0,2},{2,0},{4,6},{6,4},{8,10},{10,8},{12,14},{14,12},{16,18},{18,... | collective-permute-start | bytes 4718600 | tf_op jit(solution)/shard_map/ppermute | solution.py:676
  336.5 14.2 %collective-permute-start.74 = (bf16[96,2048]{1,0:T(8,128)(2,1)S(1)}, bf16[96,2048]{1,0:T(8,128)(2,1)S(1)}, u32[]{:S(2)}, u32[]{:S(2)}) collective-permute-start(bf16[96,2048]{1,0:T(8,128)(2,1)S(1)} %dynamic-slice_convert_fusion), channel_id=1, source_target_pairs={{0,2},{2,0},{4,6},{6,4},{8,10},{10,8},{12,14},{14,12},{16,18},{18,... | collective-permute-start | bytes 1179656 | tf_op jit(solution)/shard_map/ppermute | solution.py:676
  338.1 8.2 %collective-permute-start.51 = (bf16[1,96,768]{2,1,0:T(8,128)(2,1)S(1)}, bf16[1,96,768]{2,1,0:T(8,128)(2,1)S(1)}, u32[]{:S(2)}, u32[]{:S(2)}) collective-permute-start(bf16[1,96,768]{2,1,0:T(8,128)(2,1)S(1)} %get-tuple-element.201), channel_id=1, source_target_pairs={{0,8},{2,10},{8,16},{10,18},{16,24},{18,26},{24,28},{26,30},{28,20... | collective-permute-start | bytes 442376 | tf_op jit(solution)/shard_map/ppermute | solution.py:690
  338.5 8.4 %collective-permute-start.52 = (bf16[1,96,768]{2,1,0:T(8,128)(2,1)S(1)}, bf16[1,96,768]{2,1,0:T(8,128)(2,1)S(1)}, u32[]{:S(2)}, u32[]{:S(2)}) collective-permute-start(bf16[1,96,768]{2,1,0:T(8,128)(2,1)S(1)} %get-tuple-element.202), channel_id=1, source_target_pairs={{0,4},{2,6},{8,0},{10,2},{16,8},{18,10},{24,16},{26,18},{28,24},{3... | collective-permute-start | bytes 442376 | tf_op jit(solution)/shard_map/ppermute | solution.py:690
  340.3 27.8 %collective-permute-start.57 = (bf16[2,96,896]{2,1,0:T(8,128)(2,1)S(1)}, bf16[2,96,896]{2,1,0:T(8,128)(2,1)S(1)}, u32[]{:S(2)}, u32[]{:S(2)}) collective-permute-start(bf16[2,96,896]{2,1,0:T(8,128)(2,1)S(1)} %pad_maximum_fusion.17), channel_id=1, source_target_pairs={{0,4},{2,6},{8,0},{10,2},{16,8},{18,10},{24,16},{26,18},{28,24},{3... | collective-permute-start | bytes 1032200 | tf_op jit(solution)/shard_map/ppermute | solution.py:690
  346.3 21.9 %collective-permute-start.56 = (bf16[2,96,896]{2,1,0:T(8,128)(2,1)S(1)}, bf16[2,96,896]{2,1,0:T(8,128)(2,1)S(1)}, u32[]{:S(2)}, u32[]{:S(2)}) collective-permute-start(bf16[2,96,896]{2,1,0:T(8,128)(2,1)S(1)} %pad_maximum_fusion.16), channel_id=1, source_target_pairs={{0,8},{2,10},{8,16},{10,18},{16,24},{18,26},{24,28},{26,30},{28,20... | collective-permute-start | bytes 1032200 | tf_op jit(solution)/shard_map/ppermute | solution.py:690
  347.0 23.4 %collective-permute-start.62 = (bf16[2,96,768]{2,1,0:T(8,128)(2,1)S(1)}, bf16[2,96,768]{2,1,0:T(8,128)(2,1)S(1)}, u32[]{:S(2)}, u32[]{:S(2)}) collective-permute-start(bf16[2,96,768]{2,1,0:T(8,128)(2,1)S(1)} %pad_maximum_fusion.19), channel_id=1, source_target_pairs={{0,4},{2,6},{8,0},{10,2},{16,8},{18,10},{24,16},{26,18},{28,24},{3... | collective-permute-start | bytes 884744 | tf_op jit(solution)/shard_map/ppermute | solution.py:690
  349.1 18.4 %collective-permute-start.50 = (bf16[256,1536]{1,0:T(8,128)(2,1)S(1)}, bf16[256,1536]{1,0:T(8,128)(2,1)S(1)}, u32[]{:S(2)}, u32[]{:S(2)}) collective-permute-start(bf16[256,1536]{1,0:T(8,128)(2,1)S(1)} %slice.704), channel_id=1, source_target_pairs={{0,1},{1,0},{2,3},{3,2},{4,5},{5,4},{6,7},{7,6},{8,9},{9,8},{10,11... | collective-permute-start | bytes 2359304 | tf_op jit(solution)/shard_map/ppermute | solution.py:679
  350.7 19.7 %collective-permute-start.61 = (bf16[2,96,768]{2,1,0:T(8,128)(2,1)S(1)}, bf16[2,96,768]{2,1,0:T(8,128)(2,1)S(1)}, u32[]{:S(2)}, u32[]{:S(2)}) collective-permute-start(bf16[2,96,768]{2,1,0:T(8,128)(2,1)S(1)} %pad_maximum_fusion.18), channel_id=1, source_target_pairs={{0,8},{2,10},{8,16},{10,18},{16,24},{18,26},{24,28},{26,30},{28,20... | collective-permute-start | bytes 884744 | tf_op jit(solution)/shard_map/ppermute | solution.py:690
  368.4 12.1 %collective-permute-start.58 = (bf16[2,96,896]{2,1,0:T(8,128)(2,1)S(1)}, bf16[2,96,896]{2,1,0:T(8,128)(2,1)S(1)}, u32[]{:S(2)}, u32[]{:S(2)}) collective-permute-start(bf16[2,96,896]{2,1,0:T(8,128)(2,1)S(1)} %get-tuple-element.320), channel_id=1, source_target_pairs={{0,8},{2,10},{8,16},{10,18},{16,24},{18,26},{24,28},{26,30},{28,20... | collective-permute-start | bytes 1032200 | tf_op jit(solution)/shard_map/ppermute | solution.py:690
  369.0 11.5 %collective-permute-start.59 = (bf16[2,96,896]{2,1,0:T(8,128)(2,1)S(1)}, bf16[2,96,896]{2,1,0:T(8,128)(2,1)S(1)}, u32[]{:S(2)}, u32[]{:S(2)}) collective-permute-start(bf16[2,96,896]{2,1,0:T(8,128)(2,1)S(1)} %get-tuple-element.319), channel_id=1, source_target_pairs={{0,4},{2,6},{8,0},{10,2},{16,8},{18,10},{24,16},{26,18},{28,24},{3... | collective-permute-start | bytes 1032200 | tf_op jit(solution)/shard_map/ppermute | solution.py:690
  370.5 9.9 %collective-permute-start.55 = (f32[8,1536]{1,0:T(8,128)S(1)}, f32[8,1536]{1,0:T(8,128)S(1)}, u32[]{:S(2)}, u32[]{:S(2)}) collective-permute-start(f32[8,1536]{1,0:T(8,128)S(1)} %pad_maximum_fusion.21), channel_id=1, source_target_pairs={{0,4},{2,6},{4,0},{6,2},{8,12},{10,14},{12,8},{14,10},{16,20},{18,... | collective-permute-start | bytes 147464 | tf_op jit(solution)/shard_map/ppermute | solution.py:702
  372.1 13.5 %collective-permute-start.63 = (bf16[2,96,768]{2,1,0:T(8,128)(2,1)S(1)}, bf16[2,96,768]{2,1,0:T(8,128)(2,1)S(1)}, u32[]{:S(2)}, u32[]{:S(2)}) collective-permute-start(bf16[2,96,768]{2,1,0:T(8,128)(2,1)S(1)} %get-tuple-element.330), channel_id=1, source_target_pairs={{0,8},{2,10},{8,16},{10,18},{16,24},{18,26},{24,28},{26,30},{28,20... | collective-permute-start | bytes 884744 | tf_op jit(solution)/shard_map/ppermute | solution.py:690
  373.6 12.1 %collective-permute-start.64 = (bf16[2,96,768]{2,1,0:T(8,128)(2,1)S(1)}, bf16[2,96,768]{2,1,0:T(8,128)(2,1)S(1)}, u32[]{:S(2)}, u32[]{:S(2)}) collective-permute-start(bf16[2,96,768]{2,1,0:T(8,128)(2,1)S(1)} %get-tuple-element.329), channel_id=1, source_target_pairs={{0,4},{2,6},{8,0},{10,2},{16,8},{18,10},{24,16},{26,18},{28,24},{3... | collective-permute-start | bytes 884744 | tf_op jit(solution)/shard_map/ppermute | solution.py:690
  389.6 14.2 %collective-permute-start.68 = (bf16[2,96,896]{2,1,0:T(8,128)(2,1)}, bf16[2,96,896]{2,1,0:T(8,128)(2,1)S(1)}, u32[]{:S(2)}, u32[]{:S(2)}) collective-permute-start(bf16[2,96,896]{2,1,0:T(8,128)(2,1)} %get-tuple-element.318), channel_id=1, source_target_pairs={{0,8},{2,10},{8,16},{10,18},{16,24},{18,26},{24,28},{26,30},{28,20... | collective-permute-start | bytes 1032200 | tf_op jit(solution)/shard_map/ppermute | solution.py:690
  391.8 12.8 %collective-permute-start.69 = (bf16[2,96,896]{2,1,0:T(8,128)(2,1)}, bf16[2,96,896]{2,1,0:T(8,128)(2,1)}, u32[]{:S(2)}, u32[]{:S(2)}) collective-permute-start(bf16[2,96,896]{2,1,0:T(8,128)(2,1)} %get-tuple-element.317), channel_id=1, source_target_pairs={{0,4},{2,6},{8,0},{10,2},{16,8},{18,10},{24,16},{26,18},{28,24},{3... | collective-permute-start | bytes 1032200 | tf_op jit(solution)/shard_map/ppermute | solution.py:690
  391.8 9.2 %collective-permute-start.71 = (bf16[2,96,768]{2,1,0:T(8,128)(2,1)}, bf16[2,96,768]{2,1,0:T(8,128)(2,1)S(1)}, u32[]{:S(2)}, u32[]{:S(2)}) collective-permute-start(bf16[2,96,768]{2,1,0:T(8,128)(2,1)} %get-tuple-element.328), channel_id=1, source_target_pairs={{0,8},{2,10},{8,16},{10,18},{16,24},{18,26},{24,28},{26,30},{28,20... | collective-permute-start | bytes 884744 | tf_op jit(solution)/shard_map/ppermute | solution.py:690
  393.8 8.8 %collective-permute-start.72 = (bf16[2,96,768]{2,1,0:T(8,128)(2,1)}, bf16[2,96,768]{2,1,0:T(8,128)(2,1)}, u32[]{:S(2)}, u32[]{:S(2)}) collective-permute-start(bf16[2,96,768]{2,1,0:T(8,128)(2,1)} %get-tuple-element.327), channel_id=1, source_target_pairs={{0,4},{2,6},{8,0},{10,2},{16,8},{18,10},{24,16},{26,18},{28,24},{3... | collective-permute-start | bytes 884744 | tf_op jit(solution)/shard_map/ppermute | solution.py:690
  (63 other events, 643.8 us)

commit v6 on v5

--- a/solution.py
+++ b/solution.py
@@ -810,12 +810,19 @@
     moved = attn_ring.advance(rows_near)
     attn_ring.store()
     grad_near = at.swap_y(after(out_grad, *moved))
-    attn_ring.advance(ffn_shard)
+    def first_norm(rows):
+        rows = rows.astype(F32)
+        return rows, lax.rsqrt(jnp.mean(rows * rows, axis=1, keepdims=True) + EPSILON)
+
+    rows_all = at.join(layer_in, rows_near)
+    x_all, scale_all = first_norm(rows_all)
+    unit_all = x_all * scale_all
+    attn_ring.advance(ffn_shard, unit_all)
+    unit_all = after(unit_all, *attn_ring.came)
     attn_ring.store()
     ffn_ring = Gathering(at, after(ffn_shard, *attn_ring.came))
     attn_all = attn_ring.finish()
     w_in, wo_all = attn_all[:, :in_cols], attn_all[:, in_cols:]
-    rows_all = at.join(layer_in, rows_near)
     grad_rows = at.join(out_grad, grad_near)
     w_qkv = w_in[:, :qkv_cols]
     small = w_in[:, qkv_cols:].T
@@ -823,18 +830,13 @@
     gain_one = small[2 * heads : 2 * heads + 1].astype(F32)
     gain_two = small[2 * heads + 1 : 2 * heads + 2].astype(F32)
 
-    def first_norm(rows):
-        rows = rows.astype(F32)
-        return rows, lax.rsqrt(jnp.mean(rows * rows, axis=1, keepdims=True) + EPSILON)
-
-    x_all, scale_all = first_norm(rows_all)
-    normed_one = (x_all * scale_all * gain_one).astype(BF16)
+    normed_one = (unit_all * gain_one).astype(BF16)
     x_own, scale_one = first_norm(layer_in)
     unit_one = x_own * scale_one
     qkv = dot_nn(normed_one, w_qkv).astype(BF16)
 
     bias = lax.dynamic_slice_in_dim(forget_bias, at.core * heads, heads, 0)
-    logits = dot_nt(forget_t, normed_one) + bias[:, None]
+    logits = dot_nt(after(forget_t, qkv), normed_one) + bias[:, None]
     logs = jax.nn.log_sigmoid(logits).reshape(heads, 2, 2, rows_loc)
     steps = jnp.arange(rows_loc, dtype=jnp.int32)
     upper = (steps[:, None] <= steps[None, :]).astype(F32)

time: 416 us -> 413 us (level)
    unnamed x111 -> x107, local copies, waits for them, and re-layouts: 11.8 us -> 10.1 us
  transfers between devices with their start and end apart: 76 -> 76, of which waited for: 26 -> 27; matrix products, arithmetic and copies ran while one was open for 34% -> 35% of each run, Pallas kernels for 10% -> 10%
where the time goes in v6:
time: 413 us; the launch traced here: 406 us
  waiting for transfers between devices  109 us (26%)
  matrix products  80.8 us (20%)
  starting transfers between devices  70.5 us (17%)
  other arithmetic  53.3 us (13%)
  local copies, waits for them, and re-layouts  48.1 us (12%)
  Pallas kernels  42.1 us (10%)
    ppermute x48, waiting for transfers between devices, ring(): return lax.ppermute(value, 'dp', pairs)  65.5 us
    ppermute x48, starting transfers between devices, ring(): return lax.ppermute(value, 'dp', pairs)  51.3 us
    ppermute x9, waiting for transfers between devices, swap_y(): return lax.ppermute(value, 'tensor', [(0, 1), (1, 0)])  31.6 us
    dot_general x4, matrix products, dot_nn(): lax.dot_general(left, right, (((1,), (0,)), ((), ())), preferred_element_...  29.7 us
    dot_general x9, matrix products, dot_nt(): lax.dot_general(left, right, (((1,), (1,)), ((), ())), preferred_element_...  29.2 us
    pallas_call x1, Pallas kernels, attend_back(): pl.pallas_call(partial(attend_back_kernel, pairs), grid_spec=grid_spec, o...  21.8 us
    dot_general x5, matrix products, dot_tn(): lax.dot_general(left, right, (((0,), (0,)), ((), ())), preferred_element_...  21.7 us
    dynamic_update_slice x17, local copies, waits for them, and re-layouts, store(): self.whole = lax.dynamic_update_slice(self.whole, part[None], start)  18.5 us
  transfers between devices with their start and end apart: 76, of which 27 were waited for; matrix products, arithmetic and copies ran while one was open for 35% of the time, Pallas kernels for 10%

profile of v6, /device:TPU:0, one launch (start us, length us, event | category | flops | bytes accessed | tf_op | source)
XLA Modules:
  0.0 406.2 jit_solution(6008173895136201541)
XLA Ops:
  6.7 2.6 collective-permute-start
  10.5 1.6 collective-permute-start.3
  13.6 2.8 broadcast_in_dim.102
  17.4 10.2 %collective-permute-done = bf16[256,1536]{1,0:T(8,128)(2,1)S(1)} collective-permute-done((bf16[256,1536]{1,0:T(8,128)(2,1)}, bf16[256,1536]{1,0:T(8,128)(2,1)S(1)}, u32[]{:S(2)}, u32[]{:S(2)}) %collective-permute-start) | collective-permute-done | bytes 786464 | tf_op jit(solution)/shard_map/ppermute | solution.py:679
  29.0 1.9 collective-permute-start.5
  32.9 2.0 bitcast_dynamic-update-slice_fusion.12
  34.9 2.0 bitcast_dynamic-update-slice_fusion.11
  36.9 2.4 maximum_select_fusion
  39.3 6.7 %collective-permute-done.5 = bf16[2,96,1664]{2,1,0:T(8,128)(2,1)} collective-permute-done((bf16[2,96,1664]{2,1,0:T(8,128)(2,1)}, bf16[2,96,1664]{2,1,0:T(8,128)(2,1)}, u32[]{:S(2)}, u32[]{:S(2)}) %collective-permute-start.5) | collective-permute-done | bytes 639008 | tf_op jit(solution)/shard_map/ppermute | solution.py:690
  51.1 1.9 bitcast_dynamic-update-slice_fusion.10
  53.1 2.0 bitcast_dynamic-update-slice_fusion.9
  55.1 1.9 fusion
  57.0 3.9 convert_multiply_fusion
  60.9 2.5 collective-permute-done.7
  64.7 1.6 collective-permute-start.10
  70.0 2.4 collective-permute-done.10
  79.9 8.6 %convolution_convert_fusion.1.qkv_ref = bf16[1024,1152]{1,0:T(8,128)(2,1)} fusion(bf16[1024,1536]{1,0:T(8,128)(2,1)S(1)} %multiply_convert_fusion, bf16[1536,1664]{1,0:T(8,128)(2,1)} %bitcast.17), kind=kOutput, calls=%fused_computation.33 | convolution fusion | flops 3625058304 | bytes 9043968 | tf_op jit(solution)/shard_map/dot_general | solution.py:320
  90.7 9.0 %attend.2 = (bf16[512,384]{1,0:T(8,128)(2,1)}, f32[1024,384]{1,0:T(8,128)}, bf16[2,3,2,256,768]{4,3,2,1,0:T(8,128)(2,1)}, f32[1,3,8,128]{3,2,1,0:T(8,128)}) custom-call(s32[1]{0:T(128)} %bitcast.y_ref, bf16[1024,1152]{1,0:T(8,128)(2,1)} %convolution_convert_fusion.1.qkv_ref, f32[3,8,1024]{2,1,0:T(8,128)} %maximum_maximum_fusion.aux_ref), custom_call_target="tpu_custom_call" | custom-call | flops 603979776 | bytes 10000000 | tf_op jit(solution)/shard_map/attend/pallas_call | solution.py:396
  100.4 3.6 convolution_convert_fusion.5
  104.2 1.6 copy-done.33
  107.8 9.0 %attend.3 = (bf16[512,384]{1,0:T(8,128)(2,1)}, f32[1024,384]{1,0:T(8,128)}, bf16[2,3,2,256,768]{4,3,2,1,0:T(8,128)(2,1)}, f32[1,3,8,128]{3,2,1,0:T(8,128)}) custom-call(s32[1]{0:T(128)} %bitcast.y_ref, bf16[1024,1152]{1,0:T(8,128)(2,1)} %convolution_convert_fusion.1.qkv_ref, ...), custom_call_target="tpu_custom_call", output_to_operand_aliasing={{1}: (3, {}), {2}: (4, {})} | custom-call | flops 603979776 | bytes 10000000 | tf_op jit(solution)/shard_map/attend/pallas_call | solution.py:396
  116.8 2.5 fusion.49
  120.9 1.7 copy-done.35
  122.6 1.9 convert_add_fusion.3
  124.5 1.6 collective-permute-start.17
  126.1 8.4 %collective-permute-done.18 = bf16[2,96,3072]{2,1,0:T(8,128)(2,1)} collective-permute-done((bf16[2,96,3072]{2,1,0:T(8,128)(2,1)}, bf16[2,96,3072]{2,1,0:T(8,128)(2,1)}, u32[]{:S(2)}, u32[]{:S(2)}) %collective-permute-start.18) | collective-permute-done | bytes 1179680 | tf_op jit(solution)/shard_map/ppermute | solution.py:690
  144.1 2.2 multiply_reduce_fusion.2
  150.9 12.0 %collective-permute-done.21 = bf16[2,96,3072]{2,1,0:T(8,128)(2,1)S(1)} collective-permute-done((bf16[2,96,3072]{2,1,0:T(8,128)(2,1)}, bf16[2,96,3072]{2,1,0:T(8,128)(2,1)S(1)}, u32[]{:S(2)}, u32[]{:S(2)}) %collective-permute-start.21) | collective-permute-done | bytes 1179680 | tf_op jit(solution)/shard_map/ppermute | solution.py:690
  166.5 10.9 %collective-permute-done.24 = bf16[1,96,3072]{2,1,0:T(8,128)(2,1)S(1)} collective-permute-done((bf16[1,96,3072]{2,1,0:T(8,128)(2,1)S(1)}, bf16[1,96,3072]{2,1,0:T(8,128)(2,1)S(1)}, u32[]{:S(2)}, u32[]{:S(2)}) %collective-permute-start.24) | collective-permute-done | bytes 589856 | tf_op jit(solution)/shard_map/ppermute | solution.py:690
  179.0 8.8 %fusion.5 = f32[1024,2048]{1,0:T(8,128)} fusion(bf16[1536,3072]{1,0:T(8,128)(2,1)S(1)} %bitcast.245, bf16[512,1536]{1,0:T(8,128)(2,1)S(1)} %collective-permute-done.23, bf16[256,1536]{1,0:T(8,128)(2,1)S(1)} %collective-permute-done.20, bf16[256,1536]{1,0:T(8,128)(2,1)S(1)} %multiply_convert_fusion.4), kind=kOutput, calls=%fused_computation.9 | convolution fusion | flops 6451888128 | bytes 17825792 | tf_op jit(solution)/shard_map/dot_general | solution.py:320
  187.8 7.5 %multiply_convert_fusion.2 = (bf16[1024,1024]{1,0:T(8,128)(2,1)S(1)}, bf16[1024,1024]{1,0:T(8,128)(2,1)S(1)}, bf16[1024,1024]{1,0:T(8,128)(2,1)S(1)}) fusion(f32[1024,2048]{1,0:T(8,128)} %fusion.5, bf16[1024,1536]{1,0:T(8,128)(2,1)S(1)} %copy-done.36, bf16[1536,3072]{1,0:T(8,128)(2,1)S(1)} %bitcast.246), kind=kOutput, calls=%fused_computation.29 | convolution fusion | flops 3236954112 | bytes 20971520 | tf_op jit(solution)/shard_map/dot_general | solution.py:320
  195.3 3.7 convolution_convert_fusion.2
  200.5 3.5 fusion.16
  206.2 3.5 fusion.1
  212.7 8.6 %convolution_convert_fusion = bf16[1536,2048]{1,0:T(8,128)(2,1)S(1)} fusion(bf16[1024,2048]{1,0:T(8,128)(2,1)S(1)} %pad_maximum_fusion, bf16[512,1536]{1,0:T(8,128)(2,1)} %copy-done.45, bf16[256,1536]{1,0:T(8,128)(2,1)} %copy-done.24, bf16[256,1536]{1,0:T(8,128)(2,1)S(1)} %copy-done.17), kind=kOutput, calls=%fused_computation.2 | convolution fusion | flops 6455033856 | bytes 13631488 | tf_op jit(solution)/shard_map/dot_general | solution.py:324
  225.8 4.8 %collective-permute-done.34 = bf16[256,1536]{1,0:T(8,128)(2,1)S(1)} collective-permute-done((bf16[256,1536]{1,0:T(8,128)(2,1)}, bf16[256,1536]{1,0:T(8,128)(2,1)S(1)}, u32[]{:S(2)}, u32[]{:S(2)}) %collective-permute-start.34) | collective-permute-done | bytes 786464 | tf_op jit(solution)/shard_map/ppermute | solution.py:679
  231.3 1.8 fusion.106
  237.4 3.0 convolution_convert_fusion.4
  240.4 2.1 collective-permute-done.31
  243.6 3.5 fusion.19
  247.1 10.7 %collective-permute-done.37 = bf16[2,96,2048]{2,1,0:T(8,128)(2,1)S(1)} collective-permute-done((bf16[2,96,2048]{2,1,0:T(8,128)(2,1)S(1)}, bf16[2,96,2048]{2,1,0:T(8,128)(2,1)S(1)}, u32[]{:S(2)}, u32[]{:S(2)}) %collective-permute-start.37) | collective-permute-done | bytes 786464 | tf_op jit(solution)/shard_map/ppermute | solution.py:690
  267.3 4.9 %convolution_convert_fusion.8.do_ref = bf16[1024,384]{1,0:T(8,128)(2,1)} fusion(bf16[1536,1664]{1,0:T(8,128)(2,1)} %bitcast.17, bf16[512,1536]{1,0:T(8,128)(2,1)} %collective-permute-done.38, bf16[256,1536]{1,0:T(8,128)(2,1)} %copy-done.22, bf16[256,1536]{1,0:T(8,128)(2,1)} %copy-done.12), kind=kOutput, calls=%fused_computation.104 | convolution fusion | flops 1217789952 | bytes 5111808 | tf_op jit(solution)/shard_map/dot_general | solution.py:320
  272.2 1.9 convert_add_fusion.1
  274.1 1.6 copy-done.5
  276.7 2.3 fusion.57
  281.1 21.8 %attend_back.1 = (bf16[1024,1152]{1,0:T(8,128)(2,1)}, bf16[1024,128]{1,0:T(8,128)(2,1)}) custom-call(s32[1]{0:T(128)} %bitcast.y_ref, bf16[1024,1152]{1,0:T(8,128)(2,1)} %convolution_convert_fusion.1.qkv_ref, bf16[1024,384]{1,0:T(8,128)(2,1)} %convolution_convert_fusion.8.do_ref, f32[1024,384]{1,0:T(8,128)} %get-tuple-element.190.inv_ref, ...), custom_call_target="tpu_custom_call" | custom-call | flops 3623878656 | bytes 20000000 | tf_op jit(solution)/shard_map/attend_back/pallas_call | solution.py:534
  302.9 2.0 constant_dynamic-update-slice_fusion.4
  304.9 2.6 fusion.40
  308.2 1.8 collective-permute-start.48
  310.5 3.7 convolution_convert_fusion.3
  314.6 3.8 convolution_convert_fusion.6
  320.0 1.8 convolution_convert_fusion.7
  322.5 4.3 %fusion.13 = bf16[512,1536]{1,0:T(8,128)(2,1)S(1)} fusion(bf16[1536,1664]{1,0:T(8,128)(2,1)} %bitcast.17, bf16[1024,1280]{1,0:T(8,128)(2,1)S(1)} %constant_dynamic-update-slice_fusion.3), kind=kOutput, calls=%fused_computation.48 | convolution fusion | flops 2014052352 | bytes 6815744 | tf_op jit(solution)/shard_map/dot_general | solution.py:316
  336.6 4.3 %fusion.9 = f32[512,1536]{1,0:T(8,128)S(1)} fusion(bf16[1536,1664]{1,0:T(8,128)(2,1)} %bitcast.17, bf16[1024,1280]{1,0:T(8,128)(2,1)S(1)} %constant_dynamic-update-slice_fusion.3), kind=kOutput, calls=%fused_computation.37 | convolution fusion | flops 2013265920 | bytes 8388608 | tf_op jit(solution)/shard_map/dot_general | solution.py:316
  343.9 1.6 collective-permute-start.50
  348.5 13.8 %collective-permute-done.50 = bf16[256,1536]{1,0:T(8,128)(2,1)S(1)} collective-permute-done((bf16[256,1536]{1,0:T(8,128)(2,1)S(1)}, bf16[256,1536]{1,0:T(8,128)(2,1)S(1)}, u32[]{:S(2)}, u32[]{:S(2)}) %collective-permute-start.50) | collective-permute-done | bytes 786464 | tf_op jit(solution)/shard_map/ppermute | solution.py:679
  369.0 6.2 %collective-permute-done.55 = f32[8,1536]{1,0:T(8,128)S(1)} collective-permute-done((f32[8,1536]{1,0:T(8,128)S(1)}, f32[8,1536]{1,0:T(8,128)S(1)}, u32[]{:S(2)}, u32[]{:S(2)}) %collective-permute-start.55) | collective-permute-done | bytes 49184 | tf_op jit(solution)/shard_map/ppermute | solution.py:702
  376.4 4.1 collective-permute-done.60
  381.5 1.6 collective-permute-start.65
  384.5 1.8 collective-permute-start.68
  386.6 1.8 collective-permute-start.71
  393.6 1.6 collective-permute-done.67
  395.8 1.8 collective-permute-done.72
  403.3 2.4 assemble.1
  (388 shorter events, 127.2 us)
Async XLA Ops:
  6.7 20.9 %collective-permute-start = (bf16[256,1536]{1,0:T(8,128)(2,1)}, bf16[256,1536]{1,0:T(8,128)(2,1)S(1)}, u32[]{:S(2)}, u32[]{:S(2)}) collective-permute-start(bf16[256,1536]{1,0:T(8,128)(2,1)} %param.15), channel_id=1, source_target_pairs={{0,1},{1,0},{2,3},{3,2},{4,5},{5,4},{6,7},{7,6},{8,9},{9,8},{10,11... | collective-permute-start | bytes 2359304 | tf_op jit(solution)/shard_map/ppermute | solution.py:679
  10.5 18.4 %collective-permute-start.3 = (bf16[2,96,1664]{2,1,0:T(8,128)(2,1)S(1)}, bf16[2,96,1664]{2,1,0:T(8,128)(2,1)}, u32[]{:S(2)}, u32[]{:S(2)}) collective-permute-start(bf16[2,96,1664]{2,1,0:T(8,128)(2,1)S(1)} %maximum_select_fusion.4), channel_id=1, source_target_pairs={{0,8},{2,10},{8,16},{10,18},{16,24},{18,26},{24,28},{26,30},{28,20... | collective-permute-start | bytes 1916936 | tf_op jit(solution)/shard_map/ppermute | solution.py:690
  12.1 16.8 %collective-permute-start.4 = (bf16[2,96,1664]{2,1,0:T(8,128)(2,1)S(1)}, bf16[2,96,1664]{2,1,0:T(8,128)(2,1)}, u32[]{:S(2)}, u32[]{:S(2)}) collective-permute-start(bf16[2,96,1664]{2,1,0:T(8,128)(2,1)S(1)} %maximum_select_fusion.4), channel_id=1, source_target_pairs={{0,4},{2,6},{8,0},{10,2},{16,8},{18,10},{24,16},{26,18},{28,24},{3... | collective-permute-start | bytes 1916936 | tf_op jit(solution)/shard_map/ppermute | solution.py:690
  28.9 26.1 %collective-permute-start.1 = (bf16[512,1536]{1,0:T(8,128)(2,1)}, bf16[512,1536]{1,0:T(8,128)(2,1)}, u32[]{:S(2)}, u32[]{:S(2)}) collective-permute-start(bf16[512,1536]{1,0:T(8,128)(2,1)} %pad_maximum_fusion.4), channel_id=1, source_target_pairs={{0,2},{2,0},{4,6},{6,4},{8,10},{10,8},{12,14},{14,12},{16,18},{18,... | collective-permute-start | bytes 4718600 | tf_op jit(solution)/shard_map/ppermute | solution.py:676
  29.0 17.1 %collective-permute-start.5 = (bf16[2,96,1664]{2,1,0:T(8,128)(2,1)}, bf16[2,96,1664]{2,1,0:T(8,128)(2,1)}, u32[]{:S(2)}, u32[]{:S(2)}) collective-permute-start(bf16[2,96,1664]{2,1,0:T(8,128)(2,1)} %collective-permute-done.3), channel_id=1, source_target_pairs={{0,8},{2,10},{8,16},{10,18},{16,24},{18,26},{24,28},{26,30},{28,20... | collective-permute-start | bytes 1916936 | tf_op jit(solution)/shard_map/ppermute | solution.py:690
  30.8 16.8 %collective-permute-start.6 = (bf16[2,96,1664]{2,1,0:T(8,128)(2,1)}, bf16[2,96,1664]{2,1,0:T(8,128)(2,1)}, u32[]{:S(2)}, u32[]{:S(2)}) collective-permute-start(bf16[2,96,1664]{2,1,0:T(8,128)(2,1)} %collective-permute-done.4), channel_id=1, source_target_pairs={{0,4},{2,6},{8,0},{10,2},{16,8},{18,10},{24,16},{26,18},{28,24},{3... | collective-permute-start | bytes 1916936 | tf_op jit(solution)/shard_map/ppermute | solution.py:690
  47.6 15.8 %collective-permute-start.7 = (bf16[2,96,1664]{2,1,0:T(8,128)(2,1)}, bf16[2,96,1664]{2,1,0:T(8,128)(2,1)S(1)}, u32[]{:S(2)}, u32[]{:S(2)}) collective-permute-start(bf16[2,96,1664]{2,1,0:T(8,128)(2,1)} %collective-permute-done.5), channel_id=1, source_target_pairs={{0,8},{2,10},{8,16},{10,18},{16,24},{18,26},{24,28},{26,30},{28,20... | collective-permute-start | bytes 1916936 | tf_op jit(solution)/shard_map/ppermute | solution.py:690
  49.2 15.5 %collective-permute-start.8 = (bf16[2,96,1664]{2,1,0:T(8,128)(2,1)}, bf16[2,96,1664]{2,1,0:T(8,128)(2,1)S(1)}, u32[]{:S(2)}, u32[]{:S(2)}) collective-permute-start(bf16[2,96,1664]{2,1,0:T(8,128)(2,1)} %collective-permute-done.6), channel_id=1, source_target_pairs={{0,4},{2,6},{8,0},{10,2},{16,8},{18,10},{24,16},{26,18},{28,24},{3... | collective-permute-start | bytes 1916936 | tf_op jit(solution)/shard_map/ppermute | solution.py:690
  49.6 19.0 %collective-permute-start.13 = (bf16[256,1536]{1,0:T(8,128)(2,1)S(1)}, bf16[256,1536]{1,0:T(8,128)(2,1)S(1)}, u32[]{:S(2)}, u32[]{:S(2)}) collective-permute-start(bf16[256,1536]{1,0:T(8,128)(2,1)S(1)} %copy-done.7), channel_id=1, source_target_pairs={{0,1},{1,0},{2,3},{3,2},{4,5},{5,4},{6,7},{7,6},{8,9},{9,8},{10,11... | collective-permute-start | bytes 2359304 | tf_op jit(solution)/shard_map/ppermute | solution.py:679
  64.7 7.7 %collective-permute-start.10 = (bf16[1,96,1664]{2,1,0:T(8,128)(2,1)S(1)}, bf16[1,96,1664]{2,1,0:T(8,128)(2,1)S(1)}, u32[]{:S(2)}, u32[]{:S(2)}) collective-permute-start(bf16[1,96,1664]{2,1,0:T(8,128)(2,1)S(1)} %slice.410), channel_id=1, source_target_pairs={{0,8},{2,10},{8,16},{10,18},{16,24},{18,26},{24,28},{26,30},{28,20... | collective-permute-start | bytes 958472 | tf_op jit(solution)/shard_map/ppermute | solution.py:690
  66.4 7.4 %collective-permute-start.11 = (bf16[1,96,1664]{2,1,0:T(8,128)(2,1)S(1)}, bf16[1,96,1664]{2,1,0:T(8,128)(2,1)S(1)}, u32[]{:S(2)}, u32[]{:S(2)}) collective-permute-start(bf16[1,96,1664]{2,1,0:T(8,128)(2,1)S(1)} %slice.411), channel_id=1, source_target_pairs={{0,4},{2,6},{8,0},{10,2},{16,8},{18,10},{24,16},{26,18},{28,24},{3... | collective-permute-start | bytes 958472 | tf_op jit(solution)/shard_map/ppermute | solution.py:690
  70.0 49.4 %collective-permute-start.26 = (bf16[512,1536]{1,0:T(8,128)(2,1)}, bf16[512,1536]{1,0:T(8,128)(2,1)}, u32[]{:S(2)}, u32[]{:S(2)}) collective-permute-start(bf16[512,1536]{1,0:T(8,128)(2,1)} %pad_maximum_fusion.6), channel_id=1, source_target_pairs={{0,2},{2,0},{4,6},{6,4},{8,10},{10,8},{12,14},{14,12},{16,18},{18,... | collective-permute-start | bytes 4718600 | tf_op jit(solution)/shard_map/ppermute | solution.py:676
  73.8 25.9 %collective-permute-start.14 = (bf16[2,96,3072]{2,1,0:T(8,128)(2,1)}, bf16[2,96,3072]{2,1,0:T(8,128)(2,1)}, u32[]{:S(2)}, u32[]{:S(2)}) collective-permute-start(bf16[2,96,3072]{2,1,0:T(8,128)(2,1)} %maximum_select_fusion), channel_id=1, source_target_pairs={{0,8},{2,10},{8,16},{10,18},{16,24},{18,26},{24,28},{26,30},{28,20... | collective-permute-start | bytes 3538952 | tf_op jit(solution)/shard_map/ppermute | solution.py:690
  75.3 25.1 %collective-permute-start.15 = (bf16[2,96,3072]{2,1,0:T(8,128)(2,1)}, bf16[2,96,3072]{2,1,0:T(8,128)(2,1)}, u32[]{:S(2)}, u32[]{:S(2)}) collective-permute-start(bf16[2,96,3072]{2,1,0:T(8,128)(2,1)} %maximum_select_fusion), channel_id=1, source_target_pairs={{0,4},{2,6},{8,0},{10,2},{16,8},{18,10},{24,16},{26,18},{28,24},{3... | collective-permute-start | bytes 3538952 | tf_op jit(solution)/shard_map/ppermute | solution.py:690
  104.0 18.5 %collective-permute-start.16 = (bf16[512,1536]{1,0:T(8,128)(2,1)}, bf16[512,1536]{1,0:T(8,128)(2,1)}, u32[]{:S(2)}, u32[]{:S(2)}) collective-permute-start(bf16[512,1536]{1,0:T(8,128)(2,1)} %convolution_convert_fusion.5), channel_id=1, source_target_pairs={{0,2},{2,0},{4,6},{6,4},{8,10},{10,8},{12,14},{14,12},{16,18},{18,... | collective-permute-start | bytes 4718600 | tf_op jit(solution)/shard_map/ppermute | solution.py:676
  105.8 28.7 %collective-permute-start.18 = (bf16[2,96,3072]{2,1,0:T(8,128)(2,1)}, bf16[2,96,3072]{2,1,0:T(8,128)(2,1)}, u32[]{:S(2)}, u32[]{:S(2)}) collective-permute-start(bf16[2,96,3072]{2,1,0:T(8,128)(2,1)} %collective-permute-done.14), channel_id=1, source_target_pairs={{0,8},{2,10},{8,16},{10,18},{16,24},{18,26},{24,28},{26,30},{28,20... | collective-permute-start | bytes 3538952 | tf_op jit(solution)/shard_map/ppermute | solution.py:690
  107.1 28.4 %collective-permute-start.19 = (bf16[2,96,3072]{2,1,0:T(8,128)(2,1)}, bf16[2,96,3072]{2,1,0:T(8,128)(2,1)}, u32[]{:S(2)}, u32[]{:S(2)}) collective-permute-start(bf16[2,96,3072]{2,1,0:T(8,128)(2,1)} %collective-permute-done.15), channel_id=1, source_target_pairs={{0,4},{2,6},{8,0},{10,2},{16,8},{18,10},{24,16},{26,18},{28,24},{3... | collective-permute-start | bytes 3538952 | tf_op jit(solution)/shard_map/ppermute | solution.py:690
  124.5 19.6 %collective-permute-start.17 = (bf16[256,1536]{1,0:T(8,128)(2,1)S(1)}, bf16[256,1536]{1,0:T(8,128)(2,1)}, u32[]{:S(2)}, u32[]{:S(2)}) collective-permute-start(bf16[256,1536]{1,0:T(8,128)(2,1)S(1)} %slice.705), channel_id=1, source_target_pairs={{0,1},{1,0},{2,3},{3,2},{4,5},{5,4},{6,7},{7,6},{8,9},{9,8},{10,11... | collective-permute-start | bytes 2359304 | tf_op jit(solution)/shard_map/ppermute | solution.py:679
  135.5 27.5 %collective-permute-start.21 = (bf16[2,96,3072]{2,1,0:T(8,128)(2,1)}, bf16[2,96,3072]{2,1,0:T(8,128)(2,1)S(1)}, u32[]{:S(2)}, u32[]{:S(2)}) collective-permute-start(bf16[2,96,3072]{2,1,0:T(8,128)(2,1)} %collective-permute-done.18), channel_id=1, source_target_pairs={{0,8},{2,10},{8,16},{10,18},{16,24},{18,26},{24,28},{26,30},{28,20... | collective-permute-start | bytes 3538952 | tf_op jit(solution)/shard_map/ppermute | solution.py:690
  136.2 27.2 %collective-permute-start.22 = (bf16[2,96,3072]{2,1,0:T(8,128)(2,1)}, bf16[2,96,3072]{2,1,0:T(8,128)(2,1)S(1)}, u32[]{:S(2)}, u32[]{:S(2)}) collective-permute-start(bf16[2,96,3072]{2,1,0:T(8,128)(2,1)} %collective-permute-done.19), channel_id=1, source_target_pairs={{0,4},{2,6},{8,0},{10,2},{16,8},{18,10},{24,16},{26,18},{28,24},{3... | collective-permute-start | bytes 3538952 | tf_op jit(solution)/shard_map/ppermute | solution.py:690
  146.5 19.5 %collective-permute-start.20 = (bf16[256,1536]{1,0:T(8,128)(2,1)S(1)}, bf16[256,1536]{1,0:T(8,128)(2,1)S(1)}, u32[]{:S(2)}, u32[]{:S(2)}) collective-permute-start(bf16[256,1536]{1,0:T(8,128)(2,1)S(1)} %multiply_convert_fusion.4), channel_id=1, source_target_pairs={{0,1},{1,0},{2,3},{3,2},{4,5},{5,4},{6,7},{7,6},{8,9},{9,8},{10,11... | collective-permute-start | bytes 2359304 | tf_op jit(solution)/shard_map/ppermute | solution.py:679
  163.4 13.9 %collective-permute-start.24 = (bf16[1,96,3072]{2,1,0:T(8,128)(2,1)S(1)}, bf16[1,96,3072]{2,1,0:T(8,128)(2,1)S(1)}, u32[]{:S(2)}, u32[]{:S(2)}) collective-permute-start(bf16[1,96,3072]{2,1,0:T(8,128)(2,1)S(1)} %slice.424), channel_id=1, source_target_pairs={{0,8},{2,10},{8,16},{10,18},{16,24},{18,26},{24,28},{26,30},{28,20... | collective-permute-start | bytes 1769480 | tf_op jit(solution)/shard_map/ppermute | solution.py:690
  164.5 13.2 %collective-permute-start.25 = (bf16[1,96,3072]{2,1,0:T(8,128)(2,1)S(1)}, bf16[1,96,3072]{2,1,0:T(8,128)(2,1)S(1)}, u32[]{:S(2)}, u32[]{:S(2)}) collective-permute-start(bf16[1,96,3072]{2,1,0:T(8,128)(2,1)S(1)} %slice.425), channel_id=1, source_target_pairs={{0,4},{2,6},{8,0},{10,2},{16,8},{18,10},{24,16},{26,18},{28,24},{3... | collective-permute-start | bytes 1769480 | tf_op jit(solution)/shard_map/ppermute | solution.py:690
  166.1 11.7 %collective-permute-start.23 = (bf16[512,1536]{1,0:T(8,128)(2,1)S(1)}, bf16[512,1536]{1,0:T(8,128)(2,1)S(1)}, u32[]{:S(2)}, u32[]{:S(2)}) collective-permute-start(bf16[512,1536]{1,0:T(8,128)(2,1)S(1)} %pad_maximum_fusion.5), channel_id=1, source_target_pairs={{0,2},{2,0},{4,6},{6,4},{8,10},{10,8},{12,14},{14,12},{16,18},{18,... | collective-permute-start | bytes 4718600 | tf_op jit(solution)/shard_map/ppermute | solution.py:676
  204.0 17.2 %collective-permute-start.27 = (bf16[1,96,1024]{2,1,0:T(8,128)(2,1)}, bf16[1,96,1024]{2,1,0:T(8,128)(2,1)S(1)}, u32[]{:S(2)}, u32[]{:S(2)}) collective-permute-start(bf16[1,96,1024]{2,1,0:T(8,128)(2,1)} %get-tuple-element.316), channel_id=1, source_target_pairs={{0,8},{2,10},{8,16},{10,18},{16,24},{18,26},{24,28},{26,30},{28,20... | collective-permute-start | bytes 589832 | tf_op jit(solution)/shard_map/ppermute | solution.py:690
  204.8 16.5 %collective-permute-start.28 = (bf16[1,96,1024]{2,1,0:T(8,128)(2,1)S(1)}, bf16[1,96,1024]{2,1,0:T(8,128)(2,1)S(1)}, u32[]{:S(2)}, u32[]{:S(2)}) collective-permute-start(bf16[1,96,1024]{2,1,0:T(8,128)(2,1)S(1)} %get-tuple-element.317), channel_id=1, source_target_pairs={{0,4},{2,6},{8,0},{10,2},{16,8},{18,10},{24,16},{26,18},{28,24},{3... | collective-permute-start | bytes 589832 | tf_op jit(solution)/shard_map/ppermute | solution.py:690
  211.1 19.5 %collective-permute-start.34 = (bf16[256,1536]{1,0:T(8,128)(2,1)}, bf16[256,1536]{1,0:T(8,128)(2,1)S(1)}, u32[]{:S(2)}, u32[]{:S(2)}) collective-permute-start(bf16[256,1536]{1,0:T(8,128)(2,1)} %slice.704), channel_id=1, source_target_pairs={{0,1},{1,0},{2,3},{3,2},{4,5},{5,4},{6,7},{7,6},{8,9},{9,8},{10,11... | collective-permute-start | bytes 2359304 | tf_op jit(solution)/shard_map/ppermute | solution.py:679
  221.4 12.0 %collective-permute-start.32 = (bf16[1,96,2048]{2,1,0:T(8,128)(2,1)S(1)}, bf16[1,96,2048]{2,1,0:T(8,128)(2,1)S(1)}, u32[]{:S(2)}, u32[]{:S(2)}) collective-permute-start(bf16[1,96,2048]{2,1,0:T(8,128)(2,1)S(1)} %get-tuple-element.306), channel_id=1, source_target_pairs={{0,8},{2,10},{8,16},{10,18},{16,24},{18,26},{24,28},{26,30},{28,20... | collective-permute-start | bytes 1179656 | tf_op jit(solution)/shard_map/ppermute | solution.py:690
  222.2 12.0 %collective-permute-start.33 = (bf16[1,96,2048]{2,1,0:T(8,128)(2,1)S(1)}, bf16[1,96,2048]{2,1,0:T(8,128)(2,1)S(1)}, u32[]{:S(2)}, u32[]{:S(2)}) collective-permute-start(bf16[1,96,2048]{2,1,0:T(8,128)(2,1)S(1)} %get-tuple-element.307), channel_id=1, source_target_pairs={{0,4},{2,6},{8,0},{10,2},{16,8},{18,10},{24,16},{26,18},{28,24},{3... | collective-permute-start | bytes 1179656 | tf_op jit(solution)/shard_map/ppermute | solution.py:690
  223.7 18.9 %collective-permute-start.31 = (bf16[2,96,1024]{2,1,0:T(8,128)(2,1)S(1)}, bf16[2,96,1024]{2,1,0:T(8,128)(2,1)S(1)}, u32[]{:S(2)}, u32[]{:S(2)}) collective-permute-start(bf16[2,96,1024]{2,1,0:T(8,128)(2,1)S(1)} %pad_maximum_fusion.15), channel_id=1, source_target_pairs={{0,4},{2,6},{8,0},{10,2},{16,8},{18,10},{24,16},{26,18},{28,24},{3... | collective-permute-start | bytes 1179656 | tf_op jit(solution)/shard_map/ppermute | solution.py:690
  225.2 17.3 %collective-permute-start.30 = (bf16[2,96,1024]{2,1,0:T(8,128)(2,1)S(1)}, bf16[2,96,1024]{2,1,0:T(8,128)(2,1)S(1)}, u32[]{:S(2)}, u32[]{:S(2)}) collective-permute-start(bf16[2,96,1024]{2,1,0:T(8,128)(2,1)S(1)} %pad_maximum_fusion.14), channel_id=1, source_target_pairs={{0,8},{2,10},{8,16},{10,18},{16,24},{18,26},{24,28},{26,30},{28,20... | collective-permute-start | bytes 1179656 | tf_op jit(solution)/shard_map/ppermute | solution.py:690
  234.5 23.3 %collective-permute-start.37 = (bf16[2,96,2048]{2,1,0:T(8,128)(2,1)S(1)}, bf16[2,96,2048]{2,1,0:T(8,128)(2,1)S(1)}, u32[]{:S(2)}, u32[]{:S(2)}) collective-permute-start(bf16[2,96,2048]{2,1,0:T(8,128)(2,1)S(1)} %pad_maximum_fusion.11), channel_id=1, source_target_pairs={{0,4},{2,6},{8,0},{10,2},{16,8},{18,10},{24,16},{26,18},{28,24},{3... | collective-permute-start | bytes 2359304 | tf_op jit(solution)/shard_map/ppermute | solution.py:690
  236.0 21.8 %collective-permute-start.36 = (bf16[2,96,2048]{2,1,0:T(8,128)(2,1)S(1)}, bf16[2,96,2048]{2,1,0:T(8,128)(2,1)S(1)}, u32[]{:S(2)}, u32[]{:S(2)}) collective-permute-start(bf16[2,96,2048]{2,1,0:T(8,128)(2,1)S(1)} %pad_maximum_fusion.10), channel_id=1, source_target_pairs={{0,8},{2,10},{8,16},{10,18},{16,24},{18,26},{24,28},{26,30},{28,20... | collective-permute-start | bytes 2359304 | tf_op jit(solution)/shard_map/ppermute | solution.py:690
  236.9 22.3 %collective-permute-start.35 = (bf16[256,1536]{1,0:T(8,128)(2,1)S(1)}, bf16[256,1536]{1,0:T(8,128)(2,1)S(1)}, u32[]{:S(2)}, u32[]{:S(2)}) collective-permute-start(bf16[256,1536]{1,0:T(8,128)(2,1)S(1)} %get-tuple-element.294), channel_id=1, source_target_pairs={{0,1},{1,0},{2,3},{3,2},{4,5},{5,4},{6,7},{7,6},{8,9},{9,8},{10,11... | collective-permute-start | bytes 2359304 | tf_op jit(solution)/shard_map/ppermute | solution.py:679
  260.7 11.5 %collective-permute-start.39 = (bf16[512,1536]{1,0:T(8,128)(2,1)}, bf16[512,1536]{1,0:T(8,128)(2,1)}, u32[]{:S(2)}, u32[]{:S(2)}) collective-permute-start(bf16[512,1536]{1,0:T(8,128)(2,1)} %convolution_convert_fusion.4), channel_id=1, source_target_pairs={{0,2},{2,0},{4,6},{6,4},{8,10},{10,8},{12,14},{14,12},{16,18},{18,... | collective-permute-start | bytes 4718600 | tf_op jit(solution)/shard_map/ppermute | solution.py:676
  263.2 13.5 %collective-permute-start.41 = (bf16[2,96,1024]{2,1,0:T(8,128)(2,1)}, bf16[2,96,1024]{2,1,0:T(8,128)(2,1)S(1)}, u32[]{:S(2)}, u32[]{:S(2)}) collective-permute-start(bf16[2,96,1024]{2,1,0:T(8,128)(2,1)} %get-tuple-element.314), channel_id=1, source_target_pairs={{0,8},{2,10},{8,16},{10,18},{16,24},{18,26},{24,28},{26,30},{28,20... | collective-permute-start | bytes 1179656 | tf_op jit(solution)/shard_map/ppermute | solution.py:690
  263.7 13.0 %collective-permute-start.42 = (bf16[2,96,1024]{2,1,0:T(8,128)(2,1)S(1)}, bf16[2,96,1024]{2,1,0:T(8,128)(2,1)S(1)}, u32[]{:S(2)}, u32[]{:S(2)}) collective-permute-start(bf16[2,96,1024]{2,1,0:T(8,128)(2,1)S(1)} %get-tuple-element.313), channel_id=1, source_target_pairs={{0,4},{2,6},{8,0},{10,2},{16,8},{18,10},{24,16},{26,18},{28,24},{3... | collective-permute-start | bytes 1179656 | tf_op jit(solution)/shard_map/ppermute | solution.py:690
  265.2 39.7 %collective-permute-start.43 = (bf16[2,96,2048]{2,1,0:T(8,128)(2,1)}, bf16[2,96,2048]{2,1,0:T(8,128)(2,1)}, u32[]{:S(2)}, u32[]{:S(2)}) collective-permute-start(bf16[2,96,2048]{2,1,0:T(8,128)(2,1)} %get-tuple-element.304), channel_id=1, source_target_pairs={{0,8},{2,10},{8,16},{10,18},{16,24},{18,26},{24,28},{26,30},{28,20... | collective-permute-start | bytes 2359304 | tf_op jit(solution)/shard_map/ppermute | solution.py:690
  265.8 39.1 %collective-permute-start.44 = (bf16[2,96,2048]{2,1,0:T(8,128)(2,1)S(1)}, bf16[2,96,2048]{2,1,0:T(8,128)(2,1)}, u32[]{:S(2)}, u32[]{:S(2)}) collective-permute-start(bf16[2,96,2048]{2,1,0:T(8,128)(2,1)S(1)} %get-tuple-element.303), channel_id=1, source_target_pairs={{0,4},{2,6},{8,0},{10,2},{16,8},{18,10},{24,16},{26,18},{28,24},{3... | collective-permute-start | bytes 2359304 | tf_op jit(solution)/shard_map/ppermute | solution.py:690
  279.1 39.4 %collective-permute-start.45 = (bf16[2,96,1024]{2,1,0:T(8,128)(2,1)}, bf16[2,96,1024]{2,1,0:T(8,128)(2,1)}, u32[]{:S(2)}, u32[]{:S(2)}) collective-permute-start(bf16[2,96,1024]{2,1,0:T(8,128)(2,1)} %get-tuple-element.312), channel_id=1, source_target_pairs={{0,8},{2,10},{8,16},{10,18},{16,24},{18,26},{24,28},{26,30},{28,20... | collective-permute-start | bytes 1179656 | tf_op jit(solution)/shard_map/ppermute | solution.py:690
  279.6 38.8 %collective-permute-start.46 = (bf16[2,96,1024]{2,1,0:T(8,128)(2,1)}, bf16[2,96,1024]{2,1,0:T(8,128)(2,1)}, u32[]{:S(2)}, u32[]{:S(2)}) collective-permute-start(bf16[2,96,1024]{2,1,0:T(8,128)(2,1)} %get-tuple-element.311), channel_id=1, source_target_pairs={{0,4},{2,6},{8,0},{10,2},{16,8},{18,10},{24,16},{26,18},{28,24},{3... | collective-permute-start | bytes 1179656 | tf_op jit(solution)/shard_map/ppermute | solution.py:690
  307.5 22.1 %collective-permute-start.47 = (bf16[2,96,2048]{2,1,0:T(8,128)(2,1)S(1)}, bf16[2,96,2048]{2,1,0:T(8,128)(2,1)S(1)}, u32[]{:S(2)}, u32[]{:S(2)}) collective-permute-start(bf16[2,96,2048]{2,1,0:T(8,128)(2,1)S(1)} %get-tuple-element.302), channel_id=1, source_target_pairs={{0,8},{2,10},{8,16},{10,18},{16,24},{18,26},{24,28},{26,30},{28,20... | collective-permute-start | bytes 2359304 | tf_op jit(solution)/shard_map/ppermute | solution.py:690
  308.2 21.6 %collective-permute-start.48 = (bf16[2,96,2048]{2,1,0:T(8,128)(2,1)S(1)}, bf16[2,96,2048]{2,1,0:T(8,128)(2,1)S(1)}, u32[]{:S(2)}, u32[]{:S(2)}) collective-permute-start(bf16[2,96,2048]{2,1,0:T(8,128)(2,1)S(1)} %get-tuple-element.301), channel_id=1, source_target_pairs={{0,4},{2,6},{8,0},{10,2},{16,8},{18,10},{24,16},{26,18},{28,24},{3... | collective-permute-start | bytes 2359304 | tf_op jit(solution)/shard_map/ppermute | solution.py:690
  310.0 21.8 %collective-permute-start.40 = (bf16[256,1536]{1,0:T(8,128)(2,1)S(1)}, bf16[256,1536]{1,0:T(8,128)(2,1)S(1)}, u32[]{:S(2)}, u32[]{:S(2)}) collective-permute-start(bf16[256,1536]{1,0:T(8,128)(2,1)S(1)} %copy-done.21), channel_id=1, source_target_pairs={{0,1},{1,0},{2,3},{3,2},{4,5},{5,4},{6,7},{7,6},{8,9},{9,8},{10,11... | collective-permute-start | bytes 2359304 | tf_op jit(solution)/shard_map/ppermute | solution.py:679
  321.8 11.8 %collective-permute-start.53 = (bf16[1,96,896]{2,1,0:T(8,128)(2,1)S(1)}, bf16[1,96,896]{2,1,0:T(8,128)(2,1)S(1)}, u32[]{:S(2)}, u32[]{:S(2)}) collective-permute-start(bf16[1,96,896]{2,1,0:T(8,128)(2,1)S(1)} %get-tuple-element.200), channel_id=1, source_target_pairs={{0,8},{2,10},{8,16},{10,18},{16,24},{18,26},{24,28},{26,30},{28,20... | collective-permute-start | bytes 516104 | tf_op jit(solution)/shard_map/ppermute | solution.py:690
  327.1 8.0 %collective-permute-start.54 = (bf16[1,96,896]{2,1,0:T(8,128)(2,1)S(1)}, bf16[1,96,896]{2,1,0:T(8,128)(2,1)S(1)}, u32[]{:S(2)}, u32[]{:S(2)}) collective-permute-start(bf16[1,96,896]{2,1,0:T(8,128)(2,1)S(1)} %get-tuple-element.201), channel_id=1, source_target_pairs={{0,4},{2,6},{8,0},{10,2},{16,8},{18,10},{24,16},{26,18},{28,24},{3... | collective-permute-start | bytes 516104 | tf_op jit(solution)/shard_map/ppermute | solution.py:690
  329.6 13.7 %collective-permute-start.49 = (bf16[512,1536]{1,0:T(8,128)(2,1)S(1)}, bf16[512,1536]{1,0:T(8,128)(2,1)S(1)}, u32[]{:S(2)}, u32[]{:S(2)}) collective-permute-start(bf16[512,1536]{1,0:T(8,128)(2,1)S(1)} %fusion.13), channel_id=1, source_target_pairs={{0,2},{2,0},{4,6},{6,4},{8,10},{10,8},{12,14},{14,12},{16,18},{18,... | collective-permute-start | bytes 4718600 | tf_op jit(solution)/shard_map/ppermute | solution.py:676
  331.4 14.1 %collective-permute-start.74 = (bf16[96,2048]{1,0:T(8,128)(2,1)S(1)}, bf16[96,2048]{1,0:T(8,128)(2,1)S(1)}, u32[]{:S(2)}, u32[]{:S(2)}) collective-permute-start(bf16[96,2048]{1,0:T(8,128)(2,1)S(1)} %dynamic-slice_convert_fusion), channel_id=1, source_target_pairs={{0,2},{2,0},{4,6},{6,4},{8,10},{10,8},{12,14},{14,12},{16,18},{18,... | collective-permute-start | bytes 1179656 | tf_op jit(solution)/shard_map/ppermute | solution.py:676
  333.0 8.0 %collective-permute-start.51 = (bf16[1,96,768]{2,1,0:T(8,128)(2,1)S(1)}, bf16[1,96,768]{2,1,0:T(8,128)(2,1)S(1)}, u32[]{:S(2)}, u32[]{:S(2)}) collective-permute-start(bf16[1,96,768]{2,1,0:T(8,128)(2,1)S(1)} %get-tuple-element.205), channel_id=1, source_target_pairs={{0,8},{2,10},{8,16},{10,18},{16,24},{18,26},{24,28},{26,30},{28,20... | collective-permute-start | bytes 442376 | tf_op jit(solution)/shard_map/ppermute | solution.py:690
  333.6 8.2 %collective-permute-start.52 = (bf16[1,96,768]{2,1,0:T(8,128)(2,1)S(1)}, bf16[1,96,768]{2,1,0:T(8,128)(2,1)S(1)}, u32[]{:S(2)}, u32[]{:S(2)}) collective-permute-start(bf16[1,96,768]{2,1,0:T(8,128)(2,1)S(1)} %get-tuple-element.206), channel_id=1, source_target_pairs={{0,4},{2,6},{8,0},{10,2},{16,8},{18,10},{24,16},{26,18},{28,24},{3... | collective-permute-start | bytes 442376 | tf_op jit(solution)/shard_map/ppermute | solution.py:690
  335.2 27.7 %collective-permute-start.57 = (bf16[2,96,896]{2,1,0:T(8,128)(2,1)S(1)}, bf16[2,96,896]{2,1,0:T(8,128)(2,1)S(1)}, u32[]{:S(2)}, u32[]{:S(2)}) collective-permute-start(bf16[2,96,896]{2,1,0:T(8,128)(2,1)S(1)} %pad_maximum_fusion.17), channel_id=1, source_target_pairs={{0,4},{2,6},{8,0},{10,2},{16,8},{18,10},{24,16},{26,18},{28,24},{3... | collective-permute-start | bytes 1032200 | tf_op jit(solution)/shard_map/ppermute | solution.py:690
  341.1 21.9 %collective-permute-start.56 = (bf16[2,96,896]{2,1,0:T(8,128)(2,1)S(1)}, bf16[2,96,896]{2,1,0:T(8,128)(2,1)S(1)}, u32[]{:S(2)}, u32[]{:S(2)}) collective-permute-start(bf16[2,96,896]{2,1,0:T(8,128)(2,1)S(1)} %pad_maximum_fusion.16), channel_id=1, source_target_pairs={{0,8},{2,10},{8,16},{10,18},{16,24},{18,26},{24,28},{26,30},{28,20... | collective-permute-start | bytes 1032200 | tf_op jit(solution)/shard_map/ppermute | solution.py:690
  341.9 23.3 %collective-permute-start.62 = (bf16[2,96,768]{2,1,0:T(8,128)(2,1)S(1)}, bf16[2,96,768]{2,1,0:T(8,128)(2,1)S(1)}, u32[]{:S(2)}, u32[]{:S(2)}) collective-permute-start(bf16[2,96,768]{2,1,0:T(8,128)(2,1)S(1)} %pad_maximum_fusion.19), channel_id=1, source_target_pairs={{0,4},{2,6},{8,0},{10,2},{16,8},{18,10},{24,16},{26,18},{28,24},{3... | collective-permute-start | bytes 884744 | tf_op jit(solution)/shard_map/ppermute | solution.py:690
  343.9 18.4 %collective-permute-start.50 = (bf16[256,1536]{1,0:T(8,128)(2,1)S(1)}, bf16[256,1536]{1,0:T(8,128)(2,1)S(1)}, u32[]{:S(2)}, u32[]{:S(2)}) collective-permute-start(bf16[256,1536]{1,0:T(8,128)(2,1)S(1)} %slice.702), channel_id=1, source_target_pairs={{0,1},{1,0},{2,3},{3,2},{4,5},{5,4},{6,7},{7,6},{8,9},{9,8},{10,11... | collective-permute-start | bytes 2359304 | tf_op jit(solution)/shard_map/ppermute | solution.py:679
  345.5 19.7 %collective-permute-start.61 = (bf16[2,96,768]{2,1,0:T(8,128)(2,1)S(1)}, bf16[2,96,768]{2,1,0:T(8,128)(2,1)S(1)}, u32[]{:S(2)}, u32[]{:S(2)}) collective-permute-start(bf16[2,96,768]{2,1,0:T(8,128)(2,1)S(1)} %pad_maximum_fusion.18), channel_id=1, source_target_pairs={{0,8},{2,10},{8,16},{10,18},{16,24},{18,26},{24,28},{26,30},{28,20... | collective-permute-start | bytes 884744 | tf_op jit(solution)/shard_map/ppermute | solution.py:690
  363.2 12.1 %collective-permute-start.58 = (bf16[2,96,896]{2,1,0:T(8,128)(2,1)S(1)}, bf16[2,96,896]{2,1,0:T(8,128)(2,1)S(1)}, u32[]{:S(2)}, u32[]{:S(2)}) collective-permute-start(bf16[2,96,896]{2,1,0:T(8,128)(2,1)S(1)} %get-tuple-element.324), channel_id=1, source_target_pairs={{0,8},{2,10},{8,16},{10,18},{16,24},{18,26},{24,28},{26,30},{28,20... | collective-permute-start | bytes 1032200 | tf_op jit(solution)/shard_map/ppermute | solution.py:690
  363.9 11.4 %collective-permute-start.59 = (bf16[2,96,896]{2,1,0:T(8,128)(2,1)S(1)}, bf16[2,96,896]{2,1,0:T(8,128)(2,1)S(1)}, u32[]{:S(2)}, u32[]{:S(2)}) collective-permute-start(bf16[2,96,896]{2,1,0:T(8,128)(2,1)S(1)} %get-tuple-element.323), channel_id=1, source_target_pairs={{0,4},{2,6},{8,0},{10,2},{16,8},{18,10},{24,16},{26,18},{28,24},{3... | collective-permute-start | bytes 1032200 | tf_op jit(solution)/shard_map/ppermute | solution.py:690
  365.3 9.9 %collective-permute-start.55 = (f32[8,1536]{1,0:T(8,128)S(1)}, f32[8,1536]{1,0:T(8,128)S(1)}, u32[]{:S(2)}, u32[]{:S(2)}) collective-permute-start(f32[8,1536]{1,0:T(8,128)S(1)} %pad_maximum_fusion.21), channel_id=1, source_target_pairs={{0,4},{2,6},{4,0},{6,2},{8,12},{10,14},{12,8},{14,10},{16,20},{18,... | collective-permute-start | bytes 147464 | tf_op jit(solution)/shard_map/ppermute | solution.py:702
  366.9 13.5 %collective-permute-start.63 = (bf16[2,96,768]{2,1,0:T(8,128)(2,1)S(1)}, bf16[2,96,768]{2,1,0:T(8,128)(2,1)S(1)}, u32[]{:S(2)}, u32[]{:S(2)}) collective-permute-start(bf16[2,96,768]{2,1,0:T(8,128)(2,1)S(1)} %get-tuple-element.334), channel_id=1, source_target_pairs={{0,8},{2,10},{8,16},{10,18},{16,24},{18,26},{24,28},{26,30},{28,20... | collective-permute-start | bytes 884744 | tf_op jit(solution)/shard_map/ppermute | solution.py:690
  368.3 12.2 %collective-permute-start.64 = (bf16[2,96,768]{2,1,0:T(8,128)(2,1)S(1)}, bf16[2,96,768]{2,1,0:T(8,128)(2,1)S(1)}, u32[]{:S(2)}, u32[]{:S(2)}) collective-permute-start(bf16[2,96,768]{2,1,0:T(8,128)(2,1)S(1)} %get-tuple-element.333), channel_id=1, source_target_pairs={{0,4},{2,6},{8,0},{10,2},{16,8},{18,10},{24,16},{26,18},{28,24},{3... | collective-permute-start | bytes 884744 | tf_op jit(solution)/shard_map/ppermute | solution.py:690
  384.5 14.3 %collective-permute-start.68 = (bf16[2,96,896]{2,1,0:T(8,128)(2,1)}, bf16[2,96,896]{2,1,0:T(8,128)(2,1)S(1)}, u32[]{:S(2)}, u32[]{:S(2)}) collective-permute-start(bf16[2,96,896]{2,1,0:T(8,128)(2,1)} %get-tuple-element.322), channel_id=1, source_target_pairs={{0,8},{2,10},{8,16},{10,18},{16,24},{18,26},{24,28},{26,30},{28,20... | collective-permute-start | bytes 1032200 | tf_op jit(solution)/shard_map/ppermute | solution.py:690
  386.3 13.3 %collective-permute-start.69 = (bf16[2,96,896]{2,1,0:T(8,128)(2,1)}, bf16[2,96,896]{2,1,0:T(8,128)(2,1)}, u32[]{:S(2)}, u32[]{:S(2)}) collective-permute-start(bf16[2,96,896]{2,1,0:T(8,128)(2,1)} %get-tuple-element.321), channel_id=1, source_target_pairs={{0,4},{2,6},{8,0},{10,2},{16,8},{18,10},{24,16},{26,18},{28,24},{3... | collective-permute-start | bytes 1032200 | tf_op jit(solution)/shard_map/ppermute | solution.py:690
  386.6 9.2 %collective-permute-start.71 = (bf16[2,96,768]{2,1,0:T(8,128)(2,1)}, bf16[2,96,768]{2,1,0:T(8,128)(2,1)S(1)}, u32[]{:S(2)}, u32[]{:S(2)}) collective-permute-start(bf16[2,96,768]{2,1,0:T(8,128)(2,1)} %get-tuple-element.332), channel_id=1, source_target_pairs={{0,8},{2,10},{8,16},{10,18},{16,24},{18,26},{24,28},{26,30},{28,20... | collective-permute-start | bytes 884744 | tf_op jit(solution)/shard_map/ppermute | solution.py:690
  388.4 9.2 %collective-permute-start.72 = (bf16[2,96,768]{2,1,0:T(8,128)(2,1)}, bf16[2,96,768]{2,1,0:T(8,128)(2,1)}, u32[]{:S(2)}, u32[]{:S(2)}) collective-permute-start(bf16[2,96,768]{2,1,0:T(8,128)(2,1)} %get-tuple-element.331), channel_id=1, source_target_pairs={{0,4},{2,6},{8,0},{10,2},{16,8},{18,10},{24,16},{26,18},{28,24},{3... | collective-permute-start | bytes 884744 | tf_op jit(solution)/shard_map/ppermute | solution.py:690
  (61 other events, 626.7 us)

commit v7 on v6

--- a/solution.py
+++ b/solution.py
@@ -833,7 +833,7 @@
     normed_one = (unit_all * gain_one).astype(BF16)
     x_own, scale_one = first_norm(layer_in)
     unit_one = x_own * scale_one
-    qkv = dot_nn(normed_one, w_qkv).astype(BF16)
+    qkv = dot_nn(normed_one, w_in).astype(BF16)
 
     bias = lax.dynamic_slice_in_dim(forget_bias, at.core * heads, heads, 0)
     logits = dot_nt(after(forget_t, qkv), normed_one) + bias[:, None]

time: 413 us -> 413 us (level)
  no operation moved by 1% of the time
where the time goes in v7:
time: 413 us; the launch traced here: 406 us
  waiting for transfers between devices  109 us (26%)
  matrix products  80.9 us (20%)
  starting transfers between devices  70.4 us (17%)
  other arithmetic  53.3 us (13%)
  local copies, waits for them, and re-layouts  48.2 us (12%)
  Pallas kernels  42.2 us (10%)
    ppermute x48, waiting for transfers between devices, ring(): return lax.ppermute(value, 'dp', pairs)  65 us
    ppermute x48, starting transfers between devices, ring(): return lax.ppermute(value, 'dp', pairs)  51.6 us
    ppermute x9, waiting for transfers between devices, swap_y(): return lax.ppermute(value, 'tensor', [(0, 1), (1, 0)])  31.9 us
    dot_general x4, matrix products, dot_nn(): lax.dot_general(left, right, (((1,), (0,)), ((), ())), preferred_element_...  29.8 us
    dot_general x9, matrix products, dot_nt(): lax.dot_general(left, right, (((1,), (1,)), ((), ())), preferred_element_...  29.2 us
    pallas_call x1, Pallas kernels, attend_back(): pl.pallas_call(partial(attend_back_kernel, pairs), grid_spec=grid_spec, o...  21.8 us
    dot_general x5, matrix products, dot_tn(): lax.dot_general(left, right, (((0,), (0,)), ((), ())), preferred_element_...  21.7 us
    dynamic_update_slice x17, local copies, waits for them, and re-layouts, store(): self.whole = lax.dynamic_update_slice(self.whole, part[None], start)  18.5 us
  transfers between devices with their start and end apart: 76, of which 27 were waited for; matrix products, arithmetic and copies ran while one was open for 35% of the time, Pallas kernels for 10%

profile of v7, /device:TPU:0, one launch (start us, length us, event | category | flops | bytes accessed | tf_op | source)
XLA Modules:
  0.0 406.2 jit_solution(15313822030974315554)
XLA Ops:
  6.7 2.6 collective-permute-start
  10.5 1.6 collective-permute-start.3
  13.6 2.8 broadcast_in_dim.102
  17.4 10.2 %collective-permute-done = bf16[256,1536]{1,0:T(8,128)(2,1)S(1)} collective-permute-done((bf16[256,1536]{1,0:T(8,128)(2,1)}, bf16[256,1536]{1,0:T(8,128)(2,1)S(1)}, u32[]{:S(2)}, u32[]{:S(2)}) %collective-permute-start) | collective-permute-done | bytes 786464 | tf_op jit(solution)/shard_map/ppermute | solution.py:679
  29.0 1.9 collective-permute-start.5
  32.9 2.0 bitcast_dynamic-update-slice_fusion.12
  34.9 2.0 bitcast_dynamic-update-slice_fusion.11
  36.9 2.5 maximum_select_fusion
  39.3 6.7 %collective-permute-done.5 = bf16[2,96,1664]{2,1,0:T(8,128)(2,1)} collective-permute-done((bf16[2,96,1664]{2,1,0:T(8,128)(2,1)}, bf16[2,96,1664]{2,1,0:T(8,128)(2,1)}, u32[]{:S(2)}, u32[]{:S(2)}) %collective-permute-start.5) | collective-permute-done | bytes 639008 | tf_op jit(solution)/shard_map/ppermute | solution.py:690
  51.1 1.9 bitcast_dynamic-update-slice_fusion.10
  53.1 2.0 bitcast_dynamic-update-slice_fusion.9
  55.1 1.9 fusion
  57.0 3.9 convert_multiply_fusion
  60.9 2.5 collective-permute-done.7
  64.7 1.6 collective-permute-start.10
  70.0 2.4 collective-permute-done.10
  79.9 8.7 %convolution_convert_fusion.1.qkv_ref = bf16[1024,1280]{1,0:T(8,128)(2,1)} fusion(bf16[1024,1536]{1,0:T(8,128)(2,1)S(1)} %multiply_convert_fusion, bf16[1536,1664]{1,0:T(8,128)(2,1)} %bitcast.17), kind=kOutput, calls=%fused_computation.33 | convolution fusion | flops 4027842560 | bytes 9699328 | tf_op jit(solution)/shard_map/dot_general | solution.py:320
  90.9 9.0 %attend.2 = (bf16[512,384]{1,0:T(8,128)(2,1)}, f32[1024,384]{1,0:T(8,128)}, bf16[2,3,2,256,768]{4,3,2,1,0:T(8,128)(2,1)}, f32[1,3,8,128]{3,2,1,0:T(8,128)}) custom-call(s32[1]{0:T(128)} %bitcast.y_ref, bf16[1024,1280]{1,0:T(8,128)(2,1)} %convolution_convert_fusion.1.qkv_ref, f32[3,8,1024]{2,1,0:T(8,128)} %maximum_maximum_fusion.aux_ref), custom_call_target="tpu_custom_call" | custom-call | flops 603979776 | bytes 10000000 | tf_op jit(solution)/shard_map/attend/pallas_call | solution.py:396
  100.4 3.6 convolution_convert_fusion.5
  104.1 1.6 copy-done.33
  107.8 9.0 %attend.3 = (bf16[512,384]{1,0:T(8,128)(2,1)}, f32[1024,384]{1,0:T(8,128)}, bf16[2,3,2,256,768]{4,3,2,1,0:T(8,128)(2,1)}, f32[1,3,8,128]{3,2,1,0:T(8,128)}) custom-call(s32[1]{0:T(128)} %bitcast.y_ref, bf16[1024,1280]{1,0:T(8,128)(2,1)} %convolution_convert_fusion.1.qkv_ref, ...), custom_call_target="tpu_custom_call", output_to_operand_aliasing={{1}: (3, {}), {2}: (4, {})} | custom-call | flops 603979776 | bytes 10000000 | tf_op jit(solution)/shard_map/attend/pallas_call | solution.py:396
  116.8 2.5 fusion.49
  120.9 1.7 copy-done.35
  122.6 1.9 convert_add_fusion.3
  124.6 1.6 collective-permute-start.17
  126.2 8.3 %collective-permute-done.18 = bf16[2,96,3072]{2,1,0:T(8,128)(2,1)} collective-permute-done((bf16[2,96,3072]{2,1,0:T(8,128)(2,1)}, bf16[2,96,3072]{2,1,0:T(8,128)(2,1)}, u32[]{:S(2)}, u32[]{:S(2)}) %collective-permute-start.18) | collective-permute-done | bytes 1179680 | tf_op jit(solution)/shard_map/ppermute | solution.py:690
  144.1 2.2 multiply_reduce_fusion.2
  146.6 1.6 collective-permute-start.20
  151.0 12.0 %collective-permute-done.21 = bf16[2,96,3072]{2,1,0:T(8,128)(2,1)S(1)} collective-permute-done((bf16[2,96,3072]{2,1,0:T(8,128)(2,1)}, bf16[2,96,3072]{2,1,0:T(8,128)(2,1)S(1)}, u32[]{:S(2)}, u32[]{:S(2)}) %collective-permute-start.21) | collective-permute-done | bytes 1179680 | tf_op jit(solution)/shard_map/ppermute | solution.py:690
  166.5 10.9 %collective-permute-done.24 = bf16[1,96,3072]{2,1,0:T(8,128)(2,1)S(1)} collective-permute-done((bf16[1,96,3072]{2,1,0:T(8,128)(2,1)S(1)}, bf16[1,96,3072]{2,1,0:T(8,128)(2,1)S(1)}, u32[]{:S(2)}, u32[]{:S(2)}) %collective-permute-start.24) | collective-permute-done | bytes 589856 | tf_op jit(solution)/shard_map/ppermute | solution.py:690
  179.0 8.7 %fusion.5 = f32[1024,2048]{1,0:T(8,128)} fusion(bf16[1536,3072]{1,0:T(8,128)(2,1)S(1)} %bitcast.245, bf16[512,1536]{1,0:T(8,128)(2,1)S(1)} %collective-permute-done.23, bf16[256,1536]{1,0:T(8,128)(2,1)S(1)} %collective-permute-done.20, bf16[256,1536]{1,0:T(8,128)(2,1)S(1)} %multiply_convert_fusion.4), kind=kOutput, calls=%fused_computation.9 | convolution fusion | flops 6451888128 | bytes 17825792 | tf_op jit(solution)/shard_map/dot_general | solution.py:320
  187.8 7.5 %multiply_convert_fusion.2 = (bf16[1024,1024]{1,0:T(8,128)(2,1)S(1)}, bf16[1024,1024]{1,0:T(8,128)(2,1)S(1)}, bf16[1024,1024]{1,0:T(8,128)(2,1)S(1)}) fusion(f32[1024,2048]{1,0:T(8,128)} %fusion.5, bf16[1024,1536]{1,0:T(8,128)(2,1)S(1)} %copy-done.36, bf16[1536,3072]{1,0:T(8,128)(2,1)S(1)} %bitcast.246), kind=kOutput, calls=%fused_computation.29 | convolution fusion | flops 3236954112 | bytes 20971520 | tf_op jit(solution)/shard_map/dot_general | solution.py:320
  195.3 3.7 convolution_convert_fusion.2
  200.5 3.5 fusion.16
  206.3 3.5 fusion.1
  212.7 8.6 %convolution_convert_fusion = bf16[1536,2048]{1,0:T(8,128)(2,1)S(1)} fusion(bf16[1024,2048]{1,0:T(8,128)(2,1)S(1)} %pad_maximum_fusion, bf16[512,1536]{1,0:T(8,128)(2,1)} %copy-done.45, bf16[256,1536]{1,0:T(8,128)(2,1)} %copy-done.24, bf16[256,1536]{1,0:T(8,128)(2,1)S(1)} %copy-done.17), kind=kOutput, calls=%fused_computation.2 | convolution fusion | flops 6455033856 | bytes 13631488 | tf_op jit(solution)/shard_map/dot_general | solution.py:324
  225.9 4.8 %collective-permute-done.34 = bf16[256,1536]{1,0:T(8,128)(2,1)S(1)} collective-permute-done((bf16[256,1536]{1,0:T(8,128)(2,1)}, bf16[256,1536]{1,0:T(8,128)(2,1)S(1)}, u32[]{:S(2)}, u32[]{:S(2)}) %collective-permute-start.34) | collective-permute-done | bytes 786464 | tf_op jit(solution)/shard_map/ppermute | solution.py:679
  231.3 1.7 fusion.106
  237.4 3.0 convolution_convert_fusion.4
  240.4 2.2 collective-permute-done.31
  243.7 3.5 fusion.19
  247.1 10.6 %collective-permute-done.37 = bf16[2,96,2048]{2,1,0:T(8,128)(2,1)S(1)} collective-permute-done((bf16[2,96,2048]{2,1,0:T(8,128)(2,1)S(1)}, bf16[2,96,2048]{2,1,0:T(8,128)(2,1)S(1)}, u32[]{:S(2)}, u32[]{:S(2)}) %collective-permute-start.37) | collective-permute-done | bytes 786464 | tf_op jit(solution)/shard_map/ppermute | solution.py:690
  267.3 4.9 %convolution_convert_fusion.8.do_ref = bf16[1024,384]{1,0:T(8,128)(2,1)} fusion(bf16[1536,1664]{1,0:T(8,128)(2,1)} %bitcast.17, bf16[512,1536]{1,0:T(8,128)(2,1)} %collective-permute-done.38, bf16[256,1536]{1,0:T(8,128)(2,1)} %copy-done.22, bf16[256,1536]{1,0:T(8,128)(2,1)} %copy-done.12), kind=kOutput, calls=%fused_computation.104 | convolution fusion | flops 1217789952 | bytes 5111808 | tf_op jit(solution)/shard_map/dot_general | solution.py:320
  272.2 1.9 convert_add_fusion.1
  274.1 1.6 copy-done.5
  276.7 2.3 fusion.57
  281.1 21.8 %attend_back.1 = (bf16[1024,1152]{1,0:T(8,128)(2,1)}, bf16[1024,128]{1,0:T(8,128)(2,1)}) custom-call(s32[1]{0:T(128)} %bitcast.y_ref, bf16[1024,1280]{1,0:T(8,128)(2,1)} %convolution_convert_fusion.1.qkv_ref, bf16[1024,384]{1,0:T(8,128)(2,1)} %convolution_convert_fusion.8.do_ref, f32[1024,384]{1,0:T(8,128)} %get-tuple-element.190.inv_ref, ...), custom_call_target="tpu_custom_call" | custom-call | flops 3623878656 | bytes 20000000 | tf_op jit(solution)/shard_map/attend_back/pallas_call | solution.py:534
  302.9 2.0 constant_dynamic-update-slice_fusion.4
  304.9 2.6 fusion.40
  308.2 1.8 collective-permute-start.48
  310.4 3.7 convolution_convert_fusion.3
  314.5 3.8 convolution_convert_fusion.6
  319.9 1.8 convolution_convert_fusion.7
  322.5 4.3 %fusion.13 = bf16[512,1536]{1,0:T(8,128)(2,1)S(1)} fusion(bf16[1536,1664]{1,0:T(8,128)(2,1)} %bitcast.17, bf16[1024,1280]{1,0:T(8,128)(2,1)S(1)} %constant_dynamic-update-slice_fusion.3), kind=kOutput, calls=%fused_computation.48 | convolution fusion | flops 2014052352 | bytes 6815744 | tf_op jit(solution)/shard_map/dot_general | solution.py:316
  336.6 4.3 %fusion.8 = f32[512,1536]{1,0:T(8,128)S(1)} fusion(bf16[1536,1664]{1,0:T(8,128)(2,1)} %bitcast.17, bf16[1024,1280]{1,0:T(8,128)(2,1)S(1)} %constant_dynamic-update-slice_fusion.3), kind=kOutput, calls=%fused_computation.43 | convolution fusion | flops 2013265920 | bytes 8388608 | tf_op jit(solution)/shard_map/dot_general | solution.py:316
  343.9 1.6 collective-permute-start.50
  348.5 13.8 %collective-permute-done.50 = bf16[256,1536]{1,0:T(8,128)(2,1)S(1)} collective-permute-done((bf16[256,1536]{1,0:T(8,128)(2,1)S(1)}, bf16[256,1536]{1,0:T(8,128)(2,1)S(1)}, u32[]{:S(2)}, u32[]{:S(2)}) %collective-permute-start.50) | collective-permute-done | bytes 786464 | tf_op jit(solution)/shard_map/ppermute | solution.py:679
  369.0 6.2 %collective-permute-done.55 = f32[8,1536]{1,0:T(8,128)S(1)} collective-permute-done((f32[8,1536]{1,0:T(8,128)S(1)}, f32[8,1536]{1,0:T(8,128)S(1)}, u32[]{:S(2)}, u32[]{:S(2)}) %collective-permute-start.55) | collective-permute-done | bytes 49184 | tf_op jit(solution)/shard_map/ppermute | solution.py:702
  376.4 4.1 collective-permute-done.60
  381.5 1.6 collective-permute-start.65
  384.5 2.3 collective-permute-start.68
  386.8 2.0 collective-permute-start.71
  393.6 1.9 collective-permute-done.67
  403.3 2.4 assemble.1
  (388 shorter events, 126.4 us)
Async XLA Ops:
  6.7 20.9 %collective-permute-start = (bf16[256,1536]{1,0:T(8,128)(2,1)}, bf16[256,1536]{1,0:T(8,128)(2,1)S(1)}, u32[]{:S(2)}, u32[]{:S(2)}) collective-permute-start(bf16[256,1536]{1,0:T(8,128)(2,1)} %param.15), channel_id=1, source_target_pairs={{0,1},{1,0},{2,3},{3,2},{4,5},{5,4},{6,7},{7,6},{8,9},{9,8},{10,11... | collective-permute-start | bytes 2359304 | tf_op jit(solution)/shard_map/ppermute | solution.py:679
  10.5 18.4 %collective-permute-start.3 = (bf16[2,96,1664]{2,1,0:T(8,128)(2,1)S(1)}, bf16[2,96,1664]{2,1,0:T(8,128)(2,1)}, u32[]{:S(2)}, u32[]{:S(2)}) collective-permute-start(bf16[2,96,1664]{2,1,0:T(8,128)(2,1)S(1)} %maximum_select_fusion.4), channel_id=1, source_target_pairs={{0,8},{2,10},{8,16},{10,18},{16,24},{18,26},{24,28},{26,30},{28,20... | collective-permute-start | bytes 1916936 | tf_op jit(solution)/shard_map/ppermute | solution.py:690
  12.1 16.8 %collective-permute-start.4 = (bf16[2,96,1664]{2,1,0:T(8,128)(2,1)S(1)}, bf16[2,96,1664]{2,1,0:T(8,128)(2,1)}, u32[]{:S(2)}, u32[]{:S(2)}) collective-permute-start(bf16[2,96,1664]{2,1,0:T(8,128)(2,1)S(1)} %maximum_select_fusion.4), channel_id=1, source_target_pairs={{0,4},{2,6},{8,0},{10,2},{16,8},{18,10},{24,16},{26,18},{28,24},{3... | collective-permute-start | bytes 1916936 | tf_op jit(solution)/shard_map/ppermute | solution.py:690
  28.9 26.1 %collective-permute-start.1 = (bf16[512,1536]{1,0:T(8,128)(2,1)}, bf16[512,1536]{1,0:T(8,128)(2,1)}, u32[]{:S(2)}, u32[]{:S(2)}) collective-permute-start(bf16[512,1536]{1,0:T(8,128)(2,1)} %pad_maximum_fusion.4), channel_id=1, source_target_pairs={{0,2},{2,0},{4,6},{6,4},{8,10},{10,8},{12,14},{14,12},{16,18},{18,... | collective-permute-start | bytes 4718600 | tf_op jit(solution)/shard_map/ppermute | solution.py:676
  29.0 17.1 %collective-permute-start.5 = (bf16[2,96,1664]{2,1,0:T(8,128)(2,1)}, bf16[2,96,1664]{2,1,0:T(8,128)(2,1)}, u32[]{:S(2)}, u32[]{:S(2)}) collective-permute-start(bf16[2,96,1664]{2,1,0:T(8,128)(2,1)} %collective-permute-done.3), channel_id=1, source_target_pairs={{0,8},{2,10},{8,16},{10,18},{16,24},{18,26},{24,28},{26,30},{28,20... | collective-permute-start | bytes 1916936 | tf_op jit(solution)/shard_map/ppermute | solution.py:690
  30.8 16.8 %collective-permute-start.6 = (bf16[2,96,1664]{2,1,0:T(8,128)(2,1)}, bf16[2,96,1664]{2,1,0:T(8,128)(2,1)}, u32[]{:S(2)}, u32[]{:S(2)}) collective-permute-start(bf16[2,96,1664]{2,1,0:T(8,128)(2,1)} %collective-permute-done.4), channel_id=1, source_target_pairs={{0,4},{2,6},{8,0},{10,2},{16,8},{18,10},{24,16},{26,18},{28,24},{3... | collective-permute-start | bytes 1916936 | tf_op jit(solution)/shard_map/ppermute | solution.py:690
  47.6 15.8 %collective-permute-start.7 = (bf16[2,96,1664]{2,1,0:T(8,128)(2,1)}, bf16[2,96,1664]{2,1,0:T(8,128)(2,1)S(1)}, u32[]{:S(2)}, u32[]{:S(2)}) collective-permute-start(bf16[2,96,1664]{2,1,0:T(8,128)(2,1)} %collective-permute-done.5), channel_id=1, source_target_pairs={{0,8},{2,10},{8,16},{10,18},{16,24},{18,26},{24,28},{26,30},{28,20... | collective-permute-start | bytes 1916936 | tf_op jit(solution)/shard_map/ppermute | solution.py:690
  49.2 15.5 %collective-permute-start.8 = (bf16[2,96,1664]{2,1,0:T(8,128)(2,1)}, bf16[2,96,1664]{2,1,0:T(8,128)(2,1)S(1)}, u32[]{:S(2)}, u32[]{:S(2)}) collective-permute-start(bf16[2,96,1664]{2,1,0:T(8,128)(2,1)} %collective-permute-done.6), channel_id=1, source_target_pairs={{0,4},{2,6},{8,0},{10,2},{16,8},{18,10},{24,16},{26,18},{28,24},{3... | collective-permute-start | bytes 1916936 | tf_op jit(solution)/shard_map/ppermute | solution.py:690
  49.6 19.0 %collective-permute-start.13 = (bf16[256,1536]{1,0:T(8,128)(2,1)S(1)}, bf16[256,1536]{1,0:T(8,128)(2,1)S(1)}, u32[]{:S(2)}, u32[]{:S(2)}) collective-permute-start(bf16[256,1536]{1,0:T(8,128)(2,1)S(1)} %copy-done.7), channel_id=1, source_target_pairs={{0,1},{1,0},{2,3},{3,2},{4,5},{5,4},{6,7},{7,6},{8,9},{9,8},{10,11... | collective-permute-start | bytes 2359304 | tf_op jit(solution)/shard_map/ppermute | solution.py:679
  64.7 7.7 %collective-permute-start.10 = (bf16[1,96,1664]{2,1,0:T(8,128)(2,1)S(1)}, bf16[1,96,1664]{2,1,0:T(8,128)(2,1)S(1)}, u32[]{:S(2)}, u32[]{:S(2)}) collective-permute-start(bf16[1,96,1664]{2,1,0:T(8,128)(2,1)S(1)} %slice.406), channel_id=1, source_target_pairs={{0,8},{2,10},{8,16},{10,18},{16,24},{18,26},{24,28},{26,30},{28,20... | collective-permute-start | bytes 958472 | tf_op jit(solution)/shard_map/ppermute | solution.py:690
  66.4 7.4 %collective-permute-start.11 = (bf16[1,96,1664]{2,1,0:T(8,128)(2,1)S(1)}, bf16[1,96,1664]{2,1,0:T(8,128)(2,1)S(1)}, u32[]{:S(2)}, u32[]{:S(2)}) collective-permute-start(bf16[1,96,1664]{2,1,0:T(8,128)(2,1)S(1)} %slice.407), channel_id=1, source_target_pairs={{0,4},{2,6},{8,0},{10,2},{16,8},{18,10},{24,16},{26,18},{28,24},{3... | collective-permute-start | bytes 958472 | tf_op jit(solution)/shard_map/ppermute | solution.py:690
  70.0 49.3 %collective-permute-start.26 = (bf16[512,1536]{1,0:T(8,128)(2,1)}, bf16[512,1536]{1,0:T(8,128)(2,1)}, u32[]{:S(2)}, u32[]{:S(2)}) collective-permute-start(bf16[512,1536]{1,0:T(8,128)(2,1)} %pad_maximum_fusion.6), channel_id=1, source_target_pairs={{0,2},{2,0},{4,6},{6,4},{8,10},{10,8},{12,14},{14,12},{16,18},{18,... | collective-permute-start | bytes 4718600 | tf_op jit(solution)/shard_map/ppermute | solution.py:676
  73.8 26.1 %collective-permute-start.14 = (bf16[2,96,3072]{2,1,0:T(8,128)(2,1)}, bf16[2,96,3072]{2,1,0:T(8,128)(2,1)}, u32[]{:S(2)}, u32[]{:S(2)}) collective-permute-start(bf16[2,96,3072]{2,1,0:T(8,128)(2,1)} %maximum_select_fusion), channel_id=1, source_target_pairs={{0,8},{2,10},{8,16},{10,18},{16,24},{18,26},{24,28},{26,30},{28,20... | collective-permute-start | bytes 3538952 | tf_op jit(solution)/shard_map/ppermute | solution.py:690
  75.3 25.1 %collective-permute-start.15 = (bf16[2,96,3072]{2,1,0:T(8,128)(2,1)}, bf16[2,96,3072]{2,1,0:T(8,128)(2,1)}, u32[]{:S(2)}, u32[]{:S(2)}) collective-permute-start(bf16[2,96,3072]{2,1,0:T(8,128)(2,1)} %maximum_select_fusion), channel_id=1, source_target_pairs={{0,4},{2,6},{8,0},{10,2},{16,8},{18,10},{24,16},{26,18},{28,24},{3... | collective-permute-start | bytes 3538952 | tf_op jit(solution)/shard_map/ppermute | solution.py:690
  104.0 18.6 %collective-permute-start.16 = (bf16[512,1536]{1,0:T(8,128)(2,1)}, bf16[512,1536]{1,0:T(8,128)(2,1)}, u32[]{:S(2)}, u32[]{:S(2)}) collective-permute-start(bf16[512,1536]{1,0:T(8,128)(2,1)} %convolution_convert_fusion.5), channel_id=1, source_target_pairs={{0,2},{2,0},{4,6},{6,4},{8,10},{10,8},{12,14},{14,12},{16,18},{18,... | collective-permute-start | bytes 4718600 | tf_op jit(solution)/shard_map/ppermute | solution.py:676
  105.8 28.7 %collective-permute-start.18 = (bf16[2,96,3072]{2,1,0:T(8,128)(2,1)}, bf16[2,96,3072]{2,1,0:T(8,128)(2,1)}, u32[]{:S(2)}, u32[]{:S(2)}) collective-permute-start(bf16[2,96,3072]{2,1,0:T(8,128)(2,1)} %collective-permute-done.14), channel_id=1, source_target_pairs={{0,8},{2,10},{8,16},{10,18},{16,24},{18,26},{24,28},{26,30},{28,20... | collective-permute-start | bytes 3538952 | tf_op jit(solution)/shard_map/ppermute | solution.py:690
  107.1 28.4 %collective-permute-start.19 = (bf16[2,96,3072]{2,1,0:T(8,128)(2,1)}, bf16[2,96,3072]{2,1,0:T(8,128)(2,1)}, u32[]{:S(2)}, u32[]{:S(2)}) collective-permute-start(bf16[2,96,3072]{2,1,0:T(8,128)(2,1)} %collective-permute-done.15), channel_id=1, source_target_pairs={{0,4},{2,6},{8,0},{10,2},{16,8},{18,10},{24,16},{26,18},{28,24},{3... | collective-permute-start | bytes 3538952 | tf_op jit(solution)/shard_map/ppermute | solution.py:690
  124.6 19.6 %collective-permute-start.17 = (bf16[256,1536]{1,0:T(8,128)(2,1)S(1)}, bf16[256,1536]{1,0:T(8,128)(2,1)}, u32[]{:S(2)}, u32[]{:S(2)}) collective-permute-start(bf16[256,1536]{1,0:T(8,128)(2,1)S(1)} %slice.699), channel_id=1, source_target_pairs={{0,1},{1,0},{2,3},{3,2},{4,5},{5,4},{6,7},{7,6},{8,9},{9,8},{10,11... | collective-permute-start | bytes 2359304 | tf_op jit(solution)/shard_map/ppermute | solution.py:679
  135.5 27.5 %collective-permute-start.21 = (bf16[2,96,3072]{2,1,0:T(8,128)(2,1)}, bf16[2,96,3072]{2,1,0:T(8,128)(2,1)S(1)}, u32[]{:S(2)}, u32[]{:S(2)}) collective-permute-start(bf16[2,96,3072]{2,1,0:T(8,128)(2,1)} %collective-permute-done.18), channel_id=1, source_target_pairs={{0,8},{2,10},{8,16},{10,18},{16,24},{18,26},{24,28},{26,30},{28,20... | collective-permute-start | bytes 3538952 | tf_op jit(solution)/shard_map/ppermute | solution.py:690
  136.3 27.2 %collective-permute-start.22 = (bf16[2,96,3072]{2,1,0:T(8,128)(2,1)}, bf16[2,96,3072]{2,1,0:T(8,128)(2,1)S(1)}, u32[]{:S(2)}, u32[]{:S(2)}) collective-permute-start(bf16[2,96,3072]{2,1,0:T(8,128)(2,1)} %collective-permute-done.19), channel_id=1, source_target_pairs={{0,4},{2,6},{8,0},{10,2},{16,8},{18,10},{24,16},{26,18},{28,24},{3... | collective-permute-start | bytes 3538952 | tf_op jit(solution)/shard_map/ppermute | solution.py:690
  146.6 19.5 %collective-permute-start.20 = (bf16[256,1536]{1,0:T(8,128)(2,1)S(1)}, bf16[256,1536]{1,0:T(8,128)(2,1)S(1)}, u32[]{:S(2)}, u32[]{:S(2)}) collective-permute-start(bf16[256,1536]{1,0:T(8,128)(2,1)S(1)} %multiply_convert_fusion.4), channel_id=1, source_target_pairs={{0,1},{1,0},{2,3},{3,2},{4,5},{5,4},{6,7},{7,6},{8,9},{9,8},{10,11... | collective-permute-start | bytes 2359304 | tf_op jit(solution)/shard_map/ppermute | solution.py:679
  163.5 13.9 %collective-permute-start.24 = (bf16[1,96,3072]{2,1,0:T(8,128)(2,1)S(1)}, bf16[1,96,3072]{2,1,0:T(8,128)(2,1)S(1)}, u32[]{:S(2)}, u32[]{:S(2)}) collective-permute-start(bf16[1,96,3072]{2,1,0:T(8,128)(2,1)S(1)} %slice.420), channel_id=1, source_target_pairs={{0,8},{2,10},{8,16},{10,18},{16,24},{18,26},{24,28},{26,30},{28,20... | collective-permute-start | bytes 1769480 | tf_op jit(solution)/shard_map/ppermute | solution.py:690
  164.5 13.2 %collective-permute-start.25 = (bf16[1,96,3072]{2,1,0:T(8,128)(2,1)S(1)}, bf16[1,96,3072]{2,1,0:T(8,128)(2,1)S(1)}, u32[]{:S(2)}, u32[]{:S(2)}) collective-permute-start(bf16[1,96,3072]{2,1,0:T(8,128)(2,1)S(1)} %slice.421), channel_id=1, source_target_pairs={{0,4},{2,6},{8,0},{10,2},{16,8},{18,10},{24,16},{26,18},{28,24},{3... | collective-permute-start | bytes 1769480 | tf_op jit(solution)/shard_map/ppermute | solution.py:690
  166.2 11.7 %collective-permute-start.23 = (bf16[512,1536]{1,0:T(8,128)(2,1)S(1)}, bf16[512,1536]{1,0:T(8,128)(2,1)S(1)}, u32[]{:S(2)}, u32[]{:S(2)}) collective-permute-start(bf16[512,1536]{1,0:T(8,128)(2,1)S(1)} %pad_maximum_fusion.5), channel_id=1, source_target_pairs={{0,2},{2,0},{4,6},{6,4},{8,10},{10,8},{12,14},{14,12},{16,18},{18,... | collective-permute-start | bytes 4718600 | tf_op jit(solution)/shard_map/ppermute | solution.py:676
  204.0 17.2 %collective-permute-start.27 = (bf16[1,96,1024]{2,1,0:T(8,128)(2,1)}, bf16[1,96,1024]{2,1,0:T(8,128)(2,1)S(1)}, u32[]{:S(2)}, u32[]{:S(2)}) collective-permute-start(bf16[1,96,1024]{2,1,0:T(8,128)(2,1)} %get-tuple-element.316), channel_id=1, source_target_pairs={{0,8},{2,10},{8,16},{10,18},{16,24},{18,26},{24,28},{26,30},{28,20... | collective-permute-start | bytes 589832 | tf_op jit(solution)/shard_map/ppermute | solution.py:690
  204.8 16.5 %collective-permute-start.28 = (bf16[1,96,1024]{2,1,0:T(8,128)(2,1)S(1)}, bf16[1,96,1024]{2,1,0:T(8,128)(2,1)S(1)}, u32[]{:S(2)}, u32[]{:S(2)}) collective-permute-start(bf16[1,96,1024]{2,1,0:T(8,128)(2,1)S(1)} %get-tuple-element.317), channel_id=1, source_target_pairs={{0,4},{2,6},{8,0},{10,2},{16,8},{18,10},{24,16},{26,18},{28,24},{3... | collective-permute-start | bytes 589832 | tf_op jit(solution)/shard_map/ppermute | solution.py:690
  211.2 19.5 %collective-permute-start.34 = (bf16[256,1536]{1,0:T(8,128)(2,1)}, bf16[256,1536]{1,0:T(8,128)(2,1)S(1)}, u32[]{:S(2)}, u32[]{:S(2)}) collective-permute-start(bf16[256,1536]{1,0:T(8,128)(2,1)} %slice.698), channel_id=1, source_target_pairs={{0,1},{1,0},{2,3},{3,2},{4,5},{5,4},{6,7},{7,6},{8,9},{9,8},{10,11... | collective-permute-start | bytes 2359304 | tf_op jit(solution)/shard_map/ppermute | solution.py:679
  221.4 12.0 %collective-permute-start.32 = (bf16[1,96,2048]{2,1,0:T(8,128)(2,1)S(1)}, bf16[1,96,2048]{2,1,0:T(8,128)(2,1)S(1)}, u32[]{:S(2)}, u32[]{:S(2)}) collective-permute-start(bf16[1,96,2048]{2,1,0:T(8,128)(2,1)S(1)} %get-tuple-element.306), channel_id=1, source_target_pairs={{0,8},{2,10},{8,16},{10,18},{16,24},{18,26},{24,28},{26,30},{28,20... | collective-permute-start | bytes 1179656 | tf_op jit(solution)/shard_map/ppermute | solution.py:690
  222.2 12.0 %collective-permute-start.33 = (bf16[1,96,2048]{2,1,0:T(8,128)(2,1)S(1)}, bf16[1,96,2048]{2,1,0:T(8,128)(2,1)S(1)}, u32[]{:S(2)}, u32[]{:S(2)}) collective-permute-start(bf16[1,96,2048]{2,1,0:T(8,128)(2,1)S(1)} %get-tuple-element.307), channel_id=1, source_target_pairs={{0,4},{2,6},{8,0},{10,2},{16,8},{18,10},{24,16},{26,18},{28,24},{3... | collective-permute-start | bytes 1179656 | tf_op jit(solution)/shard_map/ppermute | solution.py:690
  223.7 18.9 %collective-permute-start.31 = (bf16[2,96,1024]{2,1,0:T(8,128)(2,1)S(1)}, bf16[2,96,1024]{2,1,0:T(8,128)(2,1)S(1)}, u32[]{:S(2)}, u32[]{:S(2)}) collective-permute-start(bf16[2,96,1024]{2,1,0:T(8,128)(2,1)S(1)} %pad_maximum_fusion.15), channel_id=1, source_target_pairs={{0,4},{2,6},{8,0},{10,2},{16,8},{18,10},{24,16},{26,18},{28,24},{3... | collective-permute-start | bytes 1179656 | tf_op jit(solution)/shard_map/ppermute | solution.py:690
  225.3 17.3 %collective-permute-start.30 = (bf16[2,96,1024]{2,1,0:T(8,128)(2,1)S(1)}, bf16[2,96,1024]{2,1,0:T(8,128)(2,1)S(1)}, u32[]{:S(2)}, u32[]{:S(2)}) collective-permute-start(bf16[2,96,1024]{2,1,0:T(8,128)(2,1)S(1)} %pad_maximum_fusion.14), channel_id=1, source_target_pairs={{0,8},{2,10},{8,16},{10,18},{16,24},{18,26},{24,28},{26,30},{28,20... | collective-permute-start | bytes 1179656 | tf_op jit(solution)/shard_map/ppermute | solution.py:690
  234.5 23.3 %collective-permute-start.37 = (bf16[2,96,2048]{2,1,0:T(8,128)(2,1)S(1)}, bf16[2,96,2048]{2,1,0:T(8,128)(2,1)S(1)}, u32[]{:S(2)}, u32[]{:S(2)}) collective-permute-start(bf16[2,96,2048]{2,1,0:T(8,128)(2,1)S(1)} %pad_maximum_fusion.11), channel_id=1, source_target_pairs={{0,4},{2,6},{8,0},{10,2},{16,8},{18,10},{24,16},{26,18},{28,24},{3... | collective-permute-start | bytes 2359304 | tf_op jit(solution)/shard_map/ppermute | solution.py:690
  236.0 21.8 %collective-permute-start.36 = (bf16[2,96,2048]{2,1,0:T(8,128)(2,1)S(1)}, bf16[2,96,2048]{2,1,0:T(8,128)(2,1)S(1)}, u32[]{:S(2)}, u32[]{:S(2)}) collective-permute-start(bf16[2,96,2048]{2,1,0:T(8,128)(2,1)S(1)} %pad_maximum_fusion.10), channel_id=1, source_target_pairs={{0,8},{2,10},{8,16},{10,18},{16,24},{18,26},{24,28},{26,30},{28,20... | collective-permute-start | bytes 2359304 | tf_op jit(solution)/shard_map/ppermute | solution.py:690
  236.9 22.3 %collective-permute-start.35 = (bf16[256,1536]{1,0:T(8,128)(2,1)S(1)}, bf16[256,1536]{1,0:T(8,128)(2,1)S(1)}, u32[]{:S(2)}, u32[]{:S(2)}) collective-permute-start(bf16[256,1536]{1,0:T(8,128)(2,1)S(1)} %get-tuple-element.294), channel_id=1, source_target_pairs={{0,1},{1,0},{2,3},{3,2},{4,5},{5,4},{6,7},{7,6},{8,9},{9,8},{10,11... | collective-permute-start | bytes 2359304 | tf_op jit(solution)/shard_map/ppermute | solution.py:679
  260.7 11.5 %collective-permute-start.39 = (bf16[512,1536]{1,0:T(8,128)(2,1)}, bf16[512,1536]{1,0:T(8,128)(2,1)}, u32[]{:S(2)}, u32[]{:S(2)}) collective-permute-start(bf16[512,1536]{1,0:T(8,128)(2,1)} %convolution_convert_fusion.4), channel_id=1, source_target_pairs={{0,2},{2,0},{4,6},{6,4},{8,10},{10,8},{12,14},{14,12},{16,18},{18,... | collective-permute-start | bytes 4718600 | tf_op jit(solution)/shard_map/ppermute | solution.py:676
  263.2 13.5 %collective-permute-start.41 = (bf16[2,96,1024]{2,1,0:T(8,128)(2,1)}, bf16[2,96,1024]{2,1,0:T(8,128)(2,1)S(1)}, u32[]{:S(2)}, u32[]{:S(2)}) collective-permute-start(bf16[2,96,1024]{2,1,0:T(8,128)(2,1)} %get-tuple-element.314), channel_id=1, source_target_pairs={{0,8},{2,10},{8,16},{10,18},{16,24},{18,26},{24,28},{26,30},{28,20... | collective-permute-start | bytes 1179656 | tf_op jit(solution)/shard_map/ppermute | solution.py:690
  263.7 13.0 %collective-permute-start.42 = (bf16[2,96,1024]{2,1,0:T(8,128)(2,1)S(1)}, bf16[2,96,1024]{2,1,0:T(8,128)(2,1)S(1)}, u32[]{:S(2)}, u32[]{:S(2)}) collective-permute-start(bf16[2,96,1024]{2,1,0:T(8,128)(2,1)S(1)} %get-tuple-element.313), channel_id=1, source_target_pairs={{0,4},{2,6},{8,0},{10,2},{16,8},{18,10},{24,16},{26,18},{28,24},{3... | collective-permute-start | bytes 1179656 | tf_op jit(solution)/shard_map/ppermute | solution.py:690
  265.2 39.7 %collective-permute-start.43 = (bf16[2,96,2048]{2,1,0:T(8,128)(2,1)}, bf16[2,96,2048]{2,1,0:T(8,128)(2,1)}, u32[]{:S(2)}, u32[]{:S(2)}) collective-permute-start(bf16[2,96,2048]{2,1,0:T(8,128)(2,1)} %get-tuple-element.304), channel_id=1, source_target_pairs={{0,8},{2,10},{8,16},{10,18},{16,24},{18,26},{24,28},{26,30},{28,20... | collective-permute-start | bytes 2359304 | tf_op jit(solution)/shard_map/ppermute | solution.py:690
  265.8 39.1 %collective-permute-start.44 = (bf16[2,96,2048]{2,1,0:T(8,128)(2,1)S(1)}, bf16[2,96,2048]{2,1,0:T(8,128)(2,1)}, u32[]{:S(2)}, u32[]{:S(2)}) collective-permute-start(bf16[2,96,2048]{2,1,0:T(8,128)(2,1)S(1)} %get-tuple-element.303), channel_id=1, source_target_pairs={{0,4},{2,6},{8,0},{10,2},{16,8},{18,10},{24,16},{26,18},{28,24},{3... | collective-permute-start | bytes 2359304 | tf_op jit(solution)/shard_map/ppermute | solution.py:690
  279.0 39.4 %collective-permute-start.45 = (bf16[2,96,1024]{2,1,0:T(8,128)(2,1)}, bf16[2,96,1024]{2,1,0:T(8,128)(2,1)}, u32[]{:S(2)}, u32[]{:S(2)}) collective-permute-start(bf16[2,96,1024]{2,1,0:T(8,128)(2,1)} %get-tuple-element.312), channel_id=1, source_target_pairs={{0,8},{2,10},{8,16},{10,18},{16,24},{18,26},{24,28},{26,30},{28,20... | collective-permute-start | bytes 1179656 | tf_op jit(solution)/shard_map/ppermute | solution.py:690
  279.6 38.8 %collective-permute-start.46 = (bf16[2,96,1024]{2,1,0:T(8,128)(2,1)}, bf16[2,96,1024]{2,1,0:T(8,128)(2,1)}, u32[]{:S(2)}, u32[]{:S(2)}) collective-permute-start(bf16[2,96,1024]{2,1,0:T(8,128)(2,1)} %get-tuple-element.311), channel_id=1, source_target_pairs={{0,4},{2,6},{8,0},{10,2},{16,8},{18,10},{24,16},{26,18},{28,24},{3... | collective-permute-start | bytes 1179656 | tf_op jit(solution)/shard_map/ppermute | solution.py:690
  307.5 22.1 %collective-permute-start.47 = (bf16[2,96,2048]{2,1,0:T(8,128)(2,1)S(1)}, bf16[2,96,2048]{2,1,0:T(8,128)(2,1)S(1)}, u32[]{:S(2)}, u32[]{:S(2)}) collective-permute-start(bf16[2,96,2048]{2,1,0:T(8,128)(2,1)S(1)} %get-tuple-element.302), channel_id=1, source_target_pairs={{0,8},{2,10},{8,16},{10,18},{16,24},{18,26},{24,28},{26,30},{28,20... | collective-permute-start | bytes 2359304 | tf_op jit(solution)/shard_map/ppermute | solution.py:690
  308.2 21.6 %collective-permute-start.48 = (bf16[2,96,2048]{2,1,0:T(8,128)(2,1)S(1)}, bf16[2,96,2048]{2,1,0:T(8,128)(2,1)S(1)}, u32[]{:S(2)}, u32[]{:S(2)}) collective-permute-start(bf16[2,96,2048]{2,1,0:T(8,128)(2,1)S(1)} %get-tuple-element.301), channel_id=1, source_target_pairs={{0,4},{2,6},{8,0},{10,2},{16,8},{18,10},{24,16},{26,18},{28,24},{3... | collective-permute-start | bytes 2359304 | tf_op jit(solution)/shard_map/ppermute | solution.py:690
  309.9 21.8 %collective-permute-start.40 = (bf16[256,1536]{1,0:T(8,128)(2,1)S(1)}, bf16[256,1536]{1,0:T(8,128)(2,1)S(1)}, u32[]{:S(2)}, u32[]{:S(2)}) collective-permute-start(bf16[256,1536]{1,0:T(8,128)(2,1)S(1)} %copy-done.21), channel_id=1, source_target_pairs={{0,1},{1,0},{2,3},{3,2},{4,5},{5,4},{6,7},{7,6},{8,9},{9,8},{10,11... | collective-permute-start | bytes 2359304 | tf_op jit(solution)/shard_map/ppermute | solution.py:679
  321.8 11.8 %collective-permute-start.53 = (bf16[1,96,896]{2,1,0:T(8,128)(2,1)S(1)}, bf16[1,96,896]{2,1,0:T(8,128)(2,1)S(1)}, u32[]{:S(2)}, u32[]{:S(2)}) collective-permute-start(bf16[1,96,896]{2,1,0:T(8,128)(2,1)S(1)} %get-tuple-element.200), channel_id=1, source_target_pairs={{0,8},{2,10},{8,16},{10,18},{16,24},{18,26},{24,28},{26,30},{28,20... | collective-permute-start | bytes 516104 | tf_op jit(solution)/shard_map/ppermute | solution.py:690
  327.1 8.0 %collective-permute-start.54 = (bf16[1,96,896]{2,1,0:T(8,128)(2,1)S(1)}, bf16[1,96,896]{2,1,0:T(8,128)(2,1)S(1)}, u32[]{:S(2)}, u32[]{:S(2)}) collective-permute-start(bf16[1,96,896]{2,1,0:T(8,128)(2,1)S(1)} %get-tuple-element.201), channel_id=1, source_target_pairs={{0,4},{2,6},{8,0},{10,2},{16,8},{18,10},{24,16},{26,18},{28,24},{3... | collective-permute-start | bytes 516104 | tf_op jit(solution)/shard_map/ppermute | solution.py:690
  329.6 13.8 %collective-permute-start.49 = (bf16[512,1536]{1,0:T(8,128)(2,1)S(1)}, bf16[512,1536]{1,0:T(8,128)(2,1)S(1)}, u32[]{:S(2)}, u32[]{:S(2)}) collective-permute-start(bf16[512,1536]{1,0:T(8,128)(2,1)S(1)} %fusion.13), channel_id=1, source_target_pairs={{0,2},{2,0},{4,6},{6,4},{8,10},{10,8},{12,14},{14,12},{16,18},{18,... | collective-permute-start | bytes 4718600 | tf_op jit(solution)/shard_map/ppermute | solution.py:676
  331.4 14.1 %collective-permute-start.74 = (bf16[96,2048]{1,0:T(8,128)(2,1)S(1)}, bf16[96,2048]{1,0:T(8,128)(2,1)S(1)}, u32[]{:S(2)}, u32[]{:S(2)}) collective-permute-start(bf16[96,2048]{1,0:T(8,128)(2,1)S(1)} %dynamic-slice_convert_fusion), channel_id=1, source_target_pairs={{0,2},{2,0},{4,6},{6,4},{8,10},{10,8},{12,14},{14,12},{16,18},{18,... | collective-permute-start | bytes 1179656 | tf_op jit(solution)/shard_map/ppermute | solution.py:676
  333.0 8.1 %collective-permute-start.51 = (bf16[1,96,768]{2,1,0:T(8,128)(2,1)S(1)}, bf16[1,96,768]{2,1,0:T(8,128)(2,1)S(1)}, u32[]{:S(2)}, u32[]{:S(2)}) collective-permute-start(bf16[1,96,768]{2,1,0:T(8,128)(2,1)S(1)} %get-tuple-element.205), channel_id=1, source_target_pairs={{0,8},{2,10},{8,16},{10,18},{16,24},{18,26},{24,28},{26,30},{28,20... | collective-permute-start | bytes 442376 | tf_op jit(solution)/shard_map/ppermute | solution.py:690
  333.6 8.2 %collective-permute-start.52 = (bf16[1,96,768]{2,1,0:T(8,128)(2,1)S(1)}, bf16[1,96,768]{2,1,0:T(8,128)(2,1)S(1)}, u32[]{:S(2)}, u32[]{:S(2)}) collective-permute-start(bf16[1,96,768]{2,1,0:T(8,128)(2,1)S(1)} %get-tuple-element.206), channel_id=1, source_target_pairs={{0,4},{2,6},{8,0},{10,2},{16,8},{18,10},{24,16},{26,18},{28,24},{3... | collective-permute-start | bytes 442376 | tf_op jit(solution)/shard_map/ppermute | solution.py:690
  335.2 27.7 %collective-permute-start.57 = (bf16[2,96,896]{2,1,0:T(8,128)(2,1)S(1)}, bf16[2,96,896]{2,1,0:T(8,128)(2,1)S(1)}, u32[]{:S(2)}, u32[]{:S(2)}) collective-permute-start(bf16[2,96,896]{2,1,0:T(8,128)(2,1)S(1)} %pad_maximum_fusion.17), channel_id=1, source_target_pairs={{0,4},{2,6},{8,0},{10,2},{16,8},{18,10},{24,16},{26,18},{28,24},{3... | collective-permute-start | bytes 1032200 | tf_op jit(solution)/shard_map/ppermute | solution.py:690
  341.1 21.9 %collective-permute-start.56 = (bf16[2,96,896]{2,1,0:T(8,128)(2,1)S(1)}, bf16[2,96,896]{2,1,0:T(8,128)(2,1)S(1)}, u32[]{:S(2)}, u32[]{:S(2)}) collective-permute-start(bf16[2,96,896]{2,1,0:T(8,128)(2,1)S(1)} %pad_maximum_fusion.16), channel_id=1, source_target_pairs={{0,8},{2,10},{8,16},{10,18},{16,24},{18,26},{24,28},{26,30},{28,20... | collective-permute-start | bytes 1032200 | tf_op jit(solution)/shard_map/ppermute | solution.py:690
  341.9 23.3 %collective-permute-start.62 = (bf16[2,96,768]{2,1,0:T(8,128)(2,1)S(1)}, bf16[2,96,768]{2,1,0:T(8,128)(2,1)S(1)}, u32[]{:S(2)}, u32[]{:S(2)}) collective-permute-start(bf16[2,96,768]{2,1,0:T(8,128)(2,1)S(1)} %pad_maximum_fusion.19), channel_id=1, source_target_pairs={{0,4},{2,6},{8,0},{10,2},{16,8},{18,10},{24,16},{26,18},{28,24},{3... | collective-permute-start | bytes 884744 | tf_op jit(solution)/shard_map/ppermute | solution.py:690
  343.9 18.4 %collective-permute-start.50 = (bf16[256,1536]{1,0:T(8,128)(2,1)S(1)}, bf16[256,1536]{1,0:T(8,128)(2,1)S(1)}, u32[]{:S(2)}, u32[]{:S(2)}) collective-permute-start(bf16[256,1536]{1,0:T(8,128)(2,1)S(1)} %slice.696), channel_id=1, source_target_pairs={{0,1},{1,0},{2,3},{3,2},{4,5},{5,4},{6,7},{7,6},{8,9},{9,8},{10,11... | collective-permute-start | bytes 2359304 | tf_op jit(solution)/shard_map/ppermute | solution.py:679
  345.5 19.7 %collective-permute-start.61 = (bf16[2,96,768]{2,1,0:T(8,128)(2,1)S(1)}, bf16[2,96,768]{2,1,0:T(8,128)(2,1)S(1)}, u32[]{:S(2)}, u32[]{:S(2)}) collective-permute-start(bf16[2,96,768]{2,1,0:T(8,128)(2,1)S(1)} %pad_maximum_fusion.18), channel_id=1, source_target_pairs={{0,8},{2,10},{8,16},{10,18},{16,24},{18,26},{24,28},{26,30},{28,20... | collective-permute-start | bytes 884744 | tf_op jit(solution)/shard_map/ppermute | solution.py:690
  363.1 12.1 %collective-permute-start.58 = (bf16[2,96,896]{2,1,0:T(8,128)(2,1)S(1)}, bf16[2,96,896]{2,1,0:T(8,128)(2,1)S(1)}, u32[]{:S(2)}, u32[]{:S(2)}) collective-permute-start(bf16[2,96,896]{2,1,0:T(8,128)(2,1)S(1)} %get-tuple-element.324), channel_id=1, source_target_pairs={{0,8},{2,10},{8,16},{10,18},{16,24},{18,26},{24,28},{26,30},{28,20... | collective-permute-start | bytes 1032200 | tf_op jit(solution)/shard_map/ppermute | solution.py:690
  363.9 11.4 %collective-permute-start.59 = (bf16[2,96,896]{2,1,0:T(8,128)(2,1)S(1)}, bf16[2,96,896]{2,1,0:T(8,128)(2,1)S(1)}, u32[]{:S(2)}, u32[]{:S(2)}) collective-permute-start(bf16[2,96,896]{2,1,0:T(8,128)(2,1)S(1)} %get-tuple-element.323), channel_id=1, source_target_pairs={{0,4},{2,6},{8,0},{10,2},{16,8},{18,10},{24,16},{26,18},{28,24},{3... | collective-permute-start | bytes 1032200 | tf_op jit(solution)/shard_map/ppermute | solution.py:690
  365.2 9.9 %collective-permute-start.55 = (f32[8,1536]{1,0:T(8,128)S(1)}, f32[8,1536]{1,0:T(8,128)S(1)}, u32[]{:S(2)}, u32[]{:S(2)}) collective-permute-start(f32[8,1536]{1,0:T(8,128)S(1)} %pad_maximum_fusion.21), channel_id=1, source_target_pairs={{0,4},{2,6},{4,0},{6,2},{8,12},{10,14},{12,8},{14,10},{16,20},{18,... | collective-permute-start | bytes 147464 | tf_op jit(solution)/shard_map/ppermute | solution.py:702
  366.9 13.5 %collective-permute-start.63 = (bf16[2,96,768]{2,1,0:T(8,128)(2,1)S(1)}, bf16[2,96,768]{2,1,0:T(8,128)(2,1)S(1)}, u32[]{:S(2)}, u32[]{:S(2)}) collective-permute-start(bf16[2,96,768]{2,1,0:T(8,128)(2,1)S(1)} %get-tuple-element.334), channel_id=1, source_target_pairs={{0,8},{2,10},{8,16},{10,18},{16,24},{18,26},{24,28},{26,30},{28,20... | collective-permute-start | bytes 884744 | tf_op jit(solution)/shard_map/ppermute | solution.py:690
  368.3 12.2 %collective-permute-start.64 = (bf16[2,96,768]{2,1,0:T(8,128)(2,1)S(1)}, bf16[2,96,768]{2,1,0:T(8,128)(2,1)S(1)}, u32[]{:S(2)}, u32[]{:S(2)}) collective-permute-start(bf16[2,96,768]{2,1,0:T(8,128)(2,1)S(1)} %get-tuple-element.333), channel_id=1, source_target_pairs={{0,4},{2,6},{8,0},{10,2},{16,8},{18,10},{24,16},{26,18},{28,24},{3... | collective-permute-start | bytes 884744 | tf_op jit(solution)/shard_map/ppermute | solution.py:690
  384.5 14.3 %collective-permute-start.68 = (bf16[2,96,896]{2,1,0:T(8,128)(2,1)}, bf16[2,96,896]{2,1,0:T(8,128)(2,1)S(1)}, u32[]{:S(2)}, u32[]{:S(2)}) collective-permute-start(bf16[2,96,896]{2,1,0:T(8,128)(2,1)} %get-tuple-element.322), channel_id=1, source_target_pairs={{0,8},{2,10},{8,16},{10,18},{16,24},{18,26},{24,28},{26,30},{28,20... | collective-permute-start | bytes 1032200 | tf_op jit(solution)/shard_map/ppermute | solution.py:690
  386.8 12.8 %collective-permute-start.69 = (bf16[2,96,896]{2,1,0:T(8,128)(2,1)}, bf16[2,96,896]{2,1,0:T(8,128)(2,1)}, u32[]{:S(2)}, u32[]{:S(2)}) collective-permute-start(bf16[2,96,896]{2,1,0:T(8,128)(2,1)} %get-tuple-element.321), channel_id=1, source_target_pairs={{0,4},{2,6},{8,0},{10,2},{16,8},{18,10},{24,16},{26,18},{28,24},{3... | collective-permute-start | bytes 1032200 | tf_op jit(solution)/shard_map/ppermute | solution.py:690
  386.8 9.2 %collective-permute-start.71 = (bf16[2,96,768]{2,1,0:T(8,128)(2,1)}, bf16[2,96,768]{2,1,0:T(8,128)(2,1)S(1)}, u32[]{:S(2)}, u32[]{:S(2)}) collective-permute-start(bf16[2,96,768]{2,1,0:T(8,128)(2,1)} %get-tuple-element.332), channel_id=1, source_target_pairs={{0,8},{2,10},{8,16},{10,18},{16,24},{18,26},{24,28},{26,30},{28,20... | collective-permute-start | bytes 884744 | tf_op jit(solution)/shard_map/ppermute | solution.py:690
  388.8 8.8 %collective-permute-start.72 = (bf16[2,96,768]{2,1,0:T(8,128)(2,1)}, bf16[2,96,768]{2,1,0:T(8,128)(2,1)}, u32[]{:S(2)}, u32[]{:S(2)}) collective-permute-start(bf16[2,96,768]{2,1,0:T(8,128)(2,1)} %get-tuple-element.331), channel_id=1, source_target_pairs={{0,4},{2,6},{8,0},{10,2},{16,8},{18,10},{24,16},{26,18},{28,24},{3... | collective-permute-start | bytes 884744 | tf_op jit(solution)/shard_map/ppermute | solution.py:690
  (61 other events, 627.8 us)
